TPU v7x, 32 devices: a whole 2x2x4 slice. The times are simulated.
32 devices in a mesh: dp: 8 (over z, y), mp: 4 (over x, core).
Axes of the slice: x: 2, y: 2, z: 4, core: 2. Of those that a mesh axis runs over, the one named last changes fastest.
Arguments:
- tokens: bfloat16 [16384, 1024], P(('dp', 'mp')), may hold values from -6 to 6
- memory: bfloat16 [16384, 1024], P(('dp', 'mp')), may hold values from -6 to 6
- cotangent: bfloat16 [16384, 1024], P(('dp', 'mp')), may hold values from -6 to 6
- target_lengths: int32 [16], P('dp'), may hold values from 1 to 1024, as said below
- memory_lengths: int32 [16], P('dp'), may hold values from 1 to 1024, as said below
- self_inputs: bfloat16 [3, 1024, 1024], P(None, None, 'mp'), may hold values from -0.176776695 to 0.176776695
- self_output: bfloat16 [1024, 1024], P('mp'), may hold values from -2 to 2
- cross_query: bfloat16 [1024, 1024], P(None, 'mp'), may hold values from -0.176776695 to 0.176776695
- cross_memory: bfloat16 [2, 1024, 1024], P(None, None, 'mp'), may hold values from -0.176776695 to 0.176776695
- cross_output: bfloat16 [1024, 1024], P('mp'), may hold values from -2 to 2
- feed_in: bfloat16 [1024, 4096], P(None, 'mp'), may hold values from -0.125 to 0.125
- feed_out: bfloat16 [4096, 1024], P('mp'), may hold values from -0.35355339 to 0.35355339
- proj_bias: bfloat16 [4, 1024], P(None, 'mp'), may hold values from -3 to 3
- feed_bias: bfloat16 [4096], P('mp'), may hold values from -3 to 3
- branch_bias: float32 [3, 1024], replicated, may hold values from -5 to 5
- norm_gain: float32 [3, 1024], replicated, may hold values from 0.25 to 1.75
- norm_shift: float32 [3, 1024], replicated, may hold values from -3 to 3
Outputs:
- block_out: bfloat16 [16384, 1024], P(('dp', 'mp'))
- grad_tokens: bfloat16 [16384, 1024], P(('dp', 'mp'))
- grad_memory: bfloat16 [16384, 1024], P(('dp', 'mp'))
- grad_self_inputs: float32 [3, 1024, 1024], P(None, None, 'mp')
- grad_self_output: float32 [1024, 1024], P('mp')
- grad_cross_query: float32 [1024, 1024], P(None, 'mp')
- grad_cross_memory: float32 [2, 1024, 1024], P(None, None, 'mp')
- grad_cross_output: float32 [1024, 1024], P('mp')
- grad_feed_in: float32 [1024, 4096], P(None, 'mp')
- grad_feed_out: float32 [4096, 1024], P('mp')
- grad_proj_bias: float32 [4, 1024], P(None, 'mp')
- grad_feed_bias: float32 [4096], P('mp')
- grad_branch_bias: float32 [3, 1024], P(None, 'mp')
- grad_norm_gain: float32 [3, 1024], P(None, 'mp')
- grad_norm_shift: float32 [3, 1024], P(None, 'mp')
Inputs may be any that keep to these rules, and one draw needn't show every extreme that they name: `target_lengths`: real target rows of each sequence; rows beyond it are padding whose keys are masked. In every group of 2 sequences on one index of dp, one sequence has exactly 1024 rows. `memory_lengths`: real memory rows of each sequence; in every group of 2 sequences on one index of dp, one has exactly 1024 rows.
All inputs are finite; a program needn't handle non-finite values.
Results may differ from a plain program's by a relative error of at most 0.03.
Values may be sent and summed in bfloat16 or wider, within the bound.
A program may use at most 256 MiB of HBM per device.

v0:
```python
import jax
import jax.numpy as jnp
from jax import lax
from jax.sharding import PartitionSpec as P

HEAD_DIM = 64
LEN = 1024
MLEN = 1024


residual_scale = 300.0**0.25
norm_epsilon = 1e-05


def project(rows, weight):
    return jnp.dot(rows, weight, preferred_element_type=jnp.float32)


def project_back(grads, weight):
    return lax.dot_general(
        grads, weight, (((1,), (1,)), ((), ())), preferred_element_type=jnp.float32
    )


def weight_grad(rows, grads):
    return lax.dot_general(
        rows, grads, (((0,), (0,)), ((), ())), preferred_element_type=jnp.float32
    )


def column_sums(rows):
    return jnp.sum(rows, axis=0, dtype=jnp.float32)


def gelu_exact(pre_rows):
    return jax.nn.gelu(pre_rows, approximate=False)


def gelu_backward(pre_rows, grad_rows):
    unused, pullback = jax.vjp(gelu_exact, pre_rows)
    return pullback(grad_rows)[0]


def norm_forward(summed, gain_row, shift_row):
    row_mean = jnp.mean(summed, axis=-1, keepdims=True)
    centred = summed - row_mean
    variance = jnp.mean(centred * centred, axis=-1, keepdims=True)
    inverse = lax.rsqrt(variance + norm_epsilon)
    unit_rows = centred * inverse
    return (unit_rows * gain_row + shift_row, unit_rows, inverse)


def norm_backward(grad_out, unit_rows, inverse, gain_row):
    grad_unit = grad_out * gain_row
    first_mean = jnp.mean(grad_unit, axis=-1, keepdims=True)
    second_mean = jnp.mean(grad_unit * unit_rows, axis=-1, keepdims=True)
    return inverse * (grad_unit - first_mean - unit_rows * second_mean)


def allowed_mask(rows_q, rows_k, length, causal):
    query_pos = jnp.arange(rows_q, dtype=jnp.int32)[:, None]
    key_pos = jnp.arange(rows_k, dtype=jnp.int32)[None, :]
    allowed = key_pos < length
    if causal:
        allowed = allowed & (key_pos <= query_pos)
    return allowed


def masked_scores(queries, key_rows, allowed):
    scores = jnp.einsum(
        "qhd,khd->hqk", queries, key_rows, preferred_element_type=jnp.float32
    ) * HEAD_DIM ** (-0.5)
    return jnp.where(allowed[None], scores, -1e30)


def attend_forward(queries, key_rows, values, allowed):
    scores = masked_scores(queries, key_rows, allowed)
    row_max = jnp.max(scores, axis=-1, keepdims=True)
    exp_scores = jnp.exp(scores - row_max)
    row_total = jnp.sum(exp_scores, axis=-1, keepdims=True)
    attn_prob = exp_scores / row_total
    mixed_rows = jnp.einsum(
        "hqk,khd->qhd", attn_prob.astype(jnp.bfloat16), values, preferred_element_type=jnp.float32
    )
    return (mixed_rows.astype(jnp.bfloat16), row_max + jnp.log(row_total))


def attend_backward(queries, key_rows, values, grad_mixed, log_total, allowed):
    scores = masked_scores(queries, key_rows, allowed)
    attn_prob = jnp.exp(scores - log_total)
    grad_values = jnp.einsum(
        "hqk,qhd->khd",
        attn_prob.astype(jnp.bfloat16),
        grad_mixed,
        preferred_element_type=jnp.float32,
    )
    grad_prob = jnp.einsum("qhd,khd->hqk", grad_mixed, values, preferred_element_type=jnp.float32)
    grad_scores = attn_prob * (grad_prob - jnp.sum(grad_prob * attn_prob, axis=-1, keepdims=True))
    grad_low = grad_scores.astype(jnp.bfloat16)
    grad_queries = jnp.einsum(
        "hqk,khd->qhd", grad_low, key_rows, preferred_element_type=jnp.float32
    ) * HEAD_DIM ** (-0.5)
    grad_keys = jnp.einsum(
        "hqk,qhd->khd", grad_low, queries, preferred_element_type=jnp.float32
    ) * HEAD_DIM ** (-0.5)
    return (grad_queries, grad_keys, grad_values)


def split_heads(rows, seq_count, length):
    return rows.reshape(seq_count, length, rows.shape[1] // HEAD_DIM, HEAD_DIM)


def attention_forward(queries, key_rows, values, lengths, causal, key_len):
    seq_count = lengths.shape[0]

    def one_seq(packed):
        query_blk, key_blk, value_blk, length = packed
        return attend_forward(
            query_blk, key_blk, value_blk, allowed_mask(LEN, key_len, length, causal)
        )

    mixed_rows, log_total = lax.map(
        one_seq,
        (
            split_heads(queries, seq_count, LEN),
            split_heads(key_rows, seq_count, key_len),
            split_heads(values, seq_count, key_len),
            lengths,
        ),
    )
    return (mixed_rows.reshape(seq_count * LEN, queries.shape[1]), log_total)


def attention_backward(queries, key_rows, values, grad_mixed, log_total, lengths, causal, key_len):
    seq_count = lengths.shape[0]
    width = queries.shape[1]

    def one_seq(packed):
        query_blk, key_blk, value_blk, grad_blk, total_blk, length = packed
        return attend_backward(
            query_blk,
            key_blk,
            value_blk,
            grad_blk,
            total_blk,
            allowed_mask(LEN, key_len, length, causal),
        )

    grad_q, grad_k, grad_v = lax.map(
        one_seq,
        (
            split_heads(queries, seq_count, LEN),
            split_heads(key_rows, seq_count, key_len),
            split_heads(values, seq_count, key_len),
            split_heads(grad_mixed, seq_count, LEN),
            log_total,
            lengths,
        ),
    )
    return (
        grad_q.reshape(seq_count * LEN, width).astype(jnp.bfloat16),
        grad_k.reshape(seq_count * key_len, width).astype(jnp.bfloat16),
        grad_v.reshape(seq_count * key_len, width).astype(jnp.bfloat16),
    )


def gather_rows(rows):
    return lax.all_gather(rows, "mp", axis=0, tiled=True)


def sum_rows(partial_value):
    return lax.psum_scatter(partial_value, "mp", scatter_dimension=0, tiled=True)


def gather_grads(grads):
    return lax.all_gather(grads, "mp", axis=0, tiled=True)


def sum_input_grads(partial_value):
    return lax.psum_scatter(
        partial_value.astype(jnp.bfloat16), "mp", scatter_dimension=0, tiled=True
    ).astype(jnp.float32)


def on_device(
    tokens,
    memory,
    cotangent,
    target_lengths,
    memory_lengths,
    self_inputs,
    self_output,
    cross_query,
    cross_memory,
    cross_output,
    feed_in,
    feed_out,
    proj_bias,
    feed_bias,
    branch_bias,
    norm_gain,
    norm_shift,
):
    low_type = jnp.bfloat16
    token_all = gather_rows(tokens)
    self_q = (project(token_all, self_inputs[0]) + proj_bias[0]).astype(low_type)
    self_k = project(token_all, self_inputs[1]).astype(low_type)
    self_v = (project(token_all, self_inputs[2]) + proj_bias[1]).astype(low_type)
    self_mixed, self_total = attention_forward(self_q, self_k, self_v, target_lengths, True, LEN)
    branch_one = sum_rows(project(self_mixed, self_output)) + branch_bias[0]
    normed_one, unit_one, inverse_one = norm_forward(
        residual_scale * tokens.astype(jnp.float32) + branch_one, norm_gain[0], norm_shift[0]
    )
    second_all = gather_rows(normed_one.astype(low_type))
    memory_all = lax.all_gather(memory, "mp", axis=0, tiled=True)
    cross_q = (project(second_all, cross_query) + proj_bias[2]).astype(low_type)
    cross_k = project(memory_all, cross_memory[0]).astype(low_type)
    cross_v = (project(memory_all, cross_memory[1]) + proj_bias[3]).astype(low_type)
    cross_mixed, cross_total = attention_forward(
        cross_q, cross_k, cross_v, memory_lengths, False, MLEN
    )
    branch_two = sum_rows(project(cross_mixed, cross_output)) + branch_bias[1]
    normed_two, unit_two, inverse_two = norm_forward(
        residual_scale * normed_one + branch_two, norm_gain[1], norm_shift[1]
    )
    third_low = normed_two.astype(low_type)
    third_all = gather_rows(third_low)
    hidden_pre = project(third_all, feed_in) + feed_bias
    hidden = gelu_exact(hidden_pre).astype(low_type)
    branch_three = sum_rows(project(hidden, feed_out)) + branch_bias[2]
    normed_three, unit_three, inverse_three = norm_forward(
        residual_scale * normed_two + branch_three, norm_gain[2], norm_shift[2]
    )
    block_out = normed_three.astype(low_type)
    cot_rows = cotangent.astype(jnp.float32)
    gain_three = jnp.sum(cot_rows * unit_three, axis=0)
    shift_three = jnp.sum(cot_rows, axis=0)
    grad_three = norm_backward(cot_rows, unit_three, inverse_three, norm_gain[2])
    grad_branch_three = grad_three.astype(low_type)
    bias_three = column_sums(grad_branch_three)
    grad_all_three = gather_grads(grad_branch_three)
    grad_hidden = project_back(grad_all_three, feed_out)
    grad_feed_out = weight_grad(hidden, grad_all_three)
    grad_pre = gelu_backward(hidden_pre, grad_hidden).astype(low_type)
    grad_feed_bias = column_sums(grad_pre)
    grad_feed_in = weight_grad(third_all, grad_pre)
    grad_normed_two = residual_scale * grad_three + sum_input_grads(project_back(grad_pre, feed_in))
    gain_two = jnp.sum(grad_normed_two * unit_two, axis=0)
    shift_two = jnp.sum(grad_normed_two, axis=0)
    grad_two = norm_backward(grad_normed_two, unit_two, inverse_two, norm_gain[1])
    grad_branch_two = grad_two.astype(low_type)
    bias_two = column_sums(grad_branch_two)
    grad_all_two = gather_grads(grad_branch_two)
    grad_cross_mixed = project_back(grad_all_two, cross_output).astype(low_type)
    grad_cross_output = weight_grad(cross_mixed, grad_all_two)
    cross_dq, cross_dk, cross_dv = attention_backward(
        cross_q, cross_k, cross_v, grad_cross_mixed, cross_total, memory_lengths, False, MLEN
    )
    grad_cross_query = weight_grad(second_all, cross_dq)
    grad_cross_memory = jnp.stack(
        [weight_grad(memory_all, cross_dk), weight_grad(memory_all, cross_dv)]
    )
    cross_bias_rows = jnp.stack([column_sums(cross_dq), column_sums(cross_dv)])
    memory_part = project_back(cross_dk, cross_memory[0]) + project_back(cross_dv, cross_memory[1])
    grad_memory = (
        lax.psum_scatter(memory_part.astype(jnp.bfloat16), "mp", scatter_dimension=0, tiled=True)
        .astype(jnp.float32)
        .astype(low_type)
    )
    grad_normed_one = residual_scale * grad_two + sum_input_grads(
        project_back(cross_dq, cross_query)
    )
    gain_one = jnp.sum(grad_normed_one * unit_one, axis=0)
    shift_one = jnp.sum(grad_normed_one, axis=0)
    grad_one = norm_backward(grad_normed_one, unit_one, inverse_one, norm_gain[0])
    grad_branch_one = grad_one.astype(low_type)
    bias_one = column_sums(grad_branch_one)
    grad_all_one = gather_grads(grad_branch_one)
    grad_self_mixed = project_back(grad_all_one, self_output).astype(low_type)
    grad_self_output = weight_grad(self_mixed, grad_all_one)
    self_dq, self_dk, self_dv = attention_backward(
        self_q, self_k, self_v, grad_self_mixed, self_total, target_lengths, True, LEN
    )
    grad_self_inputs = jnp.stack(
        [
            weight_grad(token_all, self_dq),
            weight_grad(token_all, self_dk),
            weight_grad(token_all, self_dv),
        ]
    )
    self_bias_rows = jnp.stack([column_sums(self_dq), column_sums(self_dv)])
    token_part = (
        project_back(self_dq, self_inputs[0])
        + project_back(self_dk, self_inputs[1])
        + project_back(self_dv, self_inputs[2])
    )
    grad_tokens = (residual_scale * grad_one + sum_input_grads(token_part)).astype(low_type)
    token_terms = jnp.stack(
        [
            bias_one,
            bias_two,
            bias_three,
            gain_one,
            gain_two,
            gain_three,
            shift_one,
            shift_two,
            shift_three,
        ]
    )
    token_share = lax.psum_scatter(
        token_terms.astype(jnp.bfloat16), "mp", scatter_dimension=1, tiled=True
    ).astype(jnp.float32)
    (
        grad_self_inputs,
        grad_self_output,
        self_bias_rows,
        token_share,
        grad_cross_query,
        grad_cross_memory,
        grad_cross_output,
        cross_bias_rows,
        grad_feed_in,
        grad_feed_bias,
        grad_feed_out,
    ) = (
        lax.psum(grad_self_inputs.astype(jnp.bfloat16), "dp").astype(jnp.float32),
        lax.psum(grad_self_output.astype(jnp.bfloat16), "dp").astype(jnp.float32),
        lax.psum(self_bias_rows.astype(jnp.bfloat16), "dp").astype(jnp.float32),
        lax.psum(token_share.astype(jnp.bfloat16), "dp").astype(jnp.float32),
        lax.psum(grad_cross_query.astype(jnp.bfloat16), "dp").astype(jnp.float32),
        lax.psum(grad_cross_memory.astype(jnp.bfloat16), "dp").astype(jnp.float32),
        lax.psum(grad_cross_output.astype(jnp.bfloat16), "dp").astype(jnp.float32),
        lax.psum(cross_bias_rows.astype(jnp.bfloat16), "dp").astype(jnp.float32),
        lax.psum(grad_feed_in.astype(jnp.bfloat16), "dp").astype(jnp.float32),
        lax.psum(grad_feed_bias.astype(jnp.bfloat16), "dp").astype(jnp.float32),
        lax.psum(grad_feed_out.astype(jnp.bfloat16), "dp").astype(jnp.float32),
    )
    grad_proj_bias = jnp.concatenate([self_bias_rows, cross_bias_rows], axis=0)
    return (
        block_out,
        grad_tokens,
        grad_memory,
        grad_self_inputs,
        grad_self_output,
        grad_cross_query,
        grad_cross_memory,
        grad_cross_output,
        grad_feed_in,
        grad_feed_out,
        grad_proj_bias,
        grad_feed_bias,
        token_share[0:3],
        token_share[3:6],
        token_share[6:9],
    )


def solution(mesh):
    in_specs = (
        P(("dp", "mp"), None),
        P(("dp", "mp"), None),
        P(("dp", "mp"), None),
        P("dp"),
        P("dp"),
        P(None, None, "mp"),
        P("mp", None),
        P(None, "mp"),
        P(None, None, "mp"),
        P("mp", None),
        P(None, "mp"),
        P("mp", None),
        P(None, "mp"),
        P("mp"),
        P(),
        P(),
        P(),
    )
    out_specs = (
        P(("dp", "mp"), None),
        P(("dp", "mp"), None),
        P(("dp", "mp"), None),
        P(None, None, "mp"),
        P("mp", None),
        P(None, "mp"),
        P(None, None, "mp"),
        P("mp", None),
        P(None, "mp"),
        P("mp", None),
        P(None, "mp"),
        P("mp"),
        P(None, "mp"),
        P(None, "mp"),
        P(None, "mp"),
    )
    return jax.shard_map(
        on_device, mesh=mesh, in_specs=in_specs, out_specs=out_specs, check_vma=False
    )
```

profile of v0, /device:TPU:0, one launch (start us, length us, event | category | flops | bytes accessed | tf_op | source)
XLA Modules:
  0.0 1317.1 jit_solution(9208455889316457536)
XLA Ops:
  9.4 37.4 %all-gather.8.cloned.1.call-done = bf16[2048,1024]{1,0:T(8,128)(2,1)} async-done(((bf16[512,1024]{1,0:T(8,128)(2,1)}), bf16[2048,1024]{1,0:T(8,128)(2,1)}) %all-gather.8.cloned.1.call-update) | async-done | bytes 4194320 | tf_op jit(solution)/shard_map/all_gather | solution.py:168
  78.6 31.4 %while.52 = (s32[]{:T(128)}, bf16[2,1024,4,64]{1,3,2,0:T(8,128)(2,1)}, f32[2,4,1024,1]{2,1,3,0:T(4,128)S(1)}, bf16[2,1024,4,64]{1,3,2,0:T(8,128)(2,1)S(1)}, s32[...) while((s32[]{:T(128)}, ...), condition=%wide.region_3.4_spmd, body=%wide.region_0.3_spmd.sunk | while | flops 1126429696 | bytes 65147048 | solution.py:122
  121.7 68.8 %reduce-scatter.9.cloned.1.call-done = f32[512,1024]{1,0:T(8,128)} async-done(((f32[2048,1024]{1,0:T(8,128)}), f32[512,1024]{1,0:T(8,128)}) %reduce-scatter.9.cloned.1.call-update) | async-done | bytes 2097168 | tf_op jit(solution)/shard_map/reduce_scatter | solution.py:172
  195.3 31.4 %all-gather.10.cloned.1.call-done = bf16[2048,1024]{1,0:T(8,128)(2,1)} async-done(((bf16[512,1024]{1,0:T(8,128)(2,1)}), bf16[2048,1024]{1,0:T(8,128)(2,1)}) %all-gather.10.cloned.1.call-update) | async-done | bytes 4194320 | tf_op jit(solution)/shard_map/all_gather | solution.py:215
  251.4 11.8 all-gather.12.cloned.1.call-done
  277.4 29.4 %while.53 = (s32[]{:T(128)}, bf16[2,1024,4,64]{1,3,2,0:T(8,128)(2,1)}, f32[2,4,1024,1]{2,1,3,0:T(4,128)S(1)}, bf16[2,1024,4,64]{1,3,2,0:T(8,128)(2,1)}, s32[2]{0...) while((s32[]{:T(128)}, ...), condition=%wide.region_10.11_spmd, body=%wide.region_7.10_spmd.sunk | while | flops 1124332544 | bytes 65149124 | solution.py:122
  315.2 71.6 %reduce-scatter.11.cloned.1.call-done = f32[512,1024]{1,0:T(8,128)} async-done(((f32[2048,1024]{1,0:T(8,128)}), f32[512,1024]{1,0:T(8,128)}) %reduce-scatter.11.cloned.1.call-update) | async-done | bytes 2097168 | tf_op jit(solution)/shard_map/reduce_scatter | solution.py:172
  392.7 34.6 %all-gather.14.cloned.1.call-done = bf16[2048,1024]{1,0:T(8,128)(2,1)} async-done(((bf16[512,1024]{1,0:T(8,128)(2,1)}), bf16[2048,1024]{1,0:T(8,128)(2,1)}) %all-gather.14.cloned.1.call-update) | async-done | bytes 4194320 | tf_op jit(solution)/shard_map/all_gather | solution.py:168
  427.3 25.5 %multiply_convert_fusion.2 = (bf16[2048,1024]{1,0:T(8,128)(2,1)S(1)}, f32[2048,1024]{1,0:T(8,128)}, f32[2048,1024]{1,0:T(8,128)}) fusion(f32[1024]{0:T(1024)S(1)} %convert_element_type.253, bf16[2048,1024]{1,0:T(8,128)(2,1)} %all-gather.14.cloned.1.call-done, bf16[1024,1024]{1,0:T(8,128)(2,1)S(1)} %copy-done), kind=kOutput, calls=%fused_computation.123 | convolution fusion | flops 4433379328 | bytes 27267072 | tf_op jit(solution)/shard_map/dot_general | solution.py:16
  461.5 71.8 %reduce-scatter.13.cloned.1.call-done = f32[512,1024]{1,0:T(8,128)} async-done(((f32[2048,1024]{1,0:T(8,128)}), f32[512,1024]{1,0:T(8,128)}) %reduce-scatter.13.cloned.1.call-update) | async-done | bytes 2097168 | tf_op jit(solution)/shard_map/reduce_scatter | solution.py:172
  542.6 34.2 %all-gather.16.cloned.1.call-done = bf16[2048,1024]{1,0:T(8,128)(2,1)} async-done(((bf16[512,1024]{1,0:T(8,128)(2,1)}), bf16[2048,1024]{1,0:T(8,128)(2,1)}) %all-gather.16.cloned.1.call-update) | async-done | bytes 4194320 | tf_op jit(solution)/shard_map/all_gather | solution.py:176
  576.8 13.9 %fusion.149 = (bf16[1024]{0:T(1024)(128)(2,1)}, bf16[2048,1024]{1,0:T(8,128)(2,1)S(1)}) fusion(f32[2048,1024]{1,0:T(8,128)} %get-tuple-element.460, f32[2048,1024]{1,0:T(8,128)} %get-tuple-element.491, f32[1024]{0:T(1024)S(1)} %convert_element_type.253, bf16[2048,1024]{1,0:T(8,128)(2,1)} %all-gather.16.cloned.1.call-done, bf16[1024,1024]{1,0:T(8,128)(2,1)} %param.36), kind=kOutput, calls=%fused_computation.246 | convolution fusion | flops 4328520704 | bytes 27269120 | tf_op jit(solution)/shard_map/dot_general | solution.py:20
  599.1 44.6 %reduce-scatter.15.cloned.1.call-done = bf16[512,1024]{1,0:T(8,128)(2,1)} async-done(((bf16[2048,1024]{1,0:T(8,128)(2,1)}), bf16[512,1024]{1,0:T(8,128)(2,1)}) %reduce-scatter.15.cloned.1.call-update) | async-done | bytes 1048592 | tf_op jit(solution)/shard_map/reduce_scatter | solution.py:180
  650.5 34.6 %all-gather.18.cloned.1.call-done = bf16[2048,1024]{1,0:T(8,128)(2,1)} async-done(((bf16[512,1024]{1,0:T(8,128)(2,1)}), bf16[2048,1024]{1,0:T(8,128)(2,1)}) %all-gather.18.cloned.1.call-update) | async-done | bytes 4194320 | tf_op jit(solution)/shard_map/all_gather | solution.py:176
  696.9 64.2 %while.54 = (s32[]{:T(128)}, bf16[2,1024,4,64]{1,3,2,0:T(8,128)(2,1)}, bf16[2,1024,4,64]{1,3,2,0:T(8,128)(2,1)}, bf16[2,1024,4,64]{1,3,2,0:T(8,128)(2,1)}, bf16[...) while((s32[]{:T(128)}, ...), condition=%wide.region_24.25_spmd, body=%wide.region_22.24_spmd.sunk | while | flops 2722624512 | bytes 149511440 | solution.py:149
  706.9 8.1 multiply_reduce_fusion.13
  738.8 8.1 multiply_reduce_fusion.13
  767.2 44.6 %reduce-scatter.17.cloned.1.call-done = bf16[512,1024]{1,0:T(8,128)(2,1)} async-done(((bf16[2048,1024]{1,0:T(8,128)(2,1)}), bf16[512,1024]{1,0:T(8,128)(2,1)}) %reduce-scatter.17.cloned.1.call-update) | async-done | bytes 1048592 | tf_op jit(solution)/shard_map/reduce_scatter | solution.py:180
  817.7 9.5 convolution_convert_fusion.6
  863.9 64.0 %while.55 = (s32[]{:T(128)}, bf16[2,1024,4,64]{1,3,2,0:T(8,128)(2,1)}, bf16[2,1024,4,64]{1,3,2,0:T(8,128)(2,1)}, bf16[2,1024,4,64]{1,3,2,0:T(8,128)(2,1)}, bf16[...) while((s32[]{:T(128)}, ...), condition=%wide.region_30.31_spmd, body=%wide.region_28.30_spmd.sunk | while | flops 2724721664 | bytes 155802928 | solution.py:149
  959.9 39.8 %all-reduce = (bf16[9,256]{1,0:T(8,128)(2,1)S(1)}, bf16[2,256]{1,0:T(2,128)(2,1)S(1)}, bf16[2,256]{1,0:T(2,128)(2,1)S(1)}, bf16[1024]{0:T(1024)(128)(2,1)S(1)}) all-reduce(bf16[9,256]{1,0:T(8,128)(2,1)} %reduce-scatter.23.cloned.1.call-done, bf16[2,256]{1,0:T(2,128)(2,1)S(1)} %pad_maximum_fusion.3, ...), channel_id=1, replica_groups=mesh['dp'=8,'mp'=4] {'dp'}, use_global_device_ids=true, to_apply=%region_58.59 | all-reduce | flops 4352 | bytes 17408 | tf_op jit(solution)/shard_map/psum | solution.py:330
  1001.4 215.4 %all-reduce.4.cloned.1.call-done = (bf16[3,1024,256]{1,2,0:T(8,128)(2,1)}, bf16[2,1024,256]{1,2,0:T(8,128)(2,1)}, bf16[256,1024]{1,0:T(8,128)(2,1)}, bf16[1024,2...) async-done(((bf16[3,1024,256]{1,2,0:T(8,128)(2,1)}, bf16[2,1024,256]{1,2,0:T(8,128)(2,1)}, ...) | async-done | bytes 8388624 | tf_op jit(solution)/shard_map/psum | solution.py:327
  1233.5 29.0 %reduce-scatter.19.cloned.1.call-done = bf16[512,1024]{1,0:T(8,128)(2,1)} async-done(((bf16[2048,1024]{1,0:T(8,128)(2,1)}), bf16[512,1024]{1,0:T(8,128)(2,1)}) %reduce-scatter.19.cloned.1.call-update) | async-done | bytes 1048592 | tf_op jit(solution)/shard_map/reduce_scatter | solution.py:180
  1265.7 44.4 %reduce-scatter.21.cloned.1.call-done = bf16[512,1024]{1,0:T(8,128)(2,1)} async-done(((bf16[2048,1024]{1,0:T(8,128)(2,1)}), bf16[512,1024]{1,0:T(8,128)(2,1)}) %reduce-scatter.21.cloned.1.call-update) | async-done | bytes 1048592 | tf_op jit(solution)/shard_map/reduce_scatter | solution.py:266
  (456 shorter events, 421.3 us)
Async XLA Ops:
  7.2 420.1 %copy-start = (bf16[1024,1024]{1,0:T(8,128)(2,1)S(1)}, bf16[1024,1024]{1,0:T(8,128)(2,1)}, u32[]{:S(2)}) copy-start(bf16[1024,1024]{1,0:T(8,128)(2,1)} %param.35) | copy-start | bytes 6291460
  7.2 39.6 %all-gather.8.cloned.1.call-start = ((), (), s32[]{:S(2)}) async-start(), calls=%async_computation.8 | async-start | bytes 5242880 | tf_op jit(solution)/shard_map/all_gather | solution.py:168
  7.9 182.6 %reduce-scatter.9.cloned.1.call-start = ((), (), s32[]{:S(2)}) async-start(), calls=%async_computation.9 | async-start | bytes 10485760 | tf_op jit(solution)/shard_map/reduce_scatter | solution.py:172
  118.6 71.9 %copy-start.43 = (bf16[512,1024]{1,0:T(8,128)(2,1)S(1)}, bf16[512,1024]{1,0:T(8,128)(2,1)}, u32[]{:S(2)}) copy-start(bf16[512,1024]{1,0:T(8,128)(2,1)} %param.25) | copy-start | bytes 3145732
  118.6 108.0 %all-gather.10.cloned.1.call-start = ((), (), s32[]{:S(2)}) async-start(), calls=%async_computation.10 | async-start | bytes 5242880 | tf_op jit(solution)/shard_map/all_gather | solution.py:215
  119.4 143.9 %all-gather.12.cloned.1.call-start = ((), (), s32[]{:S(2)}) async-start(), calls=%async_computation.11 | async-start | bytes 5242880 | tf_op jit(solution)/shard_map/all_gather | solution.py:168
  121.1 74.1 %copy-start.57 = (f32[1,1024]{1,0:T(1,128)}, f32[1,1024]{1,0:T(1,128)S(1)}, u32[]{:S(2)}) copy-start(f32[1,1024]{1,0:T(1,128)S(1)} %get-tuple-element.476) | copy-start | bytes 12292
  121.7 73.5 %copy-start.69 = (f32[1,1024]{1,0:T(1,128)}, f32[1,1024]{1,0:T(1,128)S(1)}, u32[]{:S(2)}) copy-start(f32[1,1024]{1,0:T(1,128)S(1)} %get-tuple-element.479) | copy-start | bytes 12292
  195.3 191.6 %reduce-scatter.11.cloned.1.call-start = ((), (), s32[]{:S(2)}) async-start(), calls=%async_computation.12 | async-start | bytes 10485760 | tf_op jit(solution)/shard_map/reduce_scatter | solution.py:172
  314.9 71.9 %copy-start.65 = (f32[512]{0:T(512)S(1)}, f32[512]{0:T(512)}, u32[]{:S(2)}) copy-start(f32[512]{0:T(512)} %copy-done.64) | copy-start | bytes 6148
  314.9 71.9 %copy-start.70 = (f32[1,1024]{1,0:T(1,128)S(1)}, f32[1,1024]{1,0:T(1,128)}, u32[]{:S(2)}) copy-start(f32[1,1024]{1,0:T(1,128)} %copy-done.69) | copy-start | bytes 12292
  315.0 71.9 %copy-start.73 = (f32[1,1024]{1,0:T(1,128)S(1)}, f32[1,1024]{1,0:T(1,128)}, u32[]{:S(2)}) copy-start(f32[1,1024]{1,0:T(1,128)} %get-tuple-element.483) | copy-start | bytes 12292
  315.0 112.3 %all-gather.14.cloned.1.call-start = ((), (), s32[]{:S(2)}) async-start(), calls=%async_computation.13 | async-start | bytes 5242880 | tf_op jit(solution)/shard_map/all_gather | solution.py:168
  392.6 140.7 %reduce-scatter.13.cloned.1.call-start = ((), (), s32[]{:S(2)}) async-start(), calls=%async_computation.14 | async-start | bytes 10485760 | tf_op jit(solution)/shard_map/reduce_scatter | solution.py:172
  461.5 115.4 %all-gather.16.cloned.1.call-start = ((), (), s32[]{:S(2)}) async-start(), calls=%async_computation.15 | async-start | bytes 5242880 | tf_op jit(solution)/shard_map/all_gather | solution.py:176
  542.2 101.5 %reduce-scatter.15.cloned.1.call-start = ((), (), s32[]{:S(2)}) async-start(), calls=%async_computation.16 | async-start | bytes 5242880 | tf_op jit(solution)/shard_map/reduce_scatter | solution.py:180
  599.0 86.1 %all-gather.18.cloned.1.call-start = ((), (), s32[]{:S(2)}) async-start(), calls=%async_computation.17 | async-start | bytes 5242880 | tf_op jit(solution)/shard_map/all_gather | solution.py:176
  650.4 161.4 %reduce-scatter.17.cloned.1.call-start = ((), (), s32[]{:S(2)}) async-start(), calls=%async_computation.18 | async-start | bytes 5242880 | tf_op jit(solution)/shard_map/reduce_scatter | solution.py:180
  767.1 85.0 %all-gather.20.cloned.1.call-start = ((), (), s32[]{:S(2)}) async-start(), calls=%async_computation.19 | async-start | bytes 5242880 | tf_op jit(solution)/shard_map/all_gather | solution.py:176
  817.5 142.3 %reduce-scatter.23.cloned.1.call-start = ((), (), s32[]{:S(2)}) async-start(), calls=%async_computation.22 | async-start | bytes 40960 | tf_op jit(solution)/shard_map/reduce_scatter | solution.py:311
  846.1 370.8 %all-reduce.4.cloned.1.call-start = ((), (), s32[]{:S(2)}) async-start(), calls=%async_computation.23 | async-start | bytes 16777216 | tf_op jit(solution)/shard_map/psum | solution.py:327
  941.5 321.0 %reduce-scatter.19.cloned.1.call-start = ((), (), s32[]{:S(2)}) async-start(), calls=%async_computation.20 | async-start | bytes 5242880 | tf_op jit(solution)/shard_map/reduce_scatter | solution.py:180
  949.0 361.1 %reduce-scatter.21.cloned.1.call-start = ((), (), s32[]{:S(2)}) async-start(), calls=%async_computation.21 | async-start | bytes 5242880 | tf_op jit(solution)/shard_map/reduce_scatter | solution.py:266
  1231.0 79.2 %copy-start.1 = (bf16[1024,1024]{1,0:T(8,128)(2,1)S(1)}, bf16[1024,1024]{1,0:T(8,128)(2,1)}, u32[]{:S(2)}) copy-start(bf16[1024,1024]{1,0:T(8,128)(2,1)} %param.35) | copy-start | bytes 6291460
  (106 other events, 897.6 us)
Sparse Core Ops, SparseCore 0:
  9.6 37.1 all-gather.7
  118.7 71.7 reduce-scatter.8
  192.1 34.4 all-gather.9
  228.7 34.4 all-gather.11
  315.1 71.6 reduce-scatter.10
  392.8 34.4 all-gather.13
  461.6 71.7 reduce-scatter.12
  542.3 34.4 all-gather.15
  599.1 44.5 reduce-scatter.14
  650.6 34.4 all-gather.17
  767.3 44.4 reduce-scatter.16
  817.6 34.4 all-gather.19
  854.7 19.3 reduce-scatter.22
  941.6 275.2 all-reduce.3
  1219.3 43.1 reduce-scatter.18
  1265.6 44.5 reduce-scatter.20
where the time goes:
time: 1330 us; the launch traced here: 1320 us
  waiting for transfers between devices  782 us (59%)
  matrix products  260 us (20%)
  local copies, waits for them, and re-layouts  112 us (8%)
  other arithmetic  105 us (8%)
  blocking collectives  39.8 us (3%)
  between operations  15.4 us (1%)
    psum x1, waiting for transfers between devices, on_device(): lax.psum(grad_self_inputs.astype(jnp.bfloat16), 'dp').astype(jnp.float32)  215 us
    reduce_scatter x3, waiting for transfers between devices, sum_rows(): lax.psum_scatter(partial_value, 'mp', scatter_dimension=0, tiled=True)  212 us
    reduce_scatter x3, waiting for transfers between devices, sum_input_grads(): lax.psum_scatter(partial_value.astype(jnp.bfloat16), 'mp', scatter_dimens...  118 us
    all_gather x3, waiting for transfers between devices, gather_rows(): return lax.all_gather(rows, 'mp', axis=0, tiled=True)  83.8 us
    all_gather x3, waiting for transfers between devices, gather_grads(): return lax.all_gather(grads, 'mp', axis=0, tiled=True)  74.8 us
    dot_general x10, matrix products, project(): return jnp.dot(rows, weight, preferred_element_type=jnp.float32)  66.4 us
    reduce_scatter x1, waiting for transfers between devices, on_device(): lax.psum_scatter(memory_part.astype(jnp.bfloat16), 'mp', scatter_dimensio...  44.4 us
    dot_general x10, matrix products, project_back(): lax.dot_general(grads, weight, (((1,), (1,)), ((), ())), preferred_elemen...  43.5 us
  transfers between devices with their start and end apart: 16, of which 15 were waited for; matrix products, arithmetic and copies ran while one was open for 14% of the time, Pallas kernels for 0%

commit v1 on v0

v1 whole, which is shorter than its diff:
```python
import functools

import jax, jax.numpy as jnp
from jax import lax
from jax.experimental import pallas as pl
from jax.experimental.pallas import tpu as pltpu
from jax.sharding import Mesh
from jax.sharding import PartitionSpec as P

HEAD = 64
NEG = -1e30

def _nt(a, b):
    return lax.dot_general(a, b, (((1,), (1,)), ((), ())), preferred_element_type=jnp.float32)

def _nn(a, b):
    return lax.dot_general(a, b, (((1,), (0,)), ((), ())), preferred_element_type=jnp.float32)

def _lanes(rows):
    return lax.broadcasted_iota(jnp.int32, (rows, 128), 1)

def _put(base, lane, pairs):
    for at, val in pairs:
        base = jnp.where(lane == at, val, base)
    return base

def fwd_kernel(len_ref, q_ref, k_ref, v_ref, o_ref, lse_ref, *, causal, bq):
    p = pl.program_id(0)
    rows, keys = q_ref.shape[0], k_ref.shape[0]
    length = len_ref[0]
    kl = _lanes(keys)
    kpos = lax.broadcasted_iota(jnp.int32, (keys, 128), 0)
    kbias = jnp.where(kpos < length, 0.0, NEG)
    k2 = k_ref[...].astype(jnp.float32)
    v2 = v_ref[...].astype(jnp.float32)
    ql = _lanes(bq)
    heads = []
    for h in range(2):
        mine = (kl // HEAD) == h
        other = HEAD * (1 - h)
        kh = jnp.where(mine, k2, jnp.where(kl == other, kbias, 0.0)).astype(jnp.bfloat16)
        vh = jnp.where(mine, v2, jnp.where(kl == other, 1.0, 0.0)).astype(jnp.bfloat16)
        heads.append((kh, vh))
    for i in range(rows // bq):
        q2 = q_ref[pl.ds(i * bq, bq), :].astype(jnp.float32) * (HEAD ** -0.5)
        out = jnp.zeros((bq, 128), jnp.float32)
        lse_all = lse_ref[pl.ds(i * bq, bq), :]
        for h in range(2):
            kh, vh = heads[h]
            mine = (ql // HEAD) == h
            other = HEAD * (1 - h)
            qh = jnp.where(mine, q2, jnp.where(ql == other, 1.0, 0.0)).astype(jnp.bfloat16)
            if causal:
                lo = i * bq
                sd = _nt(qh, kh[lo:lo + bq])
                r = lax.broadcasted_iota(jnp.int32, (bq, bq), 0)
                c = lax.broadcasted_iota(jnp.int32, (bq, bq), 1)
                sd = jnp.where(c <= r, sd, NEG)
                m = jnp.max(sd, axis=1, keepdims=True)
                if lo:
                    sl = _nt(qh, kh[:lo])
                    m = jnp.maximum(m, jnp.max(sl, axis=1, keepdims=True))
                    acc = _nn(jnp.exp(sl - m).astype(jnp.bfloat16), vh[:lo])
                    acc += _nn(jnp.exp(sd - m).astype(jnp.bfloat16), vh[lo:lo + bq])
                else:
                    acc = _nn(jnp.exp(sd - m).astype(jnp.bfloat16), vh[:bq])
            else:
                s = _nt(qh, kh)
                m = jnp.max(s, axis=1, keepdims=True)
                acc = _nn(jnp.exp(s - m).astype(jnp.bfloat16), vh)
            total = jnp.sum(jnp.where(ql == other, acc, 0.0), axis=1, keepdims=True)
            out = jnp.where(mine, acc / total, out)
            lse_all = jnp.where(ql == 2 * p + h, m + jnp.log(total), lse_all)
        o_ref[pl.ds(i * bq, bq), :] = out.astype(jnp.bfloat16)
        lse_ref[pl.ds(i * bq, bq), :] = lse_all

def attn_fwd(length, q, k, v, causal, bq=256):
    rows, cols = q.shape
    keys = k.shape[0]
    pairs = cols // 128
    el = pairs * 2 * rows * keys
    return pl.pallas_call(
        functools.partial(fwd_kernel, causal=causal, bq=bq),
        out_shape=(jax.ShapeDtypeStruct((rows, cols), jnp.bfloat16), jax.ShapeDtypeStruct((rows, 128), jnp.float32)),
        grid_spec=pltpu.PrefetchScalarGridSpec(
            num_scalar_prefetch=1, grid=(pairs,),
            in_specs=[pl.BlockSpec((rows, 128), lambda p, n: (0, p)), pl.BlockSpec((keys, 128), lambda p, n: (0, p)), pl.BlockSpec((keys, 128), lambda p, n: (0, p))],
            out_specs=[pl.BlockSpec((rows, 128), lambda p, n: (0, p)), pl.BlockSpec((rows, 128), lambda p, n: (0, 0))],
        ),
        compiler_params=pltpu.CompilerParams(dimension_semantics=("arbitrary",), vmem_limit_bytes=40 << 20),
        cost_estimate=pl.CostEstimate(flops=16 * el * 64, bytes_accessed=8 * rows * cols, transcendentals=el),
        name="attend_forward",
    )(length, q, k, v)

def split3(x):
    a = x.astype(jnp.bfloat16).astype(jnp.float32)
    b = (x - a).astype(jnp.bfloat16).astype(jnp.float32)
    return a, b, x - a - b

def bwd_kernel(len_ref, q_ref, k_ref, v_ref, o_ref, g_ref, lse_ref, dq_ref, dk_ref, dv_ref, dka, dva, *, causal, bq):
    p = pl.program_id(0)
    rows, keys = q_ref.shape[0], k_ref.shape[0]
    length = len_ref[0]
    kl = _lanes(keys)
    kpos = lax.broadcasted_iota(jnp.int32, (keys, 128), 0)
    kbias = jnp.where(kpos < length, 0.0, NEG)
    k2 = k_ref[...].astype(jnp.float32)
    v2 = v_ref[...].astype(jnp.float32)
    ql = _lanes(bq)
    heads = []
    for h in range(2):
        mine = (kl // HEAD) == h
        other = HEAD * (1 - h)
        ones = (kl > other) & (kl < other + 4)
        kh = jnp.where(mine, k2, jnp.where(kl == other, kbias, jnp.where(ones, 1.0, 0.0))).astype(jnp.bfloat16)
        vh = jnp.where(mine, v2, jnp.where(ones, 1.0, 0.0)).astype(jnp.bfloat16)
        heads.append((kh, vh, kh.T))
    for i in reversed(range(rows // bq)):
        at = pl.ds(i * bq, bq)
        q2 = q_ref[at, :].astype(jnp.float32) * (HEAD ** -0.5)
        g2 = g_ref[at, :].astype(jnp.float32)
        go = g2 * o_ref[at, :].astype(jnp.float32)
        lse_all = lse_ref[at, :]
        dqt = []
        for h in range(2):
            kh, vh, kt = heads[h]
            mine = (ql // HEAD) == h
            other = HEAD * (1 - h)
            lse = jnp.sum(jnp.where(ql == 2 * p + h, lse_all, 0.0), axis=1, keepdims=True)
            delta = jnp.sum(jnp.where(mine, go, 0.0), axis=1, keepdims=True)
            la, lb, lc = split3(-lse)
            da, db, dc = split3(-delta)
            qh = _put(jnp.where(mine, q2, 0.0), ql, ((other, 1.0), (other + 1, la), (other + 2, lb), (other + 3, lc))).astype(jnp.bfloat16)
            gh = _put(jnp.where(mine, g2, 0.0), ql, ((other + 1, da), (other + 2, db), (other + 3, dc))).astype(jnp.bfloat16)
            hi = (i + 1) * bq if causal else keys
            st = _nt(kh[:hi], qh)
            if causal:
                kr = lax.broadcasted_iota(jnp.int32, (hi, bq), 0)
                qc = lax.broadcasted_iota(jnp.int32, (hi, bq), 1) + i * bq
                pt = jnp.where(kr <= qc, jnp.exp(st), 0.0)
            else:
                pt = jnp.exp(st)
            dst = (pt * _nt(vh[:hi], gh)).astype(jnp.bfloat16)
            dvn = _nn(pt.astype(jnp.bfloat16), gh)
            dkn = _nn(dst, qh)
            if i == rows // bq - 1:
                dva[h, :hi] = dvn
                dka[h, :hi] = dkn
            else:
                dva[h, :hi] += dvn
                dka[h, :hi] += dkn
            dqt.append(_nn(kt[:, :hi], dst))
        dq = jnp.concatenate([dqt[0][:HEAD], dqt[1][HEAD:]], axis=0).T
        dq_ref[at, :] = (dq * (HEAD ** -0.5)).astype(jnp.bfloat16)
    first = kl < HEAD
    dk_ref[...] = jnp.where(first, dka[0], dka[1]).astype(jnp.bfloat16)
    dv_ref[...] = jnp.where(first, dva[0], dva[1]).astype(jnp.bfloat16)

def attn_bwd(length, q, k, v, o, g, lse, causal, bq=256):
    rows, cols = q.shape
    keys = k.shape[0]
    pairs = cols // 128
    el = pairs * 2 * rows * keys
    qs = pl.BlockSpec((rows, 128), lambda p, n: (0, p))
    ks = pl.BlockSpec((keys, 128), lambda p, n: (0, p))
    return pl.pallas_call(
        functools.partial(bwd_kernel, causal=causal, bq=bq),
        out_shape=(jax.ShapeDtypeStruct((rows, cols), jnp.bfloat16), jax.ShapeDtypeStruct((keys, cols), jnp.bfloat16), jax.ShapeDtypeStruct((keys, cols), jnp.bfloat16)),
        grid_spec=pltpu.PrefetchScalarGridSpec(
            num_scalar_prefetch=1, grid=(pairs,),
            in_specs=[qs, ks, ks, qs, qs, pl.BlockSpec((rows, 128), lambda p, n: (0, 0))],
            out_specs=[qs, ks, ks],
            scratch_shapes=[pltpu.VMEM((2, keys, 128), jnp.float32), pltpu.VMEM((2, keys, 128), jnp.float32)],
        ),
        compiler_params=pltpu.CompilerParams(dimension_semantics=("arbitrary",), vmem_limit_bytes=48 << 20),
        cost_estimate=pl.CostEstimate(flops=40 * el * 64, bytes_accessed=16 * rows * cols, transcendentals=el),
        name="attend_backward",
    )(length, q, k, v, o, g, lse)

residual_scale = 300.0**0.25
norm_epsilon = 1e-05
LOW = jnp.bfloat16
F32 = jnp.float32


def tn(rows, grads):
    return lax.dot_general(rows, grads, (((0,), (0,)), ((), ())), preferred_element_type=F32)


def gelu_exact(pre_rows):
    return jax.nn.gelu(pre_rows, approximate=False)


def gelu_backward(pre_rows, grad_rows):
    unused, pullback = jax.vjp(gelu_exact, pre_rows)
    return pullback(grad_rows)[0]


def norm_forward(summed, gain_row, shift_row):
    row_mean = jnp.mean(summed, axis=-1, keepdims=True)
    centred = summed - row_mean
    variance = jnp.mean(centred * centred, axis=-1, keepdims=True)
    inverse = lax.rsqrt(variance + norm_epsilon)
    unit_rows = centred * inverse
    return unit_rows * gain_row + shift_row, unit_rows, inverse


def norm_backward(grad_out, unit_rows, inverse, gain_row):
    grad_unit = grad_out * gain_row
    first_mean = jnp.mean(grad_unit, axis=-1, keepdims=True)
    second_mean = jnp.mean(grad_unit * unit_rows, axis=-1, keepdims=True)
    return inverse * (grad_unit - first_mean - unit_rows * second_mean)


def layer(sizes, tokens, memory, cotangent, target_lengths, memory_lengths, self_inputs, self_output, cross_query, cross_memory, cross_output, feed_in, feed_out, proj_bias, feed_bias, branch_bias, norm_gain, norm_shift):
    zn, yn, gn, cn = sizes
    seq = lax.axis_index("g")
    core = lax.axis_index("c")
    width = self_output.shape[0]
    joined = width % 128 != 0

    def swap(rows):
        return lax.ppermute(rows, "c", [(0, 1), (1, 0)])

    def gather_rows(rows):
        if cn != 2:
            return lax.all_gather(rows, "c", axis=0, tiled=True)
        got = swap(rows)
        return jnp.where(core == 0, jnp.concatenate([rows, got]), jnp.concatenate([got, rows]))

    def sum_all(part):
        part = part.astype(LOW)
        if cn != 2:
            return lax.psum(part, "c").astype(F32)
        return part.astype(F32) + swap(part).astype(F32)

    def own_rows(rows):
        size = rows.shape[0] // cn
        return lax.dynamic_slice_in_dim(rows, core * size, size, 0)

    def sum_own(part):
        if cn != 2:
            return lax.psum_scatter(part.astype(LOW), "c", scatter_dimension=0, tiled=True).astype(F32)
        size = part.shape[0] // 2
        got = swap(lax.dynamic_slice_in_dim(part, (1 - core) * size, size, 0).astype(LOW))
        return lax.dynamic_slice_in_dim(part, core * size, size, 0) + got.astype(F32)

    def spread(shard, axis):
        every = [shard] + [lax.ppermute(shard, "g", [((i + k) % gn, i) for i in range(gn)]) for k in range(1, gn)]
        return [jnp.concatenate(every, axis=axis)] if joined else every

    def collect(parts, axis):
        if joined:
            parts = jnp.split(parts[0], gn, axis=axis)
        total = parts[0]
        for k in range(1, gn):
            total = total + lax.ppermute(parts[k].astype(LOW), "g", [(i, (i + k) % gn) for i in range(gn)]).astype(F32)
        return lax.psum(total.astype(LOW), ("z", "y")).astype(F32)

    target_length = lax.dynamic_slice_in_dim(target_lengths, seq, 1, 0)
    memory_length = lax.dynamic_slice_in_dim(memory_lengths, seq, 1, 0)

    token_all = gather_rows(tokens)
    w_self = spread(self_inputs, 2)
    b_proj = spread(proj_bias, 1)
    w_self_out = spread(self_output, 0)
    memory_all = gather_rows(memory)
    w_cross_mem = spread(cross_memory, 2)
    w_cross_q = spread(cross_query, 1)
    w_cross_out = spread(cross_output, 0)
    w_in = spread(feed_in, 1)
    b_in = spread(feed_bias, 0)
    w_out = spread(feed_out, 0)
    cot_all = gather_rows(cotangent)
    shards = range(len(w_self))

    self_q = [(_nn(token_all, w_self[s][0]) + b_proj[s][0]).astype(LOW) for s in shards]
    self_k = [_nn(token_all, w_self[s][1]).astype(LOW) for s in shards]
    self_v = [(_nn(token_all, w_self[s][2]) + b_proj[s][1]).astype(LOW) for s in shards]
    self_mixed, self_lse = zip(*[attn_fwd(target_length, self_q[s], self_k[s], self_v[s], True) for s in shards])
    cross_k = [_nn(memory_all, w_cross_mem[s][0]).astype(LOW) for s in shards]
    cross_v = [(_nn(memory_all, w_cross_mem[s][1]) + b_proj[s][3]).astype(LOW) for s in shards]
    branch_one = sum_all(sum(_nn(self_mixed[s], w_self_out[s]) for s in shards)) + branch_bias[0]
    normed_one, unit_one, inverse_one = norm_forward(residual_scale * token_all.astype(F32) + branch_one, norm_gain[0], norm_shift[0])
    second = normed_one.astype(LOW)
    cross_q = [(_nn(second, w_cross_q[s]) + b_proj[s][2]).astype(LOW) for s in shards]
    cross_mixed, cross_lse = zip(*[attn_fwd(memory_length, cross_q[s], cross_k[s], cross_v[s], False) for s in shards])
    branch_two = sum_all(sum(_nn(cross_mixed[s], w_cross_out[s]) for s in shards)) + branch_bias[1]
    normed_two, unit_two, inverse_two = norm_forward(residual_scale * normed_one + branch_two, norm_gain[1], norm_shift[1])
    third = normed_two.astype(LOW)
    hidden_pre = [_nn(third, w_in[s]) + b_in[s].astype(F32) for s in shards]
    hidden = [gelu_exact(hidden_pre[s]).astype(LOW) for s in shards]
    branch_three = sum_all(sum(_nn(hidden[s], w_out[s]) for s in shards)) + branch_bias[2]
    normed_three, unit_three, inverse_three = norm_forward(residual_scale * normed_two + branch_three, norm_gain[2], norm_shift[2])
    block_out = own_rows(normed_three.astype(LOW))

    cot = cot_all.astype(F32)
    grad_three = norm_backward(cot, unit_three, inverse_three, norm_gain[2])
    low_three = grad_three.astype(LOW)
    grad_hidden = [_nt(low_three, w_out[s]) for s in shards]
    grad_feed_out = collect([tn(hidden[s], low_three) for s in shards], 0)
    grad_pre = [gelu_backward(hidden_pre[s], grad_hidden[s]).astype(LOW) for s in shards]
    grad_feed_in = collect([tn(third, grad_pre[s]) for s in shards], 1)
    grad_normed_two = residual_scale * grad_three + sum_all(sum(_nt(grad_pre[s], w_in[s]) for s in shards))
    grad_two = norm_backward(grad_normed_two, unit_two, inverse_two, norm_gain[1])
    low_two = grad_two.astype(LOW)
    grad_cross_mixed = [_nt(low_two, w_cross_out[s]).astype(LOW) for s in shards]
    grad_cross_output = collect([tn(cross_mixed[s], low_two) for s in shards], 0)
    cross_dq, cross_dk, cross_dv = zip(*[attn_bwd(memory_length, cross_q[s], cross_k[s], cross_v[s], cross_mixed[s], grad_cross_mixed[s], cross_lse[s], False) for s in shards])
    grad_normed_one = residual_scale * grad_two + sum_all(sum(_nt(cross_dq[s], w_cross_q[s]) for s in shards))
    grad_cross_query = collect([tn(second, cross_dq[s]) for s in shards], 1)
    grad_cross_memory = collect([jnp.stack([tn(memory_all, cross_dk[s]), tn(memory_all, cross_dv[s])]) for s in shards], 2)
    grad_memory = sum_own(sum(_nt(cross_dk[s], w_cross_mem[s][0]) + _nt(cross_dv[s], w_cross_mem[s][1]) for s in shards)).astype(LOW)
    grad_one = norm_backward(grad_normed_one, unit_one, inverse_one, norm_gain[0])
    low_one = grad_one.astype(LOW)
    grad_self_mixed = [_nt(low_one, w_self_out[s]).astype(LOW) for s in shards]
    grad_self_output = collect([tn(self_mixed[s], low_one) for s in shards], 0)
    self_dq, self_dk, self_dv = zip(*[attn_bwd(target_length, self_q[s], self_k[s], self_v[s], self_mixed[s], grad_self_mixed[s], self_lse[s], True) for s in shards])
    grad_self_inputs = collect([jnp.stack([tn(token_all, self_dq[s]), tn(token_all, self_dk[s]), tn(token_all, self_dv[s])]) for s in shards], 2)
    token_part = sum(_nt(self_dq[s], w_self[s][0]) + _nt(self_dk[s], w_self[s][1]) + _nt(self_dv[s], w_self[s][2]) for s in shards)
    grad_tokens = (residual_scale * own_rows(grad_one) + sum_own(token_part)).astype(LOW)

    def sums(rows):
        return jnp.sum(rows.astype(F32), axis=0)

    proj_sums = collect([jnp.stack([sums(self_dq[s]), sums(self_dv[s]), sums(cross_dq[s]), sums(cross_dv[s])]) for s in shards], 1)
    feed_sums = collect([sums(grad_pre[s]) for s in shards], 0)
    terms = jnp.stack([sums(low_one), sums(low_two), sums(low_three), sums(grad_normed_one * unit_one), sums(grad_normed_two * unit_two), sums(cot * unit_three), sums(grad_normed_one), sums(grad_normed_two), sums(cot)])
    terms = lax.psum(terms.astype(LOW), ("z", "y", "g")).astype(F32)
    terms = lax.dynamic_slice_in_dim(terms, (seq * cn + core) * width, width, 1)
    return (block_out, grad_tokens, grad_memory, grad_self_inputs, grad_self_output, grad_cross_query, grad_cross_memory, grad_cross_output, grad_feed_in, grad_feed_out, proj_sums, feed_sums, terms[0:3], terms[3:6], terms[6:9])


def solution(mesh):
    dp, mp = mesh.shape["dp"], mesh.shape["mp"]

    def whole(*args):
        yn = 2 if dp % 2 == 0 else 1
        gn = args[3].shape[0] // dp
        sizes = (dp // yn, yn, gn, mp // gn)
        fine = Mesh(mesh.devices.reshape(sizes), ("z", "y", "g", "c"))
        d, m = ("z", "y"), ("g", "c")
        rows, wide, tall = P(d + m, None), P(None, m), P(m, None)
        stack = P(None, None, m)
        in_specs = (rows, rows, rows, P(d), P(d), stack, tall, wide, stack, tall, wide, tall, wide, P(m), P(), P(), P())
        out_specs = (rows, rows, rows, stack, tall, wide, stack, tall, wide, tall, wide, P(m), wide, wide, wide)
        return jax.shard_map(functools.partial(layer, sizes), mesh=fine, in_specs=in_specs, out_specs=out_specs, check_vma=False)(*args)

    return whole
```

time: 1330 us -> 775 us (0.58)
  waiting for transfers between devices: 782 us -> 326 us
  matrix products: 260 us -> 132 us
  local copies, waits for them, and re-layouts: 112 us -> 29.7 us
  Pallas kernels: 0 us -> 79.2 us
  blocking collectives: 39.8 us -> 99.1 us
  other arithmetic: 105 us -> 61.9 us
  starting transfers between devices: 1.99 us -> 21.7 us
    reduce_scatter x8 -> x0, waiting for transfers between devices: 375 us -> none  [the longest x3 212 us: sum_rows(): lax.psum_scatter(partial_value, 'mp', scatter_dimension=0, tiled=True)]
    all_gather x7 -> x0, waiting for transfers between devices: 190 us -> none  [the longest x3 83.8 us: gather_rows(): return lax.all_gather(rows, 'mp', axis=0, tiled=True)]
    ppermute x0 -> x28, waiting for transfers between devices: none -> 186 us  [the longest x9 94.1 us: spread(): lax.ppermute(shard, 'g', [((i + k) % gn, i) for i in range(gn)])]
    dot_general x58 -> x60, matrix products: 260 us -> 132 us  [the longest x20 55.2 us: _nn(): lax.dot_general(a, b, (((1,), (0,)), ((), ())), preferred_element_type=jn...]
    pallas_call x0 -> x8, Pallas kernels: none -> 79.2 us  [the longest x4 44.9 us: attn_bwd(): pl.pallas_call(functools.partial(bwd_kernel, causal=causal, bq=bq), out_s...]
    psum x1, waiting for transfers between devices: 215 us -> 140 us  [collect(): return lax.psum(total.astype(LOW), ('z', 'y')).astype(F32)]
    psum x1 -> x2, blocking collectives: 39.8 us -> 99.1 us  [the longest x1 81.5 us: layer(): terms = lax.psum(terms.astype(LOW), ('z', 'y', 'g')).astype(F32)]
    while x66 -> x0, local copies, waits for them, and re-layouts: 40.8 us -> none  [the longest x8 27.2 us: attention_forward(): lax.map(one_seq, (split_heads(queries, seq_count, LEN), split_heads(key_r...]
  transfers between devices with their start and end apart: 16 -> 29, of which waited for: 15 -> 12; matrix products, arithmetic and copies ran while one was open for 14% -> 21% of each run, Pallas kernels for 0% -> 10%
where the time goes in v1:
time: 775 us; the launch traced here: 766 us
  waiting for transfers between devices  326 us (42%)
  matrix products  132 us (17%)
  blocking collectives  99.1 us (13%)
  Pallas kernels  79.2 us (10%)
  other arithmetic  61.9 us (8%)
  local copies, waits for them, and re-layouts  29.7 us (4%)
  starting transfers between devices  21.7 us (3%)
  between operations  16.4 us (2%)
    psum x1, waiting for transfers between devices, collect(): return lax.psum(total.astype(LOW), ('z', 'y')).astype(F32)  140 us
    ppermute x9, waiting for transfers between devices, spread(): lax.ppermute(shard, 'g', [((i + k) % gn, i) for i in range(gn)])  94.1 us
    ppermute x9, waiting for transfers between devices, collect(): lax.ppermute(parts[k].astype(LOW), 'g', [(i, (i + k) % gn) for i in range...  90.2 us
    psum x1, blocking collectives, layer(): terms = lax.psum(terms.astype(LOW), ('z', 'y', 'g')).astype(F32)  81.5 us
    dot_general x20, matrix products, _nn(): lax.dot_general(a, b, (((1,), (0,)), ((), ())), preferred_element_type=jn...  55.2 us
    pallas_call x4, Pallas kernels, attn_bwd(): pl.pallas_call(functools.partial(bwd_kernel, causal=causal, bq=bq), out_s...  44.9 us
    dot_general x20, matrix products, tn(): lax.dot_general(rows, grads, (((0,), (0,)), ((), ())), preferred_element_...  43 us
    pallas_call x4, Pallas kernels, attn_fwd(): pl.pallas_call(functools.partial(fwd_kernel, causal=causal, bq=bq), out_s...  34.3 us
  transfers between devices with their start and end apart: 29, of which 12 were waited for; matrix products, arithmetic and copies ran while one was open for 21% of the time, Pallas kernels for 10%

profile of v1, /device:TPU:0, one launch (start us, length us, event | category | flops | bytes accessed | tf_op | source)
XLA Modules:
  0.0 766.1 jit_solution(9393280621829014026)
XLA Ops:
  19.8 27.7 %collective-permute-done.2 = bf16[4,256]{1,0:T(4,128)(2,1)S(1)} collective-permute-done((bf16[4,256]{1,0:T(4,128)(2,1)}, bf16[4,256]{1,0:T(4,128)(2,1)S(1)}, u32[]{:S(2)}, u32[]{:S(2)}) %collective-permute-start.2) | collective-permute-done | bytes 2080 | tf_op jit(solution)/shard_map/ppermute | solution.py:249
  57.2 7.5 attend_forward.4
  74.2 7.9 %attend_forward.5 = (bf16[1024,256]{1,0:T(8,128)(2,1)S(1)}, f32[1024,128]{1,0:T(8,128)S(1)}) custom-call(s32[1]{0:T(128)} %dynamic_slice.27.len_ref, bf16[1024,256]{1,0:T(8,128)(2,1)S(1)} %fusion.27.q_ref, bf16[1024,256]{1,0:T(8,128)(2,1)S(1)} %convolution_convert_fusion.16.k_ref, bf16[1024,256]{1,0:T(8,128)(2,1)S(1)} %fusion.28.v_ref), custom_call_target="tpu_custom_call" | custom-call | flops 4294967296 | bytes 2097152 | tf_op jit(solution)/shard_map/attend_forward/pallas_call | solution.py:82
  84.9 7.5 collective-permute-done.7
  101.3 9.5 %attend_forward.6 = (bf16[1024,256]{1,0:T(8,128)(2,1)S(1)}, f32[1024,128]{1,0:T(8,128)S(1)}) custom-call(s32[1]{0:T(128)} %dynamic_slice.28.len_ref, bf16[1024,256]{1,0:T(8,128)(2,1)S(1)} %fusion.29.q_ref, bf16[1024,256]{1,0:T(8,128)(2,1)S(1)} %convolution_convert_fusion.15.k_ref, bf16[1024,256]{1,0:T(8,128)(2,1)S(1)} %fusion.30.v_ref), custom_call_target="tpu_custom_call" | custom-call | flops 4294967296 | bytes 2097152 | tf_op jit(solution)/shard_map/attend_forward/pallas_call | solution.py:82
  113.6 9.3 %attend_forward.7 = (bf16[1024,256]{1,0:T(8,128)(2,1)S(1)}, f32[1024,128]{1,0:T(8,128)S(1)}) custom-call(s32[1]{0:T(128)} %dynamic_slice.28.len_ref, bf16[1024,256]{1,0:T(8,128)(2,1)S(1)} %fusion.31.q_ref, bf16[1024,256]{1,0:T(8,128)(2,1)S(1)} %convolution_convert_fusion.14.k_ref, bf16[1024,256]{1,0:T(8,128)(2,1)S(1)} %fusion.32.v_ref), custom_call_target="tpu_custom_call" | custom-call | flops 4294967296 | bytes 2097152 | tf_op jit(solution)/shard_map/attend_forward/pallas_call | solution.py:82
  132.2 12.4 %multiply_convert_fusion.1 = (bf16[1024,1024]{1,0:T(8,128)(2,1)S(1)}, f32[1024,1024]{1,0:T(8,128)}, f32[1024,1024]{1,0:T(8,128)}) fusion(f32[1024]{0:T(1024)S(1)} %convert_element_type.331, bf16[1024,1024]{0,1:T(8,128)(2,1)S(1)} %fusion.20, bf16[1024,1024]{1,0:T(8,128)(2,1)S(1)} %copy-done.106), kind=kOutput, calls=%fused_computation.46 | convolution fusion | flops 2216689664 | bytes 14684160 | tf_op jit(solution)/shard_map/dot_general | solution.py:17
  147.0 27.3 %collective-permute-done.10 = bf16[1024,1024]{1,0:T(8,128)(2,1)S(1)} collective-permute-done((bf16[1024,1024]{1,0:T(8,128)(2,1)S(1)}, bf16[1024,1024]{1,0:T(8,128)(2,1)S(1)}, u32[]{:S(2)}, u32[]{:S(2)}) %collective-permute-start.10) | collective-permute-done | bytes 2097184 | tf_op jit(solution)/shard_map/ppermute | solution.py:249
  174.4 12.5 %multiply_convert_fusion = (bf16[1024,1024]{1,0:T(8,128)(2,1)S(1)}, f32[1024,1024]{1,0:T(8,128)}, f32[1024,1024]{1,0:T(8,128)}) fusion(f32[1024]{0:T(1024)S(1)} %convert_element_type.333, bf16[1024,1024]{0,1:T(8,128)(2,1)S(1)} %fusion.20, bf16[1024,1024]{1,0:T(8,128)(2,1)S(1)} %collective-permute-done.10), kind=kOutput, calls=%fused_computation.33 | convolution fusion | flops 2216689664 | bytes 14684160 | tf_op jit(solution)/shard_map/dot_general | solution.py:17
  186.9 31.6 %collective-permute-done.12 = bf16[1024,1024]{1,0:T(8,128)(2,1)S(1)} collective-permute-done((bf16[1024,1024]{1,0:T(8,128)(2,1)S(1)}, bf16[1024,1024]{1,0:T(8,128)(2,1)S(1)}, u32[]{:S(2)}, u32[]{:S(2)}) %collective-permute-start.12) | collective-permute-done | bytes 2097184 | tf_op jit(solution)/shard_map/ppermute | solution.py:249
  240.3 4.7 convert_reduce_fusion
  248.5 6.0 fusion.76
  275.5 12.8 %attend_backward.5 = (bf16[1024,256]{1,0:T(8,128)(2,1)S(1)}, bf16[1024,256]{1,0:T(8,128)(2,1)S(1)}, bf16[1024,256]{1,0:T(8,128)(2,1)S(1)}) custom-call(s32[1]{0:T(128)} %dynamic_slice.28.len_ref, bf16[1024,256]{1,0:T(8,128)(2,1)S(1)} %fusion.31.q_ref, bf16[1024,256]{1,0:T(8,128)(2,1)S(1)} %convolution_convert_fusion.14.k_ref, ...), custom_call_target="tpu_custom_call" | custom-call | flops 10737418240 | bytes 4194304 | tf_op jit(solution)/shard_map/attend_backward/pallas_call | solution.py:166
  288.4 13.0 %attend_backward.4 = (bf16[1024,256]{1,0:T(8,128)(2,1)S(1)}, bf16[1024,256]{1,0:T(8,128)(2,1)S(1)}, bf16[1024,256]{1,0:T(8,128)(2,1)S(1)}) custom-call(s32[1]{0:T(128)} %dynamic_slice.28.len_ref, bf16[1024,256]{1,0:T(8,128)(2,1)S(1)} %copy-done.19, bf16[1024,256]{1,0:T(8,128)(2,1)S(1)} %copy-done.35, bf16[1024,256]{1,0:T(8,128)(2,1)S(1)} %copy-done.37, ...), custom_call_target="tpu_custom_call" | custom-call | flops 10737418240 | bytes 4194304 | tf_op jit(solution)/shard_map/attend_backward/pallas_call | solution.py:166
  310.2 5.7 add_convert_fusion
  315.9 38.8 %collective-permute-done.24 = bf16[1024,1024]{1,0:T(8,128)(2,1)} collective-permute-done((bf16[1024,1024]{1,0:T(8,128)(2,1)}, bf16[1024,1024]{1,0:T(8,128)(2,1)}, u32[]{:S(2)}, u32[]{:S(2)}) %collective-permute-start.24) | collective-permute-done | bytes 2097184 | tf_op jit(solution)/shard_map/ppermute | solution.py:257
  354.7 5.2 add_convert_fusion.1
  367.4 31.6 %collective-permute-done.21 = bf16[1024,256]{1,0:T(8,128)(2,1)S(1)} collective-permute-done((bf16[1024,256]{1,0:T(8,128)(2,1)S(1)}, bf16[1024,256]{1,0:T(8,128)(2,1)S(1)}, u32[]{:S(2)}, u32[]{:S(2)}) %collective-permute-start.21) | collective-permute-done | bytes 524320 | tf_op jit(solution)/shard_map/ppermute | solution.py:257
  413.0 9.7 %attend_backward.7 = (bf16[1024,256]{1,0:T(8,128)(2,1)S(1)}, bf16[1024,256]{1,0:T(8,128)(2,1)S(1)}, bf16[1024,256]{1,0:T(8,128)(2,1)S(1)}) custom-call(s32[1]{0:T(128)} %dynamic_slice.27.len_ref, bf16[1024,256]{1,0:T(8,128)(2,1)S(1)} %copy-done.29, bf16[1024,256]{1,0:T(8,128)(2,1)S(1)} %copy-done.33, bf16[1024,256]{1,0:T(8,128)(2,1)S(1)} %copy-done.31, ...), custom_call_target="tpu_custom_call" | custom-call | flops 10737418240 | bytes 4194304 | tf_op jit(solution)/shard_map/attend_backward/pallas_call | solution.py:166
  432.0 9.4 %attend_backward.6 = (bf16[1024,256]{1,0:T(8,128)(2,1)S(1)}, bf16[1024,256]{1,0:T(8,128)(2,1)S(1)}, bf16[1024,256]{1,0:T(8,128)(2,1)S(1)}) custom-call(s32[1]{0:T(128)} %dynamic_slice.27.len_ref, bf16[1024,256]{1,0:T(8,128)(2,1)S(1)} %copy-done.21, bf16[1024,256]{1,0:T(8,128)(2,1)S(1)} %copy-done.23, bf16[1024,256]{1,0:T(8,128)(2,1)S(1)} %copy-done.25, ...), custom_call_target="tpu_custom_call" | custom-call | flops 10737418240 | bytes 4194304 | tf_op jit(solution)/shard_map/attend_backward/pallas_call | solution.py:166
  450.1 15.7 %collective-permute-done.19 = bf16[3,1024,256]{2,1,0:T(8,128)(2,1)S(1)} collective-permute-done((bf16[3,1024,256]{2,1,0:T(8,128)(2,1)S(1)}, bf16[3,1024,256]{2,1,0:T(8,128)(2,1)S(1)}, u32[]{:S(2)}, u32[]{:S(2)}) %collective-permute-start.19) | collective-permute-done | bytes 1572896 | tf_op jit(solution)/shard_map/ppermute | solution.py:257
  499.7 81.5 %psum.79 = bf16[9,1024]{1,0:T(8,128)(2,1)S(1)} all-reduce(bf16[9,1024]{1,0:T(8,128)(2,1)S(1)} %stack.157), channel_id=1, replica_groups=mesh['z'=4,'y'=2,'g'=2,'c'=2] {'z','y','g'}, use_global_device_ids=true, to_apply=%region_40.41 | all-reduce | flops 9216 | bytes 36864 | tf_op jit(solution)/shard_map/psum | solution.py:329
  582.1 17.5 %all-reduce = (bf16[4,256]{1,0:T(4,128)(2,1)S(1)}, bf16[1024]{0:T(1024)(128)(2,1)S(1)}) all-reduce(bf16[4,256]{1,0:T(4,128)(2,1)S(1)} %fusion.68, bf16[1024]{0:T(1024)(128)(2,1)S(1)} %add_convert_fusion.14), channel_id=1, replica_groups=mesh['z'=4,'y'=2,'g'=2,'c'=2] {'z','y'}, use_global_device_ids=true, to_apply=%region_27.28 | all-reduce | flops 2048 | bytes 8192 | tf_op jit(solution)/shard_map/psum | solution.py:258
  605.1 140.4 %all-reduce.4.cloned.1.call-done = (bf16[3,1024,256]{2,1,0:T(8,128)(2,1)}, bf16[256,1024]{1,0:T(8,128)(2,1)}, bf16[1024,256]{1,0:T(8,128)(2,1)}, bf16[2,1024,256...) async-done(((bf16[3,1024,256]{2,1,0:T(8,128)(2,1)}, bf16[256,1024]{1,0:T(8,128)(2,1)}, ...) | async-done | bytes 8388624 | tf_op jit(solution)/shard_map/psum | solution.py:258
  (439 shorter events, 204.3 us)
Async XLA Ops:
  7.2 738.3 %all-reduce.4.cloned.1.call-start = ((), (), s32[]{:S(2)}) async-start(), calls=%async_computation | async-start | bytes 16777216 | tf_op jit(solution)/shard_map/psum | solution.py:258
  8.9 38.7 %collective-permute-start = (bf16[512,1024]{0,1:T(8,128)(2,1)S(1)}, bf16[512,1024]{0,1:T(8,128)(2,1)}, u32[]{:S(2)}, u32[]{:S(2)}) collective-permute-start(bf16[512,1024]{0,1:T(8,128)(2,1)S(1)} %copy.33), channel_id=1, source_target_pairs={{0,1},{1,0},{2,3},{3,2},{4,5},{5,4},{6,7},{7,6},{8,9},{9,8},{10,11... | collective-permute-start | bytes 3145736 | tf_op jit(solution)/shard_map/ppermute | solution.py:223
  9.4 56.3 %collective-permute-start.1 = (bf16[3,1024,256]{2,1,0:T(8,128)(2,1)}, bf16[3,1024,256]{2,1,0:T(8,128)(2,1)}, u32[]{:S(2)}, u32[]{:S(2)}) collective-permute-start(bf16[3,1024,256]{2,1,0:T(8,128)(2,1)} %param.22), channel_id=1, source_target_pairs={{2,0},{0,2},{3,1},{1,3},{6,4},{4,6},{7,5},{5,7},{10,8},{8,10},{11,... | collective-permute-start | bytes 4718600 | tf_op jit(solution)/shard_map/ppermute | solution.py:249
  12.0 35.6 %collective-permute-start.2 = (bf16[4,256]{1,0:T(4,128)(2,1)}, bf16[4,256]{1,0:T(4,128)(2,1)S(1)}, u32[]{:S(2)}, u32[]{:S(2)}) collective-permute-start(bf16[4,256]{1,0:T(4,128)(2,1)} %param.29), channel_id=1, source_target_pairs={{2,0},{0,2},{3,1},{1,3},{6,4},{4,6},{7,5},{5,7},{10,8},{8,10},{11,... | collective-permute-start | bytes 6152 | tf_op jit(solution)/shard_map/ppermute | solution.py:249
  12.1 70.2 %collective-permute-start.3 = (bf16[256,1024]{1,0:T(8,128)(2,1)}, bf16[256,1024]{1,0:T(8,128)(2,1)S(1)}, u32[]{:S(2)}, u32[]{:S(2)}) collective-permute-start(bf16[256,1024]{1,0:T(8,128)(2,1)} %param.23), channel_id=1, source_target_pairs={{2,0},{0,2},{3,1},{1,3},{6,4},{4,6},{7,5},{5,7},{10,8},{8,10},{11,... | collective-permute-start | bytes 1572872 | tf_op jit(solution)/shard_map/ppermute | solution.py:249
  14.0 97.8 %collective-permute-start.6 = (bf16[1024,256]{1,0:T(8,128)(2,1)}, bf16[1024,256]{1,0:T(8,128)(2,1)}, u32[]{:S(2)}, u32[]{:S(2)}) collective-permute-start(bf16[1024,256]{1,0:T(8,128)(2,1)} %param.24), channel_id=1, source_target_pairs={{2,0},{0,2},{3,1},{1,3},{6,4},{4,6},{7,5},{5,7},{10,8},{8,10},{11,... | collective-permute-start | bytes 1572872 | tf_op jit(solution)/shard_map/ppermute | solution.py:249
  47.5 36.4 %collective-permute-start.5 = (bf16[512,1024]{0,1:T(8,128)(2,1)}, bf16[512,1024]{0,1:T(8,128)(2,1)S(1)}, u32[]{:S(2)}, u32[]{:S(2)}) collective-permute-start(bf16[512,1024]{0,1:T(8,128)(2,1)} %copy.36), channel_id=1, source_target_pairs={{0,1},{1,0},{2,3},{3,2},{4,5},{5,4},{6,7},{7,6},{8,9},{9,8},{10,11... | collective-permute-start | bytes 3145736 | tf_op jit(solution)/shard_map/ppermute | solution.py:223
  47.6 44.9 %collective-permute-start.7 = (bf16[2,1024,256]{2,1,0:T(8,128)(2,1)}, bf16[2,1024,256]{2,1,0:T(8,128)(2,1)S(1)}, u32[]{:S(2)}, u32[]{:S(2)}) collective-permute-start(bf16[2,1024,256]{2,1,0:T(8,128)(2,1)} %param.25), channel_id=1, source_target_pairs={{2,0},{0,2},{3,1},{1,3},{6,4},{4,6},{7,5},{5,7},{10,8},{8,10},{11,... | collective-permute-start | bytes 3145736 | tf_op jit(solution)/shard_map/ppermute | solution.py:249
  66.1 56.9 %collective-permute-start.8 = (bf16[256,1024]{1,0:T(8,128)(2,1)S(1)}, bf16[256,1024]{1,0:T(8,128)(2,1)S(1)}, u32[]{:S(2)}, u32[]{:S(2)}) collective-permute-start(bf16[256,1024]{1,0:T(8,128)(2,1)S(1)} %copy-done.80), channel_id=1, source_target_pairs={{2,0},{0,2},{3,1},{1,3},{6,4},{4,6},{7,5},{5,7},{10,8},{8,10},{11,... | collective-permute-start | bytes 1572872 | tf_op jit(solution)/shard_map/ppermute | solution.py:249
  83.0 12.0 %collective-permute-start.4 = (bf16[1024,1024]{0,1:T(8,128)(2,1)S(1)}, bf16[1024,1024]{0,1:T(8,128)(2,1)S(1)}, u32[]{:S(2)}, u32[]{:S(2)}) collective-permute-start(bf16[1024,1024]{0,1:T(8,128)(2,1)S(1)} %add_convert_fusion.8), channel_id=1, source_target_pairs={{0,1},{1,0},{2,3},{3,2},{4,5},{5,4},{6,7},{7,6},{8,9},{9,8},{10,11... | collective-permute-start | bytes 6291464 | tf_op jit(solution)/shard_map/ppermute | solution.py:223
  125.9 48.5 %collective-permute-start.10 = (bf16[1024,1024]{1,0:T(8,128)(2,1)S(1)}, bf16[1024,1024]{1,0:T(8,128)(2,1)S(1)}, u32[]{:S(2)}, u32[]{:S(2)}) collective-permute-start(bf16[1024,1024]{1,0:T(8,128)(2,1)S(1)} %copy-done.106), channel_id=1, source_target_pairs={{2,0},{0,2},{3,1},{1,3},{6,4},{4,6},{7,5},{5,7},{10,8},{8,10},{11,... | collective-permute-start | bytes 6291464 | tf_op jit(solution)/shard_map/ppermute | solution.py:249
  126.9 91.6 %collective-permute-start.12 = (bf16[1024,1024]{1,0:T(8,128)(2,1)S(1)}, bf16[1024,1024]{1,0:T(8,128)(2,1)S(1)}, u32[]{:S(2)}, u32[]{:S(2)}) collective-permute-start(bf16[1024,1024]{1,0:T(8,128)(2,1)S(1)} %copy-done.104), channel_id=1, source_target_pairs={{2,0},{0,2},{3,1},{1,3},{6,4},{4,6},{7,5},{5,7},{10,8},{8,10},{11,... | collective-permute-start | bytes 6291464 | tf_op jit(solution)/shard_map/ppermute | solution.py:249
  257.0 9.6 %collective-permute-start.15 = (bf16[1024,1024]{0,1:T(8,128)(2,1)S(1)}, bf16[1024,1024]{0,1:T(8,128)(2,1)S(1)}, u32[]{:S(2)}, u32[]{:S(2)}) collective-permute-start(bf16[1024,1024]{0,1:T(8,128)(2,1)S(1)} %add_convert_fusion.3), channel_id=1, source_target_pairs={{0,1},{1,0},{2,3},{3,2},{4,5},{5,4},{6,7},{7,6},{8,9},{9,8},{10,11... | collective-permute-start | bytes 6291464 | tf_op jit(solution)/shard_map/ppermute | solution.py:223
  260.9 48.8 %collective-permute-start.25 = (bf16[1024,1024]{1,0:T(8,128)(2,1)}, bf16[1024,1024]{1,0:T(8,128)(2,1)}, u32[]{:S(2)}, u32[]{:S(2)}) collective-permute-start(bf16[1024,1024]{1,0:T(8,128)(2,1)} %convolution_convert_fusion), channel_id=1, source_target_pairs={{0,2},{2,0},{1,3},{3,1},{4,6},{6,4},{5,7},{7,5},{8,10},{10,8},{9,1... | collective-permute-start | bytes 6291464 | tf_op jit(solution)/shard_map/ppermute | solution.py:257
  265.0 89.7 %collective-permute-start.24 = (bf16[1024,1024]{1,0:T(8,128)(2,1)}, bf16[1024,1024]{1,0:T(8,128)(2,1)}, u32[]{:S(2)}, u32[]{:S(2)}) collective-permute-start(bf16[1024,1024]{1,0:T(8,128)(2,1)} %convolution_convert_fusion.1), channel_id=1, source_target_pairs={{0,2},{2,0},{1,3},{3,1},{4,6},{6,4},{5,7},{7,5},{8,10},{10,8},{9,1... | collective-permute-start | bytes 6291464 | tf_op jit(solution)/shard_map/ppermute | solution.py:257
  304.1 97.6 %collective-permute-start.16 = (bf16[1024,1024]{0,1:T(8,128)(2,1)S(1)}, bf16[1024,1024]{0,1:T(8,128)(2,1)S(1)}, u32[]{:S(2)}, u32[]{:S(2)}) collective-permute-start(bf16[1024,1024]{0,1:T(8,128)(2,1)S(1)} %add_convert_fusion.2), channel_id=1, source_target_pairs={{0,1},{1,0},{2,3},{3,2},{4,5},{5,4},{6,7},{7,6},{8,9},{9,8},{10,11... | collective-permute-start | bytes 6291464 | tf_op jit(solution)/shard_map/ppermute | solution.py:223
  305.0 60.8 %collective-permute-start.23 = (bf16[256,1024]{1,0:T(8,128)(2,1)S(1)}, bf16[256,1024]{1,0:T(8,128)(2,1)S(1)}, u32[]{:S(2)}, u32[]{:S(2)}) collective-permute-start(bf16[256,1024]{1,0:T(8,128)(2,1)S(1)} %convolution_convert_fusion.2), channel_id=1, source_target_pairs={{0,2},{2,0},{1,3},{3,1},{4,6},{6,4},{5,7},{7,5},{8,10},{10,8},{9,1... | collective-permute-start | bytes 1572872 | tf_op jit(solution)/shard_map/ppermute | solution.py:257
  307.0 93.5 %collective-permute-start.22 = (bf16[2,1024,256]{2,1,0:T(8,128)(2,1)S(1)}, bf16[2,1024,256]{2,1,0:T(8,128)(2,1)S(1)}, u32[]{:S(2)}, u32[]{:S(2)}) collective-permute-start(bf16[2,1024,256]{2,1,0:T(8,128)(2,1)S(1)} %pad_maximum_fusion.1), channel_id=1, source_target_pairs={{0,2},{2,0},{1,3},{3,1},{4,6},{6,4},{5,7},{7,5},{8,10},{10,8},{9,1... | collective-permute-start | bytes 3145736 | tf_op jit(solution)/shard_map/ppermute | solution.py:257
  309.7 89.2 %collective-permute-start.21 = (bf16[1024,256]{1,0:T(8,128)(2,1)S(1)}, bf16[1024,256]{1,0:T(8,128)(2,1)S(1)}, u32[]{:S(2)}, u32[]{:S(2)}) collective-permute-start(bf16[1024,256]{1,0:T(8,128)(2,1)S(1)} %convolution_convert_fusion.5), channel_id=1, source_target_pairs={{0,2},{2,0},{1,3},{3,1},{4,6},{6,4},{5,7},{7,5},{8,10},{10,8},{9,1... | collective-permute-start | bytes 1572872 | tf_op jit(solution)/shard_map/ppermute | solution.py:257
  411.7 36.8 %collective-permute-start.20 = (bf16[256,1024]{1,0:T(8,128)(2,1)S(1)}, bf16[256,1024]{1,0:T(8,128)(2,1)S(1)}, u32[]{:S(2)}, u32[]{:S(2)}) collective-permute-start(bf16[256,1024]{1,0:T(8,128)(2,1)S(1)} %convolution_convert_fusion.6), channel_id=1, source_target_pairs={{0,2},{2,0},{1,3},{3,1},{4,6},{6,4},{5,7},{7,5},{8,10},{10,8},{9,1... | collective-permute-start | bytes 1572872 | tf_op jit(solution)/shard_map/ppermute | solution.py:257
  430.2 35.6 %collective-permute-start.19 = (bf16[3,1024,256]{2,1,0:T(8,128)(2,1)S(1)}, bf16[3,1024,256]{2,1,0:T(8,128)(2,1)S(1)}, u32[]{:S(2)}, u32[]{:S(2)}) collective-permute-start(bf16[3,1024,256]{2,1,0:T(8,128)(2,1)S(1)} %pad_maximum_fusion), channel_id=1, source_target_pairs={{0,2},{2,0},{1,3},{3,1},{4,6},{6,4},{5,7},{7,5},{8,10},{10,8},{9,1... | collective-permute-start | bytes 4718600 | tf_op jit(solution)/shard_map/ppermute | solution.py:257
  481.9 13.4 %collective-permute-start.18 = (bf16[512,1024]{1,0:T(8,128)(2,1)}, bf16[512,1024]{1,0:T(8,128)(2,1)}, u32[]{:S(2)}, u32[]{:S(2)}) collective-permute-start(bf16[512,1024]{1,0:T(8,128)(2,1)} %dynamic-slice_convert_fusion), channel_id=1, source_target_pairs={{0,1},{1,0},{2,3},{3,2},{4,5},{5,4},{6,7},{7,6},{8,9},{9,8},{10,11... | collective-permute-start | bytes 3145736 | tf_op jit(solution)/shard_map/ppermute | solution.py:223
  495.3 105.6 %collective-permute-start.17 = (bf16[512,1024]{0,1:T(8,128)(2,1)}, bf16[512,1024]{0,1:T(8,128)(2,1)S(1)}, u32[]{:S(2)}, u32[]{:S(2)}) collective-permute-start(bf16[512,1024]{0,1:T(8,128)(2,1)} %dynamic-slice_convert_fusion.1), channel_id=1, source_target_pairs={{0,1},{1,0},{2,3},{3,2},{4,5},{5,4},{6,7},{7,6},{8,9},{9,8},{10,11... | collective-permute-start | bytes 3145736 | tf_op jit(solution)/shard_map/ppermute | solution.py:223
  498.9 83.2 %collective-permute-start.26 = (bf16[4,256]{1,0:T(4,128)(2,1)S(1)}, bf16[4,256]{1,0:T(4,128)(2,1)S(1)}, u32[]{:S(2)}, u32[]{:S(2)}) collective-permute-start(bf16[4,256]{1,0:T(4,128)(2,1)S(1)} %pad_maximum_fusion.2), channel_id=1, source_target_pairs={{0,2},{2,0},{1,3},{3,1},{4,6},{6,4},{5,7},{7,5},{8,10},{10,8},{9,1... | collective-permute-start | bytes 6152 | tf_op jit(solution)/shard_map/ppermute | solution.py:257
  (130 other events, 1238.9 us)
Sparse Core Ops, SparseCore 0:
  467.6 277.8 all-reduce.3

commit v2 on v1

--- a/solution.py
+++ b/solution.py
@@ -249,13 +249,43 @@
         every = [shard] + [lax.ppermute(shard, "g", [((i + k) % gn, i) for i in range(gn)]) for k in range(1, gn)]
         return [jnp.concatenate(every, axis=axis)] if joined else every
 
-    def collect(parts, axis):
-        if joined:
-            parts = jnp.split(parts[0], gn, axis=axis)
+    def send_home(parts):
         total = parts[0]
         for k in range(1, gn):
             total = total + lax.ppermute(parts[k].astype(LOW), "g", [(i, (i + k) % gn) for i in range(gn)]).astype(F32)
-        return lax.psum(total.astype(LOW), ("z", "y")).astype(F32)
+        return total
+
+    steps = [("y", 1, lax.axis_index("y"), yn)] if yn == 2 else []
+    steps += [("z", 1 << b, lax.axis_index("z"), zn) for b in range((zn - 1).bit_length())]
+
+    def pairwise(rows, axis, far, size):
+        return lax.ppermute(rows, axis, [(i, i ^ far) for i in range(size)])
+
+    def sum_groups(total):
+        for axis, far, at, size in steps:
+            half = total.shape[0] // 2
+            bit = (at // far) % 2
+            away = lax.dynamic_slice_in_dim(total, (1 - bit) * half, half, 0).astype(LOW)
+            keep = lax.dynamic_slice_in_dim(total, bit * half, half, 0)
+            total = keep + pairwise(away, axis, far, size).astype(F32)
+        total = total.astype(LOW)
+        for axis, far, at, size in reversed(steps):
+            got = pairwise(total, axis, far, size)
+            total = jnp.where((at // far) % 2 == 0, jnp.concatenate([total, got]), jnp.concatenate([got, total]))
+        return total.astype(F32)
+
+    def spread_wide(shard, axis):
+        size = shard.shape[0] // (zn * yn)
+        at = lax.axis_index("z") * yn + lax.axis_index("y")
+        piece = lax.dynamic_slice_in_dim(shard, at * size, size, 0)
+        every = [shard]
+        for k in range(1, gn):
+            got = lax.ppermute(piece, "g", [((i + k) % gn, i) for i in range(gn)])
+            every.append(lax.all_gather(got, ("z", "y"), axis=0, tiled=True))
+        return [jnp.concatenate(every, axis=axis)] if joined else every
+
+    def parts_of(values, axis):
+        return jnp.split(values[0], gn, axis=axis) if joined else values
 
     target_length = lax.dynamic_slice_in_dim(target_lengths, seq, 1, 0)
     memory_length = lax.dynamic_slice_in_dim(memory_lengths, seq, 1, 0)
@@ -268,9 +298,9 @@
     w_cross_mem = spread(cross_memory, 2)
     w_cross_q = spread(cross_query, 1)
     w_cross_out = spread(cross_output, 0)
-    w_in = spread(feed_in, 1)
+    w_in = spread_wide(feed_in, 1)
     b_in = spread(feed_bias, 0)
-    w_out = spread(feed_out, 0)
+    w_out = spread_wide(feed_out, 0)
     cot_all = gather_rows(cotangent)
     shards = range(len(w_self))
 
@@ -298,37 +328,49 @@
     grad_three = norm_backward(cot, unit_three, inverse_three, norm_gain[2])
     low_three = grad_three.astype(LOW)
     grad_hidden = [_nt(low_three, w_out[s]) for s in shards]
-    grad_feed_out = collect([tn(hidden[s], low_three) for s in shards], 0)
+    grad_feed_out = sum_groups(send_home(parts_of([tn(hidden[s], low_three) for s in shards], 0)))
     grad_pre = [gelu_backward(hidden_pre[s], grad_hidden[s]).astype(LOW) for s in shards]
-    grad_feed_in = collect([tn(third, grad_pre[s]) for s in shards], 1)
+    grad_feed_in = sum_groups(send_home(parts_of([tn(third, grad_pre[s]) for s in shards], 1)))
     grad_normed_two = residual_scale * grad_three + sum_all(sum(_nt(grad_pre[s], w_in[s]) for s in shards))
     grad_two = norm_backward(grad_normed_two, unit_two, inverse_two, norm_gain[1])
     low_two = grad_two.astype(LOW)
     grad_cross_mixed = [_nt(low_two, w_cross_out[s]).astype(LOW) for s in shards]
-    grad_cross_output = collect([tn(cross_mixed[s], low_two) for s in shards], 0)
+    cross_out_parts = parts_of([tn(low_two, cross_mixed[s]) for s in shards], 1)
     cross_dq, cross_dk, cross_dv = zip(*[attn_bwd(memory_length, cross_q[s], cross_k[s], cross_v[s], cross_mixed[s], grad_cross_mixed[s], cross_lse[s], False) for s in shards])
     grad_normed_one = residual_scale * grad_two + sum_all(sum(_nt(cross_dq[s], w_cross_q[s]) for s in shards))
-    grad_cross_query = collect([tn(second, cross_dq[s]) for s in shards], 1)
-    grad_cross_memory = collect([jnp.stack([tn(memory_all, cross_dk[s]), tn(memory_all, cross_dv[s])]) for s in shards], 2)
+    cross_parts = [cross_out_parts, parts_of([tn(second, cross_dq[s]) for s in shards], 1)]
+    cross_parts += [parts_of([tn(memory_all, cross_dk[s]) for s in shards], 1), parts_of([tn(memory_all, cross_dv[s]) for s in shards], 1)]
+    cross_total = sum_groups(send_home([jnp.concatenate([part[k] for part in cross_parts]) for k in range(gn)]))
     grad_memory = sum_own(sum(_nt(cross_dk[s], w_cross_mem[s][0]) + _nt(cross_dv[s], w_cross_mem[s][1]) for s in shards)).astype(LOW)
     grad_one = norm_backward(grad_normed_one, unit_one, inverse_one, norm_gain[0])
     low_one = grad_one.astype(LOW)
     grad_self_mixed = [_nt(low_one, w_self_out[s]).astype(LOW) for s in shards]
-    grad_self_output = collect([tn(self_mixed[s], low_one) for s in shards], 0)
+    self_out_parts = parts_of([tn(low_one, self_mixed[s]) for s in shards], 1)
     self_dq, self_dk, self_dv = zip(*[attn_bwd(target_length, self_q[s], self_k[s], self_v[s], self_mixed[s], grad_self_mixed[s], self_lse[s], True) for s in shards])
-    grad_self_inputs = collect([jnp.stack([tn(token_all, self_dq[s]), tn(token_all, self_dk[s]), tn(token_all, self_dv[s])]) for s in shards], 2)
     token_part = sum(_nt(self_dq[s], w_self[s][0]) + _nt(self_dk[s], w_self[s][1]) + _nt(self_dv[s], w_self[s][2]) for s in shards)
     grad_tokens = (residual_scale * own_rows(grad_one) + sum_own(token_part)).astype(LOW)
 
     def sums(rows):
         return jnp.sum(rows.astype(F32), axis=0)
 
-    proj_sums = collect([jnp.stack([sums(self_dq[s]), sums(self_dv[s]), sums(cross_dq[s]), sums(cross_dv[s])]) for s in shards], 1)
-    feed_sums = collect([sums(grad_pre[s]) for s in shards], 0)
     terms = jnp.stack([sums(low_one), sums(low_two), sums(low_three), sums(grad_normed_one * unit_one), sums(grad_normed_two * unit_two), sums(cot * unit_three), sums(grad_normed_one), sums(grad_normed_two), sums(cot)])
-    terms = lax.psum(terms.astype(LOW), ("z", "y", "g")).astype(F32)
-    terms = lax.dynamic_slice_in_dim(terms, (seq * cn + core) * width, width, 1)
-    return (block_out, grad_tokens, grad_memory, grad_self_inputs, grad_self_output, grad_cross_query, grad_cross_memory, grad_cross_output, grad_feed_in, grad_feed_out, proj_sums, feed_sums, terms[0:3], terms[3:6], terms[6:9])
+    proj_sums = parts_of([jnp.stack([sums(self_dq[s]), sums(self_dv[s]), sums(cross_dq[s]), sums(cross_dv[s])]) for s in shards], 1)
+    feed_sums = parts_of([sums(grad_pre[s]) for s in shards], 0)
+    self_parts = [self_out_parts] + [parts_of([tn(token_all, grads[s]) for s in shards], 1) for grads in (self_dq, self_dk, self_dv)]
+    packed = []
+    for k in range(gn):
+        small = lax.dynamic_slice_in_dim(terms, ((seq + k) % gn * cn + core) * width, width, 1)
+        small = jnp.concatenate([small, proj_sums[k], feed_sums[k].reshape(-1, width)])
+        small = jnp.pad(small, ((0, 16 * zn * yn - small.shape[0]), (0, 0)))
+        packed.append(jnp.concatenate([part[k] for part in self_parts] + [small]))
+    self_total = sum_groups(send_home(packed))
+    model = tokens.shape[1]
+    take = lambda rows, at: lax.slice_in_dim(rows, at * model, (at + 1) * model)
+    small = self_total[4 * model:]
+    grad_self_inputs = jnp.stack([take(self_total, 1), take(self_total, 2), take(self_total, 3)])
+    grad_cross_memory = jnp.stack([take(cross_total, 2), take(cross_total, 3)])
+    feed_rows = feed_bias.shape[0] // width
+    return (block_out, grad_tokens, grad_memory, grad_self_inputs, take(self_total, 0).T, take(cross_total, 1), grad_cross_memory, take(cross_total, 0).T, grad_feed_in, grad_feed_out, small[9:13], small[13:13 + feed_rows].reshape(-1), small[0:3], small[3:6], small[6:9])
 
 
 def solution(mesh):

time: 775 us -> 695 us (0.90)
  blocking collectives: 99.1 us -> 0 us
  waiting for transfers between devices: 326 us -> 237 us
  matrix products: 132 us -> 168 us
  other arithmetic: 61.9 us -> 92.9 us
  starting transfers between devices: 21.7 us -> 42.7 us
  local copies, waits for them, and re-layouts: 29.7 us -> 49.2 us
    psum x1 -> x0, waiting for transfers between devices: 140 us -> none  [collect(): return lax.psum(total.astype(LOW), ('z', 'y')).astype(F32)]
    ppermute x9 -> x30, waiting for transfers between devices: 90.2 us -> 205 us  [the longest x24 145 us: pairwise(): return lax.ppermute(rows, axis, [(i, i ^ far) for i in range(size)])]
    psum x2 -> x0, blocking collectives: 99.1 us -> none  [the longest x1 81.5 us: layer(): terms = lax.psum(terms.astype(LOW), ('z', 'y', 'g')).astype(F32)]
    ppermute x9 -> x7, waiting for transfers between devices: 94.1 us -> 19.8 us  [spread(): lax.ppermute(shard, 'g', [((i + k) % gn, i) for i in range(gn)])]
    ppermute x9 -> x30, starting transfers between devices: 9.26 us -> 34.1 us  [the longest x24 27.3 us: pairwise(): return lax.ppermute(rows, axis, [(i, i ^ far) for i in range(size)])]
    dot_general x20, matrix products: 55.2 us -> 72.3 us  [_nn(): lax.dot_general(a, b, (((1,), (0,)), ((), ())), preferred_element_type=jn...]
    unnamed x255 -> x253, local copies, waits for them, and re-layouts: 23.3 us -> 35.6 us
    all_gather x0 -> x2, waiting for transfers between devices: none -> 10.8 us  [spread_wide(): every.append(lax.all_gather(got, ('z', 'y'), axis=0, tiled=True))]
  transfers between devices with their start and end apart: 29 -> 49, of which waited for: 12 -> 22; matrix products, arithmetic and copies ran while one was open for 21% -> 36% of each run, Pallas kernels for 10% -> 12%
where the time goes in v2:
time: 695 us; the launch traced here: 685 us
  waiting for transfers between devices  237 us (34%)
  matrix products  168 us (24%)
  other arithmetic  92.9 us (13%)
  Pallas kernels  79.3 us (11%)
  local copies, waits for them, and re-layouts  49.2 us (7%)
  starting transfers between devices  42.7 us (6%)
  between operations  16.2 us (2%)
    ppermute x24, waiting for transfers between devices, pairwise(): return lax.ppermute(rows, axis, [(i, i ^ far) for i in range(size)])  145 us
    dot_general x20, matrix products, _nn(): lax.dot_general(a, b, (((1,), (0,)), ((), ())), preferred_element_type=jn...  72.3 us
    dot_general x20, matrix products, tn(): lax.dot_general(rows, grads, (((0,), (0,)), ((), ())), preferred_element_...  52.3 us
    pallas_call x4, Pallas kernels, attn_bwd(): pl.pallas_call(functools.partial(bwd_kernel, causal=causal, bq=bq), out_s...  44.9 us
    dot_general x20, matrix products, _nt(): lax.dot_general(a, b, (((1,), (1,)), ((), ())), preferred_element_type=jn...  43.3 us
    unnamed x253, local copies, waits for them, and re-layouts  35.6 us
    pallas_call x4, Pallas kernels, attn_fwd(): pl.pallas_call(functools.partial(fwd_kernel, causal=causal, bq=bq), out_s...  34.4 us
    ppermute x4, waiting for transfers between devices, send_home(): lax.ppermute(parts[k].astype(LOW), 'g', [(i, (i + k) % gn) for i in range...  30.4 us
  transfers between devices with their start and end apart: 49, of which 22 were waited for; matrix products, arithmetic and copies ran while one was open for 36% of the time, Pallas kernels for 12%

profile of v2, /device:TPU:0, one launch (start us, length us, event | category | flops | bytes accessed | tf_op | source)
XLA Modules:
  0.0 685.3 jit_solution(13002591522517316312)
XLA Ops:
  28.5 7.6 %attend_forward.4 = (bf16[1024,256]{1,0:T(8,128)(2,1)S(1)}, f32[1024,128]{1,0:T(8,128)S(1)}) custom-call(s32[1]{0:T(128)} %dynamic_slice.108.len_ref, bf16[1024,256]{1,0:T(8,128)(2,1)S(1)} %fusion.31.q_ref, bf16[1024,256]{1,0:T(8,128)(2,1)S(1)} %convolution_convert_fusion.17.k_ref, bf16[1024,256]{1,0:T(8,128)(2,1)S(1)} %fusion.32.v_ref), custom_call_target="tpu_custom_call" | custom-call | flops 4294967296 | bytes 2097152 | tf_op jit(solution)/shard_map/attend_forward/pallas_call | solution.py:82
  37.1 13.1 %collective-permute-done.1 = bf16[3,1024,256]{2,1,0:T(8,128)(2,1)} collective-permute-done((bf16[3,1024,256]{2,1,0:T(8,128)(2,1)}, bf16[3,1024,256]{2,1,0:T(8,128)(2,1)}, u32[]{:S(2)}, u32[]{:S(2)}) %collective-permute-start.1) | collective-permute-done | bytes 1572896 | tf_op jit(solution)/shard_map/ppermute | solution.py:249
  58.3 7.9 %attend_forward.5 = (bf16[1024,256]{1,0:T(8,128)(2,1)S(1)}, f32[1024,128]{1,0:T(8,128)S(1)}) custom-call(s32[1]{0:T(128)} %dynamic_slice.108.len_ref, bf16[1024,256]{1,0:T(8,128)(2,1)S(1)} %fusion.33.q_ref, bf16[1024,256]{1,0:T(8,128)(2,1)S(1)} %convolution_convert_fusion.16.k_ref, bf16[1024,256]{1,0:T(8,128)(2,1)S(1)} %fusion.34.v_ref), custom_call_target="tpu_custom_call" | custom-call | flops 4294967296 | bytes 2097152 | tf_op jit(solution)/shard_map/attend_forward/pallas_call | solution.py:82
  70.4 29.6 %collective-permute-done.10 = bf16[128,1024]{1,0:T(8,128)(2,1)} collective-permute-done((bf16[128,1024]{1,0:T(8,128)(2,1)S(1)}, bf16[128,1024]{1,0:T(8,128)(2,1)}, u32[]{:S(2)}, u32[]{:S(2)}) %collective-permute-start.10) | collective-permute-done | bytes 262176 | tf_op jit(solution)/shard_map/ppermute | solution.py:283
  118.8 9.4 %attend_forward.6 = (bf16[1024,256]{1,0:T(8,128)(2,1)S(1)}, f32[1024,128]{1,0:T(8,128)S(1)}) custom-call(s32[1]{0:T(128)} %dynamic_slice.109.len_ref, bf16[1024,256]{1,0:T(8,128)(2,1)S(1)} %fusion.35.q_ref, bf16[1024,256]{1,0:T(8,128)(2,1)S(1)} %convolution_convert_fusion.15.k_ref, bf16[1024,256]{1,0:T(8,128)(2,1)S(1)} %fusion.36.v_ref), custom_call_target="tpu_custom_call" | custom-call | flops 4294967296 | bytes 2097152 | tf_op jit(solution)/shard_map/attend_forward/pallas_call | solution.py:82
  131.0 9.5 %attend_forward.7 = (bf16[1024,256]{1,0:T(8,128)(2,1)S(1)}, f32[1024,128]{1,0:T(8,128)S(1)}) custom-call(s32[1]{0:T(128)} %dynamic_slice.109.len_ref, bf16[1024,256]{1,0:T(8,128)(2,1)S(1)} %fusion.37.q_ref, bf16[1024,256]{1,0:T(8,128)(2,1)S(1)} %convolution_convert_fusion.14.k_ref, bf16[1024,256]{1,0:T(8,128)(2,1)S(1)} %fusion.38.v_ref), custom_call_target="tpu_custom_call" | custom-call | flops 4294967296 | bytes 2097152 | tf_op jit(solution)/shard_map/attend_forward/pallas_call | solution.py:82
  161.4 12.6 %multiply_convert_fusion.1 = (bf16[1024,1024]{1,0:T(8,128)(2,1)S(1)}, f32[1024,1024]{1,0:T(8,128)}, f32[1024,1024]{1,0:T(8,128)}) fusion(f32[1024]{0:T(1024)S(1)} %convert_element_type.348, bf16[1024,1024]{0,1:T(8,128)(2,1)S(1)} %fusion.20, bf16[1024,1024]{1,0:T(8,128)(2,1)S(1)} %copy-done), kind=kOutput, calls=%fused_computation.52 | convolution fusion | flops 2216689664 | bytes 14684160 | tf_op jit(solution)/shard_map/dot_general | solution.py:17
  179.8 15.3 %multiply_convert_fusion = (bf16[1024,1024]{1,0:T(8,128)(2,1)}, f32[1024,1024]{1,0:T(8,128)}, f32[1024,1024]{1,0:T(8,128)}) fusion(f32[1024]{0:T(1024)S(1)} %convert_element_type.350, bf16[1024,1024]{0,1:T(8,128)(2,1)} %copy-done.64, bf16[1024,1024]{1,0:T(8,128)(2,1)} %all-gather.3.cloned.1.call-done), kind=kOutput, calls=%fused_computation.39 | convolution fusion | flops 2216689664 | bytes 14684160 | tf_op jit(solution)/shard_map/dot_general | solution.py:17
  195.1 10.8 %all-gather.5.cloned.1.call-done = bf16[1024,1024]{1,0:T(8,128)(2,1)} async-done(((bf16[128,1024]{1,0:T(8,128)(2,1)}), bf16[1024,1024]{1,0:T(8,128)(2,1)}) %all-gather.5.cloned.1.call-update) | async-done | bytes 2097168 | tf_op jit(solution)/shard_map/all_gather | solution.py:284
  274.3 12.7 %attend_backward.4 = (bf16[1024,256]{1,0:T(8,128)(2,1)S(1)}, bf16[1024,256]{1,0:T(8,128)(2,1)S(1)}, bf16[1024,256]{1,0:T(8,128)(2,1)S(1)}) custom-call(s32[1]{0:T(128)} %dynamic_slice.109.len_ref, bf16[1024,256]{1,0:T(8,128)(2,1)S(1)} %copy-done.18, bf16[1024,256]{1,0:T(8,128)(2,1)S(1)} %copy-done.14, bf16[1024,256]{1,0:T(8,128)(2,1)S(1)} %copy-done.22, ...), custom_call_target="tpu_custom_call" | custom-call | flops 10737418240 | bytes 4194304 | tf_op jit(solution)/shard_map/attend_backward/pallas_call | solution.py:166
  290.8 12.9 %attend_backward.5 = (bf16[1024,256]{1,0:T(8,128)(2,1)S(1)}, bf16[1024,256]{1,0:T(8,128)(2,1)S(1)}, bf16[1024,256]{1,0:T(8,128)(2,1)S(1)}) custom-call(s32[1]{0:T(128)} %dynamic_slice.109.len_ref, bf16[1024,256]{1,0:T(8,128)(2,1)S(1)} %copy-done.16, bf16[1024,256]{1,0:T(8,128)(2,1)S(1)} %copy-done.12, bf16[1024,256]{1,0:T(8,128)(2,1)S(1)} %copy-done.20, ...), custom_call_target="tpu_custom_call" | custom-call | flops 10737418240 | bytes 4194304 | tf_op jit(solution)/shard_map/attend_backward/pallas_call | solution.py:166
  321.0 30.4 %collective-permute-done.40 = bf16[1024,1024]{1,0:T(8,128)(2,1)} collective-permute-done((bf16[1024,1024]{1,0:T(8,128)(2,1)}, bf16[1024,1024]{1,0:T(8,128)(2,1)}, u32[]{:S(2)}, u32[]{:S(2)}) %collective-permute-start.40) | collective-permute-done | bytes 2097184 | tf_op jit(solution)/shard_map/ppermute | solution.py:255
  368.6 11.6 %collective-permute-done.41 = bf16[512,1024]{1,0:T(8,128)(2,1)S(1)} collective-permute-done((bf16[512,1024]{1,0:T(8,128)(2,1)S(1)}, bf16[512,1024]{1,0:T(8,128)(2,1)S(1)}, u32[]{:S(2)}, u32[]{:S(2)}) %collective-permute-start.41) | collective-permute-done | bytes 1048608 | tf_op jit(solution)/shard_map/ppermute | solution.py:262
  383.8 15.1 %collective-permute-done.42 = bf16[256,1024]{1,0:T(8,128)(2,1)S(1)} collective-permute-done((bf16[256,1024]{1,0:T(8,128)(2,1)S(1)}, bf16[256,1024]{1,0:T(8,128)(2,1)S(1)}, u32[]{:S(2)}, u32[]{:S(2)}) %collective-permute-start.42) | collective-permute-done | bytes 524320 | tf_op jit(solution)/shard_map/ppermute | solution.py:262
  407.0 10.7 %collective-permute-done.43 = bf16[128,1024]{1,0:T(8,128)(2,1)} collective-permute-done((bf16[128,1024]{1,0:T(8,128)(2,1)S(1)}, bf16[128,1024]{1,0:T(8,128)(2,1)}, u32[]{:S(2)}, u32[]{:S(2)}) %collective-permute-start.43) | collective-permute-done | bytes 262176 | tf_op jit(solution)/shard_map/ppermute | solution.py:262
  419.0 8.1 %multiply_reduce_fusion.1 = (f32[1024]{0:T(1024)S(1)}, f32[1024]{0:T(1024)S(1)}, f32[1024]{0:T(1024)S(1)}, f32[1024]{0:T(1024)S(1)}, f32[1024,1024]{0,1:T(8,128)S(1)}) fusion(f32[1024,1024]{0,1:T(8,128)} %copy-done.41, f32[1024]{0:T(1024)S(1)} %copy-done.93, f32[1024]{0:T(1024)S(1)} %copy-done.91, f32[1024]{0:T(1024)S(1)} %bitcast.191, ...), kind=kLoop, calls=%fused_computation.20 | loop fusion | flops 22016000 | bytes 21020672 | tf_op jit(solution)/shard_map/reduce_sum | solution.py:354
  434.9 9.7 %attend_backward.7 = (bf16[1024,256]{1,0:T(8,128)(2,1)S(1)}, bf16[1024,256]{1,0:T(8,128)(2,1)S(1)}, bf16[1024,256]{1,0:T(8,128)(2,1)S(1)}) custom-call(s32[1]{0:T(128)} %dynamic_slice.108.len_ref, bf16[1024,256]{1,0:T(8,128)(2,1)S(1)} %copy-done.32, bf16[1024,256]{1,0:T(8,128)(2,1)S(1)} %copy-done.36, bf16[1024,256]{1,0:T(8,128)(2,1)S(1)} %copy-done.34, ...), custom_call_target="tpu_custom_call" | custom-call | flops 10737418240 | bytes 4194304 | tf_op jit(solution)/shard_map/attend_backward/pallas_call | solution.py:166
  457.5 9.6 %attend_backward.6 = (bf16[1024,256]{1,0:T(8,128)(2,1)S(1)}, bf16[1024,256]{1,0:T(8,128)(2,1)S(1)}, bf16[1024,256]{1,0:T(8,128)(2,1)S(1)}) custom-call(s32[1]{0:T(128)} %dynamic_slice.108.len_ref, bf16[1024,256]{1,0:T(8,128)(2,1)S(1)} %copy-done.24, bf16[1024,256]{1,0:T(8,128)(2,1)S(1)} %copy-done.26, bf16[1024,256]{1,0:T(8,128)(2,1)S(1)} %copy-done.28, ...), custom_call_target="tpu_custom_call" | custom-call | flops 10737418240 | bytes 4194304 | tf_op jit(solution)/shard_map/attend_backward/pallas_call | solution.py:166
  518.6 15.8 %collective-permute-done.20 = bf16[2112,256]{1,0:T(8,128)(2,1)} collective-permute-done((bf16[2112,256]{1,0:T(8,128)(2,1)}, bf16[2112,256]{1,0:T(8,128)(2,1)}, u32[]{:S(2)}, u32[]{:S(2)}) %collective-permute-start.20) | collective-permute-done | bytes 1081376 | tf_op jit(solution)/shard_map/ppermute | solution.py:262
  540.2 13.4 %collective-permute-done.29 = bf16[512,256]{1,0:T(8,128)(2,1)S(1)} collective-permute-done((bf16[512,256]{1,0:T(8,128)(2,1)S(1)}, bf16[512,256]{1,0:T(8,128)(2,1)S(1)}, u32[]{:S(2)}, u32[]{:S(2)}) %collective-permute-start.29) | collective-permute-done | bytes 262176 | tf_op jit(solution)/shard_map/ppermute | solution.py:262
  564.3 9.0 %collective-permute-done.38 = bf16[256,1024]{1,0:T(8,128)(2,1)S(1)} collective-permute-done((bf16[256,1024]{1,0:T(8,128)(2,1)S(1)}, bf16[256,1024]{1,0:T(8,128)(2,1)S(1)}, u32[]{:S(2)}, u32[]{:S(2)}) %collective-permute-start.38) | collective-permute-done | bytes 524320 | tf_op jit(solution)/shard_map/ppermute | solution.py:262
  583.6 11.5 %collective-permute-done.45 = bf16[256,1024]{1,0:T(8,128)(2,1)S(1)} collective-permute-done((bf16[256,1024]{1,0:T(8,128)(2,1)S(1)}, bf16[256,1024]{1,0:T(8,128)(2,1)S(1)}, u32[]{:S(2)}, u32[]{:S(2)}) %collective-permute-start.45) | collective-permute-done | bytes 524320 | tf_op jit(solution)/shard_map/ppermute | solution.py:262
  626.6 18.2 %collective-permute-done.32 = bf16[2048,256]{1,0:T(8,128)(2,1)} collective-permute-done((bf16[2048,256]{1,0:T(8,128)(2,1)}, bf16[2048,256]{1,0:T(8,128)(2,1)}, u32[]{:S(2)}, u32[]{:S(2)}) %collective-permute-start.32) | collective-permute-done | bytes 1048608 | tf_op jit(solution)/shard_map/ppermute | solution.py:262
  653.5 12.5 %collective-permute-done.25 = bf16[2112,256]{1,0:T(8,128)(2,1)} collective-permute-done((bf16[2112,256]{1,0:T(8,128)(2,1)S(1)}, bf16[2112,256]{1,0:T(8,128)(2,1)}, u32[]{:S(2)}, u32[]{:S(2)}) %collective-permute-start.25) | collective-permute-done | bytes 1081376 | tf_op jit(solution)/shard_map/ppermute | solution.py:262
  (505 shorter events, 352.1 us)
Async XLA Ops:
  7.2 172.6 %all-gather.3.cloned.1.call-start = ((), (), s32[]{:S(2)}) async-start(), calls=%async_computation | async-start | bytes 2359296 | tf_op jit(solution)/shard_map/all_gather | solution.py:284
  12.6 37.5 %collective-permute-start.1 = (bf16[3,1024,256]{2,1,0:T(8,128)(2,1)}, bf16[3,1024,256]{2,1,0:T(8,128)(2,1)}, u32[]{:S(2)}, u32[]{:S(2)}) collective-permute-start(bf16[3,1024,256]{2,1,0:T(8,128)(2,1)} %param.22), channel_id=1, source_target_pairs={{2,0},{0,2},{3,1},{1,3},{6,4},{4,6},{7,5},{5,7},{10,8},{8,10},{11,... | collective-permute-start | bytes 4718600 | tf_op jit(solution)/shard_map/ppermute | solution.py:249
  12.7 53.6 %collective-permute-start.3 = (bf16[256,1024]{1,0:T(8,128)(2,1)}, bf16[256,1024]{1,0:T(8,128)(2,1)S(1)}, u32[]{:S(2)}, u32[]{:S(2)}) collective-permute-start(bf16[256,1024]{1,0:T(8,128)(2,1)} %param.23), channel_id=1, source_target_pairs={{2,0},{0,2},{3,1},{1,3},{6,4},{4,6},{7,5},{5,7},{10,8},{8,10},{11,... | collective-permute-start | bytes 1572872 | tf_op jit(solution)/shard_map/ppermute | solution.py:249
  16.9 83.5 %collective-permute-start.5 = (bf16[512,1024]{0,1:T(8,128)(2,1)}, bf16[512,1024]{0,1:T(8,128)(2,1)}, u32[]{:S(2)}, u32[]{:S(2)}) collective-permute-start(bf16[512,1024]{0,1:T(8,128)(2,1)} %copy.36), channel_id=1, source_target_pairs={{0,1},{1,0},{2,3},{3,2},{4,5},{5,4},{6,7},{7,6},{8,9},{9,8},{10,11... | collective-permute-start | bytes 3145736 | tf_op jit(solution)/shard_map/ppermute | solution.py:223
  17.7 111.5 %collective-permute-start.6 = (bf16[1024,256]{1,0:T(8,128)(2,1)}, bf16[1024,256]{1,0:T(8,128)(2,1)}, u32[]{:S(2)}, u32[]{:S(2)}) collective-permute-start(bf16[1024,256]{1,0:T(8,128)(2,1)} %param.24), channel_id=1, source_target_pairs={{2,0},{0,2},{3,1},{1,3},{6,4},{4,6},{7,5},{5,7},{10,8},{8,10},{11,... | collective-permute-start | bytes 1572872 | tf_op jit(solution)/shard_map/ppermute | solution.py:249
  17.7 86.6 %collective-permute-start.7 = (bf16[2,1024,256]{2,1,0:T(8,128)(2,1)}, bf16[2,1024,256]{2,1,0:T(8,128)(2,1)}, u32[]{:S(2)}, u32[]{:S(2)}) collective-permute-start(bf16[2,1024,256]{2,1,0:T(8,128)(2,1)} %param.25), channel_id=1, source_target_pairs={{2,0},{0,2},{3,1},{1,3},{6,4},{4,6},{7,5},{5,7},{10,8},{8,10},{11,... | collective-permute-start | bytes 3145736 | tf_op jit(solution)/shard_map/ppermute | solution.py:249
  50.2 49.9 %collective-permute-start.10 = (bf16[128,1024]{1,0:T(8,128)(2,1)S(1)}, bf16[128,1024]{1,0:T(8,128)(2,1)}, u32[]{:S(2)}, u32[]{:S(2)}) collective-permute-start(bf16[128,1024]{1,0:T(8,128)(2,1)S(1)} %constant_dynamic-slice_fusion.2), channel_id=1, source_target_pairs={{2,0},{0,2},{3,1},{1,3},{6,4},{4,6},{7,5},{5,7},{10,8},{8,10},{11,... | collective-permute-start | bytes 786440 | tf_op jit(solution)/shard_map/ppermute | solution.py:283
  69.1 40.0 %collective-permute-start.4 = (bf16[1024,1024]{0,1:T(8,128)(2,1)}, bf16[1024,1024]{0,1:T(8,128)(2,1)}, u32[]{:S(2)}, u32[]{:S(2)}) collective-permute-start(bf16[1024,1024]{0,1:T(8,128)(2,1)} %add_convert_fusion.6), channel_id=1, source_target_pairs={{0,1},{1,0},{2,3},{3,2},{4,5},{5,4},{6,7},{7,6},{8,9},{9,8},{10,11... | collective-permute-start | bytes 6291464 | tf_op jit(solution)/shard_map/ppermute | solution.py:223
  100.0 40.5 %collective-permute-start.8 = (bf16[256,1024]{1,0:T(8,128)(2,1)}, bf16[256,1024]{1,0:T(8,128)(2,1)}, u32[]{:S(2)}, u32[]{:S(2)}) collective-permute-start(bf16[256,1024]{1,0:T(8,128)(2,1)} %param.26), channel_id=1, source_target_pairs={{2,0},{0,2},{3,1},{1,3},{6,4},{4,6},{7,5},{5,7},{10,8},{8,10},{11,... | collective-permute-start | bytes 1572872 | tf_op jit(solution)/shard_map/ppermute | solution.py:249
  100.4 105.5 %all-gather.5.cloned.1.call-start = ((), (), s32[]{:S(2)}) async-start(), calls=%async_computation.1 | async-start | bytes 2359296 | tf_op jit(solution)/shard_map/all_gather | solution.py:284
  258.1 49.5 %collective-permute-start.33 = (bf16[1024,1024]{1,0:T(8,128)(2,1)}, bf16[1024,1024]{1,0:T(8,128)(2,1)}, u32[]{:S(2)}, u32[]{:S(2)}) collective-permute-start(bf16[1024,1024]{1,0:T(8,128)(2,1)} %convolution_convert_fusion.1), channel_id=1, source_target_pairs={{0,2},{2,0},{1,3},{3,1},{4,6},{6,4},{5,7},{7,5},{8,10},{10,8},{9,1... | collective-permute-start | bytes 6291464 | tf_op jit(solution)/shard_map/ppermute | solution.py:255
  263.4 88.0 %collective-permute-start.40 = (bf16[1024,1024]{1,0:T(8,128)(2,1)}, bf16[1024,1024]{1,0:T(8,128)(2,1)}, u32[]{:S(2)}, u32[]{:S(2)}) collective-permute-start(bf16[1024,1024]{1,0:T(8,128)(2,1)} %convolution_convert_fusion), channel_id=1, source_target_pairs={{0,2},{2,0},{1,3},{3,1},{4,6},{6,4},{5,7},{7,5},{8,10},{10,8},{9,1... | collective-permute-start | bytes 6291464 | tf_op jit(solution)/shard_map/ppermute | solution.py:255
  306.9 112.0 %collective-permute-start.16 = (bf16[1024,1024]{0,1:T(8,128)(2,1)}, bf16[1024,1024]{0,1:T(8,128)(2,1)}, u32[]{:S(2)}, u32[]{:S(2)}) collective-permute-start(bf16[1024,1024]{0,1:T(8,128)(2,1)} %add_convert_fusion), channel_id=1, source_target_pairs={{0,1},{1,0},{2,3},{3,2},{4,5},{5,4},{6,7},{7,6},{8,9},{9,8},{10,11... | collective-permute-start | bytes 6291464 | tf_op jit(solution)/shard_map/ppermute | solution.py:223
  313.3 52.2 %collective-permute-start.34 = (bf16[512,1024]{1,0:T(8,128)(2,1)S(1)}, bf16[512,1024]{1,0:T(8,128)(2,1)}, u32[]{:S(2)}, u32[]{:S(2)}) collective-permute-start(bf16[512,1024]{1,0:T(8,128)(2,1)S(1)} %dynamic-slice_convert_fusion.2), channel_id=1, source_target_pairs={{0,4},{4,0},{1,5},{5,1},{2,6},{6,2},{3,7},{7,3},{8,12},{12,8},{9,1... | collective-permute-start | bytes 3145736 | tf_op jit(solution)/shard_map/ppermute | solution.py:262
  382.4 197.4 %collective-permute-start.18 = (bf16[512,1024]{1,0:T(8,128)(2,1)}, bf16[512,1024]{1,0:T(8,128)(2,1)}, u32[]{:S(2)}, u32[]{:S(2)}) collective-permute-start(bf16[512,1024]{1,0:T(8,128)(2,1)} %dynamic-slice_convert_fusion.4), channel_id=1, source_target_pairs={{0,1},{1,0},{2,3},{3,2},{4,5},{5,4},{6,7},{7,6},{8,9},{9,8},{10,11... | collective-permute-start | bytes 3145736 | tf_op jit(solution)/shard_map/ppermute | solution.py:223
  401.8 71.3 %collective-permute-start.26 = (bf16[4096,256]{1,0:T(8,128)(2,1)}, bf16[4096,256]{1,0:T(8,128)(2,1)}, u32[]{:S(2)}, u32[]{:S(2)}) collective-permute-start(bf16[4096,256]{1,0:T(8,128)(2,1)} %pad_maximum_fusion.1), channel_id=1, source_target_pairs={{0,2},{2,0},{1,3},{3,1},{4,6},{6,4},{5,7},{7,5},{8,10},{10,8},{9,1... | collective-permute-start | bytes 6291464 | tf_op jit(solution)/shard_map/ppermute | solution.py:255
  404.1 134.6 %collective-permute-start.37 = (bf16[128,1024]{1,0:T(8,128)(2,1)}, bf16[128,1024]{1,0:T(8,128)(2,1)}, u32[]{:S(2)}, u32[]{:S(2)}) collective-permute-start(bf16[128,1024]{1,0:T(8,128)(2,1)} %add_convert_fusion.11), channel_id=1, source_target_pairs={{0,16},{8,24},{16,0},{24,8},{1,17},{9,25},{17,1},{25,9},{2,18},{10... | collective-permute-start | bytes 786440 | tf_op jit(solution)/shard_map/ppermute | solution.py:262
  418.9 141.3 %collective-permute-start.44 = (bf16[128,1024]{1,0:T(8,128)(2,1)S(1)}, bf16[128,1024]{1,0:T(8,128)(2,1)}, u32[]{:S(2)}, u32[]{:S(2)}) collective-permute-start(bf16[128,1024]{1,0:T(8,128)(2,1)S(1)} %add_convert_fusion.10), channel_id=1, source_target_pairs={{0,16},{8,24},{16,0},{24,8},{1,17},{9,25},{17,1},{25,9},{2,18},{10... | collective-permute-start | bytes 786440 | tf_op jit(solution)/shard_map/ppermute | solution.py:262
  456.0 51.0 %collective-permute-start.19 = (bf16[4224,256]{1,0:T(8,128)(2,1)}, bf16[4224,256]{1,0:T(8,128)(2,1)}, u32[]{:S(2)}, u32[]{:S(2)}) collective-permute-start(bf16[4224,256]{1,0:T(8,128)(2,1)} %pad_dynamic-update-slice_fusion.1), channel_id=1, source_target_pairs={{0,2},{2,0},{1,3},{3,1},{4,6},{6,4},{5,7},{7,5},{8,10},{10,8},{9,1... | collective-permute-start | bytes 6488072 | tf_op jit(solution)/shard_map/ppermute | solution.py:255
  538.7 69.3 %collective-permute-start.17 = (bf16[512,1024]{0,1:T(8,128)(2,1)S(1)}, bf16[512,1024]{0,1:T(8,128)(2,1)S(1)}, u32[]{:S(2)}, u32[]{:S(2)}) collective-permute-start(bf16[512,1024]{0,1:T(8,128)(2,1)S(1)} %dynamic-slice_convert_fusion.5), channel_id=1, source_target_pairs={{0,1},{1,0},{2,3},{3,2},{4,5},{5,4},{6,7},{7,6},{8,9},{9,8},{10,11... | collective-permute-start | bytes 3145736 | tf_op jit(solution)/shard_map/ppermute | solution.py:223
  573.8 38.2 %collective-permute-start.39 = (bf16[512,1024]{1,0:T(8,128)(2,1)S(1)}, bf16[512,1024]{1,0:T(8,128)(2,1)}, u32[]{:S(2)}, u32[]{:S(2)}) collective-permute-start(bf16[512,1024]{1,0:T(8,128)(2,1)S(1)} %maximum_select_fusion.9), channel_id=1, source_target_pairs={{0,4},{4,0},{1,5},{5,1},{2,6},{6,2},{3,7},{7,3},{8,12},{12,8},{9,1... | collective-permute-start | bytes 3145736 | tf_op jit(solution)/shard_map/ppermute | solution.py:262
  579.0 26.9 %collective-permute-start.31 = (bf16[1024,256]{1,0:T(8,128)(2,1)S(1)}, bf16[1024,256]{1,0:T(8,128)(2,1)S(1)}, u32[]{:S(2)}, u32[]{:S(2)}) collective-permute-start(bf16[1024,256]{1,0:T(8,128)(2,1)S(1)} %maximum_select_fusion.12), channel_id=1, source_target_pairs={{0,8},{8,0},{16,24},{24,16},{1,9},{9,1},{17,25},{25,17},{2,10},{10... | collective-permute-start | bytes 1572872 | tf_op jit(solution)/shard_map/ppermute | solution.py:262
  607.2 37.6 %collective-permute-start.32 = (bf16[2048,256]{1,0:T(8,128)(2,1)}, bf16[2048,256]{1,0:T(8,128)(2,1)}, u32[]{:S(2)}, u32[]{:S(2)}) collective-permute-start(bf16[2048,256]{1,0:T(8,128)(2,1)} %maximum_select_fusion.8), channel_id=1, source_target_pairs={{0,4},{4,0},{1,5},{5,1},{2,6},{6,2},{3,7},{7,3},{8,12},{12,8},{9,1... | collective-permute-start | bytes 3145736 | tf_op jit(solution)/shard_map/ppermute | solution.py:262
  618.3 47.7 %collective-permute-start.25 = (bf16[2112,256]{1,0:T(8,128)(2,1)S(1)}, bf16[2112,256]{1,0:T(8,128)(2,1)}, u32[]{:S(2)}, u32[]{:S(2)}) collective-permute-start(bf16[2112,256]{1,0:T(8,128)(2,1)S(1)} %maximum_select_fusion.7), channel_id=1, source_target_pairs={{0,4},{4,0},{1,5},{5,1},{2,6},{6,2},{3,7},{7,3},{8,12},{12,8},{9,1... | collective-permute-start | bytes 3244040 | tf_op jit(solution)/shard_map/ppermute | solution.py:262
  (147 other events, 1366.6 us)
Sparse Core Ops, SparseCore 0:
  100.5 50.7 all-gather.2
  155.1 50.7 all-gather.4

commit v3 on v2

--- a/solution.py
+++ b/solution.py
@@ -177,6 +177,149 @@
         name="attend_backward",
     )(length, q, k, v, o, g, lse)
 
+CHUNK = 512
+SPAN = 256
+
+
+def reduce_kernel(spots, count, results, *refs):
+    own, other, out, rest = refs[:count], refs[count : 2 * count], refs[2 * count : 2 * count + results], refs[2 * count + results :]
+    held, ysum, zgot, full, mine, load, store, xs, xr, ys, yr, zs, zr, bs, br, es, er = rest
+    seq, ya, za = lax.axis_index("g"), lax.axis_index("y"), lax.axis_index("z")
+    peers = {1: za + 1 - 2 * (za % 2), 2: (za + 2) % 4, 3: 3 - za}
+    total = len(spots)
+
+    def remote(src, dst, send, recv, where):
+        return pltpu.make_async_remote_copy(src_ref=src, dst_ref=dst, send_sem=send, recv_sem=recv, device_id=where, device_id_type=pl.DeviceIdType.MESH)
+
+    def block(at, size):
+        return pl.ds(pl.multiple_of(at * size, size), size)
+
+    def x_copy(k):
+        a, r, c, n, o, q = spots[k]
+        return remote(other[a].at[pl.ds(r, n), pl.ds(c, SPAN)], held.at[k, pl.ds(0, n)], xs.at[k], xr.at[k], {"g": 1 - seq})
+
+    def own_copy(k):
+        a, r, c, n, o, q = spots[k]
+        return pltpu.make_async_copy(own[a].at[pl.ds(r, n), pl.ds(c, SPAN)], mine.at[k % 4, pl.ds(0, n)], load.at[k % 4])
+
+    def y_copy(k):
+        h = spots[k][3] // 2
+        return remote(held.at[k, block(1 - ya, h)], ysum.at[k, pl.ds(0, h)], ys.at[k], yr.at[k], {"y": 1 - ya})
+
+    def z_copy(k, d):
+        p = spots[k][3] // 8
+        return remote(ysum.at[k, block(peers[d], p)], zgot.at[k, d - 1, pl.ds(0, p)], zs.at[k, d - 1], zr.at[k, d - 1], {"z": peers[d]})
+
+    def zb_copy(k, d):
+        rows = full.at[k, block(ya * 4 + za, spots[k][3] // 8)]
+        return remote(rows, rows, bs.at[k, d - 1], br.at[k, d - 1], {"z": peers[d]})
+
+    def yb_copy(k):
+        rows = full.at[k, block(ya, spots[k][3] // 2)]
+        return remote(rows, rows, es.at[k], er.at[k], {"y": 1 - ya})
+
+    def out_copy(k):
+        a, r, c, n, o, q = spots[k]
+        return pltpu.make_async_copy(full.at[k, pl.ds(0, n)], out[o].at[pl.ds(q, n), pl.ds(c, SPAN)], store.at[k])
+
+    def to_y(k):
+        n = spots[k][3]
+        own_copy(k).wait()
+        x_copy(k).wait_recv()
+        held[k, :n] = held[k, :n] + mine[k % 4, :n]
+        y_copy(k).start()
+
+    def to_z(k):
+        h = spots[k][3] // 2
+        y_copy(k).wait_recv()
+        ysum[k, :h] = ysum[k, :h] + held[k, block(ya, h)]
+        for d in (1, 2, 3):
+            z_copy(k, d).start()
+
+    def back_z(k):
+        p = spots[k][3] // 8
+        for d in (1, 2, 3):
+            z_copy(k, d).wait_recv()
+        rows = ysum[k, block(za, p)].astype(F32)
+        for d in (1, 2, 3):
+            rows = rows + zgot[k, d - 1, :p].astype(F32)
+        full[k, block(ya * 4 + za, p)] = rows.astype(LOW)
+        for d in (1, 2, 3):
+            zb_copy(k, d).start()
+
+    def back_y(k):
+        for d in (1, 2, 3):
+            zb_copy(k, d).wait_recv()
+        yb_copy(k).start()
+
+    def finish(k):
+        yb_copy(k).wait_recv()
+        out_copy(k).start()
+
+    barrier = pltpu.get_barrier_semaphore()
+    everyone = [{"g": 1 - seq}, {"y": 1 - ya}] + [{"z": peers[d]} for d in (1, 2, 3)]
+    for where in everyone:
+        pl.semaphore_signal(barrier, inc=1, device_id=where, device_id_type=pl.DeviceIdType.MESH)
+    for k in range(3):
+        own_copy(k).start()
+    pl.semaphore_wait(barrier, len(everyone))
+    stages = (to_y, to_z, back_z, back_y, finish)
+    ahead = 3
+    for k in range(min(ahead, total)):
+        x_copy(k).start()
+    for step in range(total + len(stages) - 1):
+        if step + ahead < total:
+            x_copy(step + ahead).start()
+        for at, stage in enumerate(stages):
+            if 0 <= step - at < total:
+                stage(step - at)
+        if step + 3 < total:
+            own_copy(step + 3).start()
+    for k in range(total):
+        x_copy(k).wait_send()
+        y_copy(k).wait_send()
+        yb_copy(k).wait_send()
+        out_copy(k).wait()
+        for d in (1, 2, 3):
+            z_copy(k, d).wait_send()
+            zb_copy(k, d).wait_send()
+
+
+def reduce_all(pairs, places, results):
+    spots = []
+    for a, (part, unused) in enumerate(pairs):
+        rows, cols = part.shape
+        size = min(CHUNK, rows)
+        for r in range(0, rows, size):
+            for c in range(0, cols, SPAN):
+                spots.append((a, r, c, size, places[a][0], places[a][1] + r))
+    count, total = len(pairs), len(spots)
+    most = max(s[3] for s in spots)
+    any_space = pl.BlockSpec(memory_space=pl.ANY)
+    dma = pltpu.SemaphoreType.DMA
+    size = sum(own.size for own, unused in pairs)
+    return pl.pallas_call(
+        functools.partial(reduce_kernel, tuple(spots), count, len(results)),
+        out_shape=[jax.ShapeDtypeStruct(shape, LOW) for shape in results],
+        in_specs=[any_space] * (2 * count),
+        out_specs=[any_space] * len(results),
+        scratch_shapes=[
+            pltpu.VMEM((total, most, SPAN), LOW),
+            pltpu.VMEM((total, most // 2, SPAN), LOW),
+            pltpu.VMEM((total, 3, most // 8, SPAN), LOW),
+            pltpu.VMEM((total, most, SPAN), LOW),
+            pltpu.VMEM((4, most, SPAN), LOW),
+            dma((4,)), dma((total,)),
+            dma((total,)), dma((total,)), dma((total,)), dma((total,)),
+            dma((total, 3)), dma((total, 3)), dma((total, 3)), dma((total, 3)),
+            dma((total,)), dma((total,)),
+        ],
+        compiler_params=pltpu.CompilerParams(collective_id=0, has_side_effects=True, vmem_limit_bytes=48 << 20),
+        cost_estimate=pl.CostEstimate(flops=4 * size, bytes_accessed=400 * size, transcendentals=0),
+        name="reduce_gradients",
+    )(*[p[0] for p in pairs], *[p[1] for p in pairs])
+
+
 residual_scale = 300.0**0.25
 norm_epsilon = 1e-05
 LOW = jnp.bfloat16
@@ -328,24 +471,22 @@
     grad_three = norm_backward(cot, unit_three, inverse_three, norm_gain[2])
     low_three = grad_three.astype(LOW)
     grad_hidden = [_nt(low_three, w_out[s]) for s in shards]
-    grad_feed_out = sum_groups(send_home(parts_of([tn(hidden[s], low_three) for s in shards], 0)))
+    feed_out_parts = parts_of([tn(hidden[s], low_three) for s in shards], 0)
     grad_pre = [gelu_backward(hidden_pre[s], grad_hidden[s]).astype(LOW) for s in shards]
-    grad_feed_in = sum_groups(send_home(parts_of([tn(third, grad_pre[s]) for s in shards], 1)))
+    feed_in_parts = parts_of([tn(third, grad_pre[s]) for s in shards], 1)
     grad_normed_two = residual_scale * grad_three + sum_all(sum(_nt(grad_pre[s], w_in[s]) for s in shards))
     grad_two = norm_backward(grad_normed_two, unit_two, inverse_two, norm_gain[1])
     low_two = grad_two.astype(LOW)
     grad_cross_mixed = [_nt(low_two, w_cross_out[s]).astype(LOW) for s in shards]
-    cross_out_parts = parts_of([tn(low_two, cross_mixed[s]) for s in shards], 1)
+    cross_out_parts = parts_of([tn(cross_mixed[s], low_two) for s in shards], 0)
     cross_dq, cross_dk, cross_dv = zip(*[attn_bwd(memory_length, cross_q[s], cross_k[s], cross_v[s], cross_mixed[s], grad_cross_mixed[s], cross_lse[s], False) for s in shards])
     grad_normed_one = residual_scale * grad_two + sum_all(sum(_nt(cross_dq[s], w_cross_q[s]) for s in shards))
-    cross_parts = [cross_out_parts, parts_of([tn(second, cross_dq[s]) for s in shards], 1)]
-    cross_parts += [parts_of([tn(memory_all, cross_dk[s]) for s in shards], 1), parts_of([tn(memory_all, cross_dv[s]) for s in shards], 1)]
-    cross_total = sum_groups(send_home([jnp.concatenate([part[k] for part in cross_parts]) for k in range(gn)]))
+    cross_parts = [parts_of([tn(second, cross_dq[s]) for s in shards], 1), parts_of([tn(memory_all, cross_dk[s]) for s in shards], 1), parts_of([tn(memory_all, cross_dv[s]) for s in shards], 1)]
     grad_memory = sum_own(sum(_nt(cross_dk[s], w_cross_mem[s][0]) + _nt(cross_dv[s], w_cross_mem[s][1]) for s in shards)).astype(LOW)
     grad_one = norm_backward(grad_normed_one, unit_one, inverse_one, norm_gain[0])
     low_one = grad_one.astype(LOW)
     grad_self_mixed = [_nt(low_one, w_self_out[s]).astype(LOW) for s in shards]
-    self_out_parts = parts_of([tn(low_one, self_mixed[s]) for s in shards], 1)
+    self_out_parts = parts_of([tn(self_mixed[s], low_one) for s in shards], 0)
     self_dq, self_dk, self_dv = zip(*[attn_bwd(target_length, self_q[s], self_k[s], self_v[s], self_mixed[s], grad_self_mixed[s], self_lse[s], True) for s in shards])
     token_part = sum(_nt(self_dq[s], w_self[s][0]) + _nt(self_dk[s], w_self[s][1]) + _nt(self_dv[s], w_self[s][2]) for s in shards)
     grad_tokens = (residual_scale * own_rows(grad_one) + sum_own(token_part)).astype(LOW)
@@ -356,21 +497,29 @@
     terms = jnp.stack([sums(low_one), sums(low_two), sums(low_three), sums(grad_normed_one * unit_one), sums(grad_normed_two * unit_two), sums(cot * unit_three), sums(grad_normed_one), sums(grad_normed_two), sums(cot)])
     proj_sums = parts_of([jnp.stack([sums(self_dq[s]), sums(self_dv[s]), sums(cross_dq[s]), sums(cross_dv[s])]) for s in shards], 1)
     feed_sums = parts_of([sums(grad_pre[s]) for s in shards], 0)
-    self_parts = [self_out_parts] + [parts_of([tn(token_all, grads[s]) for s in shards], 1) for grads in (self_dq, self_dk, self_dv)]
-    packed = []
+    self_parts = [parts_of([tn(token_all, grads[s]) for s in shards], 1) for grads in (self_dq, self_dk, self_dv)]
+    smalls = []
     for k in range(gn):
         small = lax.dynamic_slice_in_dim(terms, ((seq + k) % gn * cn + core) * width, width, 1)
         small = jnp.concatenate([small, proj_sums[k], feed_sums[k].reshape(-1, width)])
-        small = jnp.pad(small, ((0, 16 * zn * yn - small.shape[0]), (0, 0)))
-        packed.append(jnp.concatenate([part[k] for part in self_parts] + [small]))
-    self_total = sum_groups(send_home(packed))
+        smalls.append(jnp.pad(small, ((0, 16 * zn * yn - small.shape[0]), (0, 0))))
     model = tokens.shape[1]
-    take = lambda rows, at: lax.slice_in_dim(rows, at * model, (at + 1) * model)
-    small = self_total[4 * model:]
-    grad_self_inputs = jnp.stack([take(self_total, 1), take(self_total, 2), take(self_total, 3)])
-    grad_cross_memory = jnp.stack([take(cross_total, 2), take(cross_total, 3)])
+    groups = [[feed_out_parts], [feed_in_parts], [cross_out_parts], cross_parts[:1], cross_parts[1:], [self_out_parts], self_parts, [smalls]]
+    if (zn, yn, gn, cn, width) == (4, 2, 2, 2, SPAN):
+        pairs, places, results = [], [], []
+        for at, group in enumerate(groups):
+            rows = 0
+            for part in group:
+                pairs.append((part[0].astype(LOW), part[1].astype(LOW)))
+                places.append((at, rows))
+                rows += part[0].shape[0]
+            results.append((rows, group[0][0].shape[1]))
+        sums_low = reduce_all(pairs, places, results)
+    else:
+        sums_low = [sum_groups(send_home([jnp.concatenate([part[k] for part in group]) for k in range(gn)])) for group in groups]
+    feed_out_sum, feed_in_sum, cross_out_sum, cross_q_sum, cross_mem_sum, self_out_sum, self_in_sum, small = [rows.astype(F32) for rows in sums_low]
     feed_rows = feed_bias.shape[0] // width
-    return (block_out, grad_tokens, grad_memory, grad_self_inputs, take(self_total, 0).T, take(cross_total, 1), grad_cross_memory, take(cross_total, 0).T, grad_feed_in, grad_feed_out, small[9:13], small[13:13 + feed_rows].reshape(-1), small[0:3], small[3:6], small[6:9])
+    return (block_out, grad_tokens, grad_memory, self_in_sum.reshape(3, model, width), self_out_sum, cross_q_sum, cross_mem_sum.reshape(2, model, width), cross_out_sum, feed_in_sum, feed_out_sum, small[9:13], small[13:13 + feed_rows].reshape(-1), small[0:3], small[3:6], small[6:9])
 
 
 def solution(mesh):

time: 695 us -> 677 us (0.974)
  Pallas kernels: 79.3 us -> 301 us
  waiting for transfers between devices: 237 us -> 57.3 us
  starting transfers between devices: 42.7 us -> 13.1 us
  other arithmetic: 92.9 us -> 64.5 us
  local copies, waits for them, and re-layouts: 49.2 us -> 35.5 us
  matrix products: 168 us -> 181 us
    pallas_call x0 -> x1, Pallas kernels: none -> 223 us  [reduce_all(): pl.pallas_call(functools.partial(reduce_kernel, tuple(spots), count, len(...]
    ppermute x28 -> x0, waiting for transfers between devices: 175 us -> none  [the longest x24 145 us: pairwise(): return lax.ppermute(rows, axis, [(i, i ^ far) for i in range(size)])]
    ppermute x28 -> x0, starting transfers between devices: 32.3 us -> none  [the longest x24 27.3 us: pairwise(): return lax.ppermute(rows, axis, [(i, i ^ far) for i in range(size)])]
    ppermute x2, waiting for transfers between devices: 29.6 us -> 10.7 us  [spread_wide(): got = lax.ppermute(piece, 'g', [((i + k) % gn, i) for i in range(gn)])]
    ppermute x7, waiting for transfers between devices: 19.8 us -> 35 us  [spread(): lax.ppermute(shard, 'g', [((i + k) % gn, i) for i in range(gn)])]
    add x10 -> x0, other arithmetic: 10.7 us -> none  [the longest x8 6.49 us: sum_groups(): total = keep + pairwise(away, axis, far, size).astype(F32)]
    select_n x9 -> x0, other arithmetic: 9.78 us -> none  [the longest x8 6.74 us: sum_groups(): jnp.where(at // far % 2 == 0, jnp.concatenate([total, got]), jnp.concaten...]
    unnamed x253 -> x261, local copies, waits for them, and re-layouts: 35.6 us -> 26.6 us
  transfers between devices with their start and end apart: 49 -> 21, of which waited for: 22 -> 5; matrix products, arithmetic and copies ran while one was open for 36% -> 26% of each run, Pallas kernels for 12% -> 38%
where the time goes in v3:
time: 677 us; the launch traced here: 668 us
  Pallas kernels  301 us (44%)
  matrix products  181 us (27%)
  other arithmetic  64.5 us (10%)
  waiting for transfers between devices  57.3 us (8%)
  local copies, waits for them, and re-layouts  35.5 us (5%)
  between operations  16.1 us (2%)
  starting transfers between devices  13.1 us (2%)
    pallas_call x1, Pallas kernels, reduce_all(): pl.pallas_call(functools.partial(reduce_kernel, tuple(spots), count, len(...  223 us
    dot_general x20, matrix products, _nn(): lax.dot_general(a, b, (((1,), (0,)), ((), ())), preferred_element_type=jn...  76.8 us
    dot_general x20, matrix products, tn(): lax.dot_general(rows, grads, (((0,), (0,)), ((), ())), preferred_element_...  57.2 us
    dot_general x20, matrix products, _nt(): lax.dot_general(a, b, (((1,), (1,)), ((), ())), preferred_element_type=jn...  46.7 us
    pallas_call x4, Pallas kernels, attn_bwd(): pl.pallas_call(functools.partial(bwd_kernel, causal=causal, bq=bq), out_s...  44.2 us
    ppermute x7, waiting for transfers between devices, spread(): lax.ppermute(shard, 'g', [((i + k) % gn, i) for i in range(gn)])  35 us
    pallas_call x4, Pallas kernels, attn_fwd(): pl.pallas_call(functools.partial(fwd_kernel, causal=causal, bq=bq), out_s...  34.2 us
    reduce_sum x14, other arithmetic, sums(): return jnp.sum(rows.astype(F32), axis=0)  29.5 us
  transfers between devices with their start and end apart: 21, of which 5 were waited for; matrix products, arithmetic and copies ran while one was open for 26% of the time, Pallas kernels for 38%

profile of v3, /device:TPU:0, one launch (start us, length us, event | category | flops | bytes accessed | tf_op | source)
XLA Modules:
  0.0 668.4 jit_solution(8517489506400012535)
XLA Ops:
  19.3 28.3 %collective-permute-done.2 = bf16[4,256]{1,0:T(4,128)(2,1)S(1)} collective-permute-done((bf16[4,256]{1,0:T(4,128)(2,1)}, bf16[4,256]{1,0:T(4,128)(2,1)S(1)}, u32[]{:S(2)}, u32[]{:S(2)}) %collective-permute-start.2) | collective-permute-done | bytes 2080 | tf_op jit(solution)/shard_map/ppermute | solution.py:392
  57.5 7.5 %attend_forward.4 = (bf16[1024,256]{1,0:T(8,128)(2,1)S(1)}, f32[1024,128]{1,0:T(8,128)S(1)}) custom-call(s32[1]{0:T(128)} %dynamic_slice.36.len_ref, bf16[1024,256]{1,0:T(8,128)(2,1)S(1)} %fusion.23.q_ref, bf16[1024,256]{1,0:T(8,128)(2,1)S(1)} %convolution_convert_fusion.27.k_ref, bf16[1024,256]{1,0:T(8,128)(2,1)S(1)} %fusion.24.v_ref), custom_call_target="tpu_custom_call" | custom-call | flops 4294967296 | bytes 2097152 | tf_op jit(solution)/shard_map/attend_forward/pallas_call | solution.py:82
  74.1 7.7 %attend_forward.5 = (bf16[1024,256]{1,0:T(8,128)(2,1)S(1)}, f32[1024,128]{1,0:T(8,128)S(1)}) custom-call(s32[1]{0:T(128)} %dynamic_slice.36.len_ref, bf16[1024,256]{1,0:T(8,128)(2,1)S(1)} %fusion.25.q_ref, bf16[1024,256]{1,0:T(8,128)(2,1)S(1)} %convolution_convert_fusion.26.k_ref, bf16[1024,256]{1,0:T(8,128)(2,1)S(1)} %fusion.26.v_ref), custom_call_target="tpu_custom_call" | custom-call | flops 4294967296 | bytes 2097152 | tf_op jit(solution)/shard_map/attend_forward/pallas_call | solution.py:82
  87.2 10.7 %collective-permute-done.10 = bf16[128,1024]{1,0:T(8,128)(2,1)} collective-permute-done((bf16[128,1024]{1,0:T(8,128)(2,1)S(1)}, bf16[128,1024]{1,0:T(8,128)(2,1)}, u32[]{:S(2)}, u32[]{:S(2)}) %collective-permute-start.10) | collective-permute-done | bytes 262176 | tf_op jit(solution)/shard_map/ppermute | solution.py:426
  111.2 5.0 fusion.70
  119.1 9.4 %attend_forward.6 = (bf16[1024,256]{1,0:T(8,128)(2,1)S(1)}, f32[1024,128]{1,0:T(8,128)S(1)}) custom-call(s32[1]{0:T(128)} %dynamic_slice.37.len_ref, bf16[1024,256]{1,0:T(8,128)(2,1)S(1)} %fusion.27.q_ref, bf16[1024,256]{1,0:T(8,128)(2,1)S(1)} %convolution_convert_fusion.25.k_ref, bf16[1024,256]{1,0:T(8,128)(2,1)S(1)} %fusion.28.v_ref), custom_call_target="tpu_custom_call" | custom-call | flops 4294967296 | bytes 2097152 | tf_op jit(solution)/shard_map/attend_forward/pallas_call | solution.py:82
  131.4 9.6 %attend_forward.7 = (bf16[1024,256]{1,0:T(8,128)(2,1)S(1)}, f32[1024,128]{1,0:T(8,128)S(1)}) custom-call(s32[1]{0:T(128)} %dynamic_slice.37.len_ref, bf16[1024,256]{1,0:T(8,128)(2,1)S(1)} %fusion.29.q_ref, bf16[1024,256]{1,0:T(8,128)(2,1)S(1)} %convolution_convert_fusion.24.k_ref, bf16[1024,256]{1,0:T(8,128)(2,1)S(1)} %fusion.30.v_ref), custom_call_target="tpu_custom_call" | custom-call | flops 4294967296 | bytes 2097152 | tf_op jit(solution)/shard_map/attend_forward/pallas_call | solution.py:82
  148.0 6.7 %collective-permute-done.11 = bf16[1024]{0:T(1024)(128)(2,1)S(1)} collective-permute-done((bf16[1024]{0:T(1024)(128)(2,1)S(1)}, bf16[1024]{0:T(1024)(128)(2,1)S(1)}, u32[]{:S(2)}, u32[]{:S(2)}) %collective-permute-start.11) | collective-permute-done | bytes 2080 | tf_op jit(solution)/shard_map/ppermute | solution.py:392
  161.8 12.6 %multiply_convert_fusion.1 = (bf16[1024,1024]{1,0:T(8,128)(2,1)S(1)}, f32[1024,1024]{1,0:T(8,128)}, f32[1024,1024]{1,0:T(8,128)}) fusion(f32[1024]{0:T(1024)S(1)} %convert_element_type.314, bf16[1024,1024]{0,1:T(8,128)(2,1)S(1)} %fusion.20, bf16[1024,1024]{1,0:T(8,128)(2,1)S(1)} %copy-done), kind=kOutput, calls=%fused_computation.47 | convolution fusion | flops 2216689664 | bytes 14684160 | tf_op jit(solution)/shard_map/dot_general | solution.py:17
  180.2 15.3 %multiply_convert_fusion = (bf16[1024,1024]{1,0:T(8,128)(2,1)}, f32[1024,1024]{1,0:T(8,128)}, f32[1024,1024]{1,0:T(8,128)}) fusion(f32[1024]{0:T(1024)S(1)} %convert_element_type.316, bf16[1024,1024]{0,1:T(8,128)(2,1)} %copy-done.73, bf16[1024,1024]{1,0:T(8,128)(2,1)} %all-gather.3.cloned.1.call-done), kind=kOutput, calls=%fused_computation.34 | convolution fusion | flops 2216689664 | bytes 14684160 | tf_op jit(solution)/shard_map/dot_general | solution.py:17
  195.5 9.8 %all-gather.5.cloned.1.call-done = bf16[1024,1024]{1,0:T(8,128)(2,1)} async-done(((bf16[128,1024]{1,0:T(8,128)(2,1)}), bf16[1024,1024]{1,0:T(8,128)(2,1)}) %all-gather.5.cloned.1.call-update) | async-done | bytes 2097168 | tf_op jit(solution)/shard_map/all_gather | solution.py:427
  205.2 7.2 %add_convert_fusion.4 = bf16[1024,1024]{0,1:T(8,128)(2,1)} fusion(f32[1024,1024]{0,1:T(8,128)} %fusion.77, bf16[1024,1024]{1,0:T(8,128)(2,1)} %get-tuple-element.114, bf16[1024,1024]{1,0:T(8,128)(2,1)} %all-gather.5.cloned.1.call-done), kind=kOutput, calls=%fused_computation.33 | convolution fusion | flops 2149580800 | bytes 10485760 | tf_op jit(solution)/shard_map/dot_general | solution.py:17
  216.9 4.8 fusion.66
  222.9 4.7 fusion.8
  227.6 4.8 convert_reduce_fusion.1
  252.9 6.1 convolution_convert_fusion.1.refs_11_
  270.9 7.6 %multiply_reduce_fusion = (f32[1024]{0:T(1024)S(1)}, f32[1024]{0:T(1024)S(1)}, f32[1024]{0:T(1024)S(1)}, f32[1024]{0:T(1024)S(1)}, f32[1024,1024]{0,1:T(8,128)S(1)}) fusion(f32[1024,1024]{0,1:T(8,128)S(1)} %copy-done.52, f32[1024]{0:T(1024)S(1)} %add_rsqrt_fusion.1, f32[1024]{0:T(1024)S(1)} %broadcast_multiply_fusion.7, f32[1024]{0:T(1024)S(1)} %bitcast.164, ...), kind=kLoop, calls=%fused_computation.14 | loop fusion | flops 30404608 | bytes 18919424 | tf_op jit(solution)/shard_map/reduce_sum | solution.py:495
  283.0 12.6 %attend_backward.4 = (bf16[1024,256]{1,0:T(8,128)(2,1)S(1)}, bf16[1024,256]{1,0:T(8,128)(2,1)S(1)}, bf16[1024,256]{1,0:T(8,128)(2,1)S(1)}) custom-call(s32[1]{0:T(128)} %dynamic_slice.37.len_ref, bf16[1024,256]{1,0:T(8,128)(2,1)S(1)} %copy-done.22, bf16[1024,256]{1,0:T(8,128)(2,1)S(1)} %copy-done.44, bf16[1024,256]{1,0:T(8,128)(2,1)S(1)} %copy-done.46, ...), custom_call_target="tpu_custom_call" | custom-call | flops 10737418240 | bytes 4194304 | tf_op jit(solution)/shard_map/attend_backward/pallas_call | solution.py:166
  298.4 12.9 %attend_backward.5 = (bf16[1024,256]{1,0:T(8,128)(2,1)S(1)}, bf16[1024,256]{1,0:T(8,128)(2,1)S(1)}, bf16[1024,256]{1,0:T(8,128)(2,1)S(1)}) custom-call(s32[1]{0:T(128)} %dynamic_slice.37.len_ref, bf16[1024,256]{1,0:T(8,128)(2,1)S(1)} %copy-done.20, bf16[1024,256]{1,0:T(8,128)(2,1)S(1)} %copy-done.40, bf16[1024,256]{1,0:T(8,128)(2,1)S(1)} %copy-done.42, ...), custom_call_target="tpu_custom_call" | custom-call | flops 10737418240 | bytes 4194304 | tf_op jit(solution)/shard_map/attend_backward/pallas_call | solution.py:166
  346.5 6.0 multiply_reduce_fusion.1
  359.3 9.4 %attend_backward.6 = (bf16[1024,256]{1,0:T(8,128)(2,1)S(1)}, bf16[1024,256]{1,0:T(8,128)(2,1)S(1)}, bf16[1024,256]{1,0:T(8,128)(2,1)S(1)}) custom-call(s32[1]{0:T(128)} %dynamic_slice.36.len_ref, bf16[1024,256]{1,0:T(8,128)(2,1)S(1)} %copy-done.26, bf16[1024,256]{1,0:T(8,128)(2,1)S(1)} %copy-done.30, bf16[1024,256]{1,0:T(8,128)(2,1)S(1)} %copy-done.32, ...), custom_call_target="tpu_custom_call" | custom-call | flops 10737418240 | bytes 4194304 | tf_op jit(solution)/shard_map/attend_backward/pallas_call | solution.py:166
  378.8 9.4 %attend_backward.7 = (bf16[1024,256]{1,0:T(8,128)(2,1)S(1)}, bf16[1024,256]{1,0:T(8,128)(2,1)S(1)}, bf16[1024,256]{1,0:T(8,128)(2,1)S(1)}) custom-call(s32[1]{0:T(128)} %dynamic_slice.36.len_ref, bf16[1024,256]{1,0:T(8,128)(2,1)S(1)} %copy-done.24, bf16[1024,256]{1,0:T(8,128)(2,1)S(1)} %copy-done.34, bf16[1024,256]{1,0:T(8,128)(2,1)S(1)} %copy-done.28, ...), custom_call_target="tpu_custom_call" | custom-call | flops 10737418240 | bytes 4194304 | tf_op jit(solution)/shard_map/attend_backward/pallas_call | solution.py:166
  397.2 4.8 add_add_fusion.1
  421.3 222.9 %reduce_gradients.1 = (bf16[1024,1024]{1,0:T(8,128)(2,1)}, bf16[1024,1024]{1,0:T(8,128)(2,1)}, bf16[256,1024]{1,0:T(8,128)(2,1)S(1)}, bf16[1024,256]{1,0:T(8,128...) custom-call(bf16[1024,1024]{1,0:T(8,128)(2,1)} %convolution_convert_, ...), custom_call_target="tpu_custom_call" | custom-call | flops 16908288 | bytes 1690828800 | tf_op jit(solution)/shard_map/reduce_gradients/pallas_call | solution.py:301
  (425 shorter events, 216.7 us)
Async XLA Ops:
  7.2 173.0 %all-gather.3.cloned.1.call-start = ((), (), s32[]{:S(2)}) async-start(), calls=%async_computation | async-start | bytes 2359296 | tf_op jit(solution)/shard_map/all_gather | solution.py:427
  8.9 102.3 %copy-start.68 = (bf16[512,1024]{0,1:T(8,128)(2,1)}, bf16[512,1024]{0,1:T(8,128)(2,1)S(1)}, u32[]{:S(2)}) copy-start(bf16[512,1024]{0,1:T(8,128)(2,1)S(1)} %copy.33) | copy-start | bytes 3145732
  8.9 38.7 %collective-permute-start = (bf16[512,1024]{0,1:T(8,128)(2,1)S(1)}, bf16[512,1024]{0,1:T(8,128)(2,1)}, u32[]{:S(2)}, u32[]{:S(2)}) collective-permute-start(bf16[512,1024]{0,1:T(8,128)(2,1)S(1)} %copy.33), channel_id=1, source_target_pairs={{0,1},{1,0},{2,3},{3,2},{4,5},{5,4},{6,7},{7,6},{8,9},{9,8},{10,11... | collective-permute-start | bytes 3145736 | tf_op jit(solution)/shard_map/ppermute | solution.py:366
  9.4 56.6 %collective-permute-start.1 = (bf16[3,1024,256]{2,1,0:T(8,128)(2,1)}, bf16[3,1024,256]{2,1,0:T(8,128)(2,1)}, u32[]{:S(2)}, u32[]{:S(2)}) collective-permute-start(bf16[3,1024,256]{2,1,0:T(8,128)(2,1)} %param.22), channel_id=1, source_target_pairs={{2,0},{0,2},{3,1},{1,3},{6,4},{4,6},{7,5},{5,7},{10,8},{8,10},{11,... | collective-permute-start | bytes 4718600 | tf_op jit(solution)/shard_map/ppermute | solution.py:392
  12.0 35.6 %collective-permute-start.2 = (bf16[4,256]{1,0:T(4,128)(2,1)}, bf16[4,256]{1,0:T(4,128)(2,1)S(1)}, u32[]{:S(2)}, u32[]{:S(2)}) collective-permute-start(bf16[4,256]{1,0:T(4,128)(2,1)} %param.29), channel_id=1, source_target_pairs={{2,0},{0,2},{3,1},{1,3},{6,4},{4,6},{7,5},{5,7},{10,8},{8,10},{11,... | collective-permute-start | bytes 6152 | tf_op jit(solution)/shard_map/ppermute | solution.py:392
  12.1 69.7 %collective-permute-start.3 = (bf16[256,1024]{1,0:T(8,128)(2,1)}, bf16[256,1024]{1,0:T(8,128)(2,1)}, u32[]{:S(2)}, u32[]{:S(2)}) collective-permute-start(bf16[256,1024]{1,0:T(8,128)(2,1)} %param.23), channel_id=1, source_target_pairs={{2,0},{0,2},{3,1},{1,3},{6,4},{4,6},{7,5},{5,7},{10,8},{8,10},{11,... | collective-permute-start | bytes 1572872 | tf_op jit(solution)/shard_map/ppermute | solution.py:392
  14.0 115.5 %collective-permute-start.6 = (bf16[1024,256]{1,0:T(8,128)(2,1)}, bf16[1024,256]{1,0:T(8,128)(2,1)}, u32[]{:S(2)}, u32[]{:S(2)}) collective-permute-start(bf16[1024,256]{1,0:T(8,128)(2,1)} %param.24), channel_id=1, source_target_pairs={{2,0},{0,2},{3,1},{1,3},{6,4},{4,6},{7,5},{5,7},{10,8},{8,10},{11,... | collective-permute-start | bytes 1572872 | tf_op jit(solution)/shard_map/ppermute | solution.py:392
  47.6 52.2 %collective-permute-start.5 = (bf16[512,1024]{0,1:T(8,128)(2,1)}, bf16[512,1024]{0,1:T(8,128)(2,1)}, u32[]{:S(2)}, u32[]{:S(2)}) collective-permute-start(bf16[512,1024]{0,1:T(8,128)(2,1)} %copy.36), channel_id=1, source_target_pairs={{0,1},{1,0},{2,3},{3,2},{4,5},{5,4},{6,7},{7,6},{8,9},{9,8},{10,11... | collective-permute-start | bytes 3145736 | tf_op jit(solution)/shard_map/ppermute | solution.py:366
  47.6 55.5 %collective-permute-start.7 = (bf16[2,1024,256]{2,1,0:T(8,128)(2,1)}, bf16[2,1024,256]{2,1,0:T(8,128)(2,1)}, u32[]{:S(2)}, u32[]{:S(2)}) collective-permute-start(bf16[2,1024,256]{2,1,0:T(8,128)(2,1)} %param.25), channel_id=1, source_target_pairs={{2,0},{0,2},{3,1},{1,3},{6,4},{4,6},{7,5},{5,7},{10,8},{8,10},{11,... | collective-permute-start | bytes 3145736 | tf_op jit(solution)/shard_map/ppermute | solution.py:392
  66.0 31.9 %collective-permute-start.10 = (bf16[128,1024]{1,0:T(8,128)(2,1)S(1)}, bf16[128,1024]{1,0:T(8,128)(2,1)}, u32[]{:S(2)}, u32[]{:S(2)}) collective-permute-start(bf16[128,1024]{1,0:T(8,128)(2,1)S(1)} %constant_dynamic-slice_fusion.1), channel_id=1, source_target_pairs={{2,0},{0,2},{3,1},{1,3},{6,4},{4,6},{7,5},{5,7},{10,8},{8,10},{11,... | collective-permute-start | bytes 786440 | tf_op jit(solution)/shard_map/ppermute | solution.py:426
  85.8 25.5 %collective-permute-start.4 = (bf16[1024,1024]{0,1:T(8,128)(2,1)}, bf16[1024,1024]{0,1:T(8,128)(2,1)}, u32[]{:S(2)}, u32[]{:S(2)}) collective-permute-start(bf16[1024,1024]{0,1:T(8,128)(2,1)} %add_convert_fusion.6), channel_id=1, source_target_pairs={{0,1},{1,0},{2,3},{3,2},{4,5},{5,4},{6,7},{7,6},{8,9},{9,8},{10,11... | collective-permute-start | bytes 6291464 | tf_op jit(solution)/shard_map/ppermute | solution.py:366
  85.9 69.5 %copy-start.101 = (f32[1,1024]{1,0:T(1,128)}, f32[1,1024]{1,0:T(1,128)S(1)}, u32[]{:S(2)}) copy-start(f32[1,1024]{1,0:T(1,128)S(1)} %get-tuple-element.131) | copy-start | bytes 12292
  97.9 43.9 %collective-permute-start.8 = (bf16[256,1024]{1,0:T(8,128)(2,1)}, bf16[256,1024]{1,0:T(8,128)(2,1)}, u32[]{:S(2)}, u32[]{:S(2)}) collective-permute-start(bf16[256,1024]{1,0:T(8,128)(2,1)} %param.26), channel_id=1, source_target_pairs={{2,0},{0,2},{3,1},{1,3},{6,4},{4,6},{7,5},{5,7},{10,8},{8,10},{11,... | collective-permute-start | bytes 1572872 | tf_op jit(solution)/shard_map/ppermute | solution.py:392
  99.7 105.5 %all-gather.5.cloned.1.call-start = ((), (), s32[]{:S(2)}) async-start(), calls=%async_computation.1 | async-start | bytes 2359296 | tf_op jit(solution)/shard_map/all_gather | solution.py:427
  116.3 39.2 %copy-start.97 = (f32[1024]{0:T(1024)}, f32[1024]{0:T(1024)S(1)}, u32[]{:S(2)}) copy-start(f32[1024]{0:T(1024)S(1)} %broadcast_multiply_fusion.8) | copy-start | bytes 12292
  144.9 10.5 %collective-permute-start.9 = (bf16[1024,1024]{0,1:T(8,128)(2,1)}, bf16[1024,1024]{0,1:T(8,128)(2,1)}, u32[]{:S(2)}, u32[]{:S(2)}) collective-permute-start(bf16[1024,1024]{0,1:T(8,128)(2,1)} %add_convert_fusion.5), channel_id=1, source_target_pairs={{0,1},{1,0},{2,3},{3,2},{4,5},{5,4},{6,7},{7,6},{8,9},{9,8},{10,11... | collective-permute-start | bytes 6291464 | tf_op jit(solution)/shard_map/ppermute | solution.py:366
  145.9 8.8 %collective-permute-start.12 = (bf16[128,1024]{1,0:T(8,128)(2,1)S(1)}, bf16[128,1024]{1,0:T(8,128)(2,1)S(1)}, u32[]{:S(2)}, u32[]{:S(2)}) collective-permute-start(bf16[128,1024]{1,0:T(8,128)(2,1)S(1)} %constant_dynamic-slice_fusion), channel_id=1, source_target_pairs={{2,0},{0,2},{3,1},{1,3},{6,4},{4,6},{7,5},{5,7},{10,8},{8,10},{11,... | collective-permute-start | bytes 786440 | tf_op jit(solution)/shard_map/ppermute | solution.py:426
  146.2 8.5 %collective-permute-start.11 = (bf16[1024]{0:T(1024)(128)(2,1)S(1)}, bf16[1024]{0:T(1024)(128)(2,1)S(1)}, u32[]{:S(2)}, u32[]{:S(2)}) collective-permute-start(bf16[1024]{0:T(1024)(128)(2,1)S(1)} %copy-done.112), channel_id=1, source_target_pairs={{2,0},{0,2},{3,1},{1,3},{6,4},{4,6},{7,5},{5,7},{10,8},{8,10},{11,... | collective-permute-start | bytes 6152 | tf_op jit(solution)/shard_map/ppermute | solution.py:392
  212.4 4.5 collective-permute-start.13
  214.7 7.5 %collective-permute-start.14 = (bf16[512,1024]{0,1:T(8,128)(2,1)}, bf16[512,1024]{0,1:T(8,128)(2,1)}, u32[]{:S(2)}, u32[]{:S(2)}) collective-permute-start(bf16[512,1024]{0,1:T(8,128)(2,1)} %copy.41), channel_id=1, source_target_pairs={{0,1},{1,0},{2,3},{3,2},{4,5},{5,4},{6,7},{7,6},{8,9},{9,8},{10,11... | collective-permute-start | bytes 3145736 | tf_op jit(solution)/shard_map/ppermute | solution.py:366
  249.3 20.9 %collective-permute-start.15 = (bf16[1024,1024]{0,1:T(8,128)(2,1)}, bf16[1024,1024]{0,1:T(8,128)(2,1)}, u32[]{:S(2)}, u32[]{:S(2)}) collective-permute-start(bf16[1024,1024]{0,1:T(8,128)(2,1)} %add_convert_fusion.1), channel_id=1, source_target_pairs={{0,1},{1,0},{2,3},{3,2},{4,5},{5,4},{6,7},{7,6},{8,9},{9,8},{10,11... | collective-permute-start | bytes 6291464 | tf_op jit(solution)/shard_map/ppermute | solution.py:366
  316.0 29.0 %collective-permute-start.16 = (bf16[1024,1024]{0,1:T(8,128)(2,1)}, bf16[1024,1024]{0,1:T(8,128)(2,1)}, u32[]{:S(2)}, u32[]{:S(2)}) collective-permute-start(bf16[1024,1024]{0,1:T(8,128)(2,1)} %add_convert_fusion), channel_id=1, source_target_pairs={{0,1},{1,0},{2,3},{3,2},{4,5},{5,4},{6,7},{7,6},{8,9},{9,8},{10,11... | collective-permute-start | bytes 6291464 | tf_op jit(solution)/shard_map/ppermute | solution.py:366
  328.3 15.4 %collective-permute-start.18 = (bf16[512,1024]{1,0:T(8,128)(2,1)}, bf16[512,1024]{1,0:T(8,128)(2,1)S(1)}, u32[]{:S(2)}, u32[]{:S(2)}) collective-permute-start(bf16[512,1024]{1,0:T(8,128)(2,1)} %dynamic-slice_convert_fusion), channel_id=1, source_target_pairs={{0,1},{1,0},{2,3},{3,2},{4,5},{5,4},{6,7},{7,6},{8,9},{9,8},{10,11... | collective-permute-start | bytes 3145736 | tf_op jit(solution)/shard_map/ppermute | solution.py:366
  403.7 255.6 %collective-permute-start.17 = (bf16[512,1024]{0,1:T(8,128)(2,1)S(1)}, bf16[512,1024]{0,1:T(8,128)(2,1)S(1)}, u32[]{:S(2)}, u32[]{:S(2)}) collective-permute-start(bf16[512,1024]{0,1:T(8,128)(2,1)S(1)} %dynamic-slice_convert_fusion.1), channel_id=1, source_target_pairs={{0,1},{1,0},{2,3},{3,2},{4,5},{5,4},{6,7},{7,6},{8,9},{9,8},{10,11... | collective-permute-start | bytes 3145736 | tf_op jit(solution)/shard_map/ppermute | solution.py:366
  (124 other events, 663.6 us)
Sparse Core Ops, SparseCore 0:
  99.8 49.5 all-gather.2
  155.6 49.6 all-gather.4

commit v4 on v3

--- a/solution.py
+++ b/solution.py
@@ -417,15 +417,19 @@
             total = jnp.where((at // far) % 2 == 0, jnp.concatenate([total, got]), jnp.concatenate([got, total]))
         return total.astype(F32)
 
-    def spread_wide(shard, axis):
-        size = shard.shape[0] // (zn * yn)
+    def fetch_slices(shards):
         at = lax.axis_index("z") * yn + lax.axis_index("y")
-        piece = lax.dynamic_slice_in_dim(shard, at * size, size, 0)
-        every = [shard]
-        for k in range(1, gn):
-            got = lax.ppermute(piece, "g", [((i + k) % gn, i) for i in range(gn)])
-            every.append(lax.all_gather(got, ("z", "y"), axis=0, tiled=True))
-        return [jnp.concatenate(every, axis=axis)] if joined else every
+        pieces = [lax.dynamic_slice_in_dim(shard, at * (shard.shape[0] // (zn * yn)), shard.shape[0] // (zn * yn), 0) for shard in shards]
+        pieces = [jnp.stack(pieces)] if pieces[0].shape == pieces[1].shape else [piece[None] for piece in pieces]
+        return [[lax.ppermute(piece, "g", [((i + k) % gn, i) for i in range(gn)]) for piece in pieces] for k in range(1, gn)]
+
+    def spread_wide(shards, slices):
+        every = [[shard] for shard in shards]
+        for got in slices:
+            whole = [rows for piece in got for rows in lax.all_gather(piece, ("z", "y"), axis=1, tiled=True)]
+            for at, rows in enumerate(whole):
+                every[at].append(rows)
+        return [[jnp.concatenate(part, axis=1 - at)] if joined else part for at, part in enumerate(every)]
 
     def parts_of(values, axis):
         return jnp.split(values[0], gn, axis=axis) if joined else values
@@ -433,24 +437,38 @@
     target_length = lax.dynamic_slice_in_dim(target_lengths, seq, 1, 0)
     memory_length = lax.dynamic_slice_in_dim(memory_lengths, seq, 1, 0)
 
+    def after(value, *needed):
+        return lax.optimization_barrier((value,) + needed)[0]
+
     token_all = gather_rows(tokens)
-    w_self = spread(self_inputs, 2)
-    b_proj = spread(proj_bias, 1)
-    w_self_out = spread(self_output, 0)
-    memory_all = gather_rows(memory)
-    w_cross_mem = spread(cross_memory, 2)
-    w_cross_q = spread(cross_query, 1)
-    w_cross_out = spread(cross_output, 0)
-    w_in = spread_wide(feed_in, 1)
-    b_in = spread(feed_bias, 0)
-    w_out = spread_wide(feed_out, 0)
-    cot_all = gather_rows(cotangent)
+    biases = spread(jnp.concatenate([proj_bias, feed_bias.reshape(-1, width)]), 1)
+    feed_rows = feed_bias.shape[0] // width
+    if joined:
+        halves = jnp.split(biases[0], gn, axis=1)
+        b_in = [jnp.concatenate([part[4:].reshape(-1) for part in halves])]
+    else:
+        b_in = [part[4:].reshape(-1) for part in biases]
+    b_proj = [part[:4] for part in biases]
+    slices = fetch_slices((feed_in, feed_out))
+    w_self = spread(after(self_inputs, token_all, biases[-1], slices[-1][0]), 2)
+    w_in, w_out = spread_wide((feed_in, feed_out), slices)
+    self_q, self_k, self_v, self_mixed, self_lse = [], [], [], [], []
     shards = range(len(w_self))
-
-    self_q = [(_nn(token_all, w_self[s][0]) + b_proj[s][0]).astype(LOW) for s in shards]
-    self_k = [_nn(token_all, w_self[s][1]).astype(LOW) for s in shards]
-    self_v = [(_nn(token_all, w_self[s][2]) + b_proj[s][1]).astype(LOW) for s in shards]
-    self_mixed, self_lse = zip(*[attn_fwd(target_length, self_q[s], self_k[s], self_v[s], True) for s in shards])
+    for s in shards:
+        self_q.append((_nn(token_all, w_self[s][0]) + b_proj[s][0]).astype(LOW))
+        self_k.append(_nn(token_all, w_self[s][1]).astype(LOW))
+        self_v.append((_nn(token_all, w_self[s][2]) + b_proj[s][1]).astype(LOW))
+        mixed, lse = attn_fwd(target_length, self_q[s], self_k[s], self_v[s], True)
+        self_mixed.append(mixed)
+        self_lse.append(lse)
+    first = self_mixed[0]
+    w_self_out = spread(after(self_output, first), 0)
+    memory_all = gather_rows(after(memory, first))
+    w_cross_mem = spread(after(cross_memory, first), 2)
+    w_cross_q = spread(after(cross_query, first), 1)
+    w_cross_out = spread(after(cross_output, first), 0)
+    cot_all = gather_rows(after(cotangent, self_mixed[-1]))
+
     cross_k = [_nn(memory_all, w_cross_mem[s][0]).astype(LOW) for s in shards]
     cross_v = [(_nn(memory_all, w_cross_mem[s][1]) + b_proj[s][3]).astype(LOW) for s in shards]
     branch_one = sum_all(sum(_nn(self_mixed[s], w_self_out[s]) for s in shards)) + branch_bias[0]
@@ -474,6 +492,7 @@
     feed_out_parts = parts_of([tn(hidden[s], low_three) for s in shards], 0)
     grad_pre = [gelu_backward(hidden_pre[s], grad_hidden[s]).astype(LOW) for s in shards]
     feed_in_parts = parts_of([tn(third, grad_pre[s]) for s in shards], 1)
+    feed_out_sum, feed_in_sum = [lax.psum(send_home(part).astype(LOW), ("z", "y")).astype(F32) for part in (feed_out_parts, feed_in_parts)]
     grad_normed_two = residual_scale * grad_three + sum_all(sum(_nt(grad_pre[s], w_in[s]) for s in shards))
     grad_two = norm_backward(grad_normed_two, unit_two, inverse_two, norm_gain[1])
     low_two = grad_two.astype(LOW)
@@ -504,7 +523,7 @@
         small = jnp.concatenate([small, proj_sums[k], feed_sums[k].reshape(-1, width)])
         smalls.append(jnp.pad(small, ((0, 16 * zn * yn - small.shape[0]), (0, 0))))
     model = tokens.shape[1]
-    groups = [[feed_out_parts], [feed_in_parts], [cross_out_parts], cross_parts[:1], cross_parts[1:], [self_out_parts], self_parts, [smalls]]
+    groups = [[cross_out_parts], cross_parts[:1], cross_parts[1:], [self_out_parts], self_parts, [smalls]]
     if (zn, yn, gn, cn, width) == (4, 2, 2, 2, SPAN):
         pairs, places, results = [], [], []
         for at, group in enumerate(groups):
@@ -517,8 +536,7 @@
         sums_low = reduce_all(pairs, places, results)
     else:
         sums_low = [sum_groups(send_home([jnp.concatenate([part[k] for part in group]) for k in range(gn)])) for group in groups]
-    feed_out_sum, feed_in_sum, cross_out_sum, cross_q_sum, cross_mem_sum, self_out_sum, self_in_sum, small = [rows.astype(F32) for rows in sums_low]
-    feed_rows = feed_bias.shape[0] // width
+    cross_out_sum, cross_q_sum, cross_mem_sum, self_out_sum, self_in_sum, small = [rows.astype(F32) for rows in sums_low]
     return (block_out, grad_tokens, grad_memory, self_in_sum.reshape(3, model, width), self_out_sum, cross_q_sum, cross_mem_sum.reshape(2, model, width), cross_out_sum, feed_in_sum, feed_out_sum, small[9:13], small[13:13 + feed_rows].reshape(-1), small[0:3], small[3:6], small[6:9])
 
 

time: 677 us -> 630 us (0.931)
  Pallas kernels: 301 us -> 242 us
  waiting for transfers between devices: 57.3 us -> 84.9 us
  matrix products: 181 us -> 166 us
    pallas_call x1, Pallas kernels: 223 us -> 163 us  [reduce_all(): pl.pallas_call(functools.partial(reduce_kernel, tuple(spots), count, len(...]
    dot_general x20, matrix products: 76.8 us -> 61.4 us  [_nn(): lax.dot_general(a, b, (((1,), (0,)), ((), ())), preferred_element_type=jn...]
    ppermute x2 -> x3, waiting for transfers between devices: 10.7 us -> 23.6 us  [the longest x2 23.6 us: send_home(): lax.ppermute(parts[k].astype(LOW), 'g', [(i, (i + k) % gn) for i in range...]
    ppermute x7 -> x6, waiting for transfers between devices: 35 us -> 47.4 us  [spread(): lax.ppermute(shard, 'g', [((i + k) % gn, i) for i in range(gn)])]
    unnamed x261 -> x272, local copies, waits for them, and re-layouts: 26.6 us -> 27.6 us
  transfers between devices with their start and end apart: 21 -> 21, of which waited for: 5 -> 7; matrix products, arithmetic and copies ran while one was open for 26% -> 32% of each run, Pallas kernels for 38% -> 39%
where the time goes in v4:
time: 630 us; the launch traced here: 621 us
  Pallas kernels  242 us (38%)
  matrix products  166 us (26%)
  waiting for transfers between devices  84.9 us (13%)
  other arithmetic  60.8 us (10%)
  local copies, waits for them, and re-layouts  38.8 us (6%)
  between operations  16.3 us (3%)
  starting transfers between devices  12.4 us (2%)
    pallas_call x1, Pallas kernels, reduce_all(): pl.pallas_call(functools.partial(reduce_kernel, tuple(spots), count, len(...  163 us
    dot_general x20, matrix products, _nn(): lax.dot_general(a, b, (((1,), (0,)), ((), ())), preferred_element_type=jn...  61.4 us
    dot_general x20, matrix products, tn(): lax.dot_general(rows, grads, (((0,), (0,)), ((), ())), preferred_element_...  55.1 us
    dot_general x20, matrix products, _nt(): lax.dot_general(a, b, (((1,), (1,)), ((), ())), preferred_element_type=jn...  49.8 us
    ppermute x6, waiting for transfers between devices, spread(): lax.ppermute(shard, 'g', [((i + k) % gn, i) for i in range(gn)])  47.4 us
    pallas_call x4, Pallas kernels, attn_bwd(): pl.pallas_call(functools.partial(bwd_kernel, causal=causal, bq=bq), out_s...  44.8 us
    pallas_call x4, Pallas kernels, attn_fwd(): pl.pallas_call(functools.partial(fwd_kernel, causal=causal, bq=bq), out_s...  34.5 us
    unnamed x272, local copies, waits for them, and re-layouts  27.6 us
  transfers between devices with their start and end apart: 21, of which 7 were waited for; matrix products, arithmetic and copies ran while one was open for 32% of the time, Pallas kernels for 39%

profile of v4, /device:TPU:0, one launch (start us, length us, event | category | flops | bytes accessed | tf_op | source)
XLA Modules:
  0.0 621.4 jit_solution(15398697262577855076)
XLA Ops:
  15.7 10.9 %collective-permute-done.1 = bf16[8,256]{1,0:T(8,128)(2,1)S(1)} collective-permute-done((bf16[8,256]{1,0:T(8,128)(2,1)S(1)}, bf16[8,256]{1,0:T(8,128)(2,1)S(1)}, u32[]{:S(2)}, u32[]{:S(2)}) %collective-permute-start.1) | collective-permute-done | bytes 4128 | tf_op jit(solution)/shard_map/ppermute | solution.py:392
  34.2 7.6 %attend_forward.4 = (bf16[1024,256]{1,0:T(8,128)(2,1)S(1)}, f32[1024,128]{1,0:T(8,128)S(1)}) custom-call(s32[1]{0:T(128)} %dynamic_slice.36.len_ref, bf16[1024,256]{1,0:T(8,128)(2,1)S(1)} %fusion.25.q_ref, bf16[1024,256]{1,0:T(8,128)(2,1)S(1)} %convolution_convert_fusion.25.k_ref, bf16[1024,256]{1,0:T(8,128)(2,1)S(1)} %fusion.26.v_ref), custom_call_target="tpu_custom_call" | custom-call | flops 4294967296 | bytes 2097152 | tf_op jit(solution)/shard_map/attend_forward/pallas_call | solution.py:82
  49.0 17.7 %collective-permute-done.3 = bf16[3,1024,256]{2,1,0:T(8,128)(2,1)} collective-permute-done((bf16[3,1024,256]{2,1,0:T(8,128)(2,1)}, bf16[3,1024,256]{2,1,0:T(8,128)(2,1)}, u32[]{:S(2)}, u32[]{:S(2)}) %collective-permute-start.3) | collective-permute-done | bytes 1572896 | tf_op jit(solution)/shard_map/ppermute | solution.py:392
  72.5 7.8 %attend_forward.5 = (bf16[1024,256]{1,0:T(8,128)(2,1)S(1)}, f32[1024,128]{1,0:T(8,128)S(1)}) custom-call(s32[1]{0:T(128)} %dynamic_slice.36.len_ref, bf16[1024,256]{1,0:T(8,128)(2,1)S(1)} %fusion.27.q_ref, bf16[1024,256]{1,0:T(8,128)(2,1)S(1)} %convolution_convert_fusion.24.k_ref, bf16[1024,256]{1,0:T(8,128)(2,1)S(1)} %fusion.28.v_ref), custom_call_target="tpu_custom_call" | custom-call | flops 4294967296 | bytes 2097152 | tf_op jit(solution)/shard_map/attend_forward/pallas_call | solution.py:82
  80.4 18.8 %collective-permute-done.4 = bf16[256,1024]{1,0:T(8,128)(2,1)S(1)} collective-permute-done((bf16[256,1024]{1,0:T(8,128)(2,1)}, bf16[256,1024]{1,0:T(8,128)(2,1)S(1)}, u32[]{:S(2)}, u32[]{:S(2)}) %collective-permute-start.4) | collective-permute-done | bytes 524320 | tf_op jit(solution)/shard_map/ppermute | solution.py:392
  120.9 9.8 %attend_forward.6 = (bf16[1024,256]{1,0:T(8,128)(2,1)S(1)}, f32[1024,128]{1,0:T(8,128)S(1)}) custom-call(s32[1]{0:T(128)} %dynamic_slice.39.len_ref, bf16[1024,256]{1,0:T(8,128)(2,1)S(1)} %fusion.29.q_ref, bf16[1024,256]{1,0:T(8,128)(2,1)S(1)} %convolution_convert_fusion.23.k_ref, bf16[1024,256]{1,0:T(8,128)(2,1)S(1)} %fusion.30.v_ref), custom_call_target="tpu_custom_call" | custom-call | flops 4294967296 | bytes 2097152 | tf_op jit(solution)/shard_map/attend_forward/pallas_call | solution.py:82
  132.5 9.3 %attend_forward.7 = (bf16[1024,256]{1,0:T(8,128)(2,1)S(1)}, f32[1024,128]{1,0:T(8,128)S(1)}) custom-call(s32[1]{0:T(128)} %dynamic_slice.39.len_ref, bf16[1024,256]{1,0:T(8,128)(2,1)S(1)} %fusion.31.q_ref, bf16[1024,256]{1,0:T(8,128)(2,1)S(1)} %convolution_convert_fusion.22.k_ref, bf16[1024,256]{1,0:T(8,128)(2,1)S(1)} %fusion.32.v_ref), custom_call_target="tpu_custom_call" | custom-call | flops 4294967296 | bytes 2097152 | tf_op jit(solution)/shard_map/attend_forward/pallas_call | solution.py:82
  152.0 12.4 %multiply_convert_fusion.1 = (bf16[1024,1024]{1,0:T(8,128)(2,1)S(1)}, f32[1024,1024]{1,0:T(8,128)}, f32[1024,1024]{1,0:T(8,128)}) fusion(f32[1024]{0:T(1024)S(1)} %convert_element_type.327, bf16[1024,1024]{0,1:T(8,128)(2,1)S(1)} %fusion.20, bf16[1024,1024]{1,0:T(8,128)(2,1)S(1)} %copy-done.105), kind=kOutput, calls=%fused_computation.49 | convolution fusion | flops 2216689664 | bytes 14684160 | tf_op jit(solution)/shard_map/dot_general | solution.py:17
  170.1 6.3 %all-gather.2.cloned.1.call-done = bf16[2,1024,1024]{2,1,0:T(8,128)(2,1)} async-done(((bf16[2,128,1024]{2,1,0:T(8,128)(2,1)}), bf16[2,1024,1024]{2,1,0:T(8,128)(2,1)}) %all-gather.2.cloned.1.call-update) | async-done | bytes 4194320 | tf_op jit(solution)/shard_map/all_gather | solution.py:429
  176.4 14.6 %multiply_convert_fusion = (bf16[1024,1024]{1,0:T(8,128)(2,1)S(1)}, f32[1024,1024]{1,0:T(8,128)}, f32[1024,1024]{1,0:T(8,128)}) fusion(f32[1024]{0:T(1024)S(1)} %bitcast.221, bf16[1024,1024]{0,1:T(8,128)(2,1)S(1)} %fusion.20, bf16[2,1024,1024]{2,1,0:T(8,128)(2,1)} %all-gather.2.cloned.1.call-done), kind=kOutput, calls=%fused_computation.36 | convolution fusion | flops 2216689664 | bytes 14684160 | tf_op jit(solution)/shard_map/dot_general | solution.py:17
  199.4 4.4 fusion.67
  222.1 4.5 fusion.76
  230.5 6.0 convolution_convert_fusion
  247.4 7.5 %multiply_reduce_fusion = (f32[1024]{0:T(1024)S(1)}, f32[1024]{0:T(1024)S(1)}, f32[1024]{0:T(1024)S(1)}, f32[1024]{0:T(1024)S(1)}, f32[1024,1024]{0,1:T(8,128)S(1)}) fusion(f32[1024,1024]{0,1:T(8,128)} %copy-done.49, f32[1024]{0:T(1024)S(1)} %add_rsqrt_fusion.1, f32[1024]{0:T(1024)S(1)} %broadcast_multiply_fusion.7, f32[1024]{0:T(1024)S(1)} %bitcast.193, ...), kind=kLoop, calls=%fused_computation.16 | loop fusion | flops 30404608 | bytes 18919424 | tf_op jit(solution)/shard_map/reduce_sum | solution.py:514
  259.4 12.6 %attend_backward.5 = (bf16[1024,256]{1,0:T(8,128)(2,1)S(1)}, bf16[1024,256]{1,0:T(8,128)(2,1)S(1)}, bf16[1024,256]{1,0:T(8,128)(2,1)S(1)}) custom-call(s32[1]{0:T(128)} %dynamic_slice.39.len_ref, bf16[1024,256]{1,0:T(8,128)(2,1)S(1)} %copy-done.26, bf16[1024,256]{1,0:T(8,128)(2,1)S(1)} %copy-done.44, bf16[1024,256]{1,0:T(8,128)(2,1)S(1)} %copy-done.46, ...), custom_call_target="tpu_custom_call" | custom-call | flops 10737418240 | bytes 4194304 | tf_op jit(solution)/shard_map/attend_backward/pallas_call | solution.py:166
  272.1 12.9 %attend_backward.4 = (bf16[1024,256]{1,0:T(8,128)(2,1)S(1)}, bf16[1024,256]{1,0:T(8,128)(2,1)S(1)}, bf16[1024,256]{1,0:T(8,128)(2,1)S(1)}) custom-call(s32[1]{0:T(128)} %dynamic_slice.39.len_ref, bf16[1024,256]{1,0:T(8,128)(2,1)S(1)} %copy-done.24, bf16[1024,256]{1,0:T(8,128)(2,1)S(1)} %copy-done.40, bf16[1024,256]{1,0:T(8,128)(2,1)S(1)} %copy-done.42, ...), custom_call_target="tpu_custom_call" | custom-call | flops 10737418240 | bytes 4194304 | tf_op jit(solution)/shard_map/attend_backward/pallas_call | solution.py:166
  300.7 5.5 add_convert_fusion
  306.1 23.6 %collective-permute-done.17 = bf16[1024,1024]{1,0:T(8,128)(2,1)} collective-permute-done((bf16[1024,1024]{1,0:T(8,128)(2,1)}, bf16[1024,1024]{1,0:T(8,128)(2,1)}, u32[]{:S(2)}, u32[]{:S(2)}) %collective-permute-start.17) | collective-permute-done | bytes 2097184 | tf_op jit(solution)/shard_map/ppermute | solution.py:398
  329.7 5.3 add_convert_fusion.1
  365.6 6.1 multiply_reduce_fusion.1
  377.6 9.7 %attend_backward.6 = (bf16[1024,256]{1,0:T(8,128)(2,1)S(1)}, bf16[1024,256]{1,0:T(8,128)(2,1)S(1)}, bf16[1024,256]{1,0:T(8,128)(2,1)S(1)}) custom-call(s32[1]{0:T(128)} %dynamic_slice.36.len_ref, bf16[1024,256]{1,0:T(8,128)(2,1)S(1)} %copy-done.28, bf16[1024,256]{1,0:T(8,128)(2,1)S(1)} %copy-done.20, bf16[1024,256]{1,0:T(8,128)(2,1)S(1)} %copy-done.30, ...), custom_call_target="tpu_custom_call" | custom-call | flops 10737418240 | bytes 4194304 | tf_op jit(solution)/shard_map/attend_backward/pallas_call | solution.py:166
  397.1 9.5 %attend_backward.7 = (bf16[1024,256]{1,0:T(8,128)(2,1)S(1)}, bf16[1024,256]{1,0:T(8,128)(2,1)S(1)}, bf16[1024,256]{1,0:T(8,128)(2,1)S(1)}) custom-call(s32[1]{0:T(128)} %dynamic_slice.36.len_ref, bf16[1024,256]{1,0:T(8,128)(2,1)S(1)} %copy-done.34, bf16[1024,256]{1,0:T(8,128)(2,1)S(1)} %copy-done.22, bf16[1024,256]{1,0:T(8,128)(2,1)S(1)} %copy-done.32, ...), custom_call_target="tpu_custom_call" | custom-call | flops 10737418240 | bytes 4194304 | tf_op jit(solution)/shard_map/attend_backward/pallas_call | solution.py:166
  415.8 4.9 add_add_fusion.1
  432.6 162.7 %reduce_gradients.1 = (bf16[256,1024]{1,0:T(8,128)(2,1)S(1)}, bf16[1024,256]{1,0:T(8,128)(2,1)S(1)}, bf16[2048,256]{1,0:T(8,128)(2,1)}, bf16[256,1024]{1,0:T(8,1...) custom-call(bf16[256,1024]{1,0:T(8,128)(2,1)S(1)} %copy-done.11, bf16[1024,256]{1,0:T(8,128)(2,1)S(1)} %copy-done.12, ...), custom_call_target="tpu_custom_call" | custom-call | flops 8519680 | bytes 851968000 | tf_op jit(solution)/shard_map/reduce_gradients/pallas_call | solution.py:301
  (442 shorter events, 214.6 us)
Async XLA Ops:
  7.2 169.2 %all-gather.2.cloned.1.call-start = ((), (), s32[]{:S(2)}) async-start(), calls=%async_computation | async-start | bytes 4718592 | tf_op jit(solution)/shard_map/all_gather | solution.py:429
  8.8 17.9 %collective-permute-start = (bf16[512,1024]{0,1:T(8,128)(2,1)S(1)}, bf16[512,1024]{0,1:T(8,128)(2,1)}, u32[]{:S(2)}, u32[]{:S(2)}) collective-permute-start(bf16[512,1024]{0,1:T(8,128)(2,1)S(1)} %copy.33), channel_id=1, source_target_pairs={{0,1},{1,0},{2,3},{3,2},{4,5},{5,4},{6,7},{7,6},{8,9},{9,8},{10,11... | collective-permute-start | bytes 3145736 | tf_op jit(solution)/shard_map/ppermute | solution.py:366
  11.2 17.7 %collective-permute-start.2 = (bf16[2,128,1024]{2,1,0:T(8,128)(2,1)}, bf16[2,128,1024]{2,1,0:T(8,128)(2,1)}, u32[]{:S(2)}, u32[]{:S(2)}) collective-permute-start(bf16[2,128,1024]{2,1,0:T(8,128)(2,1)} %pad_maximum_fusion), channel_id=1, source_target_pairs={{2,0},{0,2},{3,1},{1,3},{6,4},{4,6},{7,5},{5,7},{10,8},{8,10},{11,... | collective-permute-start | bytes 1572872 | tf_op jit(solution)/shard_map/ppermute | solution.py:424
  13.8 12.9 %collective-permute-start.1 = (bf16[8,256]{1,0:T(8,128)(2,1)S(1)}, bf16[8,256]{1,0:T(8,128)(2,1)S(1)}, u32[]{:S(2)}, u32[]{:S(2)}) collective-permute-start(bf16[8,256]{1,0:T(8,128)(2,1)S(1)} %pad_maximum_fusion.1), channel_id=1, source_target_pairs={{2,0},{0,2},{3,1},{1,3},{6,4},{4,6},{7,5},{5,7},{10,8},{8,10},{11,... | collective-permute-start | bytes 12296 | tf_op jit(solution)/shard_map/ppermute | solution.py:392
  28.9 41.5 %copy-start.65 = (bf16[1024,1024]{0,1:T(8,128)(2,1)}, bf16[1024,1024]{0,1:T(8,128)(2,1)S(1)}, u32[]{:S(2)}) copy-start(bf16[1024,1024]{0,1:T(8,128)(2,1)S(1)} %maximum_select_fusion) | copy-start | bytes 6291460
  29.0 37.6 %collective-permute-start.3 = (bf16[3,1024,256]{2,1,0:T(8,128)(2,1)}, bf16[3,1024,256]{2,1,0:T(8,128)(2,1)}, u32[]{:S(2)}, u32[]{:S(2)}) collective-permute-start(bf16[3,1024,256]{2,1,0:T(8,128)(2,1)} %param.22), channel_id=1, source_target_pairs={{2,0},{0,2},{3,1},{1,3},{6,4},{4,6},{7,5},{5,7},{10,8},{8,10},{11,... | collective-permute-start | bytes 4718600 | tf_op jit(solution)/shard_map/ppermute | solution.py:392
  45.1 58.5 %collective-permute-start.6 = (bf16[512,1024]{0,1:T(8,128)(2,1)}, bf16[512,1024]{0,1:T(8,128)(2,1)}, u32[]{:S(2)}, u32[]{:S(2)}) collective-permute-start(bf16[512,1024]{0,1:T(8,128)(2,1)} %copy.36), channel_id=1, source_target_pairs={{0,1},{1,0},{2,3},{3,2},{4,5},{5,4},{6,7},{7,6},{8,9},{9,8},{10,11... | collective-permute-start | bytes 3145736 | tf_op jit(solution)/shard_map/ppermute | solution.py:366
  45.1 61.8 %collective-permute-start.8 = (bf16[2,1024,256]{2,1,0:T(8,128)(2,1)}, bf16[2,1024,256]{2,1,0:T(8,128)(2,1)}, u32[]{:S(2)}, u32[]{:S(2)}) collective-permute-start(bf16[2,1024,256]{2,1,0:T(8,128)(2,1)} %param.25), channel_id=1, source_target_pairs={{2,0},{0,2},{3,1},{1,3},{6,4},{4,6},{7,5},{5,7},{10,8},{8,10},{11,... | collective-permute-start | bytes 3145736 | tf_op jit(solution)/shard_map/ppermute | solution.py:392
  46.2 53.0 %collective-permute-start.4 = (bf16[256,1024]{1,0:T(8,128)(2,1)}, bf16[256,1024]{1,0:T(8,128)(2,1)S(1)}, u32[]{:S(2)}, u32[]{:S(2)}) collective-permute-start(bf16[256,1024]{1,0:T(8,128)(2,1)} %param.23), channel_id=1, source_target_pairs={{2,0},{0,2},{3,1},{1,3},{6,4},{4,6},{7,5},{5,7},{10,8},{8,10},{11,... | collective-permute-start | bytes 1572872 | tf_op jit(solution)/shard_map/ppermute | solution.py:392
  100.8 14.4 %collective-permute-start.5 = (bf16[1024,1024]{0,1:T(8,128)(2,1)S(1)}, bf16[1024,1024]{0,1:T(8,128)(2,1)}, u32[]{:S(2)}, u32[]{:S(2)}) collective-permute-start(bf16[1024,1024]{0,1:T(8,128)(2,1)S(1)} %add_convert_fusion.8), channel_id=1, source_target_pairs={{0,1},{1,0},{2,3},{3,2},{4,5},{5,4},{6,7},{7,6},{8,9},{9,8},{10,11... | collective-permute-start | bytes 6291464 | tf_op jit(solution)/shard_map/ppermute | solution.py:366
  100.8 46.1 %copy-start.101 = (f32[1,1024]{1,0:T(1,128)}, f32[1,1024]{1,0:T(1,128)S(1)}, u32[]{:S(2)}) copy-start(f32[1,1024]{1,0:T(1,128)S(1)} %get-tuple-element.141) | copy-start | bytes 12292
  101.4 505.9 %all-reduce.5.cloned.1.call-start = ((), (), s32[]{:S(2)}) async-start(), calls=%async_computation.1 | async-start | bytes 8388608 | tf_op jit(solution)/shard_map/psum | solution.py:495
  101.5 30.2 %collective-permute-start.7 = (bf16[1024,256]{1,0:T(8,128)(2,1)}, bf16[1024,256]{1,0:T(8,128)(2,1)S(1)}, u32[]{:S(2)}, u32[]{:S(2)}) collective-permute-start(bf16[1024,256]{1,0:T(8,128)(2,1)} %param.24), channel_id=1, source_target_pairs={{2,0},{0,2},{3,1},{1,3},{6,4},{4,6},{7,5},{5,7},{10,8},{8,10},{11,... | collective-permute-start | bytes 1572872 | tf_op jit(solution)/shard_map/ppermute | solution.py:392
  103.1 38.7 %collective-permute-start.9 = (bf16[256,1024]{1,0:T(8,128)(2,1)}, bf16[256,1024]{1,0:T(8,128)(2,1)S(1)}, u32[]{:S(2)}, u32[]{:S(2)}) collective-permute-start(bf16[256,1024]{1,0:T(8,128)(2,1)} %param.26), channel_id=1, source_target_pairs={{2,0},{0,2},{3,1},{1,3},{6,4},{4,6},{7,5},{5,7},{10,8},{8,10},{11,... | collective-permute-start | bytes 1572872 | tf_op jit(solution)/shard_map/ppermute | solution.py:392
  142.6 4.2 collective-permute-start.10
  194.9 4.5 collective-permute-start.11
  195.5 8.8 %collective-permute-start.12 = (bf16[512,1024]{0,1:T(8,128)(2,1)S(1)}, bf16[512,1024]{0,1:T(8,128)(2,1)S(1)}, u32[]{:S(2)}, u32[]{:S(2)}) collective-permute-start(bf16[512,1024]{0,1:T(8,128)(2,1)S(1)} %copy.41), channel_id=1, source_target_pairs={{0,1},{1,0},{2,3},{3,2},{4,5},{5,4},{6,7},{7,6},{8,9},{9,8},{10,11... | collective-permute-start | bytes 3145736 | tf_op jit(solution)/shard_map/ppermute | solution.py:366
  230.4 17.1 %collective-permute-start.13 = (bf16[1024,1024]{0,1:T(8,128)(2,1)}, bf16[1024,1024]{0,1:T(8,128)(2,1)}, u32[]{:S(2)}, u32[]{:S(2)}) collective-permute-start(bf16[1024,1024]{0,1:T(8,128)(2,1)} %add_convert_fusion.3), channel_id=1, source_target_pairs={{0,1},{1,0},{2,3},{3,2},{4,5},{5,4},{6,7},{7,6},{8,9},{9,8},{10,11... | collective-permute-start | bytes 6291464 | tf_op jit(solution)/shard_map/ppermute | solution.py:366
  236.5 64.1 %collective-permute-start.18 = (bf16[1024,1024]{1,0:T(8,128)(2,1)}, bf16[1024,1024]{1,0:T(8,128)(2,1)}, u32[]{:S(2)}, u32[]{:S(2)}) collective-permute-start(bf16[1024,1024]{1,0:T(8,128)(2,1)} %convolution_convert_fusion), channel_id=1, source_target_pairs={{0,2},{2,0},{1,3},{3,1},{4,6},{6,4},{5,7},{7,5},{8,10},{10,8},{9,1... | collective-permute-start | bytes 6291464 | tf_op jit(solution)/shard_map/ppermute | solution.py:398
  241.7 88.0 %collective-permute-start.17 = (bf16[1024,1024]{1,0:T(8,128)(2,1)}, bf16[1024,1024]{1,0:T(8,128)(2,1)}, u32[]{:S(2)}, u32[]{:S(2)}) collective-permute-start(bf16[1024,1024]{1,0:T(8,128)(2,1)} %convolution_convert_fusion.1), channel_id=1, source_target_pairs={{0,2},{2,0},{1,3},{3,1},{4,6},{6,4},{5,7},{7,5},{8,10},{10,8},{9,1... | collective-permute-start | bytes 6291464 | tf_op jit(solution)/shard_map/ppermute | solution.py:398
  288.4 75.6 %collective-permute-start.14 = (bf16[1024,1024]{0,1:T(8,128)(2,1)}, bf16[1024,1024]{0,1:T(8,128)(2,1)}, u32[]{:S(2)}, u32[]{:S(2)}) collective-permute-start(bf16[1024,1024]{0,1:T(8,128)(2,1)} %add_convert_fusion.2), channel_id=1, source_target_pairs={{0,1},{1,0},{2,3},{3,2},{4,5},{5,4},{6,7},{7,6},{8,9},{9,8},{10,11... | collective-permute-start | bytes 6291464 | tf_op jit(solution)/shard_map/ppermute | solution.py:366
  300.6 29.1 %copy-start.123 = (bf16[1024,1024]{1,0:T(8,128)(2,1)S(1)}, bf16[1024,1024]{1,0:T(8,128)(2,1)}, u32[]{:S(2)}) copy-start(bf16[1024,1024]{1,0:T(8,128)(2,1)} %copy-done.122) | copy-start | bytes 6291460
  347.0 15.6 %collective-permute-start.16 = (bf16[512,1024]{1,0:T(8,128)(2,1)}, bf16[512,1024]{1,0:T(8,128)(2,1)S(1)}, u32[]{:S(2)}, u32[]{:S(2)}) collective-permute-start(bf16[512,1024]{1,0:T(8,128)(2,1)} %dynamic-slice_convert_fusion), channel_id=1, source_target_pairs={{0,1},{1,0},{2,3},{3,2},{4,5},{5,4},{6,7},{7,6},{8,9},{9,8},{10,11... | collective-permute-start | bytes 3145736 | tf_op jit(solution)/shard_map/ppermute | solution.py:366
  422.4 182.9 %collective-permute-start.15 = (bf16[512,1024]{0,1:T(8,128)(2,1)S(1)}, bf16[512,1024]{0,1:T(8,128)(2,1)S(1)}, u32[]{:S(2)}, u32[]{:S(2)}) collective-permute-start(bf16[512,1024]{0,1:T(8,128)(2,1)S(1)} %dynamic-slice_convert_fusion.1), channel_id=1, source_target_pairs={{0,1},{1,0},{2,3},{3,2},{4,5},{5,4},{6,7},{7,6},{8,9},{9,8},{10,11... | collective-permute-start | bytes 3145736 | tf_op jit(solution)/shard_map/ppermute | solution.py:366
  (130 other events, 887.4 us)
Sparse Core Ops, SparseCore 0:
  101.6 74.8 all-gather.1
  335.2 198.8 all-reduce.4

commit v5 on v2

--- a/solution.py
+++ b/solution.py
@@ -97,16 +97,12 @@
     b = (x - a).astype(jnp.bfloat16).astype(jnp.float32)
     return a, b, x - a - b
 
-def bwd_kernel(len_ref, q_ref, k_ref, v_ref, o_ref, g_ref, lse_ref, dq_ref, dk_ref, dv_ref, dka, dva, *, causal, bq):
-    p = pl.program_id(0)
-    rows, keys = q_ref.shape[0], k_ref.shape[0]
-    length = len_ref[0]
+
+def key_side(k2, v2, length):
+    keys = k2.shape[0]
     kl = _lanes(keys)
-    kpos = lax.broadcasted_iota(jnp.int32, (keys, 128), 0)
-    kbias = jnp.where(kpos < length, 0.0, NEG)
-    k2 = k_ref[...].astype(jnp.float32)
-    v2 = v_ref[...].astype(jnp.float32)
-    ql = _lanes(bq)
+    kbias = jnp.where(lax.broadcasted_iota(jnp.int32, (keys, 128), 0) < length, 0.0, NEG)
+    k2, v2 = k2.astype(jnp.float32), v2.astype(jnp.float32)
     heads = []
     for h in range(2):
         mine = (kl // HEAD) == h
@@ -115,44 +111,57 @@
         kh = jnp.where(mine, k2, jnp.where(kl == other, kbias, jnp.where(ones, 1.0, 0.0))).astype(jnp.bfloat16)
         vh = jnp.where(mine, v2, jnp.where(ones, 1.0, 0.0)).astype(jnp.bfloat16)
         heads.append((kh, vh, kh.T))
-    for i in reversed(range(rows // bq)):
+    return heads
+
+
+def query_block(heads, q2, o2, g2, lse_all, pair, i, last, causal, dka, dva):
+    bq = q2.shape[0]
+    keys = heads[0][0].shape[0]
+    ql = _lanes(bq)
+    q2 = q2.astype(jnp.float32) * (HEAD ** -0.5)
+    g2 = g2.astype(jnp.float32)
+    go = g2 * o2.astype(jnp.float32)
+    dqt = []
+    for h in range(2):
+        kh, vh, kt = heads[h]
+        mine = (ql // HEAD) == h
+        other = HEAD * (1 - h)
+        lse = jnp.sum(jnp.where(ql == 2 * pair + h, lse_all, 0.0), axis=1, keepdims=True)
+        delta = jnp.sum(jnp.where(mine, go, 0.0), axis=1, keepdims=True)
+        la, lb, lc = split3(-lse)
+        da, db, dc = split3(-delta)
+        qh = _put(jnp.where(mine, q2, 0.0), ql, ((other, 1.0), (other + 1, la), (other + 2, lb), (other + 3, lc))).astype(jnp.bfloat16)
+        gh = _put(jnp.where(mine, g2, 0.0), ql, ((other + 1, da), (other + 2, db), (other + 3, dc))).astype(jnp.bfloat16)
+        hi = (i + 1) * bq if causal else keys
+        st = _nt(kh[:hi], qh)
+        if causal:
+            kr = lax.broadcasted_iota(jnp.int32, (hi, bq), 0)
+            qc = lax.broadcasted_iota(jnp.int32, (hi, bq), 1) + i * bq
+            pt = jnp.where(kr <= qc, jnp.exp(st), 0.0)
+        else:
+            pt = jnp.exp(st)
+        dst = (pt * _nt(vh[:hi], gh)).astype(jnp.bfloat16)
+        dvn = _nn(pt.astype(jnp.bfloat16), gh)
+        dkn = _nn(dst, qh)
+        if last:
+            dva[h, :hi] = dvn
+            dka[h, :hi] = dkn
+        else:
+            dva[h, :hi] += dvn
+            dka[h, :hi] += dkn
+        dqt.append(_nn(kt[:, :hi], dst))
+    dq = jnp.concatenate([dqt[0][:HEAD], dqt[1][HEAD:]], axis=0).T
+    return (dq * (HEAD ** -0.5)).astype(jnp.bfloat16)
+
+
+def bwd_kernel(len_ref, q_ref, k_ref, v_ref, o_ref, g_ref, lse_ref, dq_ref, dk_ref, dv_ref, dka, dva, *, causal, bq):
+    rows, keys = q_ref.shape[0], k_ref.shape[0]
+    heads = key_side(k_ref[...], v_ref[...], len_ref[0])
+    blocks = rows // bq
+    for i in reversed(range(blocks)):
         at = pl.ds(i * bq, bq)
-        q2 = q_ref[at, :].astype(jnp.float32) * (HEAD ** -0.5)
-        g2 = g_ref[at, :].astype(jnp.float32)
-        go = g2 * o_ref[at, :].astype(jnp.float32)
-        lse_all = lse_ref[at, :]
-        dqt = []
-        for h in range(2):
-            kh, vh, kt = heads[h]
-            mine = (ql // HEAD) == h
-            other = HEAD * (1 - h)
-            lse = jnp.sum(jnp.where(ql == 2 * p + h, lse_all, 0.0), axis=1, keepdims=True)
-            delta = jnp.sum(jnp.where(mine, go, 0.0), axis=1, keepdims=True)
-            la, lb, lc = split3(-lse)
-            da, db, dc = split3(-delta)
-            qh = _put(jnp.where(mine, q2, 0.0), ql, ((other, 1.0), (other + 1, la), (other + 2, lb), (other + 3, lc))).astype(jnp.bfloat16)
-            gh = _put(jnp.where(mine, g2, 0.0), ql, ((other + 1, da), (other + 2, db), (other + 3, dc))).astype(jnp.bfloat16)
-            hi = (i + 1) * bq if causal else keys
-            st = _nt(kh[:hi], qh)
-            if causal:
-                kr = lax.broadcasted_iota(jnp.int32, (hi, bq), 0)
-                qc = lax.broadcasted_iota(jnp.int32, (hi, bq), 1) + i * bq
-                pt = jnp.where(kr <= qc, jnp.exp(st), 0.0)
-            else:
-                pt = jnp.exp(st)
-            dst = (pt * _nt(vh[:hi], gh)).astype(jnp.bfloat16)
-            dvn = _nn(pt.astype(jnp.bfloat16), gh)
-            dkn = _nn(dst, qh)
-            if i == rows // bq - 1:
-                dva[h, :hi] = dvn
-                dka[h, :hi] = dkn
-            else:
-                dva[h, :hi] += dvn
-                dka[h, :hi] += dkn
-            dqt.append(_nn(kt[:, :hi], dst))
-        dq = jnp.concatenate([dqt[0][:HEAD], dqt[1][HEAD:]], axis=0).T
-        dq_ref[at, :] = (dq * (HEAD ** -0.5)).astype(jnp.bfloat16)
-    first = kl < HEAD
+        dq_ref[at, :] = query_block(heads, q_ref[at, :], o_ref[at, :], g_ref[at, :], lse_ref[at, :], pl.program_id(0), i, i == blocks - 1, causal, dka, dva)
+    first = _lanes(keys) < HEAD
     dk_ref[...] = jnp.where(first, dka[0], dka[1]).astype(jnp.bfloat16)
     dv_ref[...] = jnp.where(first, dva[0], dva[1]).astype(jnp.bfloat16)
 
@@ -177,6 +186,248 @@
         name="attend_backward",
     )(length, q, k, v, o, g, lse)
 
+CHUNK = 512
+SPAN = 256
+
+
+class Pipeline:
+    AHEAD = 3
+
+    def __init__(self, total, scratch):
+        self.spots, self.total, self.step, self.sent, self.loaded = [], total, 0, 0, 0
+        (self.held, self.ysum, self.zgot, self.full, self.mine, self.load, self.store, self.xs, self.xr, self.ys, self.yr, self.zs, self.zr, self.bs, self.br, self.es, self.er) = scratch
+        self.seq, self.ya, za = lax.axis_index("g"), lax.axis_index("y"), lax.axis_index("z")
+        self.za = za
+        self.peers = {1: za + 1 - 2 * (za % 2), 2: (za + 2) % 4, 3: 3 - za}
+        self.stages = (self.to_y, self.to_z, self.back_z, self.back_y, self.finish)
+
+    @staticmethod
+    def scratch(total, most):
+        dma = pltpu.SemaphoreType.DMA
+        return [
+            pltpu.VMEM((total, most, SPAN), LOW),
+            pltpu.VMEM((total, most // 2, SPAN), LOW),
+            pltpu.VMEM((total, 3, most // 8, SPAN), LOW),
+            pltpu.VMEM((total, most, SPAN), LOW),
+            pltpu.VMEM((4, most, SPAN), LOW),
+            dma((4,)), dma((total,)),
+            dma((total,)), dma((total,)), dma((total,)), dma((total,)),
+            dma((total, 3)), dma((total, 3)), dma((total, 3)), dma((total, 3)),
+            dma((total,)), dma((total,)),
+        ]
+
+    def greet(self, more=()):
+        barrier = pltpu.get_barrier_semaphore()
+        everyone = [{"g": 1 - self.seq}, {"y": 1 - self.ya}] + [{"z": self.peers[d]} for d in (1, 2, 3)] + list(more)
+        for where in everyone:
+            pl.semaphore_signal(barrier, inc=1, device_id=where, device_id_type=pl.DeviceIdType.MESH)
+        pl.semaphore_wait(barrier, len(everyone))
+
+    def add(self, own, other, out, out_row):
+        rows, cols = own.shape
+        size = min(CHUNK, rows)
+        for r in range(0, rows, size):
+            for c in range(0, cols, SPAN):
+                self.spots.append((own, other, r, c, size, out, out_row + r))
+        self.feed()
+
+    def feed(self):
+        while self.sent < min(len(self.spots), self.step + self.AHEAD):
+            self.x_copy(self.sent).start()
+            self.own_copy(self.sent).start()
+            self.sent += 1
+
+    def tick(self, times=1):
+        for unused in range(times):
+            if self.step >= self.total + len(self.stages) - 1:
+                return
+            for at, stage in enumerate(self.stages):
+                if 0 <= self.step - at < self.total:
+                    stage(self.step - at)
+            self.step += 1
+            self.feed()
+
+    def drain(self):
+        assert len(self.spots) == self.total
+        self.tick(self.total + len(self.stages))
+        for k in range(self.total):
+            self.x_copy(k).wait_send()
+            self.y_copy(k).wait_send()
+            self.yb_copy(k).wait_send()
+            self.out_copy(k).wait()
+            for d in (1, 2, 3):
+                self.z_copy(k, d).wait_send()
+                self.zb_copy(k, d).wait_send()
+
+    @staticmethod
+    def remote(src, dst, send, recv, where):
+        return pltpu.make_async_remote_copy(src_ref=src, dst_ref=dst, send_sem=send, recv_sem=recv, device_id=where, device_id_type=pl.DeviceIdType.MESH)
+
+    @staticmethod
+    def block(at, size):
+        return pl.ds(pl.multiple_of(at * size, size), size)
+
+    def x_copy(self, k):
+        own, other, r, c, n, o, q = self.spots[k]
+        return self.remote(other.at[pl.ds(r, n), pl.ds(c, SPAN)], self.held.at[k, pl.ds(0, n)], self.xs.at[k], self.xr.at[k], {"g": 1 - self.seq})
+
+    def own_copy(self, k):
+        own, other, r, c, n, o, q = self.spots[k]
+        return pltpu.make_async_copy(own.at[pl.ds(r, n), pl.ds(c, SPAN)], self.mine.at[k % 4, pl.ds(0, n)], self.load.at[k % 4])
+
+    def y_copy(self, k):
+        h = self.spots[k][4] // 2
+        return self.remote(self.held.at[k, self.block(1 - self.ya, h)], self.ysum.at[k, pl.ds(0, h)], self.ys.at[k], self.yr.at[k], {"y": 1 - self.ya})
+
+    def z_copy(self, k, d):
+        p = self.spots[k][4] // 8
+        return self.remote(self.ysum.at[k, self.block(self.peers[d], p)], self.zgot.at[k, d - 1, pl.ds(0, p)], self.zs.at[k, d - 1], self.zr.at[k, d - 1], {"z": self.peers[d]})
+
+    def zb_copy(self, k, d):
+        rows = self.full.at[k, self.block(self.ya * 4 + self.za, self.spots[k][4] // 8)]
+        return self.remote(rows, rows, self.bs.at[k, d - 1], self.br.at[k, d - 1], {"z": self.peers[d]})
+
+    def yb_copy(self, k):
+        rows = self.full.at[k, self.block(self.ya, self.spots[k][4] // 2)]
+        return self.remote(rows, rows, self.es.at[k], self.er.at[k], {"y": 1 - self.ya})
+
+    def out_copy(self, k):
+        own, other, r, c, n, o, q = self.spots[k]
+        return pltpu.make_async_copy(self.full.at[k, pl.ds(0, n)], o.at[pl.ds(q, n), pl.ds(c, SPAN)], self.store.at[k])
+
+    def to_y(self, k):
+        n = self.spots[k][4]
+        self.own_copy(k).wait()
+        self.x_copy(k).wait_recv()
+        self.held[k, :n] = self.held[k, :n] + self.mine[k % 4, :n]
+        self.y_copy(k).start()
+
+    def to_z(self, k):
+        h = self.spots[k][4] // 2
+        self.y_copy(k).wait_recv()
+        self.ysum[k, :h] = self.ysum[k, :h] + self.held[k, self.block(self.ya, h)]
+        for d in (1, 2, 3):
+            self.z_copy(k, d).start()
+
+    def back_z(self, k):
+        p = self.spots[k][4] // 8
+        for d in (1, 2, 3):
+            self.z_copy(k, d).wait_recv()
+        rows = self.ysum[k, self.block(self.za, p)].astype(F32)
+        for d in (1, 2, 3):
+            rows = rows + self.zgot[k, d - 1, :p].astype(F32)
+        self.full[k, self.block(self.ya * 4 + self.za, p)] = rows.astype(LOW)
+        for d in (1, 2, 3):
+            self.zb_copy(k, d).start()
+
+    def back_y(self, k):
+        for d in (1, 2, 3):
+            self.zb_copy(k, d).wait_recv()
+        self.yb_copy(k).start()
+
+    def finish(self, k):
+        self.yb_copy(k).wait_recv()
+        self.out_copy(k).start()
+
+
+def spot_count(shapes):
+    return sum((rows // min(CHUNK, rows)) * (cols // SPAN) for rows, cols in shapes)
+
+
+def self_back_kernel(carried, bq, len_ref, low, q0, k0, v0, o0, l0, q1, k1, v1, o1, l1, wo0, wo1, xt, w0, w1, small0, small1, *rest):
+    own, other, rest = rest[:carried], rest[carried : 2 * carried], rest[2 * carried :]
+    token_out, rest = rest[0], rest[1:]
+    outs, rest = rest[: carried + 3], rest[carried + 3 :]
+    gm, dq, dk, dv, dka, dva, go_own, go_other, gi_own, gi_other, sm_own, sm_other, part, got, part_send, part_recv = rest[:16]
+    core = lax.axis_index("c")
+    total = spot_count([ref.shape for ref in own] + [go_own.shape, gi_own.shape, sm_own.shape])
+    pipe = Pipeline(total, rest[16:])
+    pipe.greet([{"c": 1 - core}])
+    for a, b, out in zip(own, other, outs):
+        pipe.add(a, b, out, 0)
+    shards = ((q0, k0, v0, o0, l0, wo0, w0, go_own, gi_own, sm_own, small0), (q1, k1, v1, o1, l1, wo1, w1, go_other, gi_other, sm_other, small1))
+    rows = low.shape[0]
+    blocks = rows // bq
+    for s, (q, k, v, o, l, wo, w, go, gi, sm, small) in enumerate(shards):
+        for c in range(0, low.shape[1], SPAN):
+            go[:, c : c + SPAN] = tn(o[...], low[:, c : c + SPAN]).astype(LOW)
+        for i in range(blocks):
+            at = pl.ds(i * bq, bq)
+            gm[s, at, :] = _nt(low[at, :], wo[...]).astype(LOW)
+    pipe.add(go_own, go_other, outs[carried], 0)
+    for s, (q, k, v, o, l, wo, w, go, gi, sm, small) in enumerate(shards):
+        width = q.shape[1]
+        for p in range(width // 128):
+            cols = pl.ds(p * 128, 128)
+            heads = key_side(k[:, cols], v[:, cols], len_ref[0])
+            for i in reversed(range(blocks)):
+                at = pl.ds(i * bq, bq)
+                dq[s, at, cols] = query_block(heads, q[at, cols], o[at, cols], gm[s, at, cols], l[at, :], p, i, i == blocks - 1, True, dka, dva)
+            first = _lanes(rows) < HEAD
+            dk[s, :, cols] = jnp.where(first, dka[0], dka[1]).astype(LOW)
+            dv[s, :, cols] = jnp.where(first, dva[0], dva[1]).astype(LOW)
+            pipe.tick()
+    for s, (q, k, v, o, l, wo, w, go, gi, sm, small) in enumerate(shards):
+        for m, grads in enumerate((dq, dk, dv)):
+            for i in range(blocks):
+                at = pl.ds(i * bq, bq)
+                gi[pl.ds(m * rows + i * bq, bq), :] = _nn(xt[at, :], grads[s]).astype(LOW)
+        row = lax.broadcasted_iota(jnp.int32, sm.shape, 0)
+        sums = [jnp.sum(grads[s].astype(F32), axis=0, keepdims=True) for grads in (dq, dv)]
+        sm[...] = jnp.where(row == 9, sums[0], jnp.where(row == 10, sums[1], small[...])).astype(LOW)
+    pipe.add(gi_own, gi_other, outs[carried + 1], 0)
+    pipe.add(sm_own, sm_other, outs[carried + 2], 0)
+    half = rows // 2
+    exchange = Pipeline.remote(part, got, part_send, part_recv, {"c": 1 - core})
+
+    def token_rows(start, size):
+        at = pl.ds(pl.multiple_of(start, size), size)
+        both = jnp.zeros((size, low.shape[1]), F32)
+        for s, w in ((0, w0), (1, w1)):
+            for m, grads in enumerate((dq, dk, dv)):
+                both = both + _nt(grads[s, at, :], w[m])
+        return both
+
+    for i in range(0, half, bq):
+        part[pl.ds(i, bq), :] = token_rows((1 - core) * half + i, bq).astype(LOW)
+    exchange.start()
+    pipe.tick()
+    for i in range(0, half, bq):
+        token_out[pl.ds(i, bq), :] = token_rows(core * half + i, bq)
+    pipe.tick()
+    exchange.wait()
+    for i in range(0, half, bq):
+        token_out[pl.ds(i, bq), :] += got[pl.ds(i, bq), :].astype(F32)
+    pipe.drain()
+
+
+def self_back(length, low, first, second, wo, xt, w, smalls, pairs, places, results, bq=256):
+    rows, model = low.shape
+    width = wo[0].shape[0]
+    carried = len(pairs)
+    any_space = pl.BlockSpec(memory_space=pl.ANY)
+    vmem = pl.BlockSpec(memory_space=pltpu.VMEM)
+    ends = [(width, model), (3 * rows, width), smalls[0].shape]
+    total = spot_count([own.shape for own, unused in pairs] + ends)
+    low_ram = lambda *shape: pltpu.VMEM(shape, LOW)
+    return pl.pallas_call(
+        functools.partial(self_back_kernel, carried, bq),
+        out_shape=[jax.ShapeDtypeStruct((rows // 2, model), F32)] + [jax.ShapeDtypeStruct(own.shape, LOW) for own, unused in pairs] + [jax.ShapeDtypeStruct(shape, LOW) for shape in ends],
+        in_specs=[pl.BlockSpec(memory_space=pltpu.SMEM)] + [vmem] * 18 + [any_space] * (2 * carried),
+        out_specs=[vmem] + [any_space] * (carried + 3),
+        scratch_shapes=[
+            low_ram(2, rows, width), low_ram(2, rows, width), low_ram(2, rows, width), low_ram(2, rows, width),
+            pltpu.VMEM((2, rows, 128), F32), pltpu.VMEM((2, rows, 128), F32),
+            low_ram(width, model), low_ram(width, model), low_ram(3 * rows, width), low_ram(3 * rows, width),
+            low_ram(*smalls[0].shape), low_ram(*smalls[0].shape),
+            low_ram(rows // 2, model), low_ram(rows // 2, model), pltpu.SemaphoreType.DMA, pltpu.SemaphoreType.DMA,
+        ] + Pipeline.scratch(total, CHUNK),
+        compiler_params=pltpu.CompilerParams(collective_id=0, has_side_effects=True, vmem_limit_bytes=58 << 20),
+        cost_estimate=pl.CostEstimate(flops=20 * rows * model * width, bytes_accessed=200 << 20, transcendentals=8 * rows * rows),
+        name="self_backward",
+    )(length, low, *first, *second, *wo, xt, *w, *smalls, *[p[0] for p in pairs], *[p[1] for p in pairs])
+
+
 residual_scale = 300.0**0.25
 norm_epsilon = 1e-05
 LOW = jnp.bfloat16
@@ -274,15 +525,19 @@
             total = jnp.where((at // far) % 2 == 0, jnp.concatenate([total, got]), jnp.concatenate([got, total]))
         return total.astype(F32)
 
-    def spread_wide(shard, axis):
-        size = shard.shape[0] // (zn * yn)
+    def fetch_slices(shards):
         at = lax.axis_index("z") * yn + lax.axis_index("y")
-        piece = lax.dynamic_slice_in_dim(shard, at * size, size, 0)
-        every = [shard]
-        for k in range(1, gn):
-            got = lax.ppermute(piece, "g", [((i + k) % gn, i) for i in range(gn)])
-            every.append(lax.all_gather(got, ("z", "y"), axis=0, tiled=True))
-        return [jnp.concatenate(every, axis=axis)] if joined else every
+        pieces = [lax.dynamic_slice_in_dim(shard, at * (shard.shape[0] // (zn * yn)), shard.shape[0] // (zn * yn), 0) for shard in shards]
+        pieces = [jnp.stack(pieces)] if pieces[0].shape == pieces[1].shape else [piece[None] for piece in pieces]
+        return [[lax.ppermute(piece, "g", [((i + k) % gn, i) for i in range(gn)]) for piece in pieces] for k in range(1, gn)]
+
+    def spread_wide(shards, slices):
+        every = [[shard] for shard in shards]
+        for got in slices:
+            whole = [rows for piece in got for rows in lax.all_gather(piece, ("z", "y"), axis=1, tiled=True)]
+            for at, rows in enumerate(whole):
+                every[at].append(rows)
+        return [[jnp.concatenate(part, axis=1 - at)] if joined else part for at, part in enumerate(every)]
 
     def parts_of(values, axis):
         return jnp.split(values[0], gn, axis=axis) if joined else values
@@ -290,24 +545,38 @@
     target_length = lax.dynamic_slice_in_dim(target_lengths, seq, 1, 0)
     memory_length = lax.dynamic_slice_in_dim(memory_lengths, seq, 1, 0)
 
+    def after(value, *needed):
+        return lax.optimization_barrier((value,) + needed)[0]
+
     token_all = gather_rows(tokens)
-    w_self = spread(self_inputs, 2)
-    b_proj = spread(proj_bias, 1)
-    w_self_out = spread(self_output, 0)
-    memory_all = gather_rows(memory)
-    w_cross_mem = spread(cross_memory, 2)
-    w_cross_q = spread(cross_query, 1)
-    w_cross_out = spread(cross_output, 0)
-    w_in = spread_wide(feed_in, 1)
-    b_in = spread(feed_bias, 0)
-    w_out = spread_wide(feed_out, 0)
-    cot_all = gather_rows(cotangent)
+    biases = spread(jnp.concatenate([proj_bias, feed_bias.reshape(-1, width)]), 1)
+    feed_rows = feed_bias.shape[0] // width
+    if joined:
+        halves = jnp.split(biases[0], gn, axis=1)
+        b_in = [jnp.concatenate([part[4:].reshape(-1) for part in halves])]
+    else:
+        b_in = [part[4:].reshape(-1) for part in biases]
+    b_proj = [part[:4] for part in biases]
+    slices = fetch_slices((feed_in, feed_out))
+    w_self = spread(after(self_inputs, token_all, biases[-1], slices[-1][0]), 2)
+    w_in, w_out = spread_wide((feed_in, feed_out), slices)
+    self_q, self_k, self_v, self_mixed, self_lse = [], [], [], [], []
     shards = range(len(w_self))
-
-    self_q = [(_nn(token_all, w_self[s][0]) + b_proj[s][0]).astype(LOW) for s in shards]
-    self_k = [_nn(token_all, w_self[s][1]).astype(LOW) for s in shards]
-    self_v = [(_nn(token_all, w_self[s][2]) + b_proj[s][1]).astype(LOW) for s in shards]
-    self_mixed, self_lse = zip(*[attn_fwd(target_length, self_q[s], self_k[s], self_v[s], True) for s in shards])
+    for s in shards:
+        self_q.append((_nn(token_all, w_self[s][0]) + b_proj[s][0]).astype(LOW))
+        self_k.append(_nn(token_all, w_self[s][1]).astype(LOW))
+        self_v.append((_nn(token_all, w_self[s][2]) + b_proj[s][1]).astype(LOW))
+        mixed, lse = attn_fwd(target_length, self_q[s], self_k[s], self_v[s], True)
+        self_mixed.append(mixed)
+        self_lse.append(lse)
+    first = self_mixed[0]
+    w_self_out = spread(after(self_output, first), 0)
+    memory_all = gather_rows(after(memory, first))
+    w_cross_mem = spread(after(cross_memory, first), 2)
+    w_cross_q = spread(after(cross_query, first), 1)
+    w_cross_out = spread(after(cross_output, first), 0)
+    cot_all = gather_rows(after(cotangent, self_mixed[-1]))
+
     cross_k = [_nn(memory_all, w_cross_mem[s][0]).astype(LOW) for s in shards]
     cross_v = [(_nn(memory_all, w_cross_mem[s][1]) + b_proj[s][3]).astype(LOW) for s in shards]
     branch_one = sum_all(sum(_nn(self_mixed[s], w_self_out[s]) for s in shards)) + branch_bias[0]
@@ -328,49 +597,57 @@
     grad_three = norm_backward(cot, unit_three, inverse_three, norm_gain[2])
     low_three = grad_three.astype(LOW)
     grad_hidden = [_nt(low_three, w_out[s]) for s in shards]
-    grad_feed_out = sum_groups(send_home(parts_of([tn(hidden[s], low_three) for s in shards], 0)))
+    feed_out_parts = parts_of([tn(hidden[s], low_three) for s in shards], 0)
     grad_pre = [gelu_backward(hidden_pre[s], grad_hidden[s]).astype(LOW) for s in shards]
-    grad_feed_in = sum_groups(send_home(parts_of([tn(third, grad_pre[s]) for s in shards], 1)))
+    feed_in_parts = parts_of([tn(third, grad_pre[s]) for s in shards], 1)
+    feed_out_sum, feed_in_sum = [lax.psum(send_home(part).astype(LOW), ("z", "y")).astype(F32) for part in (feed_out_parts, feed_in_parts)]
     grad_normed_two = residual_scale * grad_three + sum_all(sum(_nt(grad_pre[s], w_in[s]) for s in shards))
     grad_two = norm_backward(grad_normed_two, unit_two, inverse_two, norm_gain[1])
     low_two = grad_two.astype(LOW)
     grad_cross_mixed = [_nt(low_two, w_cross_out[s]).astype(LOW) for s in shards]
-    cross_out_parts = parts_of([tn(low_two, cross_mixed[s]) for s in shards], 1)
+    cross_out_parts = parts_of([tn(cross_mixed[s], low_two) for s in shards], 0)
     cross_dq, cross_dk, cross_dv = zip(*[attn_bwd(memory_length, cross_q[s], cross_k[s], cross_v[s], cross_mixed[s], grad_cross_mixed[s], cross_lse[s], False) for s in shards])
     grad_normed_one = residual_scale * grad_two + sum_all(sum(_nt(cross_dq[s], w_cross_q[s]) for s in shards))
-    cross_parts = [cross_out_parts, parts_of([tn(second, cross_dq[s]) for s in shards], 1)]
-    cross_parts += [parts_of([tn(memory_all, cross_dk[s]) for s in shards], 1), parts_of([tn(memory_all, cross_dv[s]) for s in shards], 1)]
-    cross_total = sum_groups(send_home([jnp.concatenate([part[k] for part in cross_parts]) for k in range(gn)]))
+    cross_parts = [parts_of([tn(second, cross_dq[s]) for s in shards], 1), parts_of([tn(memory_all, cross_dk[s]) for s in shards], 1), parts_of([tn(memory_all, cross_dv[s]) for s in shards], 1)]
     grad_memory = sum_own(sum(_nt(cross_dk[s], w_cross_mem[s][0]) + _nt(cross_dv[s], w_cross_mem[s][1]) for s in shards)).astype(LOW)
     grad_one = norm_backward(grad_normed_one, unit_one, inverse_one, norm_gain[0])
     low_one = grad_one.astype(LOW)
-    grad_self_mixed = [_nt(low_one, w_self_out[s]).astype(LOW) for s in shards]
-    self_out_parts = parts_of([tn(low_one, self_mixed[s]) for s in shards], 1)
-    self_dq, self_dk, self_dv = zip(*[attn_bwd(target_length, self_q[s], self_k[s], self_v[s], self_mixed[s], grad_self_mixed[s], self_lse[s], True) for s in shards])
-    token_part = sum(_nt(self_dq[s], w_self[s][0]) + _nt(self_dk[s], w_self[s][1]) + _nt(self_dv[s], w_self[s][2]) for s in shards)
-    grad_tokens = (residual_scale * own_rows(grad_one) + sum_own(token_part)).astype(LOW)
 
     def sums(rows):
         return jnp.sum(rows.astype(F32), axis=0)
 
+    model = tokens.shape[1]
     terms = jnp.stack([sums(low_one), sums(low_two), sums(low_three), sums(grad_normed_one * unit_one), sums(grad_normed_two * unit_two), sums(cot * unit_three), sums(grad_normed_one), sums(grad_normed_two), sums(cot)])
-    proj_sums = parts_of([jnp.stack([sums(self_dq[s]), sums(self_dv[s]), sums(cross_dq[s]), sums(cross_dv[s])]) for s in shards], 1)
     feed_sums = parts_of([sums(grad_pre[s]) for s in shards], 0)
-    self_parts = [self_out_parts] + [parts_of([tn(token_all, grads[s]) for s in shards], 1) for grads in (self_dq, self_dk, self_dv)]
-    packed = []
+    groups = [[cross_out_parts], cross_parts[:1], cross_parts[1:]]
+    in_kernel = (zn, yn, gn, cn, width, joined) == (4, 2, 2, 2, SPAN, False)
+    if not in_kernel:
+        grad_self_mixed = [_nt(low_one, w_self_out[s]).astype(LOW) for s in shards]
+        self_out_parts = parts_of([tn(self_mixed[s], low_one) for s in shards], 0)
+        self_dq, self_dk, self_dv = zip(*[attn_bwd(target_length, self_q[s], self_k[s], self_v[s], self_mixed[s], grad_self_mixed[s], self_lse[s], True) for s in shards])
+        token_part = sum_own(sum(_nt(self_dq[s], w_self[s][0]) + _nt(self_dk[s], w_self[s][1]) + _nt(self_dv[s], w_self[s][2]) for s in shards))
+        self_sums = parts_of([jnp.stack([sums(self_dq[s]), sums(self_dv[s])]) for s in shards], 1)
+    else:
+        self_sums = [jnp.zeros((2, width), F32)] * gn
+    cross_sums = parts_of([jnp.stack([sums(cross_dq[s]), sums(cross_dv[s])]) for s in shards], 1)
+    smalls = []
     for k in range(gn):
         small = lax.dynamic_slice_in_dim(terms, ((seq + k) % gn * cn + core) * width, width, 1)
-        small = jnp.concatenate([small, proj_sums[k], feed_sums[k].reshape(-1, width)])
-        small = jnp.pad(small, ((0, 16 * zn * yn - small.shape[0]), (0, 0)))
-        packed.append(jnp.concatenate([part[k] for part in self_parts] + [small]))
-    self_total = sum_groups(send_home(packed))
-    model = tokens.shape[1]
-    take = lambda rows, at: lax.slice_in_dim(rows, at * model, (at + 1) * model)
-    small = self_total[4 * model:]
-    grad_self_inputs = jnp.stack([take(self_total, 1), take(self_total, 2), take(self_total, 3)])
-    grad_cross_memory = jnp.stack([take(cross_total, 2), take(cross_total, 3)])
-    feed_rows = feed_bias.shape[0] // width
-    return (block_out, grad_tokens, grad_memory, grad_self_inputs, take(self_total, 0).T, take(cross_total, 1), grad_cross_memory, take(cross_total, 0).T, grad_feed_in, grad_feed_out, small[9:13], small[13:13 + feed_rows].reshape(-1), small[0:3], small[3:6], small[6:9])
+        small = jnp.concatenate([small, self_sums[k], cross_sums[k], feed_sums[k].reshape(-1, width)])
+        smalls.append(jnp.pad(small, ((0, 16 * zn * yn - small.shape[0]), (0, 0))))
+    if in_kernel:
+        pairs = [(part[0].astype(LOW), part[1].astype(LOW)) for group in groups for part in group]
+        per_shard = [(self_q[s], self_k[s], self_v[s], self_mixed[s], self_lse[s]) for s in shards]
+        token_part, *sums_low = self_back(target_length, low_one, per_shard[0], per_shard[1], w_self_out, token_all.T, w_self, smalls, pairs, None, None)
+        sums_low = [rows.astype(F32) for rows in sums_low]
+        cross_out_sum, cross_q_sum, cross_k_sum, cross_v_sum, self_out_sum, self_in_sum, small = sums_low
+        cross_mem_sum = jnp.stack([cross_k_sum, cross_v_sum])
+    else:
+        groups += [[self_out_parts], [parts_of([tn(token_all, grads[s]) for s in shards], 1) for grads in (self_dq, self_dk, self_dv)], [smalls]]
+        sums_low = [sum_groups(send_home([jnp.concatenate([part[k] for part in group]) for k in range(gn)])) for group in groups]
+        cross_out_sum, cross_q_sum, cross_mem_sum, self_out_sum, self_in_sum, small = [rows.astype(F32) for rows in sums_low]
+    grad_tokens = (residual_scale * own_rows(grad_one) + token_part).astype(LOW)
+    return (block_out, grad_tokens, grad_memory, self_in_sum.reshape(3, model, width), self_out_sum, cross_q_sum, cross_mem_sum.reshape(2, model, width), cross_out_sum, feed_in_sum, feed_out_sum, small[9:13], small[13:13 + feed_rows].reshape(-1), small[0:3], small[3:6], small[6:9])
 
 
 def solution(mesh):

time: 695 us -> 606 us (0.87)
  Pallas kernels: 79.3 us -> 254 us
  waiting for transfers between devices: 237 us -> 86.1 us
  matrix products: 168 us -> 131 us
  other arithmetic: 92.9 us -> 61.8 us
  starting transfers between devices: 42.7 us -> 12.4 us
  local copies, waits for them, and re-layouts: 49.2 us -> 35.8 us
    pallas_call x0 -> x1, Pallas kernels: none -> 193 us  [self_back(): pl.pallas_call(functools.partial(self_back_kernel, carried, bq), out_shap...]
    ppermute x26 -> x1, waiting for transfers between devices: 174 us -> 0.01 us  [fetch_slices(): lax.ppermute(piece, 'g', [((i + k) % gn, i) for i in range(gn)])]
    ppermute x7 -> x6, waiting for transfers between devices: 19.8 us -> 46.8 us  [spread(): lax.ppermute(shard, 'g', [((i + k) % gn, i) for i in range(gn)])]
    ppermute x26 -> x1, starting transfers between devices: 29.1 us -> 2.8 us  [fetch_slices(): lax.ppermute(piece, 'g', [((i + k) % gn, i) for i in range(gn)])]
    pallas_call x4 -> x2, Pallas kernels: 44.9 us -> 25.7 us  [attn_bwd(): pl.pallas_call(functools.partial(bwd_kernel, causal=causal, bq=bq), out_s...]
    unnamed x253 -> x216, local copies, waits for them, and re-layouts: 35.6 us -> 20.3 us
    dot_general x20 -> x12, matrix products: 43.3 us -> 30.3 us  [_nt(): lax.dot_general(a, b, (((1,), (1,)), ((), ())), preferred_element_type=jn...]
    dot_general x20 -> x12, matrix products: 52.3 us -> 39.5 us  [tn(): lax.dot_general(rows, grads, (((0,), (0,)), ((), ())), preferred_element_...]
  transfers between devices with their start and end apart: 49 -> 20, of which waited for: 22 -> 7; matrix products, arithmetic and copies ran while one was open for 36% -> 28% of each run, Pallas kernels for 12% -> 43%
where the time goes in v5:
time: 606 us; the launch traced here: 597 us
  Pallas kernels  254 us (42%)
  matrix products  131 us (22%)
  waiting for transfers between devices  86.1 us (14%)
  other arithmetic  61.8 us (10%)
  local copies, waits for them, and re-layouts  35.8 us (6%)
  between operations  16 us (3%)
  starting transfers between devices  12.4 us (2%)
    pallas_call x1, Pallas kernels, self_back(): pl.pallas_call(functools.partial(self_back_kernel, carried, bq), out_shap...  193 us
    dot_general x20, matrix products, _nn(): lax.dot_general(a, b, (((1,), (0,)), ((), ())), preferred_element_type=jn...  61.3 us
    ppermute x6, waiting for transfers between devices, spread(): lax.ppermute(shard, 'g', [((i + k) % gn, i) for i in range(gn)])  46.8 us
    dot_general x12, matrix products, tn(): lax.dot_general(rows, grads, (((0,), (0,)), ((), ())), preferred_element_...  39.5 us
    pallas_call x4, Pallas kernels, attn_fwd(): pl.pallas_call(functools.partial(fwd_kernel, causal=causal, bq=bq), out_s...  34.6 us
    dot_general x12, matrix products, _nt(): lax.dot_general(a, b, (((1,), (1,)), ((), ())), preferred_element_type=jn...  30.3 us
    pallas_call x2, Pallas kernels, attn_bwd(): pl.pallas_call(functools.partial(bwd_kernel, causal=causal, bq=bq), out_s...  25.7 us
    ppermute x2, waiting for transfers between devices, send_home(): lax.ppermute(parts[k].astype(LOW), 'g', [(i, (i + k) % gn) for i in range...  25.4 us
  transfers between devices with their start and end apart: 20, of which 7 were waited for; matrix products, arithmetic and copies ran while one was open for 28% of the time, Pallas kernels for 43%

profile of v5, /device:TPU:0, one launch (start us, length us, event | category | flops | bytes accessed | tf_op | source)
XLA Modules:
  0.0 597.0 jit_solution(565048004240686571)
XLA Ops:
  16.1 10.5 %collective-permute-done.1 = bf16[8,256]{1,0:T(8,128)(2,1)S(1)} collective-permute-done((bf16[8,256]{1,0:T(8,128)(2,1)S(1)}, bf16[8,256]{1,0:T(8,128)(2,1)S(1)}, u32[]{:S(2)}, u32[]{:S(2)}) %collective-permute-start.1) | collective-permute-done | bytes 4128 | tf_op jit(solution)/shard_map/ppermute | solution.py:500
  34.9 7.6 %attend_forward.4 = (bf16[1024,256]{1,0:T(8,128)(2,1)S(1)}, f32[1024,128]{1,0:T(8,128)S(1)}) custom-call(s32[1]{0:T(128)} %dynamic_slice.30.len_ref, bf16[1024,256]{1,0:T(8,128)(2,1)S(1)} %fusion.25.q_ref.q0, bf16[1024,256]{1,0:T(8,128)(2,1)S(1)} %convolution_convert_fusion.15.k_ref.k0, bf16[1024,256]{1,0:T(8,128)(2,1)S(1)} %fusion.26.v_ref.v0), custom_call_target="tpu_custom_call" | custom-call | flops 4294967296 | bytes 2097152 | tf_op jit(solution)/shard_map/attend_forward/pallas_call | solution.py:82
  49.7 17.7 %collective-permute-done.3.w1 = bf16[3,1024,256]{2,1,0:T(8,128)(2,1)} collective-permute-done((bf16[3,1024,256]{2,1,0:T(8,128)(2,1)}, bf16[3,1024,256]{2,1,0:T(8,128)(2,1)}, u32[]{:S(2)}, u32[]{:S(2)}) %collective-permute-start.3) | collective-permute-done | bytes 1572896 | tf_op jit(solution)/shard_map/ppermute | solution.py:500
  73.2 7.8 %attend_forward.5 = (bf16[1024,256]{1,0:T(8,128)(2,1)S(1)}, f32[1024,128]{1,0:T(8,128)S(1)}) custom-call(s32[1]{0:T(128)} %dynamic_slice.30.len_ref, bf16[1024,256]{1,0:T(8,128)(2,1)S(1)} %fusion.27.q_ref.q1, bf16[1024,256]{1,0:T(8,128)(2,1)S(1)} %convolution_convert_fusion.14.k_ref.k1, bf16[1024,256]{1,0:T(8,128)(2,1)S(1)} %fusion.28.v_ref.v1), custom_call_target="tpu_custom_call" | custom-call | flops 4294967296 | bytes 2097152 | tf_op jit(solution)/shard_map/attend_forward/pallas_call | solution.py:82
  81.1 18.5 %collective-permute-done.4.wo1 = bf16[256,1024]{1,0:T(8,128)(2,1)S(1)} collective-permute-done((bf16[256,1024]{1,0:T(8,128)(2,1)}, bf16[256,1024]{1,0:T(8,128)(2,1)S(1)}, u32[]{:S(2)}, u32[]{:S(2)}) %collective-permute-start.4) | collective-permute-done | bytes 524320 | tf_op jit(solution)/shard_map/ppermute | solution.py:500
  120.6 9.9 %attend_forward.6 = (bf16[1024,256]{1,0:T(8,128)(2,1)S(1)}, f32[1024,128]{1,0:T(8,128)S(1)}) custom-call(s32[1]{0:T(128)} %dynamic_slice.33.len_ref, bf16[1024,256]{1,0:T(8,128)(2,1)S(1)} %fusion.29.q_ref, bf16[1024,256]{1,0:T(8,128)(2,1)S(1)} %convolution_convert_fusion.13.k_ref, bf16[1024,256]{1,0:T(8,128)(2,1)S(1)} %fusion.30.v_ref), custom_call_target="tpu_custom_call" | custom-call | flops 4294967296 | bytes 2097152 | tf_op jit(solution)/shard_map/attend_forward/pallas_call | solution.py:82
  132.1 9.3 %attend_forward.7 = (bf16[1024,256]{1,0:T(8,128)(2,1)S(1)}, f32[1024,128]{1,0:T(8,128)S(1)}) custom-call(s32[1]{0:T(128)} %dynamic_slice.33.len_ref, bf16[1024,256]{1,0:T(8,128)(2,1)S(1)} %fusion.31.q_ref, bf16[1024,256]{1,0:T(8,128)(2,1)S(1)} %convolution_convert_fusion.12.k_ref, bf16[1024,256]{1,0:T(8,128)(2,1)S(1)} %fusion.32.v_ref), custom_call_target="tpu_custom_call" | custom-call | flops 4294967296 | bytes 2097152 | tf_op jit(solution)/shard_map/attend_forward/pallas_call | solution.py:82
  142.4 4.1 collective-permute-done.10
  151.6 12.4 %multiply_convert_fusion.1 = (bf16[1024,1024]{1,0:T(8,128)(2,1)S(1)}, f32[1024,1024]{1,0:T(8,128)}, f32[1024,1024]{1,0:T(8,128)}) fusion(f32[1024]{0:T(1024)S(1)} %convert_element_type.278, bf16[1024,1024]{0,1:T(8,128)(2,1)S(1)} %fusion.20, bf16[1024,1024]{1,0:T(8,128)(2,1)S(1)} %copy-done.79), kind=kOutput, calls=%fused_computation.50 | convolution fusion | flops 2216689664 | bytes 14684160 | tf_op jit(solution)/shard_map/dot_general | solution.py:17
  165.4 4.3 fusion.65
  169.7 6.4 %all-gather.2.cloned.1.call-done = bf16[2,1024,1024]{2,1,0:T(8,128)(2,1)} async-done(((bf16[2,128,1024]{2,1,0:T(8,128)(2,1)}), bf16[2,1024,1024]{2,1,0:T(8,128)(2,1)}) %all-gather.2.cloned.1.call-update) | async-done | bytes 4194320 | tf_op jit(solution)/shard_map/all_gather | solution.py:537
  176.0 14.5 %multiply_convert_fusion = (bf16[1024,1024]{1,0:T(8,128)(2,1)S(1)}, f32[1024,1024]{1,0:T(8,128)}, f32[1024,1024]{1,0:T(8,128)}) fusion(f32[1024]{0:T(1024)S(1)} %bitcast.195, bf16[1024,1024]{0,1:T(8,128)(2,1)S(1)} %fusion.20, bf16[2,1024,1024]{2,1,0:T(8,128)(2,1)} %all-gather.2.cloned.1.call-done), kind=kOutput, calls=%fused_computation.37 | convolution fusion | flops 2216689664 | bytes 14684160 | tf_op jit(solution)/shard_map/dot_general | solution.py:17
  198.9 4.4 fusion.54
  228.9 6.1 %convolution_convert_fusion = bf16[1024,1024]{1,0:T(8,128)(2,1)} fusion(bf16[1024,1024]{1,0:T(8,128)(2,1)} %copy-done.98, bf16[1024,1024]{0,1:T(8,128)(2,1)} %copy-done.47), kind=kOutput, calls=%fused_computation.91 | convolution fusion | flops 2148532224 | bytes 6291456 | tf_op jit(solution)/shard_map/dot_general | solution.py:438
  245.9 7.4 %multiply_reduce_fusion = (f32[1024]{0:T(1024)S(1)}, f32[1024]{0:T(1024)S(1)}, f32[1024]{0:T(1024)S(1)}, f32[1024]{0:T(1024)S(1)}, f32[1024,1024]{0,1:T(8,128)S(1)}) fusion(f32[1024,1024]{0,1:T(8,128)} %copy-done.28, f32[1024]{0:T(1024)S(1)} %add_rsqrt_fusion.1, f32[1024]{0:T(1024)S(1)} %broadcast_multiply_fusion.7, f32[1024]{0:T(1024)S(1)} %bitcast.163, ...), kind=kLoop, calls=%fused_computation.19 | loop fusion | flops 30404608 | bytes 18919424 | tf_op jit(solution)/shard_map/reduce_sum | solution.py:617
  257.6 12.7 %attend_backward.2 = (bf16[1024,256]{1,0:T(8,128)(2,1)S(1)}, bf16[1024,256]{1,0:T(8,128)(2,1)S(1)}, bf16[1024,256]{1,0:T(8,128)(2,1)S(1)}) custom-call(s32[1]{0:T(128)} %dynamic_slice.33.len_ref, bf16[1024,256]{1,0:T(8,128)(2,1)S(1)} %copy-done.17, bf16[1024,256]{1,0:T(8,128)(2,1)S(1)} %copy-done.23, bf16[1024,256]{1,0:T(8,128)(2,1)S(1)} %copy-done.25, ...), custom_call_target="tpu_custom_call" | custom-call | flops 10737418240 | bytes 4194304 | tf_op jit(solution)/shard_map/attend_backward/pallas_call | solution.py:175
  273.0 13.0 %attend_backward.3 = (bf16[1024,256]{1,0:T(8,128)(2,1)S(1)}, bf16[1024,256]{1,0:T(8,128)(2,1)S(1)}, bf16[1024,256]{1,0:T(8,128)(2,1)S(1)}) custom-call(s32[1]{0:T(128)} %dynamic_slice.33.len_ref, bf16[1024,256]{1,0:T(8,128)(2,1)S(1)} %copy-done.15, bf16[1024,256]{1,0:T(8,128)(2,1)S(1)} %copy-done.19, bf16[1024,256]{1,0:T(8,128)(2,1)S(1)} %copy-done.21, ...), custom_call_target="tpu_custom_call" | custom-call | flops 10737418240 | bytes 4194304 | tf_op jit(solution)/shard_map/attend_backward/pallas_call | solution.py:175
  297.4 5.4 add_convert_fusion
  302.8 25.4 %collective-permute-done.16 = bf16[1024,1024]{1,0:T(8,128)(2,1)} collective-permute-done((bf16[1024,1024]{1,0:T(8,128)(2,1)}, bf16[1024,1024]{1,0:T(8,128)(2,1)}, u32[]{:S(2)}, u32[]{:S(2)}) %collective-permute-start.16) | collective-permute-done | bytes 2097184 | tf_op jit(solution)/shard_map/ppermute | solution.py:506
  328.2 5.2 add_convert_fusion.1
  335.8 4.2 add_add_fusion
  358.3 6.0 %multiply_reduce_fusion.1 = (f32[1024]{0:T(1024)S(1)}, f32[1024]{0:T(1024)S(1)}, f32[1024]{0:T(1024)S(1)}, f32[1024]{0:T(1024)S(1)}, f32[1024,1024]{0,1:T(8,128)S(1)}) fusion(f32[1024,1024]{0,1:T(8,128)S(1)} %copy-done.32, f32[1024]{0:T(1024)S(1)} %copy-done.74, f32[1024]{0:T(1024)S(1)} %copy-done.72, f32[1024]{0:T(1024)S(1)} %bitcast.168, ...), kind=kLoop, calls=%fused_computation.20 | loop fusion | flops 22016000 | bytes 21020672 | tf_op jit(solution)/shard_map/reduce_sum | solution.py:617
  371.8 193.5 %self_backward.1 = (f32[512,1024]{1,0:T(8,128)}, bf16[256,1024]{1,0:T(8,128)(2,1)}, bf16[1024,256]{1,0:T(8,128)(2,1)}, bf16[1024,256]{1,0:T(8,128)(2,1)}, bf16[1...) custom-call(s32[1]{0:T(128)} %dynamic_slice.30.len_ref, ...), custom_call_target="tpu_custom_call" | custom-call | flops 5368709120 | bytes 209715200 | tf_op jit(solution)/shard_map/self_backward/pallas_call | solution.py:413
  583.0 4.2 convert_element_type.328
  (356 shorter events, 170.4 us)
Async XLA Ops:
  7.2 168.8 %all-gather.2.cloned.1.call-start = ((), (), s32[]{:S(2)}) async-start(), calls=%async_computation | async-start | bytes 4718592 | tf_op jit(solution)/shard_map/all_gather | solution.py:537
  8.8 17.8 %collective-permute-start = (bf16[512,1024]{0,1:T(8,128)(2,1)S(1)}, bf16[512,1024]{0,1:T(8,128)(2,1)}, u32[]{:S(2)}, u32[]{:S(2)}) collective-permute-start(bf16[512,1024]{0,1:T(8,128)(2,1)S(1)} %copy.33), channel_id=1, source_target_pairs={{0,1},{1,0},{2,3},{3,2},{4,5},{5,4},{6,7},{7,6},{8,9},{9,8},{10,11... | collective-permute-start | bytes 3145736 | tf_op jit(solution)/shard_map/ppermute | solution.py:474
  11.2 18.4 %collective-permute-start.2 = (bf16[2,128,1024]{2,1,0:T(8,128)(2,1)}, bf16[2,128,1024]{2,1,0:T(8,128)(2,1)S(1)}, u32[]{:S(2)}, u32[]{:S(2)}) collective-permute-start(bf16[2,128,1024]{2,1,0:T(8,128)(2,1)} %pad_maximum_fusion), channel_id=1, source_target_pairs={{2,0},{0,2},{3,1},{1,3},{6,4},{4,6},{7,5},{5,7},{10,8},{8,10},{11,... | collective-permute-start | bytes 1572872 | tf_op jit(solution)/shard_map/ppermute | solution.py:532
  14.1 12.5 %collective-permute-start.1 = (bf16[8,256]{1,0:T(8,128)(2,1)S(1)}, bf16[8,256]{1,0:T(8,128)(2,1)S(1)}, u32[]{:S(2)}, u32[]{:S(2)}) collective-permute-start(bf16[8,256]{1,0:T(8,128)(2,1)S(1)} %pad_maximum_fusion.1), channel_id=1, source_target_pairs={{2,0},{0,2},{3,1},{1,3},{6,4},{4,6},{7,5},{5,7},{10,8},{8,10},{11,... | collective-permute-start | bytes 12296 | tf_op jit(solution)/shard_map/ppermute | solution.py:500
  29.6 41.5 %copy-start.37 = (bf16[1024,1024]{0,1:T(8,128)(2,1)}, bf16[1024,1024]{0,1:T(8,128)(2,1)S(1)}, u32[]{:S(2)}) copy-start(bf16[1024,1024]{0,1:T(8,128)(2,1)S(1)} %maximum_select_fusion) | copy-start | bytes 6291460
  29.7 37.7 %collective-permute-start.3 = (bf16[3,1024,256]{2,1,0:T(8,128)(2,1)}, bf16[3,1024,256]{2,1,0:T(8,128)(2,1)}, u32[]{:S(2)}, u32[]{:S(2)}) collective-permute-start(bf16[3,1024,256]{2,1,0:T(8,128)(2,1)} %w0), channel_id=1, source_target_pairs={{2,0},{0,2},{3,1},{1,3},{6,4},{4,6},{7,5},{5,7},{10,8},{8,10},{11,... | collective-permute-start | bytes 4718600 | tf_op jit(solution)/shard_map/ppermute | solution.py:500
  45.8 57.6 %collective-permute-start.6 = (bf16[512,1024]{0,1:T(8,128)(2,1)}, bf16[512,1024]{0,1:T(8,128)(2,1)}, u32[]{:S(2)}, u32[]{:S(2)}) collective-permute-start(bf16[512,1024]{0,1:T(8,128)(2,1)} %copy.36), channel_id=1, source_target_pairs={{0,1},{1,0},{2,3},{3,2},{4,5},{5,4},{6,7},{7,6},{8,9},{9,8},{10,11... | collective-permute-start | bytes 3145736 | tf_op jit(solution)/shard_map/ppermute | solution.py:474
  45.8 60.8 %collective-permute-start.8 = (bf16[2,1024,256]{2,1,0:T(8,128)(2,1)}, bf16[2,1024,256]{2,1,0:T(8,128)(2,1)}, u32[]{:S(2)}, u32[]{:S(2)}) collective-permute-start(bf16[2,1024,256]{2,1,0:T(8,128)(2,1)} %param.25), channel_id=1, source_target_pairs={{2,0},{0,2},{3,1},{1,3},{6,4},{4,6},{7,5},{5,7},{10,8},{8,10},{11,... | collective-permute-start | bytes 3145736 | tf_op jit(solution)/shard_map/ppermute | solution.py:500
  47.1 52.5 %collective-permute-start.4 = (bf16[256,1024]{1,0:T(8,128)(2,1)}, bf16[256,1024]{1,0:T(8,128)(2,1)S(1)}, u32[]{:S(2)}, u32[]{:S(2)}) collective-permute-start(bf16[256,1024]{1,0:T(8,128)(2,1)} %wo0), channel_id=1, source_target_pairs={{2,0},{0,2},{3,1},{1,3},{6,4},{4,6},{7,5},{5,7},{10,8},{8,10},{11,... | collective-permute-start | bytes 1572872 | tf_op jit(solution)/shard_map/ppermute | solution.py:500
  100.4 14.5 %collective-permute-start.5 = (bf16[1024,1024]{0,1:T(8,128)(2,1)S(1)}, bf16[1024,1024]{0,1:T(8,128)(2,1)}, u32[]{:S(2)}, u32[]{:S(2)}) collective-permute-start(bf16[1024,1024]{0,1:T(8,128)(2,1)S(1)} %add_convert_fusion.8), channel_id=1, source_target_pairs={{0,1},{1,0},{2,3},{3,2},{4,5},{5,4},{6,7},{7,6},{8,9},{9,8},{10,11... | collective-permute-start | bytes 6291464 | tf_op jit(solution)/shard_map/ppermute | solution.py:474
  100.6 45.9 %copy-start.75 = (f32[1,1024]{1,0:T(1,128)}, f32[1,1024]{1,0:T(1,128)S(1)}, u32[]{:S(2)}) copy-start(f32[1,1024]{1,0:T(1,128)S(1)} %get-tuple-element.133) | copy-start | bytes 12292
  101.2 481.8 %all-reduce.5.cloned.1.call-start = ((), (), s32[]{:S(2)}) async-start(), calls=%async_computation.1 | async-start | bytes 8388608 | tf_op jit(solution)/shard_map/psum | solution.py:603
  101.3 30.0 %collective-permute-start.7 = (bf16[1024,256]{1,0:T(8,128)(2,1)}, bf16[1024,256]{1,0:T(8,128)(2,1)S(1)}, u32[]{:S(2)}, u32[]{:S(2)}) collective-permute-start(bf16[1024,256]{1,0:T(8,128)(2,1)} %param.24), channel_id=1, source_target_pairs={{2,0},{0,2},{3,1},{1,3},{6,4},{4,6},{7,5},{5,7},{10,8},{8,10},{11,... | collective-permute-start | bytes 1572872 | tf_op jit(solution)/shard_map/ppermute | solution.py:500
  102.8 38.7 %collective-permute-start.9 = (bf16[256,1024]{1,0:T(8,128)(2,1)}, bf16[256,1024]{1,0:T(8,128)(2,1)S(1)}, u32[]{:S(2)}, u32[]{:S(2)}) collective-permute-start(bf16[256,1024]{1,0:T(8,128)(2,1)} %param.26), channel_id=1, source_target_pairs={{2,0},{0,2},{3,1},{1,3},{6,4},{4,6},{7,5},{5,7},{10,8},{8,10},{11,... | collective-permute-start | bytes 1572872 | tf_op jit(solution)/shard_map/ppermute | solution.py:500
  142.3 4.2 collective-permute-start.10
  194.4 4.5 collective-permute-start.11
  195.0 8.8 %collective-permute-start.12 = (bf16[512,1024]{0,1:T(8,128)(2,1)S(1)}, bf16[512,1024]{0,1:T(8,128)(2,1)S(1)}, u32[]{:S(2)}, u32[]{:S(2)}) collective-permute-start(bf16[512,1024]{0,1:T(8,128)(2,1)S(1)} %copy.41), channel_id=1, source_target_pairs={{0,1},{1,0},{2,3},{3,2},{4,5},{5,4},{6,7},{7,6},{8,9},{9,8},{10,11... | collective-permute-start | bytes 3145736 | tf_op jit(solution)/shard_map/ppermute | solution.py:474
  228.8 17.1 %collective-permute-start.13 = (bf16[1024,1024]{0,1:T(8,128)(2,1)}, bf16[1024,1024]{0,1:T(8,128)(2,1)}, u32[]{:S(2)}, u32[]{:S(2)}) collective-permute-start(bf16[1024,1024]{0,1:T(8,128)(2,1)} %add_convert_fusion.3), channel_id=1, source_target_pairs={{0,1},{1,0},{2,3},{3,2},{4,5},{5,4},{6,7},{7,6},{8,9},{9,8},{10,11... | collective-permute-start | bytes 6291464 | tf_op jit(solution)/shard_map/ppermute | solution.py:474
  235.0 62.3 %collective-permute-start.17 = (bf16[1024,1024]{1,0:T(8,128)(2,1)}, bf16[1024,1024]{1,0:T(8,128)(2,1)}, u32[]{:S(2)}, u32[]{:S(2)}) collective-permute-start(bf16[1024,1024]{1,0:T(8,128)(2,1)} %convolution_convert_fusion), channel_id=1, source_target_pairs={{0,2},{2,0},{1,3},{3,1},{4,6},{6,4},{5,7},{7,5},{8,10},{10,8},{9,1... | collective-permute-start | bytes 6291464 | tf_op jit(solution)/shard_map/ppermute | solution.py:506
  240.2 88.0 %collective-permute-start.16 = (bf16[1024,1024]{1,0:T(8,128)(2,1)}, bf16[1024,1024]{1,0:T(8,128)(2,1)}, u32[]{:S(2)}, u32[]{:S(2)}) collective-permute-start(bf16[1024,1024]{1,0:T(8,128)(2,1)} %convolution_convert_fusion.1), channel_id=1, source_target_pairs={{0,2},{2,0},{1,3},{3,1},{4,6},{6,4},{5,7},{7,5},{8,10},{10,8},{9,1... | collective-permute-start | bytes 6291464 | tf_op jit(solution)/shard_map/ppermute | solution.py:506
  255.3 34.9 %copy-start.49 = (bf16[1024,1024]{0,1:T(8,128)(2,1)}, bf16[1024,1024]{0,1:T(8,128)(2,1)S(1)}, u32[]{:S(2)}) copy-start(bf16[1024,1024]{0,1:T(8,128)(2,1)S(1)} %get-tuple-element.107) | copy-start | bytes 6291460
  288.1 69.7 %collective-permute-start.14 = (bf16[1024,1024]{0,1:T(8,128)(2,1)}, bf16[1024,1024]{0,1:T(8,128)(2,1)}, u32[]{:S(2)}, u32[]{:S(2)}) collective-permute-start(bf16[1024,1024]{0,1:T(8,128)(2,1)} %add_convert_fusion.2), channel_id=1, source_target_pairs={{0,1},{1,0},{2,3},{3,2},{4,5},{5,4},{6,7},{7,6},{8,9},{9,8},{10,11... | collective-permute-start | bytes 6291464 | tf_op jit(solution)/shard_map/ppermute | solution.py:474
  297.4 30.8 %copy-start.95 = (bf16[1024,1024]{1,0:T(8,128)(2,1)S(1)}, bf16[1024,1024]{1,0:T(8,128)(2,1)}, u32[]{:S(2)}) copy-start(bf16[1024,1024]{1,0:T(8,128)(2,1)} %copy-done.94) | copy-start | bytes 6291460
  343.6 12.9 %collective-permute-start.15 = (bf16[512,1024]{1,0:T(8,128)(2,1)S(1)}, bf16[512,1024]{1,0:T(8,128)(2,1)S(1)}, u32[]{:S(2)}, u32[]{:S(2)}) collective-permute-start(bf16[512,1024]{1,0:T(8,128)(2,1)S(1)} %dynamic-slice_convert_fusion), channel_id=1, source_target_pairs={{0,1},{1,0},{2,3},{3,2},{4,5},{5,4},{6,7},{7,6},{8,9},{9,8},{10,11... | collective-permute-start | bytes 3145736 | tf_op jit(solution)/shard_map/ppermute | solution.py:474
  (101 other events, 772.3 us)
Sparse Core Ops, SparseCore 0:
  101.3 74.6 all-gather.1
  333.6 220.0 all-reduce.4

commit v6 on v5

--- a/solution.py
+++ b/solution.py
@@ -187,6 +187,7 @@
     )(length, q, k, v, o, g, lse)
 
 CHUNK = 512
+LAG = 1
 SPAN = 256
 
 
@@ -195,7 +196,8 @@
 
     def __init__(self, total, scratch):
         self.spots, self.total, self.step, self.sent, self.loaded = [], total, 0, 0, 0
-        (self.held, self.ysum, self.zgot, self.full, self.mine, self.load, self.store, self.xs, self.xr, self.ys, self.yr, self.zs, self.zr, self.bs, self.br, self.es, self.er) = scratch
+        (self.held, self.ysum, self.zgot, self.mine, self.load, self.store, self.xs, self.xr, self.ys, self.yr, self.zs, self.zr, self.bs, self.br, self.es, self.er) = scratch
+        self.full = self.held
         self.seq, self.ya, za = lax.axis_index("g"), lax.axis_index("y"), lax.axis_index("z")
         self.za = za
         self.peers = {1: za + 1 - 2 * (za % 2), 2: (za + 2) % 4, 3: 3 - za}
@@ -208,7 +210,6 @@
             pltpu.VMEM((total, most, SPAN), LOW),
             pltpu.VMEM((total, most // 2, SPAN), LOW),
             pltpu.VMEM((total, 3, most // 8, SPAN), LOW),
-            pltpu.VMEM((total, most, SPAN), LOW),
             pltpu.VMEM((4, most, SPAN), LOW),
             dma((4,)), dma((total,)),
             dma((total,)), dma((total,)), dma((total,)), dma((total,)),
@@ -239,20 +240,19 @@
 
     def tick(self, times=1):
         for unused in range(times):
-            if self.step >= self.total + len(self.stages) - 1:
+            if self.step >= self.total + LAG * (len(self.stages) - 1):
                 return
             for at, stage in enumerate(self.stages):
-                if 0 <= self.step - at < self.total:
-                    stage(self.step - at)
+                if 0 <= self.step - LAG * at < self.total:
+                    stage(self.step - LAG * at)
             self.step += 1
             self.feed()
 
     def drain(self):
         assert len(self.spots) == self.total
-        self.tick(self.total + len(self.stages))
+        self.tick(self.total + LAG * len(self.stages))
         for k in range(self.total):
             self.x_copy(k).wait_send()
-            self.y_copy(k).wait_send()
             self.yb_copy(k).wait_send()
             self.out_copy(k).wait()
             for d in (1, 2, 3):
@@ -304,7 +304,7 @@
 
     def to_z(self, k):
         h = self.spots[k][4] // 2
-        self.y_copy(k).wait_recv()
+        self.y_copy(k).wait()
         self.ysum[k, :h] = self.ysum[k, :h] + self.held[k, self.block(self.ya, h)]
         for d in (1, 2, 3):
             self.z_copy(k, d).start()
@@ -332,6 +332,61 @@
 
 def spot_count(shapes):
     return sum((rows // min(CHUNK, rows)) * (cols // SPAN) for rows, cols in shapes)
+
+
+def attend_back(pipe, shards, length, low, gm, dq, dk, dv, dka, dva, causal, bq):
+    rows = low.shape[0]
+    blocks = rows // bq
+    for s, (q, k, v, o, l, wo) in enumerate(shards):
+        for i in range(blocks):
+            at = pl.ds(i * bq, bq)
+            gm[s, at, :] = _nt(low[at, :], wo[...]).astype(LOW)
+    for s, (q, k, v, o, l, wo) in enumerate(shards):
+        for p in range(q.shape[1] // 128):
+            cols = pl.ds(p * 128, 128)
+            heads = key_side(k[:, cols], v[:, cols], length)
+            for i in reversed(range(blocks)):
+                at = pl.ds(i * bq, bq)
+                dq[s, at, cols] = query_block(heads, q[at, cols], o[at, cols], gm[s, at, cols], l[at, :], p, i, i == blocks - 1, causal, dka, dva)
+            first = _lanes(k.shape[0]) < HEAD
+            dk[s, :, cols] = jnp.where(first, dka[0], dka[1]).astype(LOW)
+            dv[s, :, cols] = jnp.where(first, dva[0], dva[1]).astype(LOW)
+            pipe.tick()
+
+
+def back_rows(terms, start, size):
+    at = pl.ds(pl.multiple_of(start, size), size)
+    both = None
+    for grads, s, weight in terms:
+        term = _nt(grads[s, at, :], weight)
+        both = term if both is None else both + term
+    return both
+
+
+def output_grads(shards, low, outs):
+    for (q, k, v, o, l, wo), out in zip(shards, outs):
+        for c in range(0, low.shape[1], SPAN):
+            out[:, c : c + SPAN] = tn(o[...], low[:, c : c + SPAN]).astype(LOW)
+
+
+def input_grads(rows_t, grads, out, first, bq):
+    for i in range(0, rows_t.shape[0], bq):
+        out[pl.ds(first + i, bq), :] = _nn(rows_t[pl.ds(i, bq), :], grads).astype(LOW)
+
+
+def share_rows(terms, core, part, got, sems, out, bq, pipe):
+    half = out.shape[0]
+    copy = Pipeline.remote(part, got, sems[0], sems[1], {"c": 1 - core})
+    for i in range(0, half, bq):
+        part[pl.ds(i, bq), :] = back_rows(terms, (1 - core) * half + i, bq).astype(LOW)
+    copy.start()
+    pipe.tick()
+    for i in range(0, half, bq):
+        out[pl.ds(i, bq), :] = back_rows(terms, core * half + i, bq)
+    pipe.tick()
+    copy.wait()
+    for i in range(0, half, bq):
+        out[pl.ds(i, bq), :] += got[pl.ds(i, bq), :].astype(F32)
 
 
 def self_back_kernel(carried, bq, len_ref, low, q0, k0, v0, o0, l0, q1, k1, v1, o1, l1, wo0, wo1, xt, w0, w1, small0, small1, *rest):
@@ -345,87 +400,116 @@
     pipe.greet([{"c": 1 - core}])
     for a, b, out in zip(own, other, outs):
         pipe.add(a, b, out, 0)
-    shards = ((q0, k0, v0, o0, l0, wo0, w0, go_own, gi_own, sm_own, small0), (q1, k1, v1, o1, l1, wo1, w1, go_other, gi_other, sm_other, small1))
-    rows = low.shape[0]
-    blocks = rows // bq
-    for s, (q, k, v, o, l, wo, w, go, gi, sm, small) in enumerate(shards):
-        for c in range(0, low.shape[1], SPAN):
-            go[:, c : c + SPAN] = tn(o[...], low[:, c : c + SPAN]).astype(LOW)
-        for i in range(blocks):
-            at = pl.ds(i * bq, bq)
-            gm[s, at, :] = _nt(low[at, :], wo[...]).astype(LOW)
+    shards = ((q0, k0, v0, o0, l0, wo0), (q1, k1, v1, o1, l1, wo1))
+    output_grads(shards, low, (go_own, go_other))
     pipe.add(go_own, go_other, outs[carried], 0)
-    for s, (q, k, v, o, l, wo, w, go, gi, sm, small) in enumerate(shards):
-        width = q.shape[1]
-        for p in range(width // 128):
-            cols = pl.ds(p * 128, 128)
-            heads = key_side(k[:, cols], v[:, cols], len_ref[0])
-            for i in reversed(range(blocks)):
-                at = pl.ds(i * bq, bq)
-                dq[s, at, cols] = query_block(heads, q[at, cols], o[at, cols], gm[s, at, cols], l[at, :], p, i, i == blocks - 1, True, dka, dva)
-            first = _lanes(rows) < HEAD
-            dk[s, :, cols] = jnp.where(first, dka[0], dka[1]).astype(LOW)
-            dv[s, :, cols] = jnp.where(first, dva[0], dva[1]).astype(LOW)
-            pipe.tick()
-    for s, (q, k, v, o, l, wo, w, go, gi, sm, small) in enumerate(shards):
+    attend_back(pipe, shards, len_ref[0], low, gm, dq, dk, dv, dka, dva, True, bq)
+    for s, (gi, sm, small) in enumerate(((gi_own, sm_own, small0), (gi_other, sm_other, small1))):
         for m, grads in enumerate((dq, dk, dv)):
-            for i in range(blocks):
-                at = pl.ds(i * bq, bq)
-                gi[pl.ds(m * rows + i * bq, bq), :] = _nn(xt[at, :], grads[s]).astype(LOW)
+            input_grads(xt, grads[s], gi, m * xt.shape[0], bq)
         row = lax.broadcasted_iota(jnp.int32, sm.shape, 0)
         sums = [jnp.sum(grads[s].astype(F32), axis=0, keepdims=True) for grads in (dq, dv)]
         sm[...] = jnp.where(row == 9, sums[0], jnp.where(row == 10, sums[1], small[...])).astype(LOW)
     pipe.add(gi_own, gi_other, outs[carried + 1], 0)
     pipe.add(sm_own, sm_other, outs[carried + 2], 0)
-    half = rows // 2
-    exchange = Pipeline.remote(part, got, part_send, part_recv, {"c": 1 - core})
-
-    def token_rows(start, size):
-        at = pl.ds(pl.multiple_of(start, size), size)
-        both = jnp.zeros((size, low.shape[1]), F32)
-        for s, w in ((0, w0), (1, w1)):
-            for m, grads in enumerate((dq, dk, dv)):
-                both = both + _nt(grads[s, at, :], w[m])
-        return both
-
-    for i in range(0, half, bq):
-        part[pl.ds(i, bq), :] = token_rows((1 - core) * half + i, bq).astype(LOW)
+    terms = [(grads, s, w[m]) for s, w in ((0, w0), (1, w1)) for m, grads in enumerate((dq, dk, dv))]
+    share_rows(terms, core, part, got, (part_send, part_recv), token_out, bq, pipe)
+    pipe.drain()
+
+
+def cross_back_kernel(carried, bq, len_ref, low, q0, k0, v0, o0, l0, q1, k1, v1, o1, l1, wo0, wo1, xt, mt, wq0, wq1, wm0, wm1, *rest):
+    own, other, rest = rest[:carried], rest[carried : 2 * carried], rest[2 * carried :]
+    row_out, memory_out, sums_out, go_own, go_other, gq_own, gq_other, gm_own, gm_other = rest[:9]
+    outs, rest = rest[9 : 9 + carried], rest[9 + carried :]
+    gm, dq, dk, dv, dka, dva, part, got, part_send, part_recv, full_part, full_got, full_send, full_recv = rest[:14]
+    core = lax.axis_index("c")
+    pipe = Pipeline(spot_count([ref.shape for ref in own]), rest[14:])
+    pipe.greet([{"c": 1 - core}])
+    for a, b, out in zip(own, other, outs):
+        pipe.add(a, b, out, 0)
+    shards = ((q0, k0, v0, o0, l0, wo0), (q1, k1, v1, o1, l1, wo1))
+    attend_back(pipe, shards, len_ref[0], low, gm, dq, dk, dv, dka, dva, False, bq)
+    rows = low.shape[0]
+    terms = [(dq, 0, wq0[...]), (dq, 1, wq1[...])]
+    for i in range(0, rows, bq):
+        full_part[pl.ds(i, bq), :] = back_rows(terms, i, bq).astype(LOW)
+    exchange = Pipeline.remote(full_part, full_got, full_send, full_recv, {"c": 1 - core})
     exchange.start()
     pipe.tick()
-    for i in range(0, half, bq):
-        token_out[pl.ds(i, bq), :] = token_rows(core * half + i, bq)
+    terms = [(grads, s, w[m]) for s, w in ((0, wm0), (1, wm1)) for m, grads in enumerate((dk, dv))]
+    share_rows(terms, core, part, got, (part_send, part_recv), memory_out, bq, pipe)
+    output_grads(shards, low, (go_own, go_other))
     pipe.tick()
+    for s, (gq, gkv) in enumerate(((gq_own, gm_own), (gq_other, gm_other))):
+        input_grads(xt, dq[s], gq, 0, bq)
+        input_grads(mt, dk[s], gkv, 0, bq)
+        input_grads(mt, dv[s], gkv, mt.shape[0], bq)
+        sums_out[s, 0:1] = jnp.sum(dq[s].astype(F32), axis=0, keepdims=True)
+        sums_out[s, 1:2] = jnp.sum(dv[s].astype(F32), axis=0, keepdims=True)
+        pipe.tick()
     exchange.wait()
-    for i in range(0, half, bq):
-        token_out[pl.ds(i, bq), :] += got[pl.ds(i, bq), :].astype(F32)
+    for i in range(0, rows, bq):
+        at = pl.ds(i, bq)
+        row_out[at, :] = full_part[at, :].astype(F32) + full_got[at, :].astype(F32)
     pipe.drain()
 
 
-def self_back(length, low, first, second, wo, xt, w, smalls, pairs, places, results, bq=256):
+def low_ram(*shape):
+    return pltpu.VMEM(shape, LOW)
+
+
+def back_scratch(rows, width):
+    return [low_ram(2, rows, width) for unused in range(4)] + [pltpu.VMEM((2, rows, 128), F32), pltpu.VMEM((2, rows, 128), F32)]
+
+
+def self_back(length, low, first, second, wo, xt, w, smalls, pairs, bq=256):
     rows, model = low.shape
     width = wo[0].shape[0]
     carried = len(pairs)
     any_space = pl.BlockSpec(memory_space=pl.ANY)
     vmem = pl.BlockSpec(memory_space=pltpu.VMEM)
+    dma = pltpu.SemaphoreType.DMA
     ends = [(width, model), (3 * rows, width), smalls[0].shape]
     total = spot_count([own.shape for own, unused in pairs] + ends)
-    low_ram = lambda *shape: pltpu.VMEM(shape, LOW)
     return pl.pallas_call(
         functools.partial(self_back_kernel, carried, bq),
         out_shape=[jax.ShapeDtypeStruct((rows // 2, model), F32)] + [jax.ShapeDtypeStruct(own.shape, LOW) for own, unused in pairs] + [jax.ShapeDtypeStruct(shape, LOW) for shape in ends],
         in_specs=[pl.BlockSpec(memory_space=pltpu.SMEM)] + [vmem] * 18 + [any_space] * (2 * carried),
         out_specs=[vmem] + [any_space] * (carried + 3),
-        scratch_shapes=[
-            low_ram(2, rows, width), low_ram(2, rows, width), low_ram(2, rows, width), low_ram(2, rows, width),
-            pltpu.VMEM((2, rows, 128), F32), pltpu.VMEM((2, rows, 128), F32),
-            low_ram(width, model), low_ram(width, model), low_ram(3 * rows, width), low_ram(3 * rows, width),
-            low_ram(*smalls[0].shape), low_ram(*smalls[0].shape),
-            low_ram(rows // 2, model), low_ram(rows // 2, model), pltpu.SemaphoreType.DMA, pltpu.SemaphoreType.DMA,
-        ] + Pipeline.scratch(total, CHUNK),
+        scratch_shapes=back_scratch(rows, width)
+        + [low_ram(width, model), low_ram(width, model), low_ram(3 * rows, width), low_ram(3 * rows, width), low_ram(*smalls[0].shape), low_ram(*smalls[0].shape)]
+        + [low_ram(rows // 2, model), low_ram(rows // 2, model), dma, dma]
+        + Pipeline.scratch(total, CHUNK),
         compiler_params=pltpu.CompilerParams(collective_id=0, has_side_effects=True, vmem_limit_bytes=58 << 20),
-        cost_estimate=pl.CostEstimate(flops=20 * rows * model * width, bytes_accessed=200 << 20, transcendentals=8 * rows * rows),
+        cost_estimate=pl.CostEstimate(flops=20 * rows * model * width, bytes_accessed=300 << 20, transcendentals=8 * rows * rows),
         name="self_backward",
     )(length, low, *first, *second, *wo, xt, *w, *smalls, *[p[0] for p in pairs], *[p[1] for p in pairs])
+
+
+def cross_back(length, low, first, second, wo, xt, mt, wq, wm, pairs, bq=256):
+    rows, model = low.shape
+    width = wo[0].shape[0]
+    carried = len(pairs)
+    any_space = pl.BlockSpec(memory_space=pl.ANY)
+    vmem = pl.BlockSpec(memory_space=pltpu.VMEM)
+    dma = pltpu.SemaphoreType.DMA
+    total = spot_count([own.shape for own, unused in pairs])
+    shape = jax.ShapeDtypeStruct
+    return pl.pallas_call(
+        functools.partial(cross_back_kernel, carried, bq),
+        out_shape=[shape((rows, model), F32), shape((rows // 2, model), F32), shape((2, 8, width), F32)]
+        + [shape((width, model), LOW)] * 2 + [shape((rows, width), LOW)] * 2 + [shape((2 * rows, width), LOW)] * 2
+        + [shape(own.shape, LOW) for own, unused in pairs],
+        in_specs=[pl.BlockSpec(memory_space=pltpu.SMEM)] + [vmem] * 19 + [any_space] * (2 * carried),
+        out_specs=[vmem] * 9 + [any_space] * carried,
+        scratch_shapes=back_scratch(rows, width)
+        + [low_ram(rows // 2, model), low_ram(rows // 2, model), dma, dma]
+        + [low_ram(rows, model), low_ram(rows, model), dma, dma]
+        + Pipeline.scratch(total, CHUNK),
+        compiler_params=pltpu.CompilerParams(collective_id=1, has_side_effects=True, vmem_limit_bytes=58 << 20),
+        cost_estimate=pl.CostEstimate(flops=20 * rows * model * width, bytes_accessed=300 << 20, transcendentals=8 * rows * rows),
+        name="cross_backward",
+    )(length, low, *first, *second, *wo, xt, mt, *wq, *wm, *[p[0] for p in pairs], *[p[1] for p in pairs])
 
 
 residual_scale = 300.0**0.25
@@ -600,27 +684,39 @@
     feed_out_parts = parts_of([tn(hidden[s], low_three) for s in shards], 0)
     grad_pre = [gelu_backward(hidden_pre[s], grad_hidden[s]).astype(LOW) for s in shards]
     feed_in_parts = parts_of([tn(third, grad_pre[s]) for s in shards], 1)
-    feed_out_sum, feed_in_sum = [lax.psum(send_home(part).astype(LOW), ("z", "y")).astype(F32) for part in (feed_out_parts, feed_in_parts)]
     grad_normed_two = residual_scale * grad_three + sum_all(sum(_nt(grad_pre[s], w_in[s]) for s in shards))
     grad_two = norm_backward(grad_normed_two, unit_two, inverse_two, norm_gain[1])
     low_two = grad_two.astype(LOW)
-    grad_cross_mixed = [_nt(low_two, w_cross_out[s]).astype(LOW) for s in shards]
-    cross_out_parts = parts_of([tn(cross_mixed[s], low_two) for s in shards], 0)
-    cross_dq, cross_dk, cross_dv = zip(*[attn_bwd(memory_length, cross_q[s], cross_k[s], cross_v[s], cross_mixed[s], grad_cross_mixed[s], cross_lse[s], False) for s in shards])
-    grad_normed_one = residual_scale * grad_two + sum_all(sum(_nt(cross_dq[s], w_cross_q[s]) for s in shards))
-    cross_parts = [parts_of([tn(second, cross_dq[s]) for s in shards], 1), parts_of([tn(memory_all, cross_dk[s]) for s in shards], 1), parts_of([tn(memory_all, cross_dv[s]) for s in shards], 1)]
-    grad_memory = sum_own(sum(_nt(cross_dk[s], w_cross_mem[s][0]) + _nt(cross_dv[s], w_cross_mem[s][1]) for s in shards)).astype(LOW)
+
+    def sums(rows):
+        return jnp.sum(rows.astype(F32), axis=0)
+
+    def low_pairs(*parts):
+        return [(part[0].astype(LOW), part[1].astype(LOW)) for part in parts]
+
+    in_kernel = (zn, yn, gn, cn, width, joined) == (4, 2, 2, 2, SPAN, False)
+    if in_kernel:
+        per_shard = [(cross_q[s], cross_k[s], cross_v[s], cross_mixed[s], cross_lse[s]) for s in shards]
+        row_part, memory_part, cross_sums, go_own, go_other, gq_own, gq_other, gm_own, gm_other, feed_out_sum, feed_in_sum = cross_back(
+            memory_length, low_two, per_shard[0], per_shard[1], w_cross_out, second.T, memory_all.T, w_cross_q, w_cross_mem, low_pairs(feed_out_parts, feed_in_parts))
+        cross_sums = [cross_sums[0, :2], cross_sums[1, :2]]
+        grad_memory = memory_part.astype(LOW)
+        grad_normed_one = residual_scale * grad_two + row_part
+    else:
+        feed_out_sum, feed_in_sum = [sum_groups(send_home(part)) for part in (feed_out_parts, feed_in_parts)]
+        grad_cross_mixed = [_nt(low_two, w_cross_out[s]).astype(LOW) for s in shards]
+        cross_out_parts = parts_of([tn(cross_mixed[s], low_two) for s in shards], 0)
+        cross_dq, cross_dk, cross_dv = zip(*[attn_bwd(memory_length, cross_q[s], cross_k[s], cross_v[s], cross_mixed[s], grad_cross_mixed[s], cross_lse[s], False) for s in shards])
+        grad_normed_one = residual_scale * grad_two + sum_all(sum(_nt(cross_dq[s], w_cross_q[s]) for s in shards))
+        cross_parts = [parts_of([tn(rows, grads[s]) for s in shards], 1) for rows, grads in ((second, cross_dq), (memory_all, cross_dk), (memory_all, cross_dv))]
+        grad_memory = sum_own(sum(_nt(cross_dk[s], w_cross_mem[s][0]) + _nt(cross_dv[s], w_cross_mem[s][1]) for s in shards)).astype(LOW)
+        cross_sums = parts_of([jnp.stack([sums(cross_dq[s]), sums(cross_dv[s])]) for s in shards], 1)
     grad_one = norm_backward(grad_normed_one, unit_one, inverse_one, norm_gain[0])
     low_one = grad_one.astype(LOW)
-
-    def sums(rows):
-        return jnp.sum(rows.astype(F32), axis=0)
 
     model = tokens.shape[1]
     terms = jnp.stack([sums(low_one), sums(low_two), sums(low_three), sums(grad_normed_one * unit_one), sums(grad_normed_two * unit_two), sums(cot * unit_three), sums(grad_normed_one), sums(grad_normed_two), sums(cot)])
     feed_sums = parts_of([sums(grad_pre[s]) for s in shards], 0)
-    groups = [[cross_out_parts], cross_parts[:1], cross_parts[1:]]
-    in_kernel = (zn, yn, gn, cn, width, joined) == (4, 2, 2, 2, SPAN, False)
     if not in_kernel:
         grad_self_mixed = [_nt(low_one, w_self_out[s]).astype(LOW) for s in shards]
         self_out_parts = parts_of([tn(self_mixed[s], low_one) for s in shards], 0)
@@ -629,23 +725,20 @@
         self_sums = parts_of([jnp.stack([sums(self_dq[s]), sums(self_dv[s])]) for s in shards], 1)
     else:
         self_sums = [jnp.zeros((2, width), F32)] * gn
-    cross_sums = parts_of([jnp.stack([sums(cross_dq[s]), sums(cross_dv[s])]) for s in shards], 1)
     smalls = []
     for k in range(gn):
         small = lax.dynamic_slice_in_dim(terms, ((seq + k) % gn * cn + core) * width, width, 1)
         small = jnp.concatenate([small, self_sums[k], cross_sums[k], feed_sums[k].reshape(-1, width)])
         smalls.append(jnp.pad(small, ((0, 16 * zn * yn - small.shape[0]), (0, 0))))
     if in_kernel:
-        pairs = [(part[0].astype(LOW), part[1].astype(LOW)) for group in groups for part in group]
         per_shard = [(self_q[s], self_k[s], self_v[s], self_mixed[s], self_lse[s]) for s in shards]
-        token_part, *sums_low = self_back(target_length, low_one, per_shard[0], per_shard[1], w_self_out, token_all.T, w_self, smalls, pairs, None, None)
-        sums_low = [rows.astype(F32) for rows in sums_low]
-        cross_out_sum, cross_q_sum, cross_k_sum, cross_v_sum, self_out_sum, self_in_sum, small = sums_low
-        cross_mem_sum = jnp.stack([cross_k_sum, cross_v_sum])
+        pairs = [(go_own, go_other), (gq_own, gq_other), (gm_own, gm_other)]
+        token_part, *sums_low = self_back(target_length, low_one, per_shard[0], per_shard[1], w_self_out, token_all.T, w_self, smalls, pairs)
     else:
-        groups += [[self_out_parts], [parts_of([tn(token_all, grads[s]) for s in shards], 1) for grads in (self_dq, self_dk, self_dv)], [smalls]]
+        groups = [[cross_out_parts], cross_parts[:1], cross_parts[1:], [self_out_parts], [parts_of([tn(token_all, grads[s]) for s in shards], 1) for grads in (self_dq, self_dk, self_dv)], [smalls]]
         sums_low = [sum_groups(send_home([jnp.concatenate([part[k] for part in group]) for k in range(gn)])) for group in groups]
-        cross_out_sum, cross_q_sum, cross_mem_sum, self_out_sum, self_in_sum, small = [rows.astype(F32) for rows in sums_low]
+    cross_out_sum, cross_q_sum, cross_mem_sum, self_out_sum, self_in_sum, small = [rows.astype(F32) for rows in sums_low]
+    feed_out_sum, feed_in_sum = feed_out_sum.astype(F32), feed_in_sum.astype(F32)
     grad_tokens = (residual_scale * own_rows(grad_one) + token_part).astype(LOW)
     return (block_out, grad_tokens, grad_memory, self_in_sum.reshape(3, model, width), self_out_sum, cross_q_sum, cross_mem_sum.reshape(2, model, width), cross_out_sum, feed_in_sum, feed_out_sum, small[9:13], small[13:13 + feed_rows].reshape(-1), small[0:3], small[3:6], small[6:9])
 

time: 606 us -> 589 us (0.972)
  Pallas kernels: 254 us -> 298 us
  matrix products: 131 us -> 92.1 us
  waiting for transfers between devices: 86.1 us -> 58.2 us
    pallas_call x2 -> x1, Pallas kernels: 25.7 us -> 129 us  [cross_back(): pl.pallas_call(functools.partial(cross_back_kernel, carried, bq), out_sha...]
    pallas_call x1, Pallas kernels: 193 us -> 135 us  [self_back(): pl.pallas_call(functools.partial(self_back_kernel, carried, bq), out_shap...]
    ppermute x2 -> x0, waiting for transfers between devices: 25.4 us -> none  [send_home(): lax.ppermute(parts[k].astype(LOW), 'g', [(i, (i + k) % gn) for i in range...]
    dot_general x12 -> x4, matrix products: 39.5 us -> 17.2 us  [tn(): lax.dot_general(rows, grads, (((0,), (0,)), ((), ())), preferred_element_...]
    dot_general x12 -> x4, matrix products: 30.3 us -> 14.2 us  [_nt(): lax.dot_general(a, b, (((1,), (1,)), ((), ())), preferred_element_type=jn...]
    transpose x0 -> x2, other arithmetic: none -> 8.17 us  [layer(): row_part, memory_part, cross_sums, go_own, go_other, gq_own, gq_other, gm...]
    unnamed x216 -> x164, local copies, waits for them, and re-layouts: 20.3 us -> 16.8 us
    reduce_sum x10 -> x6, other arithmetic: 23.8 us -> 23.4 us  [sums(): return jnp.sum(rows.astype(F32), axis=0)]
  transfers between devices with their start and end apart: 20 -> 15, of which waited for: 7 -> 5; matrix products, arithmetic and copies ran while one was open for 28% -> 16% of each run, Pallas kernels for 43% -> 6%
where the time goes in v6:
time: 589 us; the launch traced here: 581 us
  Pallas kernels  298 us (51%)
  matrix products  92.1 us (16%)
  other arithmetic  65.8 us (11%)
  waiting for transfers between devices  58.2 us (10%)
  local copies, waits for them, and re-layouts  41 us (7%)
  between operations  15.5 us (3%)
  starting transfers between devices  10 us (2%)
    pallas_call x1, Pallas kernels, self_back(): pl.pallas_call(functools.partial(self_back_kernel, carried, bq), out_shap...  135 us
    pallas_call x1, Pallas kernels, cross_back(): pl.pallas_call(functools.partial(cross_back_kernel, carried, bq), out_sha...  129 us
    dot_general x20, matrix products, _nn(): lax.dot_general(a, b, (((1,), (0,)), ((), ())), preferred_element_type=jn...  60.7 us
    ppermute x6, waiting for transfers between devices, spread(): lax.ppermute(shard, 'g', [((i + k) % gn, i) for i in range(gn)])  47 us
    pallas_call x4, Pallas kernels, attn_fwd(): pl.pallas_call(functools.partial(fwd_kernel, causal=causal, bq=bq), out_s...  34.3 us
    reduce_sum x6, other arithmetic, sums(): return jnp.sum(rows.astype(F32), axis=0)  23.4 us
    dot_general x4, matrix products, tn(): lax.dot_general(rows, grads, (((0,), (0,)), ((), ())), preferred_element_...  17.2 us
    unnamed x164, local copies, waits for them, and re-layouts  16.8 us
  transfers between devices with their start and end apart: 15, of which 5 were waited for; matrix products, arithmetic and copies ran while one was open for 16% of the time, Pallas kernels for 6%

profile of v6, /device:TPU:0, one launch (start us, length us, event | category | flops | bytes accessed | tf_op | source)
XLA Modules:
  0.0 580.7 jit_solution(3700465060133176021)
XLA Ops:
  15.9 10.7 %collective-permute-done.1 = bf16[8,256]{1,0:T(8,128)(2,1)S(1)} collective-permute-done((bf16[8,256]{1,0:T(8,128)(2,1)S(1)}, bf16[8,256]{1,0:T(8,128)(2,1)S(1)}, u32[]{:S(2)}, u32[]{:S(2)}) %collective-permute-start.1) | collective-permute-done | bytes 4128 | tf_op jit(solution)/shard_map/ppermute | solution.py:584
  34.9 7.6 %attend_forward.4 = (bf16[1024,256]{1,0:T(8,128)(2,1)S(1)}, f32[1024,128]{1,0:T(8,128)S(1)}) custom-call(s32[1]{0:T(128)} %dynamic_slice.24.len_ref, bf16[1024,256]{1,0:T(8,128)(2,1)S(1)} %fusion.25.q_ref.q0, bf16[1024,256]{1,0:T(8,128)(2,1)S(1)} %convolution_convert_fusion.7.k_ref.k0, bf16[1024,256]{1,0:T(8,128)(2,1)S(1)} %fusion.26.v_ref.v0), custom_call_target="tpu_custom_call" | custom-call | flops 4294967296 | bytes 2097152 | tf_op jit(solution)/shard_map/attend_forward/pallas_call | solution.py:82
  49.6 17.7 %collective-permute-done.3.w1 = bf16[3,1024,256]{2,1,0:T(8,128)(2,1)} collective-permute-done((bf16[3,1024,256]{2,1,0:T(8,128)(2,1)}, bf16[3,1024,256]{2,1,0:T(8,128)(2,1)}, u32[]{:S(2)}, u32[]{:S(2)}) %collective-permute-start.3) | collective-permute-done | bytes 1572896 | tf_op jit(solution)/shard_map/ppermute | solution.py:584
  73.2 7.7 %attend_forward.5 = (bf16[1024,256]{1,0:T(8,128)(2,1)S(1)}, f32[1024,128]{1,0:T(8,128)S(1)}) custom-call(s32[1]{0:T(128)} %dynamic_slice.24.len_ref, bf16[1024,256]{1,0:T(8,128)(2,1)S(1)} %fusion.27.q_ref.q1, bf16[1024,256]{1,0:T(8,128)(2,1)S(1)} %convolution_convert_fusion.6.k_ref.k1, bf16[1024,256]{1,0:T(8,128)(2,1)S(1)} %fusion.28.v_ref.v1), custom_call_target="tpu_custom_call" | custom-call | flops 4294967296 | bytes 2097152 | tf_op jit(solution)/shard_map/attend_forward/pallas_call | solution.py:82
  81.0 18.6 %collective-permute-done.4.wo1 = bf16[256,1024]{1,0:T(8,128)(2,1)S(1)} collective-permute-done((bf16[256,1024]{1,0:T(8,128)(2,1)}, bf16[256,1024]{1,0:T(8,128)(2,1)S(1)}, u32[]{:S(2)}, u32[]{:S(2)}) %collective-permute-start.4) | collective-permute-done | bytes 524320 | tf_op jit(solution)/shard_map/ppermute | solution.py:584
  119.7 9.6 %attend_forward.6 = (bf16[1024,256]{1,0:T(8,128)(2,1)S(1)}, f32[1024,128]{1,0:T(8,128)S(1)}) custom-call(s32[1]{0:T(128)} %dynamic_slice.27.len_ref, bf16[1024,256]{1,0:T(8,128)(2,1)S(1)} %fusion.29.q_ref.q0, bf16[1024,256]{1,0:T(8,128)(2,1)S(1)} %convolution_convert_fusion.5.k_ref.k0, bf16[1024,256]{1,0:T(8,128)(2,1)S(1)} %fusion.30.v_ref.v0), custom_call_target="tpu_custom_call" | custom-call | flops 4294967296 | bytes 2097152 | tf_op jit(solution)/shard_map/attend_forward/pallas_call | solution.py:82
  131.2 9.4 %attend_forward.7 = (bf16[1024,256]{1,0:T(8,128)(2,1)S(1)}, f32[1024,128]{1,0:T(8,128)S(1)}) custom-call(s32[1]{0:T(128)} %dynamic_slice.27.len_ref, bf16[1024,256]{1,0:T(8,128)(2,1)S(1)} %fusion.31.q_ref.q1, bf16[1024,256]{1,0:T(8,128)(2,1)S(1)} %convolution_convert_fusion.4.k_ref.k1, bf16[1024,256]{1,0:T(8,128)(2,1)S(1)} %fusion.32.v_ref.v1), custom_call_target="tpu_custom_call" | custom-call | flops 4294967296 | bytes 2097152 | tf_op jit(solution)/shard_map/attend_forward/pallas_call | solution.py:82
  141.5 4.1 collective-permute-done.10
  150.9 12.4 %multiply_convert_fusion.1 = (bf16[1024,1024]{1,0:T(8,128)(2,1)S(1)}, f32[1024,1024]{1,0:T(8,128)}, f32[1024,1024]{1,0:T(8,128)}) fusion(f32[1024]{0:T(1024)S(1)} %convert_element_type.214, bf16[1024,1024]{0,1:T(8,128)(2,1)S(1)} %fusion.20, bf16[1024,1024]{1,0:T(8,128)(2,1)S(1)} %copy-done.53), kind=kOutput, calls=%fused_computation.46 | convolution fusion | flops 2216689664 | bytes 14684160 | tf_op jit(solution)/shard_map/dot_general | solution.py:17
  164.6 4.3 fusion.59
  168.9 7.1 %all-gather.2.cloned.1.call-done = bf16[2,1024,1024]{2,1,0:T(8,128)(2,1)} async-done(((bf16[2,128,1024]{2,1,0:T(8,128)(2,1)}), bf16[2,1024,1024]{2,1,0:T(8,128)(2,1)}) %all-gather.2.cloned.1.call-update) | async-done | bytes 4194320 | tf_op jit(solution)/shard_map/all_gather | solution.py:621
  176.0 14.6 %multiply_convert_fusion = (bf16[1024,1024]{1,0:T(8,128)(2,1)S(1)}, f32[1024,1024]{1,0:T(8,128)}, f32[1024,1024]{1,0:T(8,128)}) fusion(f32[1024]{0:T(1024)S(1)} %bitcast.166, bf16[1024,1024]{0,1:T(8,128)(2,1)S(1)} %fusion.20, bf16[2,1024,1024]{2,1,0:T(8,128)(2,1)} %all-gather.2.cloned.1.call-done), kind=kOutput, calls=%fused_computation.33 | convolution fusion | flops 2216689664 | bytes 14684160 | tf_op jit(solution)/shard_map/dot_general | solution.py:17
  190.7 3.9 add_convert_fusion.3
  199.3 4.5 fusion.99.xt
  215.6 4.0 convert_reduce_fusion.2
  225.1 4.1 convert_reduce_fusion.1
  236.6 6.1 %convolution_convert_fusion.rest_3_ = bf16[1024,1024]{1,0:T(8,128)(2,1)} fusion(bf16[1024,1024]{0,1:T(8,128)(2,1)} %copy-done.32, bf16[1024,1024]{1,0:T(8,128)(2,1)} %copy-done.74), kind=kOutput, calls=%fused_computation.85 | convolution fusion | flops 2148532224 | bytes 6291456 | tf_op jit(solution)/shard_map/dot_general | solution.py:522
  242.7 3.8 convolution_convert_fusion.1.rest_2_
  246.4 3.7 convolution_convert_fusion.2.rest_1_
  253.9 5.8 %multiply_reduce_fusion = (f32[1024]{0:T(1024)S(1)}, f32[1024]{0:T(1024)S(1)}, f32[1024]{0:T(1024)S(1)}, f32[1024]{0:T(1024)S(1)}, f32[1024,1024]{0,1:T(8,128)S(1)}) fusion(f32[1024,1024]{0,1:T(8,128)S(1)} %copy-done.24, f32[1024]{0:T(1024)S(1)} %add_rsqrt_fusion.1, f32[1024]{0:T(1024)S(1)} %broadcast_multiply_fusion.7, f32[1024]{0:T(1024)S(1)} %bitcast.141, ...), kind=kLoop, calls=%fused_computation.16 | loop fusion | flops 30404608 | bytes 18919424 | tf_op jit(solution)/shard_map/reduce_sum | solution.py:692
  264.4 128.9 %cross_backward.1 = (f32[1024,1024]{1,0:T(8,128)}, f32[512,1024]{1,0:T(8,128)}, f32[2,8,256]{2,1,0:T(8,128)}, bf16[256,1024]{1,0:T(8,128)(2,1)}, bf16[256,1024]{...) custom-call(s32[1]{0:T(128)} %dynamic_slice.27.len_ref, ...), custom_call_target="tpu_custom_call" | custom-call | flops 5368709120 | bytes 314572800 | tf_op jit(solution)/shard_map/cross_backward/pallas_call | solution.py:498
  393.3 5.3 copy.46
  398.7 7.9 %multiply_reduce_fusion.1 = (f32[1024]{0:T(1024)S(1)}, f32[1024]{0:T(1024)S(1)}, f32[1024]{0:T(1024)S(1)}, f32[1024]{0:T(1024)S(1)}, f32[1024,1024]{0,1:T(8,128)S(1)}) fusion(f32[1024,1024]{0,1:T(8,128)} %copy-done.20, f32[1024]{0:T(1024)S(1)} %add_rsqrt_fusion.2, f32[1024]{0:T(1024)S(1)} %broadcast_multiply_fusion.8, f32[1024]{0:T(1024)S(1)} %bitcast.137, ...), kind=kLoop, calls=%fused_computation.17 | loop fusion | flops 18870272 | bytes 21020672 | tf_op jit(solution)/shard_map/reduce_sum | solution.py:692
  415.0 134.9 %self_backward.1 = (f32[512,1024]{1,0:T(8,128)}, bf16[256,1024]{1,0:T(8,128)(2,1)}, bf16[1024,256]{1,0:T(8,128)(2,1)}, bf16[2048,256]{1,0:T(8,128)(2,1)}, bf16[2...) custom-call(s32[1]{0:T(128)} %dynamic_slice.24.len_ref, bf16[1024,1024]{1,0:T(8,128)(2,1)} %copy.47.low, ...), custom_call_target="tpu_custom_call" | custom-call | flops 5368709120 | bytes 314572800 | tf_op jit(solution)/shard_map/self_backward/pallas_call | solution.py:474
  (276 shorter events, 128.4 us)
Async XLA Ops:
  7.2 168.8 %all-gather.2.cloned.1.call-start = ((), (), s32[]{:S(2)}) async-start(), calls=%async_computation | async-start | bytes 4718592 | tf_op jit(solution)/shard_map/all_gather | solution.py:621
  8.8 17.8 %collective-permute-start = (bf16[512,1024]{0,1:T(8,128)(2,1)S(1)}, bf16[512,1024]{0,1:T(8,128)(2,1)}, u32[]{:S(2)}, u32[]{:S(2)}) collective-permute-start(bf16[512,1024]{0,1:T(8,128)(2,1)S(1)} %copy.33), channel_id=1, source_target_pairs={{0,1},{1,0},{2,3},{3,2},{4,5},{5,4},{6,7},{7,6},{8,9},{9,8},{10,11... | collective-permute-start | bytes 3145736 | tf_op jit(solution)/shard_map/ppermute | solution.py:558
  11.2 18.4 %collective-permute-start.2 = (bf16[2,128,1024]{2,1,0:T(8,128)(2,1)}, bf16[2,128,1024]{2,1,0:T(8,128)(2,1)S(1)}, u32[]{:S(2)}, u32[]{:S(2)}) collective-permute-start(bf16[2,128,1024]{2,1,0:T(8,128)(2,1)} %pad_maximum_fusion), channel_id=1, source_target_pairs={{2,0},{0,2},{3,1},{1,3},{6,4},{4,6},{7,5},{5,7},{10,8},{8,10},{11,... | collective-permute-start | bytes 1572872 | tf_op jit(solution)/shard_map/ppermute | solution.py:616
  14.1 12.5 %collective-permute-start.1 = (bf16[8,256]{1,0:T(8,128)(2,1)S(1)}, bf16[8,256]{1,0:T(8,128)(2,1)S(1)}, u32[]{:S(2)}, u32[]{:S(2)}) collective-permute-start(bf16[8,256]{1,0:T(8,128)(2,1)S(1)} %pad_maximum_fusion.3), channel_id=1, source_target_pairs={{2,0},{0,2},{3,1},{1,3},{6,4},{4,6},{7,5},{5,7},{10,8},{8,10},{11,... | collective-permute-start | bytes 12296 | tf_op jit(solution)/shard_map/ppermute | solution.py:584
  29.6 41.5 %copy-start.28 = (bf16[1024,1024]{0,1:T(8,128)(2,1)}, bf16[1024,1024]{0,1:T(8,128)(2,1)S(1)}, u32[]{:S(2)}) copy-start(bf16[1024,1024]{0,1:T(8,128)(2,1)S(1)} %maximum_select_fusion) | copy-start | bytes 6291460
  29.7 37.7 %collective-permute-start.3 = (bf16[3,1024,256]{2,1,0:T(8,128)(2,1)}, bf16[3,1024,256]{2,1,0:T(8,128)(2,1)}, u32[]{:S(2)}, u32[]{:S(2)}) collective-permute-start(bf16[3,1024,256]{2,1,0:T(8,128)(2,1)} %w0), channel_id=1, source_target_pairs={{2,0},{0,2},{3,1},{1,3},{6,4},{4,6},{7,5},{5,7},{10,8},{8,10},{11,... | collective-permute-start | bytes 4718600 | tf_op jit(solution)/shard_map/ppermute | solution.py:584
  45.8 57.5 %collective-permute-start.6 = (bf16[512,1024]{0,1:T(8,128)(2,1)}, bf16[512,1024]{0,1:T(8,128)(2,1)}, u32[]{:S(2)}, u32[]{:S(2)}) collective-permute-start(bf16[512,1024]{0,1:T(8,128)(2,1)} %copy.36), channel_id=1, source_target_pairs={{0,1},{1,0},{2,3},{3,2},{4,5},{5,4},{6,7},{7,6},{8,9},{9,8},{10,11... | collective-permute-start | bytes 3145736 | tf_op jit(solution)/shard_map/ppermute | solution.py:558
  45.8 60.0 %collective-permute-start.8 = (bf16[2,1024,256]{2,1,0:T(8,128)(2,1)}, bf16[2,1024,256]{2,1,0:T(8,128)(2,1)}, u32[]{:S(2)}, u32[]{:S(2)}) collective-permute-start(bf16[2,1024,256]{2,1,0:T(8,128)(2,1)} %wm0), channel_id=1, source_target_pairs={{2,0},{0,2},{3,1},{1,3},{6,4},{4,6},{7,5},{5,7},{10,8},{8,10},{11,... | collective-permute-start | bytes 3145736 | tf_op jit(solution)/shard_map/ppermute | solution.py:584
  47.1 52.6 %collective-permute-start.4 = (bf16[256,1024]{1,0:T(8,128)(2,1)}, bf16[256,1024]{1,0:T(8,128)(2,1)S(1)}, u32[]{:S(2)}, u32[]{:S(2)}) collective-permute-start(bf16[256,1024]{1,0:T(8,128)(2,1)} %wo0.1), channel_id=1, source_target_pairs={{2,0},{0,2},{3,1},{1,3},{6,4},{4,6},{7,5},{5,7},{10,8},{8,10},{11,... | collective-permute-start | bytes 1572872 | tf_op jit(solution)/shard_map/ppermute | solution.py:584
  81.0 19.4 %copy-start.19 = (f32[1024,128]{1,0:T(8,128)}, f32[1024,128]{1,0:T(8,128)S(1)}, u32[]{:S(2)}) copy-start(f32[1024,128]{1,0:T(8,128)S(1)} %get-tuple-element.63.l1) | copy-start | bytes 1572868
  81.0 19.5 %copy-start.59 = (f32[3,1024]{1,0:T(4,128)S(1)}, f32[3,1024]{1,0:T(4,128)}, u32[]{:S(2)}) copy-start(f32[3,1024]{1,0:T(4,128)} %param.32) | copy-start | bytes 36868
  81.0 19.5 %copy-start.60 = (f32[3,1024]{1,0:T(4,128)S(1)}, f32[3,1024]{1,0:T(4,128)}, u32[]{:S(2)}) copy-start(f32[3,1024]{1,0:T(4,128)} %param.33) | copy-start | bytes 36868
  81.0 22.3 %copy-start.30 = (bf16[512,1024]{0,1:T(8,128)(2,1)S(1)}, bf16[512,1024]{0,1:T(8,128)(2,1)}, u32[]{:S(2)}) copy-start(bf16[512,1024]{0,1:T(8,128)(2,1)} %copy.36) | copy-start | bytes 3145732
  100.4 13.6 %collective-permute-start.5 = (bf16[1024,1024]{0,1:T(8,128)(2,1)S(1)}, bf16[1024,1024]{0,1:T(8,128)(2,1)}, u32[]{:S(2)}, u32[]{:S(2)}) collective-permute-start(bf16[1024,1024]{0,1:T(8,128)(2,1)S(1)} %add_convert_fusion.5), channel_id=1, source_target_pairs={{0,1},{1,0},{2,3},{3,2},{4,5},{5,4},{6,7},{7,6},{8,9},{9,8},{10,11... | collective-permute-start | bytes 6291464 | tf_op jit(solution)/shard_map/ppermute | solution.py:558
  101.2 29.2 %collective-permute-start.7 = (bf16[1024,256]{1,0:T(8,128)(2,1)}, bf16[1024,256]{1,0:T(8,128)(2,1)S(1)}, u32[]{:S(2)}, u32[]{:S(2)}) collective-permute-start(bf16[1024,256]{1,0:T(8,128)(2,1)} %wq0), channel_id=1, source_target_pairs={{2,0},{0,2},{3,1},{1,3},{6,4},{4,6},{7,5},{5,7},{10,8},{8,10},{11,... | collective-permute-start | bytes 1572872 | tf_op jit(solution)/shard_map/ppermute | solution.py:584
  102.7 37.9 %collective-permute-start.9 = (bf16[256,1024]{1,0:T(8,128)(2,1)}, bf16[256,1024]{1,0:T(8,128)(2,1)S(1)}, u32[]{:S(2)}, u32[]{:S(2)}) collective-permute-start(bf16[256,1024]{1,0:T(8,128)(2,1)} %wo0), channel_id=1, source_target_pairs={{2,0},{0,2},{3,1},{1,3},{6,4},{4,6},{7,5},{5,7},{10,8},{8,10},{11,... | collective-permute-start | bytes 1572872 | tf_op jit(solution)/shard_map/ppermute | solution.py:584
  108.5 22.7 %copy-start.5 = (bf16[1024,256]{1,0:T(8,128)(2,1)}, bf16[1024,256]{1,0:T(8,128)(2,1)S(1)}, u32[]{:S(2)}) copy-start(bf16[1024,256]{1,0:T(8,128)(2,1)S(1)} %convolution_convert_fusion.4.k_ref.k1) | copy-start | bytes 1572868
  111.4 19.8 %copy-start.6 = (bf16[1024,256]{1,0:T(8,128)(2,1)}, bf16[1024,256]{1,0:T(8,128)(2,1)S(1)}, u32[]{:S(2)}) copy-start(bf16[1024,256]{1,0:T(8,128)(2,1)S(1)} %fusion.32.v_ref.v1) | copy-start | bytes 1572868
  117.0 28.6 %copy-start.20 = (f32[1024,1024]{0,1:T(8,128)}, f32[1024,1024]{0,1:T(8,128)S(1)}, u32[]{:S(2)}) copy-start(f32[1024,1024]{0,1:T(8,128)S(1)} %get-tuple-element.129) | copy-start | bytes 12582916
  141.4 4.2 collective-permute-start.10
  150.9 25.1 %copy-start.32 = (bf16[1024,1024]{0,1:T(8,128)(2,1)}, bf16[1024,1024]{0,1:T(8,128)(2,1)S(1)}, u32[]{:S(2)}) copy-start(bf16[1024,1024]{0,1:T(8,128)(2,1)S(1)} %fusion.20) | copy-start | bytes 6291460
  194.5 9.3 %collective-permute-start.11 = (bf16[1024,1024]{0,1:T(8,128)(2,1)}, bf16[1024,1024]{0,1:T(8,128)(2,1)}, u32[]{:S(2)}, u32[]{:S(2)}) collective-permute-start(bf16[1024,1024]{0,1:T(8,128)(2,1)} %add_convert_fusion.3), channel_id=1, source_target_pairs={{0,1},{1,0},{2,3},{3,2},{4,5},{5,4},{6,7},{7,6},{8,9},{9,8},{10,11... | collective-permute-start | bytes 6291464 | tf_op jit(solution)/shard_map/ppermute | solution.py:558
  198.8 8.8 %collective-permute-start.12 = (bf16[512,1024]{0,1:T(8,128)(2,1)S(1)}, bf16[512,1024]{0,1:T(8,128)(2,1)S(1)}, u32[]{:S(2)}, u32[]{:S(2)}) collective-permute-start(bf16[512,1024]{0,1:T(8,128)(2,1)S(1)} %copy.41), channel_id=1, source_target_pairs={{0,1},{1,0},{2,3},{3,2},{4,5},{5,4},{6,7},{7,6},{8,9},{9,8},{10,11... | collective-permute-start | bytes 3145736 | tf_op jit(solution)/shard_map/ppermute | solution.py:558
  232.9 21.0 %collective-permute-start.13 = (bf16[1024,1024]{0,1:T(8,128)(2,1)}, bf16[1024,1024]{0,1:T(8,128)(2,1)}, u32[]{:S(2)}, u32[]{:S(2)}) collective-permute-start(bf16[1024,1024]{0,1:T(8,128)(2,1)} %add_convert_fusion), channel_id=1, source_target_pairs={{0,1},{1,0},{2,3},{3,2},{4,5},{5,4},{6,7},{7,6},{8,9},{9,8},{10,11... | collective-permute-start | bytes 6291464 | tf_op jit(solution)/shard_map/ppermute | solution.py:558
  (70 other events, 408.2 us)
Sparse Core Ops, SparseCore 0:
  101.3 74.6 all-gather.1

commit v7 on v6

--- a/solution.py
+++ b/solution.py
@@ -1,4 +1,5 @@
 import functools
+import math
 
 import jax, jax.numpy as jnp
 from jax import lax
@@ -224,12 +225,10 @@
             pl.semaphore_signal(barrier, inc=1, device_id=where, device_id_type=pl.DeviceIdType.MESH)
         pl.semaphore_wait(barrier, len(everyone))
 
-    def add(self, own, other, out, out_row):
-        rows, cols = own.shape
-        size = min(CHUNK, rows)
-        for r in range(0, rows, size):
-            for c in range(0, cols, SPAN):
-                self.spots.append((own, other, r, c, size, out, out_row + r))
+    def add(self, own, other, out, taper=False):
+        for r, size in row_chunks(own.shape[0], taper):
+            for c in range(0, own.shape[1], SPAN):
+                self.spots.append((own, other, r, c, size, out, r))
         self.feed()
 
     def feed(self):
@@ -330,8 +329,16 @@
         self.out_copy(k).start()
 
 
-def spot_count(shapes):
-    return sum((rows // min(CHUNK, rows)) * (cols // SPAN) for rows, cols in shapes)
+def row_chunks(rows, taper=False):
+    size = min(CHUNK, rows)
+    sizes = [size] * (rows // size)
+    if taper:
+        sizes[-1:] = [size // 2, size // 4, size // 4]
+    return [(sum(sizes[:i]), n) for i, n in enumerate(sizes)]
+
+
+def spot_count(shapes, taper=()):
+    return sum(len(row_chunks(rows, at in taper)) * (cols // SPAN) for at, (rows, cols) in enumerate(shapes))
 
 
 def attend_back(pipe, shards, length, low, gm, dq, dk, dv, dka, dva, causal, bq):
@@ -369,9 +376,9 @@
             out[:, c : c + SPAN] = tn(o[...], low[:, c : c + SPAN]).astype(LOW)
 
 
-def input_grads(rows_t, grads, out, first, bq):
-    for i in range(0, rows_t.shape[0], bq):
-        out[pl.ds(first + i, bq), :] = _nn(rows_t[pl.ds(i, bq), :], grads).astype(LOW)
+def input_grads(rows_in, grads, out, first, bq):
+    for i in range(0, rows_in.shape[1], bq):
+        out[pl.ds(first + i, bq), :] = tn(rows_in[:, i : i + bq], grads).astype(LOW)
 
 
 def share_rows(terms, core, part, got, sems, out, bq, pipe):
@@ -381,52 +388,51 @@
         part[pl.ds(i, bq), :] = back_rows(terms, (1 - core) * half + i, bq).astype(LOW)
     copy.start()
     pipe.tick()
-    for i in range(0, half, bq):
-        out[pl.ds(i, bq), :] = back_rows(terms, core * half + i, bq)
+    mine = [back_rows(terms, core * half + i, bq) for i in range(0, half, bq)]
     pipe.tick()
     copy.wait()
     for i in range(0, half, bq):
-        out[pl.ds(i, bq), :] += got[pl.ds(i, bq), :].astype(F32)
-
-
-def self_back_kernel(carried, bq, len_ref, low, q0, k0, v0, o0, l0, q1, k1, v1, o1, l1, wo0, wo1, xt, w0, w1, small0, small1, *rest):
+        out[pl.ds(i, bq), :] = (mine[i // bq] + got[pl.ds(i, bq), :].astype(F32)).astype(out.dtype)
+
+
+def self_back_kernel(carried, bq, len_ref, low, q0, k0, v0, o0, l0, q1, k1, v1, o1, l1, wo0, wo1, x_in, w0, w1, small0, small1, *rest):
     own, other, rest = rest[:carried], rest[carried : 2 * carried], rest[2 * carried :]
     token_out, rest = rest[0], rest[1:]
     outs, rest = rest[: carried + 3], rest[carried + 3 :]
     gm, dq, dk, dv, dka, dva, go_own, go_other, gi_own, gi_other, sm_own, sm_other, part, got, part_send, part_recv = rest[:16]
     core = lax.axis_index("c")
-    total = spot_count([ref.shape for ref in own] + [go_own.shape, gi_own.shape, sm_own.shape])
+    total = spot_count([ref.shape for ref in own] + [go_own.shape, sm_own.shape, gi_own.shape], (carried + 2,))
     pipe = Pipeline(total, rest[16:])
     pipe.greet([{"c": 1 - core}])
     for a, b, out in zip(own, other, outs):
-        pipe.add(a, b, out, 0)
+        pipe.add(a, b, out)
     shards = ((q0, k0, v0, o0, l0, wo0), (q1, k1, v1, o1, l1, wo1))
     output_grads(shards, low, (go_own, go_other))
-    pipe.add(go_own, go_other, outs[carried], 0)
+    pipe.add(go_own, go_other, outs[carried])
     attend_back(pipe, shards, len_ref[0], low, gm, dq, dk, dv, dka, dva, True, bq)
     for s, (gi, sm, small) in enumerate(((gi_own, sm_own, small0), (gi_other, sm_other, small1))):
         for m, grads in enumerate((dq, dk, dv)):
-            input_grads(xt, grads[s], gi, m * xt.shape[0], bq)
+            input_grads(x_in, grads[s], gi, m * x_in.shape[1], bq)
         row = lax.broadcasted_iota(jnp.int32, sm.shape, 0)
         sums = [jnp.sum(grads[s].astype(F32), axis=0, keepdims=True) for grads in (dq, dv)]
         sm[...] = jnp.where(row == 9, sums[0], jnp.where(row == 10, sums[1], small[...])).astype(LOW)
-    pipe.add(gi_own, gi_other, outs[carried + 1], 0)
-    pipe.add(sm_own, sm_other, outs[carried + 2], 0)
+    pipe.add(sm_own, sm_other, outs[carried + 2])
+    pipe.add(gi_own, gi_other, outs[carried + 1], True)
     terms = [(grads, s, w[m]) for s, w in ((0, w0), (1, w1)) for m, grads in enumerate((dq, dk, dv))]
     share_rows(terms, core, part, got, (part_send, part_recv), token_out, bq, pipe)
     pipe.drain()
 
 
-def cross_back_kernel(carried, bq, len_ref, low, q0, k0, v0, o0, l0, q1, k1, v1, o1, l1, wo0, wo1, xt, mt, wq0, wq1, wm0, wm1, *rest):
+def cross_back_kernel(carried, bq, len_ref, low, q0, k0, v0, o0, l0, q1, k1, v1, o1, l1, wo0, wo1, x_in, m_in, wq0, wq1, wm0, wm1, *rest):
     own, other, rest = rest[:carried], rest[carried : 2 * carried], rest[2 * carried :]
     row_out, memory_out, sums_out, go_own, go_other, gq_own, gq_other, gm_own, gm_other = rest[:9]
     outs, rest = rest[9 : 9 + carried], rest[9 + carried :]
     gm, dq, dk, dv, dka, dva, part, got, part_send, part_recv, full_part, full_got, full_send, full_recv = rest[:14]
     core = lax.axis_index("c")
-    pipe = Pipeline(spot_count([ref.shape for ref in own]), rest[14:])
+    pipe = Pipeline(spot_count([ref.shape for ref in own], (carried - 1,)), rest[14:])
     pipe.greet([{"c": 1 - core}])
-    for a, b, out in zip(own, other, outs):
-        pipe.add(a, b, out, 0)
+    for at, (a, b, out) in enumerate(zip(own, other, outs)):
+        pipe.add(a, b, out, at == carried - 1)
     shards = ((q0, k0, v0, o0, l0, wo0), (q1, k1, v1, o1, l1, wo1))
     attend_back(pipe, shards, len_ref[0], low, gm, dq, dk, dv, dka, dva, False, bq)
     rows = low.shape[0]
@@ -441,16 +447,16 @@
     output_grads(shards, low, (go_own, go_other))
     pipe.tick()
     for s, (gq, gkv) in enumerate(((gq_own, gm_own), (gq_other, gm_other))):
-        input_grads(xt, dq[s], gq, 0, bq)
-        input_grads(mt, dk[s], gkv, 0, bq)
-        input_grads(mt, dv[s], gkv, mt.shape[0], bq)
+        input_grads(x_in, dq[s], gq, 0, bq)
+        input_grads(m_in, dk[s], gkv, 0, bq)
+        input_grads(m_in, dv[s], gkv, m_in.shape[1], bq)
         sums_out[s, 0:1] = jnp.sum(dq[s].astype(F32), axis=0, keepdims=True)
         sums_out[s, 1:2] = jnp.sum(dv[s].astype(F32), axis=0, keepdims=True)
         pipe.tick()
     exchange.wait()
     for i in range(0, rows, bq):
         at = pl.ds(i, bq)
-        row_out[at, :] = full_part[at, :].astype(F32) + full_got[at, :].astype(F32)
+        row_out[at, :] = (full_part[at, :].astype(F32) + full_got[at, :].astype(F32)).astype(LOW)
     pipe.drain()
 
 
@@ -462,7 +468,7 @@
     return [low_ram(2, rows, width) for unused in range(4)] + [pltpu.VMEM((2, rows, 128), F32), pltpu.VMEM((2, rows, 128), F32)]
 
 
-def self_back(length, low, first, second, wo, xt, w, smalls, pairs, bq=256):
+def self_back(length, low, first, second, wo, x_in, w, smalls, pairs, bq=256):
     rows, model = low.shape
     width = wo[0].shape[0]
     carried = len(pairs)
@@ -470,7 +476,7 @@
     vmem = pl.BlockSpec(memory_space=pltpu.VMEM)
     dma = pltpu.SemaphoreType.DMA
     ends = [(width, model), (3 * rows, width), smalls[0].shape]
-    total = spot_count([own.shape for own, unused in pairs] + ends)
+    total = spot_count([own.shape for own, unused in pairs] + [ends[0], ends[2], ends[1]], (carried + 2,))
     return pl.pallas_call(
         functools.partial(self_back_kernel, carried, bq),
         out_shape=[jax.ShapeDtypeStruct((rows // 2, model), F32)] + [jax.ShapeDtypeStruct(own.shape, LOW) for own, unused in pairs] + [jax.ShapeDtypeStruct(shape, LOW) for shape in ends],
@@ -483,21 +489,21 @@
         compiler_params=pltpu.CompilerParams(collective_id=0, has_side_effects=True, vmem_limit_bytes=58 << 20),
         cost_estimate=pl.CostEstimate(flops=20 * rows * model * width, bytes_accessed=300 << 20, transcendentals=8 * rows * rows),
         name="self_backward",
-    )(length, low, *first, *second, *wo, xt, *w, *smalls, *[p[0] for p in pairs], *[p[1] for p in pairs])
-
-
-def cross_back(length, low, first, second, wo, xt, mt, wq, wm, pairs, bq=256):
+    )(length, low, *first, *second, *wo, x_in, *w, *smalls, *[p[0] for p in pairs], *[p[1] for p in pairs])
+
+
+def cross_back(length, low, first, second, wo, x_in, m_in, wq, wm, pairs, bq=256):
     rows, model = low.shape
     width = wo[0].shape[0]
     carried = len(pairs)
     any_space = pl.BlockSpec(memory_space=pl.ANY)
     vmem = pl.BlockSpec(memory_space=pltpu.VMEM)
     dma = pltpu.SemaphoreType.DMA
-    total = spot_count([own.shape for own, unused in pairs])
+    total = spot_count([own.shape for own, unused in pairs], (carried - 1,))
     shape = jax.ShapeDtypeStruct
     return pl.pallas_call(
         functools.partial(cross_back_kernel, carried, bq),
-        out_shape=[shape((rows, model), F32), shape((rows // 2, model), F32), shape((2, 8, width), F32)]
+        out_shape=[shape((rows, model), LOW), shape((rows // 2, model), LOW), shape((2, 8, width), F32)]
         + [shape((width, model), LOW)] * 2 + [shape((rows, width), LOW)] * 2 + [shape((2 * rows, width), LOW)] * 2
         + [shape(own.shape, LOW) for own, unused in pairs],
         in_specs=[pl.BlockSpec(memory_space=pltpu.SMEM)] + [vmem] * 19 + [any_space] * (2 * carried),
@@ -509,7 +515,40 @@
         compiler_params=pltpu.CompilerParams(collective_id=1, has_side_effects=True, vmem_limit_bytes=58 << 20),
         cost_estimate=pl.CostEstimate(flops=20 * rows * model * width, bytes_accessed=300 << 20, transcendentals=8 * rows * rows),
         name="cross_backward",
-    )(length, low, *first, *second, *wo, xt, mt, *wq, *wm, *[p[0] for p in pairs], *[p[1] for p in pairs])
+    )(length, low, *first, *second, *wo, x_in, m_in, *wq, *wm, *[p[0] for p in pairs], *[p[1] for p in pairs])
+
+
+def feed_kernel(count, rows_in, *refs):
+    w_in, b_in, w_out, part, hidden, slope = refs[:count], refs[count : 2 * count], refs[2 * count : 3 * count], refs[3 * count], refs[3 * count + 1 : 4 * count + 1], refs[4 * count + 1 :]
+    branch = None
+    for s in range(count):
+        pre = _nn(rows_in[...], w_in[s][...]) + b_in[s][...].astype(F32)
+        spread_to = 0.5 + 0.5 * lax.erf(pre * 0.5**0.5)
+        hidden[s][...] = (pre * spread_to).astype(LOW)
+        slope[s][...] = (spread_to + pre * (jnp.exp(-0.5 * pre * pre) * (2.0 * math.pi) ** -0.5)).astype(LOW)
+        term = _nn(hidden[s][...], w_out[s][...])
+        branch = term if branch is None else branch + term
+    part[...] = branch.astype(LOW)
+
+
+def feed_forward(rows_in, w_in, b_in, w_out, bq=256):
+    count = len(w_in)
+    rows, model = rows_in.shape
+    units = w_in[0].shape[1]
+    wide = pl.BlockSpec((bq, units), lambda i: (i, 0))
+    block = pl.BlockSpec((bq, model), lambda i: (i, 0))
+    held = lambda array: pl.BlockSpec(array.shape, lambda i: (0, 0))
+    out = pl.pallas_call(
+        functools.partial(feed_kernel, count),
+        grid=(rows // bq,),
+        out_shape=[jax.ShapeDtypeStruct((rows, model), LOW)] + [jax.ShapeDtypeStruct((rows, units), LOW)] * (2 * count),
+        in_specs=[block] + [held(array) for array in (*w_in, *b_in, *w_out)],
+        out_specs=[block] + [wide] * (2 * count),
+        compiler_params=pltpu.CompilerParams(dimension_semantics=("arbitrary",), vmem_limit_bytes=50 << 20),
+        cost_estimate=pl.CostEstimate(flops=4 * count * rows * model * units, bytes_accessed=16 << 20, transcendentals=2 * count * rows * units),
+        name="feed_forward",
+    )(rows_in, *w_in, *b_in, *w_out)
+    return out[0], out[1 : 1 + count], out[1 + count :]
 
 
 residual_scale = 300.0**0.25
@@ -520,15 +559,6 @@
 
 def tn(rows, grads):
     return lax.dot_general(rows, grads, (((0,), (0,)), ((), ())), preferred_element_type=F32)
-
-
-def gelu_exact(pre_rows):
-    return jax.nn.gelu(pre_rows, approximate=False)
-
-
-def gelu_backward(pre_rows, grad_rows):
-    unused, pullback = jax.vjp(gelu_exact, pre_rows)
-    return pullback(grad_rows)[0]
 
 
 def norm_forward(summed, gain_row, shift_row):
@@ -654,7 +684,7 @@
         self_mixed.append(mixed)
         self_lse.append(lse)
     first = self_mixed[0]
-    w_self_out = spread(after(self_output, first), 0)
+    w_self_out = spread(after(self_output, self_q[0]), 0)
     memory_all = gather_rows(after(memory, first))
     w_cross_mem = spread(after(cross_memory, first), 2)
     w_cross_q = spread(after(cross_query, first), 1)
@@ -665,15 +695,14 @@
     cross_v = [(_nn(memory_all, w_cross_mem[s][1]) + b_proj[s][3]).astype(LOW) for s in shards]
     branch_one = sum_all(sum(_nn(self_mixed[s], w_self_out[s]) for s in shards)) + branch_bias[0]
     normed_one, unit_one, inverse_one = norm_forward(residual_scale * token_all.astype(F32) + branch_one, norm_gain[0], norm_shift[0])
-    second = normed_one.astype(LOW)
+    second = after(normed_one.astype(LOW), w_in[-1], w_out[-1])
     cross_q = [(_nn(second, w_cross_q[s]) + b_proj[s][2]).astype(LOW) for s in shards]
     cross_mixed, cross_lse = zip(*[attn_fwd(memory_length, cross_q[s], cross_k[s], cross_v[s], False) for s in shards])
     branch_two = sum_all(sum(_nn(cross_mixed[s], w_cross_out[s]) for s in shards)) + branch_bias[1]
     normed_two, unit_two, inverse_two = norm_forward(residual_scale * normed_one + branch_two, norm_gain[1], norm_shift[1])
     third = normed_two.astype(LOW)
-    hidden_pre = [_nn(third, w_in[s]) + b_in[s].astype(F32) for s in shards]
-    hidden = [gelu_exact(hidden_pre[s]).astype(LOW) for s in shards]
-    branch_three = sum_all(sum(_nn(hidden[s], w_out[s]) for s in shards)) + branch_bias[2]
+    feed_part, hidden, slope = feed_forward(third, w_in, [b_in[s].reshape(1, -1) for s in shards], w_out)
+    branch_three = sum_all(feed_part) + branch_bias[2]
     normed_three, unit_three, inverse_three = norm_forward(residual_scale * normed_two + branch_three, norm_gain[2], norm_shift[2])
     block_out = own_rows(normed_three.astype(LOW))
 
@@ -682,7 +711,7 @@
     low_three = grad_three.astype(LOW)
     grad_hidden = [_nt(low_three, w_out[s]) for s in shards]
     feed_out_parts = parts_of([tn(hidden[s], low_three) for s in shards], 0)
-    grad_pre = [gelu_backward(hidden_pre[s], grad_hidden[s]).astype(LOW) for s in shards]
+    grad_pre = [(grad_hidden[s] * slope[s].astype(F32)).astype(LOW) for s in shards]
     feed_in_parts = parts_of([tn(third, grad_pre[s]) for s in shards], 1)
     grad_normed_two = residual_scale * grad_three + sum_all(sum(_nt(grad_pre[s], w_in[s]) for s in shards))
     grad_two = norm_backward(grad_normed_two, unit_two, inverse_two, norm_gain[1])
@@ -698,10 +727,10 @@
     if in_kernel:
         per_shard = [(cross_q[s], cross_k[s], cross_v[s], cross_mixed[s], cross_lse[s]) for s in shards]
         row_part, memory_part, cross_sums, go_own, go_other, gq_own, gq_other, gm_own, gm_other, feed_out_sum, feed_in_sum = cross_back(
-            memory_length, low_two, per_shard[0], per_shard[1], w_cross_out, second.T, memory_all.T, w_cross_q, w_cross_mem, low_pairs(feed_out_parts, feed_in_parts))
+            memory_length, low_two, per_shard[0], per_shard[1], w_cross_out, second, memory_all, w_cross_q, w_cross_mem, low_pairs(feed_out_parts, feed_in_parts))
         cross_sums = [cross_sums[0, :2], cross_sums[1, :2]]
-        grad_memory = memory_part.astype(LOW)
-        grad_normed_one = residual_scale * grad_two + row_part
+        grad_memory = memory_part
+        grad_normed_one = residual_scale * grad_two + row_part.astype(F32)
     else:
         feed_out_sum, feed_in_sum = [sum_groups(send_home(part)) for part in (feed_out_parts, feed_in_parts)]
         grad_cross_mixed = [_nt(low_two, w_cross_out[s]).astype(LOW) for s in shards]
@@ -733,7 +762,7 @@
     if in_kernel:
         per_shard = [(self_q[s], self_k[s], self_v[s], self_mixed[s], self_lse[s]) for s in shards]
         pairs = [(go_own, go_other), (gq_own, gq_other), (gm_own, gm_other)]
-        token_part, *sums_low = self_back(target_length, low_one, per_shard[0], per_shard[1], w_self_out, token_all.T, w_self, smalls, pairs)
+        token_part, *sums_low = self_back(target_length, low_one, per_shard[0], per_shard[1], w_self_out, token_all, w_self, smalls, pairs)
     else:
         groups = [[cross_out_parts], cross_parts[:1], cross_parts[1:], [self_out_parts], [parts_of([tn(token_all, grads[s]) for s in shards], 1) for grads in (self_dq, self_dk, self_dv)], [smalls]]
         sums_low = [sum_groups(send_home([jnp.concatenate([part[k] for part in group]) for k in range(gn)])) for group in groups]

time: 589 us -> 555 us (0.942)
  matrix products: 92.1 us -> 41.6 us
  Pallas kernels: 298 us -> 341 us
  local copies, waits for them, and re-layouts: 41 us -> 21.9 us
    dot_general x20 -> x16, matrix products: 60.7 us -> 13.5 us  [_nn(): lax.dot_general(a, b, (((1,), (0,)), ((), ())), preferred_element_type=jn...]
    pallas_call x1, Pallas kernels: 129 us -> 148 us  [cross_back(): pl.pallas_call(functools.partial(cross_back_kernel, carried, bq), out_sha...]
    pallas_call x0 -> x1, Pallas kernels: none -> 16.9 us  [feed_forward(): pl.pallas_call(functools.partial(feed_kernel, count), grid=(rows // bq,),...]
    ppermute x1, waiting for transfers between devices: 0.01 us -> 9.14 us  [fetch_slices(): lax.ppermute(piece, 'g', [((i + k) % gn, i) for i in range(gn)])]
    unnamed x164 -> x145, local copies, waits for them, and re-layouts: 16.8 us -> 8.52 us
    transpose x2 -> x0, other arithmetic: 8.17 us -> none  [layer(): row_part, memory_part, cross_sums, go_own, go_other, gq_own, gq_other, gm...]
    pallas_call x2 -> x0, local copies, waits for them, and re-layouts: 7.27 us -> none  [the longest x1 5.35 us: cross_back(): pl.pallas_call(functools.partial(cross_back_kernel, carried, bq), out_sha...]
    all_gather x1, waiting for transfers between devices: 7.09 us -> 0.01 us  [spread_wide(): lax.all_gather(piece, ('z', 'y'), axis=1, tiled=True)]
  transfers between devices with their start and end apart: 15 -> 15, of which waited for: 5 -> 6; matrix products, arithmetic and copies ran while one was open for 16% -> 10% of each run, Pallas kernels for 6% -> 6%
where the time goes in v7:
time: 555 us; the launch traced here: 551 us
  Pallas kernels  341 us (61%)
  other arithmetic  63.3 us (11%)
  waiting for transfers between devices  58.1 us (10%)
  matrix products  41.6 us (7%)
  local copies, waits for them, and re-layouts  21.9 us (4%)
  between operations  15.5 us (3%)
  starting transfers between devices  10.1 us (2%)
    pallas_call x1, Pallas kernels, cross_back(): pl.pallas_call(functools.partial(cross_back_kernel, carried, bq), out_sha...  148 us
    pallas_call x1, Pallas kernels, self_back(): pl.pallas_call(functools.partial(self_back_kernel, carried, bq), out_shap...  141 us
    ppermute x6, waiting for transfers between devices, spread(): lax.ppermute(shard, 'g', [((i + k) % gn, i) for i in range(gn)])  40.4 us
    pallas_call x4, Pallas kernels, attn_fwd(): pl.pallas_call(functools.partial(fwd_kernel, causal=causal, bq=bq), out_s...  34.8 us
    reduce_sum x6, other arithmetic, sums(): return jnp.sum(rows.astype(F32), axis=0)  26.3 us
    dot_general x4, matrix products, tn(): lax.dot_general(rows, grads, (((0,), (0,)), ((), ())), preferred_element_...  17.2 us
    pallas_call x1, Pallas kernels, feed_forward(): pl.pallas_call(functools.partial(feed_kernel, count), grid=(rows // bq,),...  16.9 us
    dot_general x16, matrix products, _nn(): lax.dot_general(a, b, (((1,), (0,)), ((), ())), preferred_element_type=jn...  13.5 us
  transfers between devices with their start and end apart: 15, of which 6 were waited for; matrix products, arithmetic and copies ran while one was open for 10% of the time, Pallas kernels for 6%

profile of v7, /device:TPU:0, one launch (start us, length us, event | category | flops | bytes accessed | tf_op | source)
XLA Modules:
  0.0 551.2 jit_solution(12078170185463276059)
XLA Ops:
  14.9 9.1 %collective-permute-done.2 = bf16[2,128,1024]{2,1,0:T(8,128)(2,1)S(1)} collective-permute-done((bf16[2,128,1024]{2,1,0:T(8,128)(2,1)S(1)}, bf16[2,128,1024]{2,1,0:T(8,128)(2,1)S(1)}, u32[]{:S(2)}, u32[]{:S(2)}) %collective-permute-start.2) | collective-permute-done | bytes 524320 | tf_op jit(solution)/shard_map/ppermute | solution.py:646
  32.3 7.9 %attend_forward.4 = (bf16[1024,256]{1,0:T(8,128)(2,1)S(1)}, f32[1024,128]{1,0:T(8,128)S(1)}) custom-call(s32[1]{0:T(128)} %dynamic_slice.24.len_ref, bf16[1024,256]{1,0:T(8,128)(2,1)S(1)} %fusion.11.q_ref.q0, bf16[1024,256]{1,0:T(8,128)(2,1)S(1)} %convolution_convert_fusion.7.k_ref.k0, bf16[1024,256]{1,0:T(8,128)(2,1)S(1)} %fusion.12.v_ref.v0), custom_call_target="tpu_custom_call" | custom-call | flops 4294967296 | bytes 2097152 | tf_op jit(solution)/shard_map/attend_forward/pallas_call | solution.py:83
  42.6 22.3 %collective-permute-done.3.w1 = bf16[3,1024,256]{2,1,0:T(8,128)(2,1)S(1)} collective-permute-done((bf16[3,1024,256]{2,1,0:T(8,128)(2,1)S(1)}, bf16[3,1024,256]{2,1,0:T(8,128)(2,1)S(1)}, u32[]{:S(2)}, u32[]{:S(2)}) %collective-permute-start.3) | collective-permute-done | bytes 1572896 | tf_op jit(solution)/shard_map/ppermute | solution.py:614
  67.2 8.0 %attend_forward.5 = (bf16[1024,256]{1,0:T(8,128)(2,1)S(1)}, f32[1024,128]{1,0:T(8,128)S(1)}) custom-call(s32[1]{0:T(128)} %dynamic_slice.24.len_ref, bf16[1024,256]{1,0:T(8,128)(2,1)S(1)} %fusion.13.q_ref.q1, bf16[1024,256]{1,0:T(8,128)(2,1)S(1)} %convolution_convert_fusion.6.k_ref.k1, bf16[1024,256]{1,0:T(8,128)(2,1)S(1)} %fusion.14.v_ref.v1), custom_call_target="tpu_custom_call" | custom-call | flops 4294967296 | bytes 2097152 | tf_op jit(solution)/shard_map/attend_forward/pallas_call | solution.py:83
  81.5 17.1 %collective-permute-done.8.wm1 = bf16[2,1024,256]{2,1,0:T(8,128)(2,1)S(1)} collective-permute-done((bf16[2,1024,256]{2,1,0:T(8,128)(2,1)S(1)}, bf16[2,1024,256]{2,1,0:T(8,128)(2,1)S(1)}, u32[]{:S(2)}, u32[]{:S(2)}) %collective-permute-start.8) | collective-permute-done | bytes 1048608 | tf_op jit(solution)/shard_map/ppermute | solution.py:614
  106.1 4.8 slice_bitcast_fusion
  112.8 9.5 %attend_forward.6 = (bf16[1024,256]{1,0:T(8,128)(2,1)S(1)}, f32[1024,128]{1,0:T(8,128)S(1)}) custom-call(s32[1]{0:T(128)} %dynamic_slice.27.len_ref, bf16[1024,256]{1,0:T(8,128)(2,1)S(1)} %fusion.15.q_ref.q0, bf16[1024,256]{1,0:T(8,128)(2,1)S(1)} %convolution_convert_fusion.5.k_ref.k0, bf16[1024,256]{1,0:T(8,128)(2,1)S(1)} %fusion.16.v_ref.v0), custom_call_target="tpu_custom_call" | custom-call | flops 4294967296 | bytes 2097152 | tf_op jit(solution)/shard_map/attend_forward/pallas_call | solution.py:83
  125.1 9.4 %attend_forward.7 = (bf16[1024,256]{1,0:T(8,128)(2,1)S(1)}, f32[1024,128]{1,0:T(8,128)S(1)}) custom-call(s32[1]{0:T(128)} %dynamic_slice.27.len_ref, bf16[1024,256]{1,0:T(8,128)(2,1)S(1)} %fusion.17.q_ref.q1, bf16[1024,256]{1,0:T(8,128)(2,1)S(1)} %convolution_convert_fusion.4.k_ref.k1, bf16[1024,256]{1,0:T(8,128)(2,1)S(1)} %fusion.18.v_ref.v1), custom_call_target="tpu_custom_call" | custom-call | flops 4294967296 | bytes 2097152 | tf_op jit(solution)/shard_map/attend_forward/pallas_call | solution.py:83
  135.4 4.1 collective-permute-done.10
  144.4 16.9 %feed_forward.1 = (bf16[1024,1024]{1,0:T(8,128)(2,1)S(1)}, bf16[1024,1024]{1,0:T(8,128)(2,1)}, bf16[1024,1024]{1,0:T(8,128)(2,1)}, bf16[1024,1024]{1,0:T(8,128)(2,1)}, bf16[1024,1024]{1,0:T(8,128)(2,1)}) custom-call(bf16[1024,1024]{1,0:T(8,128)(2,1)} %fusion.8.rows_in, bf16[1024,1024]{1,0:T(8,128)(2,1)} %refs_0_.1, ...), custom_call_target="tpu_custom_call" | custom-call | flops 8589934592 | bytes 16777216 | tf_op jit(solution)/shard_map/feed_forward/pallas_call | solution.py:541
  161.9 4.4 collective-permute-done.11
  166.4 4.1 fusion.32
  171.0 3.5 fusion.6
  186.8 3.8 add_convert_fusion
  190.7 3.8 convolution_convert_fusion.rest_3_
  197.4 5.9 %convolution_convert_fusion.2.rest_1_ = bf16[1024,1024]{1,0:T(8,128)(2,1)} fusion(bf16[1024,1024]{1,0:T(8,128)(2,1)S(1)} %copy-done.37, bf16[1024,1024]{1,0:T(8,128)(2,1)} %copy-done.65), kind=kOutput, calls=%fused_computation.54 | convolution fusion | flops 2148532224 | bytes 6291456 | tf_op jit(solution)/shard_map/dot_general | solution.py:561
  203.3 3.7 convolution_convert_fusion.1.rest_2_
  207.0 3.7 convolution_convert_fusion.3.rest_0_
  211.4 7.2 %multiply_reduce_fusion = (f32[1024]{0:T(1024)S(1)}, f32[1024]{0:T(1024)S(1)}, f32[1024]{0:T(1024)S(1)}, f32[1024]{0:T(1024)S(1)}, f32[1024,1024]{1,0:T(8,128)S(1)}) fusion(f32[1024,1024]{1,0:T(8,128)S(1)} %copy-done.24, f32[1024]{0:T(1024)S(1)} %add_rsqrt_fusion.1, f32[1024]{0:T(1024)S(1)} %broadcast_multiply_fusion.7, f32[1024]{0:T(1024)S(1)} %bitcast.132, ...), kind=kLoop, calls=%fused_computation.12 | loop fusion | flops 30404608 | bytes 18919424 | tf_op jit(solution)/shard_map/reduce_sum | solution.py:721
  218.7 3.6 convert_reduce_fusion.4
  222.3 148.4 %cross_backward.1 = (bf16[1024,1024]{1,0:T(8,128)(2,1)}, bf16[512,1024]{1,0:T(8,128)(2,1)}, f32[2,8,256]{2,1,0:T(8,128)}, bf16[256,1024]{1,0:T(8,128)(2,1)}, bf1...) custom-call(s32[1]{0:T(128)} %dynamic_slice.27.len_ref, ...), custom_call_target="tpu_custom_call" | custom-call | flops 5368709120 | bytes 314572800 | tf_op jit(solution)/shard_map/cross_backward/pallas_call | solution.py:504
  370.7 4.9 multiply_reduce_fusion.1
  376.3 4.0 convert_reduce_fusion.5
  381.8 140.6 %self_backward.1 = (f32[512,1024]{1,0:T(8,128)}, bf16[256,1024]{1,0:T(8,128)(2,1)}, bf16[1024,256]{1,0:T(8,128)(2,1)}, bf16[2048,256]{1,0:T(8,128)(2,1)}, bf16[2...) custom-call(s32[1]{0:T(128)} %dynamic_slice.24.len_ref, ...), custom_call_target="tpu_custom_call" | custom-call | flops 5368709120 | bytes 314572800 | tf_op jit(solution)/shard_map/self_backward/pallas_call | solution.py:480
  (246 shorter events, 84.8 us)
Async XLA Ops:
  7.2 99.0 %all-gather.2.cloned.1.call-start = ((), (), s32[]{:S(2)}) async-start(), calls=%async_computation | async-start | bytes 4718592 | tf_op jit(solution)/shard_map/all_gather | solution.py:651
  7.2 17.7 %collective-permute-start = (bf16[512,1024]{1,0:T(8,128)(2,1)}, bf16[512,1024]{1,0:T(8,128)(2,1)S(1)}, u32[]{:S(2)}, u32[]{:S(2)}) collective-permute-start(bf16[512,1024]{1,0:T(8,128)(2,1)} %param.17), channel_id=1, source_target_pairs={{0,1},{1,0},{2,3},{3,2},{4,5},{5,4},{6,7},{7,6},{8,9},{9,8},{10,11... | collective-permute-start | bytes 3145736 | tf_op jit(solution)/shard_map/ppermute | solution.py:588
  8.9 15.2 %collective-permute-start.2 = (bf16[2,128,1024]{2,1,0:T(8,128)(2,1)S(1)}, bf16[2,128,1024]{2,1,0:T(8,128)(2,1)S(1)}, u32[]{:S(2)}, u32[]{:S(2)}) collective-permute-start(bf16[2,128,1024]{2,1,0:T(8,128)(2,1)S(1)} %pad_maximum_fusion), channel_id=1, source_target_pairs={{2,0},{0,2},{3,1},{1,3},{6,4},{4,6},{7,5},{5,7},{10,8},{8,10},{11,... | collective-permute-start | bytes 1572872 | tf_op jit(solution)/shard_map/ppermute | solution.py:646
  12.8 12.1 %collective-permute-start.1 = (bf16[8,256]{1,0:T(8,128)(2,1)S(1)}, bf16[8,256]{1,0:T(8,128)(2,1)S(1)}, u32[]{:S(2)}, u32[]{:S(2)}) collective-permute-start(bf16[8,256]{1,0:T(8,128)(2,1)S(1)} %pad_maximum_fusion.3), channel_id=1, source_target_pairs={{2,0},{0,2},{3,1},{1,3},{6,4},{4,6},{7,5},{5,7},{10,8},{8,10},{11,... | collective-permute-start | bytes 12296 | tf_op jit(solution)/shard_map/ppermute | solution.py:614
  27.6 73.3 %copy-start.33 = (bf16[1024,1024]{1,0:T(8,128)(2,1)}, bf16[1024,1024]{1,0:T(8,128)(2,1)S(1)}, u32[]{:S(2)}) copy-start(bf16[1024,1024]{1,0:T(8,128)(2,1)S(1)} %maximum_select_fusion.x_in) | copy-start | bytes 6291460
  27.6 37.3 %collective-permute-start.3 = (bf16[3,1024,256]{2,1,0:T(8,128)(2,1)S(1)}, bf16[3,1024,256]{2,1,0:T(8,128)(2,1)S(1)}, u32[]{:S(2)}, u32[]{:S(2)}) collective-permute-start(bf16[3,1024,256]{2,1,0:T(8,128)(2,1)S(1)} %copy-done.62), channel_id=1, source_target_pairs={{2,0},{0,2},{3,1},{1,3},{6,4},{4,6},{7,5},{5,7},{10,8},{8,10},{11,... | collective-permute-start | bytes 4718600 | tf_op jit(solution)/shard_map/ppermute | solution.py:614
  30.2 46.0 %collective-permute-start.4 = (bf16[256,1024]{1,0:T(8,128)(2,1)S(1)}, bf16[256,1024]{1,0:T(8,128)(2,1)S(1)}, u32[]{:S(2)}, u32[]{:S(2)}) collective-permute-start(bf16[256,1024]{1,0:T(8,128)(2,1)S(1)} %copy-done.51), channel_id=1, source_target_pairs={{2,0},{0,2},{3,1},{1,3},{6,4},{4,6},{7,5},{5,7},{10,8},{8,10},{11,... | collective-permute-start | bytes 1572872 | tf_op jit(solution)/shard_map/ppermute | solution.py:614
  40.2 39.5 %collective-permute-start.6 = (bf16[512,1024]{1,0:T(8,128)(2,1)S(1)}, bf16[512,1024]{1,0:T(8,128)(2,1)S(1)}, u32[]{:S(2)}, u32[]{:S(2)}) collective-permute-start(bf16[512,1024]{1,0:T(8,128)(2,1)S(1)} %copy-done.45), channel_id=1, source_target_pairs={{0,1},{1,0},{2,3},{3,2},{4,5},{5,4},{6,7},{7,6},{8,9},{9,8},{10,11... | collective-permute-start | bytes 3145736 | tf_op jit(solution)/shard_map/ppermute | solution.py:588
  40.3 58.3 %collective-permute-start.8 = (bf16[2,1024,256]{2,1,0:T(8,128)(2,1)S(1)}, bf16[2,1024,256]{2,1,0:T(8,128)(2,1)S(1)}, u32[]{:S(2)}, u32[]{:S(2)}) collective-permute-start(bf16[2,1024,256]{2,1,0:T(8,128)(2,1)S(1)} %copy-done.48), channel_id=1, source_target_pairs={{2,0},{0,2},{3,1},{1,3},{6,4},{4,6},{7,5},{5,7},{10,8},{8,10},{11,... | collective-permute-start | bytes 3145736 | tf_op jit(solution)/shard_map/ppermute | solution.py:614
  76.9 24.0 %collective-permute-start.5 = (bf16[1024,1024]{1,0:T(8,128)(2,1)S(1)}, bf16[1024,1024]{1,0:T(8,128)(2,1)S(1)}, u32[]{:S(2)}, u32[]{:S(2)}) collective-permute-start(bf16[1024,1024]{1,0:T(8,128)(2,1)S(1)} %add_convert_fusion.2), channel_id=1, source_target_pairs={{0,1},{1,0},{2,3},{3,2},{4,5},{5,4},{6,7},{7,6},{8,9},{9,8},{10,11... | collective-permute-start | bytes 6291464 | tf_op jit(solution)/shard_map/ppermute | solution.py:588
  77.7 45.7 %collective-permute-start.7 = (bf16[1024,256]{1,0:T(8,128)(2,1)}, bf16[1024,256]{1,0:T(8,128)(2,1)}, u32[]{:S(2)}, u32[]{:S(2)}) collective-permute-start(bf16[1024,256]{1,0:T(8,128)(2,1)} %wq0), channel_id=1, source_target_pairs={{2,0},{0,2},{3,1},{1,3},{6,4},{4,6},{7,5},{5,7},{10,8},{8,10},{11,... | collective-permute-start | bytes 1572872 | tf_op jit(solution)/shard_map/ppermute | solution.py:614
  79.5 55.0 %collective-permute-start.9 = (bf16[256,1024]{1,0:T(8,128)(2,1)S(1)}, bf16[256,1024]{1,0:T(8,128)(2,1)S(1)}, u32[]{:S(2)}, u32[]{:S(2)}) collective-permute-start(bf16[256,1024]{1,0:T(8,128)(2,1)S(1)} %copy-done.44), channel_id=1, source_target_pairs={{2,0},{0,2},{3,1},{1,3},{6,4},{4,6},{7,5},{5,7},{10,8},{8,10},{11,... | collective-permute-start | bytes 1572872 | tf_op jit(solution)/shard_map/ppermute | solution.py:614
  80.8 19.3 %copy-start.35 = (bf16[1024,1024]{1,0:T(8,128)(2,1)}, bf16[1024,1024]{1,0:T(8,128)(2,1)S(1)}, u32[]{:S(2)}) copy-start(bf16[1024,1024]{1,0:T(8,128)(2,1)S(1)} %maximum_select_fusion.1.m_in) | copy-start | bytes 6291460
  81.5 31.2 %copy-start.4 = (bf16[1024,256]{1,0:T(8,128)(2,1)}, bf16[1024,256]{1,0:T(8,128)(2,1)S(1)}, u32[]{:S(2)}) copy-start(bf16[1024,256]{1,0:T(8,128)(2,1)S(1)} %convolution_convert_fusion.5.k_ref.k0) | copy-start | bytes 1572868
  99.4 25.7 %copy-start.5 = (bf16[1024,256]{1,0:T(8,128)(2,1)}, bf16[1024,256]{1,0:T(8,128)(2,1)S(1)}, u32[]{:S(2)}) copy-start(bf16[1024,256]{1,0:T(8,128)(2,1)S(1)} %convolution_convert_fusion.4.k_ref.k1) | copy-start | bytes 1572868
  100.1 12.6 %copy-start.6 = (bf16[1024,256]{1,0:T(8,128)(2,1)}, bf16[1024,256]{1,0:T(8,128)(2,1)S(1)}, u32[]{:S(2)}) copy-start(bf16[1024,256]{1,0:T(8,128)(2,1)S(1)} %fusion.16.v_ref.v0) | copy-start | bytes 1572868
  100.9 24.2 %copy-start.7 = (bf16[1024,256]{1,0:T(8,128)(2,1)}, bf16[1024,256]{1,0:T(8,128)(2,1)S(1)}, u32[]{:S(2)}) copy-start(bf16[1024,256]{1,0:T(8,128)(2,1)S(1)} %fusion.18.v_ref.v1) | copy-start | bytes 1572868
  112.8 9.6 %copy-start.8 = (bf16[1024,256]{1,0:T(8,128)(2,1)}, bf16[1024,256]{1,0:T(8,128)(2,1)S(1)}, u32[]{:S(2)}) copy-start(bf16[1024,256]{1,0:T(8,128)(2,1)S(1)} %fusion.15.q_ref.q0) | copy-start | bytes 1572868
  135.3 4.2 collective-permute-start.10
  144.4 17.2 %copy-start.29 = (bf16[512,1024]{1,0:T(8,128)(2,1)S(1)}, bf16[512,1024]{1,0:T(8,128)(2,1)}, u32[]{:S(2)}) copy-start(bf16[512,1024]{1,0:T(8,128)(2,1)} %param.19) | copy-start | bytes 3145732
  161.3 5.0 collective-permute-start.11
  161.6 9.5 %collective-permute-start.12 = (bf16[512,1024]{1,0:T(8,128)(2,1)S(1)}, bf16[512,1024]{1,0:T(8,128)(2,1)S(1)}, u32[]{:S(2)}, u32[]{:S(2)}) collective-permute-start(bf16[512,1024]{1,0:T(8,128)(2,1)S(1)} %copy-done.29), channel_id=1, source_target_pairs={{0,1},{1,0},{2,3},{3,2},{4,5},{5,4},{6,7},{7,6},{8,9},{9,8},{10,11... | collective-permute-start | bytes 3145736 | tf_op jit(solution)/shard_map/ppermute | solution.py:588
  190.6 20.2 %collective-permute-start.13 = (bf16[1024,1024]{1,0:T(8,128)(2,1)}, bf16[1024,1024]{1,0:T(8,128)(2,1)}, u32[]{:S(2)}, u32[]{:S(2)}) collective-permute-start(bf16[1024,1024]{1,0:T(8,128)(2,1)} %add_convert_fusion), channel_id=1, source_target_pairs={{0,1},{1,0},{2,3},{3,2},{4,5},{5,4},{6,7},{7,6},{8,9},{9,8},{10,11... | collective-permute-start | bytes 6291464 | tf_op jit(solution)/shard_map/ppermute | solution.py:588
  222.2 148.4 %copy-start.22 = (f32[1024,1024]{1,0:T(8,128)S(1)}, f32[1024,1024]{1,0:T(8,128)}, u32[]{:S(2)}) copy-start(f32[1024,1024]{1,0:T(8,128)} %copy-done.20) | copy-start | bytes 12582916
  (61 other events, 262.5 us)
Sparse Core Ops, SparseCore 0:
  25.0 74.8 all-gather.1

commit v8 on v7

--- a/solution.py
+++ b/solution.py
@@ -225,10 +225,9 @@
             pl.semaphore_signal(barrier, inc=1, device_id=where, device_id_type=pl.DeviceIdType.MESH)
         pl.semaphore_wait(barrier, len(everyone))
 
-    def add(self, own, other, out, taper=False):
-        for r, size in row_chunks(own.shape[0], taper):
-            for c in range(0, own.shape[1], SPAN):
-                self.spots.append((own, other, r, c, size, out, r))
+    def add(self, own, other, out, taper=False, first=0, count=None):
+        for r, size, c in cut(own.shape[0] if count is None else count, own.shape[1], taper):
+            self.spots.append((own, other, first + r, c, size, out, first + r))
         self.feed()
 
     def feed(self):
@@ -239,7 +238,7 @@
 
     def tick(self, times=1):
         for unused in range(times):
-            if self.step >= self.total + LAG * (len(self.stages) - 1):
+            if self.step >= self.total + LAG * (len(self.stages) - 1) or len(self.spots) <= self.step < self.total:
                 return
             for at, stage in enumerate(self.stages):
                 if 0 <= self.step - LAG * at < self.total:
@@ -329,19 +328,20 @@
         self.out_copy(k).start()
 
 
-def row_chunks(rows, taper=False):
+def cut(rows, cols, taper=False):
     size = min(CHUNK, rows)
-    sizes = [size] * (rows // size)
+    chunks = [(r, size, c) for r in range(0, rows, size) for c in range(0, cols, SPAN)]
     if taper:
-        sizes[-1:] = [size // 2, size // 4, size // 4]
-    return [(sum(sizes[:i]), n) for i, n in enumerate(sizes)]
+        r, unused, c = chunks.pop()
+        chunks += [(r, size // 2, c), (r + size // 2, size // 4, c), (r + size - size // 4, size // 4, c)]
+    return chunks
 
 
 def spot_count(shapes, taper=()):
-    return sum(len(row_chunks(rows, at in taper)) * (cols // SPAN) for at, (rows, cols) in enumerate(shapes))
-
-
-def attend_back(pipe, shards, length, low, gm, dq, dk, dv, dka, dva, causal, bq):
+    return sum(len(cut(rows, cols, at in taper)) for at, (rows, cols) in enumerate(shapes))
+
+
+def attend_back(pipe, shards, length, low, gm, dq, dk, dv, dka, dva, causal, bq, every):
     rows = low.shape[0]
     blocks = rows // bq
     for s, (q, k, v, o, l, wo) in enumerate(shards):
@@ -355,10 +355,11 @@
             for i in reversed(range(blocks)):
                 at = pl.ds(i * bq, bq)
                 dq[s, at, cols] = query_block(heads, q[at, cols], o[at, cols], gm[s, at, cols], l[at, :], p, i, i == blocks - 1, causal, dka, dva)
+                if i % every == 0:
+                    pipe.tick()
             first = _lanes(k.shape[0]) < HEAD
             dk[s, :, cols] = jnp.where(first, dka[0], dka[1]).astype(LOW)
             dv[s, :, cols] = jnp.where(first, dva[0], dva[1]).astype(LOW)
-            pipe.tick()
 
 
 def back_rows(terms, start, size):
@@ -401,7 +402,7 @@
     outs, rest = rest[: carried + 3], rest[carried + 3 :]
     gm, dq, dk, dv, dka, dva, go_own, go_other, gi_own, gi_other, sm_own, sm_other, part, got, part_send, part_recv = rest[:16]
     core = lax.axis_index("c")
-    total = spot_count([ref.shape for ref in own] + [go_own.shape, sm_own.shape, gi_own.shape], (carried + 2,))
+    total = spot_count([ref.shape for ref in own] + [go_own.shape, sm_own.shape] + [(low.shape[1], gi_own.shape[1])] * 3, (carried + 4,))
     pipe = Pipeline(total, rest[16:])
     pipe.greet([{"c": 1 - core}])
     for a, b, out in zip(own, other, outs):
@@ -409,15 +410,18 @@
     shards = ((q0, k0, v0, o0, l0, wo0), (q1, k1, v1, o1, l1, wo1))
     output_grads(shards, low, (go_own, go_other))
     pipe.add(go_own, go_other, outs[carried])
-    attend_back(pipe, shards, len_ref[0], low, gm, dq, dk, dv, dka, dva, True, bq)
-    for s, (gi, sm, small) in enumerate(((gi_own, sm_own, small0), (gi_other, sm_other, small1))):
-        for m, grads in enumerate((dq, dk, dv)):
-            input_grads(x_in, grads[s], gi, m * x_in.shape[1], bq)
+    attend_back(pipe, shards, len_ref[0], low, gm, dq, dk, dv, dka, dva, True, bq, 2)
+    for s, (sm, small) in enumerate(((sm_own, small0), (sm_other, small1))):
         row = lax.broadcasted_iota(jnp.int32, sm.shape, 0)
         sums = [jnp.sum(grads[s].astype(F32), axis=0, keepdims=True) for grads in (dq, dv)]
         sm[...] = jnp.where(row == 9, sums[0], jnp.where(row == 10, sums[1], small[...])).astype(LOW)
     pipe.add(sm_own, sm_other, outs[carried + 2])
-    pipe.add(gi_own, gi_other, outs[carried + 1], True)
+    model = x_in.shape[1]
+    for m, grads in enumerate((dq, dk, dv)):
+        for s, gi in enumerate((gi_own, gi_other)):
+            input_grads(x_in, grads[s], gi, m * model, bq)
+            pipe.tick()
+        pipe.add(gi_own, gi_other, outs[carried + 1], m == 2, m * model, model)
     terms = [(grads, s, w[m]) for s, w in ((0, w0), (1, w1)) for m, grads in enumerate((dq, dk, dv))]
     share_rows(terms, core, part, got, (part_send, part_recv), token_out, bq, pipe)
     pipe.drain()
@@ -434,11 +438,13 @@
     for at, (a, b, out) in enumerate(zip(own, other, outs)):
         pipe.add(a, b, out, at == carried - 1)
     shards = ((q0, k0, v0, o0, l0, wo0), (q1, k1, v1, o1, l1, wo1))
-    attend_back(pipe, shards, len_ref[0], low, gm, dq, dk, dv, dka, dva, False, bq)
+    attend_back(pipe, shards, len_ref[0], low, gm, dq, dk, dv, dka, dva, False, bq, 1)
     rows = low.shape[0]
     terms = [(dq, 0, wq0[...]), (dq, 1, wq1[...])]
     for i in range(0, rows, bq):
         full_part[pl.ds(i, bq), :] = back_rows(terms, i, bq).astype(LOW)
+        if i % (2 * bq):
+            pipe.tick()
     exchange = Pipeline.remote(full_part, full_got, full_send, full_recv, {"c": 1 - core})
     exchange.start()
     pipe.tick()
@@ -448,7 +454,9 @@
     pipe.tick()
     for s, (gq, gkv) in enumerate(((gq_own, gm_own), (gq_other, gm_other))):
         input_grads(x_in, dq[s], gq, 0, bq)
+        pipe.tick()
         input_grads(m_in, dk[s], gkv, 0, bq)
+        pipe.tick()
         input_grads(m_in, dv[s], gkv, m_in.shape[1], bq)
         sums_out[s, 0:1] = jnp.sum(dq[s].astype(F32), axis=0, keepdims=True)
         sums_out[s, 1:2] = jnp.sum(dv[s].astype(F32), axis=0, keepdims=True)
@@ -476,7 +484,7 @@
     vmem = pl.BlockSpec(memory_space=pltpu.VMEM)
     dma = pltpu.SemaphoreType.DMA
     ends = [(width, model), (3 * rows, width), smalls[0].shape]
-    total = spot_count([own.shape for own, unused in pairs] + [ends[0], ends[2], ends[1]], (carried + 2,))
+    total = spot_count([own.shape for own, unused in pairs] + [ends[0], ends[2]] + [(model, width)] * 3, (carried + 4,))
     return pl.pallas_call(
         functools.partial(self_back_kernel, carried, bq),
         out_shape=[jax.ShapeDtypeStruct((rows // 2, model), F32)] + [jax.ShapeDtypeStruct(own.shape, LOW) for own, unused in pairs] + [jax.ShapeDtypeStruct(shape, LOW) for shape in ends],
@@ -551,6 +559,73 @@
     return out[0], out[1 : 1 + count], out[1 + count :]
 
 
+def feed_back_kernel(count, scale, core_ref, part, got, normed, cot_ref, vectors, *refs):
+    slope, w_in, w_out, refs = refs[:count], refs[count : 2 * count], refs[2 * count : 3 * count], refs[3 * count :]
+    out, low, grad, row_part, sums, refs = refs[0], refs[1], refs[2], refs[3], refs[4], refs[5:]
+    pre_grads, pre_sums = refs[:count], refs[count:]
+    step = pl.program_id(0)
+    bias, gain, shift = vectors[0:1], vectors[1:2], vectors[2:3]
+    summed = scale * normed[...] + (part[...].astype(F32) + got[...].astype(F32) + bias)
+    rows, unit, inverse = norm_forward(summed, gain, shift)
+    half = pl.num_programs(0) // 2
+
+    @pl.when(step // half == core_ref[0])
+    def mine():
+        out[...] = rows.astype(LOW)
+
+    cot = cot_ref[...].astype(F32)
+    grads = norm_backward(cot, unit, inverse, gain)
+    grad[...] = grads
+    low_rows = grads.astype(LOW)
+    low[...] = low_rows
+    totals = [jnp.sum(v, axis=0, keepdims=True) for v in (low_rows.astype(F32), cot * unit, cot)]
+    branch = None
+    for s in range(count):
+        pre = (_nt(low_rows, w_out[s][...]) * slope[s][...].astype(F32)).astype(LOW)
+        pre_grads[s][...] = pre
+        term = _nt(pre, w_in[s][...])
+        branch = term if branch is None else branch + term
+        totals.append(jnp.sum(pre.astype(F32), axis=0, keepdims=True))
+    row_part[...] = branch.astype(LOW)
+
+    @pl.when(step == 0)
+    def clear():
+        sums[...] = jnp.zeros_like(sums)
+        for s in range(count):
+            pre_sums[s][...] = jnp.zeros_like(pre_sums[s])
+
+    for at in range(3):
+        sums[at : at + 1] += totals[at]
+    for s in range(count):
+        pre_sums[s][...] += totals[3 + s]
+
+
+def feed_backward(core, part, got, normed, cot, vectors, slope, w_in, w_out, bq=256):
+    count = len(w_in)
+    rows, model = part.shape
+    units = w_in[0].shape[1]
+    half = rows // bq // 2
+    wide = pl.BlockSpec((bq, units), lambda i, c: (i, 0))
+    block = pl.BlockSpec((bq, model), lambda i, c: (i, 0))
+    held = lambda shape: pl.BlockSpec(shape, lambda i, c: (0, 0))
+    shape = jax.ShapeDtypeStruct
+    out = pl.pallas_call(
+        functools.partial(feed_back_kernel, count, residual_scale),
+        out_shape=[shape((rows // 2, model), LOW), shape((rows, model), LOW), shape((rows, model), F32), shape((rows, model), LOW), shape((8, model), F32)]
+        + [shape((rows, units), LOW)] * count + [shape((1, units), F32)] * count,
+        grid_spec=pltpu.PrefetchScalarGridSpec(
+            num_scalar_prefetch=1,
+            grid=(rows // bq,),
+            in_specs=[block, block, block, block, held((3, model))] + [wide] * count + [held(array.shape) for array in (*w_in, *w_out)],
+            out_specs=[pl.BlockSpec((bq, model), lambda i, c: (jnp.clip(i - half * c[0], 0, half - 1), 0)), block, block, block, held((8, model))] + [wide] * count + [held((1, units))] * count,
+        ),
+        compiler_params=pltpu.CompilerParams(dimension_semantics=("arbitrary",), vmem_limit_bytes=54 << 20),
+        cost_estimate=pl.CostEstimate(flops=4 * count * rows * model * units, bytes_accessed=30 << 20, transcendentals=0),
+        name="feed_backward",
+    )(core, part, got, normed, cot, vectors, *slope, *w_in, *w_out)
+    return out[0], out[1], out[2], out[3], out[4][:3], out[5 : 5 + count], out[5 + count :]
+
+
 residual_scale = 300.0**0.25
 norm_epsilon = 1e-05
 LOW = jnp.bfloat16
@@ -671,9 +746,8 @@
     else:
         b_in = [part[4:].reshape(-1) for part in biases]
     b_proj = [part[:4] for part in biases]
-    slices = fetch_slices((feed_in, feed_out))
-    w_self = spread(after(self_inputs, token_all, biases[-1], slices[-1][0]), 2)
-    w_in, w_out = spread_wide((feed_in, feed_out), slices)
+    w_self = spread(self_inputs, 2)
+    w_self_out = spread(after(self_output, token_all), 0)
     self_q, self_k, self_v, self_mixed, self_lse = [], [], [], [], []
     shards = range(len(w_self))
     for s in shards:
@@ -684,36 +758,48 @@
         self_mixed.append(mixed)
         self_lse.append(lse)
     first = self_mixed[0]
-    w_self_out = spread(after(self_output, self_q[0]), 0)
+    slices = fetch_slices([after(feed_in, first), after(feed_out, first)])
+    w_in, w_out = spread_wide((feed_in, feed_out), [[after(piece, self_mixed[-1]) for piece in got] for got in slices])
     memory_all = gather_rows(after(memory, first))
-    w_cross_mem = spread(after(cross_memory, first), 2)
-    w_cross_q = spread(after(cross_query, first), 1)
-    w_cross_out = spread(after(cross_output, first), 0)
+    w_cross_mem = spread(after(cross_memory, self_q[-1]), 2)
+    w_cross_q = spread(after(cross_query, self_q[-1]), 1)
+    w_cross_out = spread(after(cross_output, self_q[-1]), 0)
     cot_all = gather_rows(after(cotangent, self_mixed[-1]))
 
     cross_k = [_nn(memory_all, w_cross_mem[s][0]).astype(LOW) for s in shards]
     cross_v = [(_nn(memory_all, w_cross_mem[s][1]) + b_proj[s][3]).astype(LOW) for s in shards]
     branch_one = sum_all(sum(_nn(self_mixed[s], w_self_out[s]) for s in shards)) + branch_bias[0]
     normed_one, unit_one, inverse_one = norm_forward(residual_scale * token_all.astype(F32) + branch_one, norm_gain[0], norm_shift[0])
-    second = after(normed_one.astype(LOW), w_in[-1], w_out[-1])
-    cross_q = [(_nn(second, w_cross_q[s]) + b_proj[s][2]).astype(LOW) for s in shards]
-    cross_mixed, cross_lse = zip(*[attn_fwd(memory_length, cross_q[s], cross_k[s], cross_v[s], False) for s in shards])
+    second = normed_one.astype(LOW)
+    cross_q, cross_mixed, cross_lse = [], [], []
+    for s in shards:
+        rows_in = second if s == 0 else after(second, w_in[-1], w_out[-1])
+        cross_q.append((_nn(rows_in, w_cross_q[s]) + b_proj[s][2]).astype(LOW))
+        mixed, lse = attn_fwd(memory_length, cross_q[s], cross_k[s], cross_v[s], False)
+        cross_mixed.append(mixed)
+        cross_lse.append(lse)
     branch_two = sum_all(sum(_nn(cross_mixed[s], w_cross_out[s]) for s in shards)) + branch_bias[1]
     normed_two, unit_two, inverse_two = norm_forward(residual_scale * normed_one + branch_two, norm_gain[1], norm_shift[1])
     third = normed_two.astype(LOW)
     feed_part, hidden, slope = feed_forward(third, w_in, [b_in[s].reshape(1, -1) for s in shards], w_out)
-    branch_three = sum_all(feed_part) + branch_bias[2]
-    normed_three, unit_three, inverse_three = norm_forward(residual_scale * normed_two + branch_three, norm_gain[2], norm_shift[2])
-    block_out = own_rows(normed_three.astype(LOW))
-
-    cot = cot_all.astype(F32)
-    grad_three = norm_backward(cot, unit_three, inverse_three, norm_gain[2])
-    low_three = grad_three.astype(LOW)
-    grad_hidden = [_nt(low_three, w_out[s]) for s in shards]
+    if cn == 2:
+        vectors = jnp.stack([branch_bias[2], norm_gain[2], norm_shift[2]])
+        block_out, low_three, grad_three, row_part, sums_three, grad_pre, feed_sums = feed_backward(core.reshape(1), feed_part, swap(feed_part), normed_two, cot_all, vectors, slope, w_in, w_out)
+        feed_sums = [part.reshape(-1) for part in feed_sums]
+    else:
+        branch_three = sum_all(feed_part) + branch_bias[2]
+        normed_three, unit_three, inverse_three = norm_forward(residual_scale * normed_two + branch_three, norm_gain[2], norm_shift[2])
+        block_out = own_rows(normed_three.astype(LOW))
+        cot = cot_all.astype(F32)
+        grad_three = norm_backward(cot, unit_three, inverse_three, norm_gain[2])
+        low_three = grad_three.astype(LOW)
+        grad_pre = [(_nt(low_three, w_out[s]) * slope[s].astype(F32)).astype(LOW) for s in shards]
+        row_part = sum(_nt(grad_pre[s], w_in[s]) for s in shards)
+        sums_three = [jnp.sum(rows.astype(F32), axis=0) for rows in (low_three, cot * unit_three, cot)]
+        feed_sums = [jnp.sum(grad_pre[s].astype(F32), axis=0) for s in shards]
     feed_out_parts = parts_of([tn(hidden[s], low_three) for s in shards], 0)
-    grad_pre = [(grad_hidden[s] * slope[s].astype(F32)).astype(LOW) for s in shards]
     feed_in_parts = parts_of([tn(third, grad_pre[s]) for s in shards], 1)
-    grad_normed_two = residual_scale * grad_three + sum_all(sum(_nt(grad_pre[s], w_in[s]) for s in shards))
+    grad_normed_two = residual_scale * grad_three + sum_all(row_part)
     grad_two = norm_backward(grad_normed_two, unit_two, inverse_two, norm_gain[1])
     low_two = grad_two.astype(LOW)
 
@@ -744,8 +830,8 @@
     low_one = grad_one.astype(LOW)
 
     model = tokens.shape[1]
-    terms = jnp.stack([sums(low_one), sums(low_two), sums(low_three), sums(grad_normed_one * unit_one), sums(grad_normed_two * unit_two), sums(cot * unit_three), sums(grad_normed_one), sums(grad_normed_two), sums(cot)])
-    feed_sums = parts_of([sums(grad_pre[s]) for s in shards], 0)
+    terms = jnp.stack([sums(low_one), sums(low_two), sums_three[0], sums(grad_normed_one * unit_one), sums(grad_normed_two * unit_two), sums_three[1], sums(grad_normed_one), sums(grad_normed_two), sums_three[2]])
+    feed_sums = parts_of(feed_sums, 0)
     if not in_kernel:
         grad_self_mixed = [_nt(low_one, w_self_out[s]).astype(LOW) for s in shards]
         self_out_parts = parts_of([tn(self_mixed[s], low_one) for s in shards], 0)

time: 555 us -> 570 us (1.027)
  waiting for transfers between devices: 58.1 us -> 69.8 us
  other arithmetic: 63.3 us -> 51.9 us
  Pallas kernels: 341 us -> 349 us
    pallas_call x0 -> x1, Pallas kernels: none -> 21.4 us  [feed_backward(): pl.pallas_call(functools.partial(feed_back_kernel, count, residual_scale)...]
    pallas_call x1, Pallas kernels: 148 us -> 137 us  [cross_back(): pl.pallas_call(functools.partial(cross_back_kernel, carried, bq), out_sha...]
    all_gather x1, waiting for transfers between devices: 0.01 us -> 11 us  [spread_wide(): lax.all_gather(piece, ('z', 'y'), axis=1, tiled=True)]
    dot_general x4 -> x0, matrix products: 11 us -> none  [_nt(): lax.dot_general(a, b, (((1,), (1,)), ((), ())), preferred_element_type=jn...]
    reduce_sum x6 -> x4, other arithmetic: 26.3 us -> 16.4 us  [sums(): return jnp.sum(rows.astype(F32), axis=0)]
    ppermute x6, waiting for transfers between devices: 40.4 us -> 50.2 us  [spread(): lax.ppermute(shard, 'g', [((i + k) % gn, i) for i in range(gn)])]
    dot_general x16, matrix products: 13.5 us -> 22.8 us  [_nn(): lax.dot_general(a, b, (((1,), (0,)), ((), ())), preferred_element_type=jn...]
    ppermute x1, waiting for transfers between devices: 9.14 us -> 0.01 us  [fetch_slices(): lax.ppermute(piece, 'g', [((i + k) % gn, i) for i in range(gn)])]
  transfers between devices with their start and end apart: 15 -> 15, of which waited for: 6 -> 6; matrix products, arithmetic and copies ran while one was open for 10% -> 11% of each run, Pallas kernels for 6% -> 6%
where the time goes in v8:
time: 570 us; the launch traced here: 561 us
  Pallas kernels  349 us (61%)
  waiting for transfers between devices  69.8 us (12%)
  other arithmetic  51.9 us (9%)
  matrix products  41.2 us (7%)
  local copies, waits for them, and re-layouts  24.1 us (4%)
  between operations  15.5 us (3%)
  starting transfers between devices  9.06 us (2%)
    pallas_call x1, Pallas kernels, self_back(): pl.pallas_call(functools.partial(self_back_kernel, carried, bq), out_shap...  139 us
    pallas_call x1, Pallas kernels, cross_back(): pl.pallas_call(functools.partial(cross_back_kernel, carried, bq), out_sha...  137 us
    ppermute x6, waiting for transfers between devices, spread(): lax.ppermute(shard, 'g', [((i + k) % gn, i) for i in range(gn)])  50.2 us
    pallas_call x4, Pallas kernels, attn_fwd(): pl.pallas_call(functools.partial(fwd_kernel, causal=causal, bq=bq), out_s...  34.7 us
    dot_general x16, matrix products, _nn(): lax.dot_general(a, b, (((1,), (0,)), ((), ())), preferred_element_type=jn...  22.8 us
    pallas_call x1, Pallas kernels, feed_backward(): pl.pallas_call(functools.partial(feed_back_kernel, count, residual_scale)...  21.4 us
    dot_general x4, matrix products, tn(): lax.dot_general(rows, grads, (((0,), (0,)), ((), ())), preferred_element_...  18.4 us
    pallas_call x1, Pallas kernels, feed_forward(): pl.pallas_call(functools.partial(feed_kernel, count), grid=(rows // bq,),...  17 us
  transfers between devices with their start and end apart: 15, of which 6 were waited for; matrix products, arithmetic and copies ran while one was open for 11% of the time, Pallas kernels for 6%

profile of v8, /device:TPU:0, one launch (start us, length us, event | category | flops | bytes accessed | tf_op | source)
XLA Modules:
  0.0 560.9 jit_solution(7519188552484260036)
XLA Ops:
  18.7 7.6 %attend_forward.4 = (bf16[1024,256]{1,0:T(8,128)(2,1)S(1)}, f32[1024,128]{1,0:T(8,128)S(1)}) custom-call(s32[1]{0:T(128)} %dynamic_slice.21.len_ref, bf16[1024,256]{1,0:T(8,128)(2,1)S(1)} %fusion.1.q_ref.q0, bf16[1024,256]{1,0:T(8,128)(2,1)S(1)} %convolution_convert_fusion.7.k_ref.k0, bf16[1024,256]{1,0:T(8,128)(2,1)S(1)} %fusion.2.v_ref.v0), custom_call_target="tpu_custom_call" | custom-call | flops 4294967296 | bytes 2097152 | tf_op jit(solution)/shard_map/attend_forward/pallas_call | solution.py:83
  29.8 19.3 %collective-permute-done.1.w1 = bf16[3,1024,256]{2,1,0:T(8,128)(2,1)} collective-permute-done((bf16[3,1024,256]{2,1,0:T(8,128)(2,1)}, bf16[3,1024,256]{2,1,0:T(8,128)(2,1)}, u32[]{:S(2)}, u32[]{:S(2)}) %collective-permute-start.1) | collective-permute-done | bytes 1572896 | tf_op jit(solution)/shard_map/ppermute | solution.py:689
  54.9 7.8 %attend_forward.5 = (bf16[1024,256]{1,0:T(8,128)(2,1)S(1)}, f32[1024,128]{1,0:T(8,128)S(1)}) custom-call(s32[1]{0:T(128)} %dynamic_slice.21.len_ref, bf16[1024,256]{1,0:T(8,128)(2,1)S(1)} %fusion.3.q_ref.q1, bf16[1024,256]{1,0:T(8,128)(2,1)S(1)} %convolution_convert_fusion.6.k_ref.k1, bf16[1024,256]{1,0:T(8,128)(2,1)S(1)} %fusion.4.v_ref.v1), custom_call_target="tpu_custom_call" | custom-call | flops 4294967296 | bytes 2097152 | tf_op jit(solution)/shard_map/attend_forward/pallas_call | solution.py:83
  65.5 10.8 %collective-permute-done.3.wo1 = bf16[256,1024]{1,0:T(8,128)(2,1)S(1)} collective-permute-done((bf16[256,1024]{1,0:T(8,128)(2,1)}, bf16[256,1024]{1,0:T(8,128)(2,1)S(1)}, u32[]{:S(2)}, u32[]{:S(2)}) %collective-permute-start.3) | collective-permute-done | bytes 524320 | tf_op jit(solution)/shard_map/ppermute | solution.py:689
  84.0 20.0 %collective-permute-done.8.wm1 = bf16[2,1024,256]{2,1,0:T(8,128)(2,1)S(1)} collective-permute-done((bf16[2,1024,256]{2,1,0:T(8,128)(2,1)S(1)}, bf16[2,1024,256]{2,1,0:T(8,128)(2,1)S(1)}, u32[]{:S(2)}, u32[]{:S(2)}) %collective-permute-start.8) | collective-permute-done | bytes 1048608 | tf_op jit(solution)/shard_map/ppermute | solution.py:689
  111.8 9.8 %attend_forward.6 = (bf16[1024,256]{1,0:T(8,128)(2,1)S(1)}, f32[1024,128]{1,0:T(8,128)S(1)}) custom-call(s32[1]{0:T(128)} %dynamic_slice.22.len_ref, bf16[1024,256]{1,0:T(8,128)(2,1)S(1)} %fusion.5.q_ref.q0, bf16[1024,256]{1,0:T(8,128)(2,1)S(1)} %convolution_convert_fusion.5.k_ref.k0, bf16[1024,256]{1,0:T(8,128)(2,1)S(1)} %fusion.6.v_ref.v0), custom_call_target="tpu_custom_call" | custom-call | flops 4294967296 | bytes 2097152 | tf_op jit(solution)/shard_map/attend_forward/pallas_call | solution.py:83
  122.4 4.0 fusion.29
  126.4 11.0 %all-gather.2.cloned.1.call-done = bf16[2,1024,1024]{2,1,0:T(8,128)(2,1)} async-done(((bf16[2,128,1024]{2,1,0:T(8,128)(2,1)}), bf16[2,1024,1024]{2,1,0:T(8,128)(2,1)}) %all-gather.2.cloned.1.call-update) | async-done | bytes 4194320 | tf_op jit(solution)/shard_map/all_gather | solution.py:726
  137.4 4.7 slice_bitcast_fusion
  143.9 9.5 %attend_forward.7 = (bf16[1024,256]{1,0:T(8,128)(2,1)S(1)}, f32[1024,128]{1,0:T(8,128)S(1)}) custom-call(s32[1]{0:T(128)} %dynamic_slice.22.len_ref, bf16[1024,256]{1,0:T(8,128)(2,1)S(1)} %fusion.7.q_ref.q1, bf16[1024,256]{1,0:T(8,128)(2,1)S(1)} %convolution_convert_fusion.4.k_ref.k1, bf16[1024,256]{1,0:T(8,128)(2,1)S(1)} %fusion.8.v_ref.v1), custom_call_target="tpu_custom_call" | custom-call | flops 4294967296 | bytes 2097152 | tf_op jit(solution)/shard_map/attend_forward/pallas_call | solution.py:83
  155.8 4.1 collective-permute-done.10
  166.2 17.0 %feed_forward.1 = (bf16[1024,1024]{1,0:T(8,128)(2,1)S(1)}, bf16[1024,1024]{1,0:T(8,128)(2,1)}, bf16[1024,1024]{1,0:T(8,128)(2,1)}, bf16[1024,1024]{1,0:T(8,128)(2,1)}, bf16[1024,1024]{1,0:T(8,128)(2,1)}) custom-call(bf16[1024,1024]{1,0:T(8,128)(2,1)} %get-tuple-element.130.rows_in, bf16[1024,1024]{1,0:T(8,128)(2,1)} %refs_2_.1, ...), custom_call_target="tpu_custom_call" | custom-call | flops 8589934592 | bytes 16777216 | tf_op jit(solution)/shard_map/feed_forward/pallas_call | solution.py:549
  184.5 4.5 collective-permute-done.12
  189.0 3.9 maximum_select_fusion.2.cot_ref
  192.9 21.4 %feed_backward.1 = (bf16[512,1024]{1,0:T(8,128)(2,1)}, bf16[1024,1024]{1,0:T(8,128)(2,1)}, f32[1024,1024]{1,0:T(8,128)}, bf16[1024,1024]{1,0:T(8,128)(2,1)}, f32...) custom-call(s32[1]{0:T(128)} %bitcast.core_ref, ...), custom_call_target="tpu_custom_call" | custom-call | flops 8589934592 | bytes 31457280 | tf_op jit(solution)/shard_map/feed_backward/pallas_call | solution.py:612
  214.6 5.4 convolution_convert_fusion.rest_3_
  222.8 5.4 convolution_convert_fusion.2.rest_1_
  228.2 3.8 convolution_convert_fusion.1.rest_2_
  232.0 3.7 convolution_convert_fusion.3.rest_0_
  236.8 4.2 multiply_reduce_fusion
  241.0 3.8 convert_reduce_fusion
  244.9 136.8 %cross_backward.1 = (bf16[1024,1024]{1,0:T(8,128)(2,1)}, bf16[512,1024]{1,0:T(8,128)(2,1)}, f32[2,8,256]{2,1,0:T(8,128)}, bf16[256,1024]{1,0:T(8,128)(2,1)}, bf1...) custom-call(s32[1]{0:T(128)} %dynamic_slice.22.len_ref, ...), custom_call_target="tpu_custom_call" | custom-call | flops 5368709120 | bytes 314572800 | tf_op jit(solution)/shard_map/cross_backward/pallas_call | solution.py:512
  381.7 4.8 multiply_reduce_fusion.1
  392.4 139.5 %self_backward.1 = (f32[512,1024]{1,0:T(8,128)}, bf16[256,1024]{1,0:T(8,128)(2,1)}, bf16[1024,256]{1,0:T(8,128)(2,1)}, bf16[2048,256]{1,0:T(8,128)(2,1)}, bf16[2...) custom-call(s32[1]{0:T(128)} %dynamic_slice.21.len_ref, ...), custom_call_target="tpu_custom_call" | custom-call | flops 5368709120 | bytes 314572800 | tf_op jit(solution)/shard_map/self_backward/pallas_call | solution.py:488
  (223 shorter events, 82.4 us)
Async XLA Ops:
  7.2 130.2 %all-gather.2.cloned.1.call-start = ((), (), s32[]{:S(2)}) async-start(), calls=%async_computation | async-start | bytes 4718592 | tf_op jit(solution)/shard_map/all_gather | solution.py:726
  7.2 6.6 %collective-permute-start = (bf16[512,1024]{1,0:T(8,128)(2,1)}, bf16[512,1024]{1,0:T(8,128)(2,1)S(1)}, u32[]{:S(2)}, u32[]{:S(2)}) collective-permute-start(bf16[512,1024]{1,0:T(8,128)(2,1)} %param.17), channel_id=1, source_target_pairs={{0,1},{1,0},{2,3},{3,2},{4,5},{5,4},{6,7},{7,6},{8,9},{9,8},{10,11... | collective-permute-start | bytes 3145736 | tf_op jit(solution)/shard_map/ppermute | solution.py:663
  9.1 4.7 collective-permute-start.2
  11.6 37.5 %collective-permute-start.1 = (bf16[3,1024,256]{2,1,0:T(8,128)(2,1)}, bf16[3,1024,256]{2,1,0:T(8,128)(2,1)}, u32[]{:S(2)}, u32[]{:S(2)}) collective-permute-start(bf16[3,1024,256]{2,1,0:T(8,128)(2,1)} %w0.1), channel_id=1, source_target_pairs={{2,0},{0,2},{3,1},{1,3},{6,4},{4,6},{7,5},{5,7},{10,8},{8,10},{11,... | collective-permute-start | bytes 4718600 | tf_op jit(solution)/shard_map/ppermute | solution.py:689
  16.5 89.1 %copy-start.30 = (bf16[1024,1024]{1,0:T(8,128)(2,1)}, bf16[1024,1024]{1,0:T(8,128)(2,1)S(1)}, u32[]{:S(2)}) copy-start(bf16[1024,1024]{1,0:T(8,128)(2,1)S(1)} %maximum_select_fusion.x_in) | copy-start | bytes 6291460
  26.3 24.7 %copy-start.17 = (f32[1024,128]{1,0:T(8,128)}, f32[1024,128]{1,0:T(8,128)S(1)}, u32[]{:S(2)}) copy-start(f32[1024,128]{1,0:T(8,128)S(1)} %get-tuple-element.93.l0) | copy-start | bytes 1572868
  26.3 37.4 %copy-start.2 = (bf16[1024,256]{1,0:T(8,128)(2,1)}, bf16[1024,256]{1,0:T(8,128)(2,1)S(1)}, u32[]{:S(2)}) copy-start(bf16[1024,256]{1,0:T(8,128)(2,1)S(1)} %get-tuple-element.65.o0) | copy-start | bytes 1572868
  27.8 35.7 %collective-permute-start.6 = (bf16[2,128,1024]{2,1,0:T(8,128)(2,1)S(1)}, bf16[2,128,1024]{2,1,0:T(8,128)(2,1)}, u32[]{:S(2)}, u32[]{:S(2)}) collective-permute-start(bf16[2,128,1024]{2,1,0:T(8,128)(2,1)S(1)} %pad_maximum_fusion), channel_id=1, source_target_pairs={{2,0},{0,2},{3,1},{1,3},{6,4},{4,6},{7,5},{5,7},{10,8},{8,10},{11,... | collective-permute-start | bytes 1572872 | tf_op jit(solution)/shard_map/ppermute | solution.py:721
  63.5 12.8 %collective-permute-start.3 = (bf16[256,1024]{1,0:T(8,128)(2,1)}, bf16[256,1024]{1,0:T(8,128)(2,1)S(1)}, u32[]{:S(2)}, u32[]{:S(2)}) collective-permute-start(bf16[256,1024]{1,0:T(8,128)(2,1)} %wo0.1), channel_id=1, source_target_pairs={{2,0},{0,2},{3,1},{1,3},{6,4},{4,6},{7,5},{5,7},{10,8},{8,10},{11,... | collective-permute-start | bytes 1572872 | tf_op jit(solution)/shard_map/ppermute | solution.py:689
  63.6 17.9 %collective-permute-start.5 = (bf16[512,1024]{1,0:T(8,128)(2,1)}, bf16[512,1024]{1,0:T(8,128)(2,1)S(1)}, u32[]{:S(2)}, u32[]{:S(2)}) collective-permute-start(bf16[512,1024]{1,0:T(8,128)(2,1)} %param.18), channel_id=1, source_target_pairs={{0,1},{1,0},{2,3},{3,2},{4,5},{5,4},{6,7},{7,6},{8,9},{9,8},{10,11... | collective-permute-start | bytes 3145736 | tf_op jit(solution)/shard_map/ppermute | solution.py:663
  77.9 27.6 %collective-permute-start.4 = (bf16[1024,1024]{1,0:T(8,128)(2,1)S(1)}, bf16[1024,1024]{1,0:T(8,128)(2,1)S(1)}, u32[]{:S(2)}, u32[]{:S(2)}) collective-permute-start(bf16[1024,1024]{1,0:T(8,128)(2,1)S(1)} %add_convert_fusion.1), channel_id=1, source_target_pairs={{0,1},{1,0},{2,3},{3,2},{4,5},{5,4},{6,7},{7,6},{8,9},{9,8},{10,11... | collective-permute-start | bytes 6291464 | tf_op jit(solution)/shard_map/ppermute | solution.py:663
  78.0 26.0 %collective-permute-start.8 = (bf16[2,1024,256]{2,1,0:T(8,128)(2,1)S(1)}, bf16[2,1024,256]{2,1,0:T(8,128)(2,1)S(1)}, u32[]{:S(2)}, u32[]{:S(2)}) collective-permute-start(bf16[2,1024,256]{2,1,0:T(8,128)(2,1)S(1)} %copy-done.45), channel_id=1, source_target_pairs={{2,0},{0,2},{3,1},{1,3},{6,4},{4,6},{7,5},{5,7},{10,8},{8,10},{11,... | collective-permute-start | bytes 3145736 | tf_op jit(solution)/shard_map/ppermute | solution.py:689
  79.5 62.7 %collective-permute-start.7 = (bf16[1024,256]{1,0:T(8,128)(2,1)}, bf16[1024,256]{1,0:T(8,128)(2,1)}, u32[]{:S(2)}, u32[]{:S(2)}) collective-permute-start(bf16[1024,256]{1,0:T(8,128)(2,1)} %wq0), channel_id=1, source_target_pairs={{2,0},{0,2},{3,1},{1,3},{6,4},{4,6},{7,5},{5,7},{10,8},{8,10},{11,... | collective-permute-start | bytes 1572872 | tf_op jit(solution)/shard_map/ppermute | solution.py:689
  80.8 72.7 %collective-permute-start.9 = (bf16[256,1024]{1,0:T(8,128)(2,1)}, bf16[256,1024]{1,0:T(8,128)(2,1)}, u32[]{:S(2)}, u32[]{:S(2)}) collective-permute-start(bf16[256,1024]{1,0:T(8,128)(2,1)} %wo0), channel_id=1, source_target_pairs={{2,0},{0,2},{3,1},{1,3},{6,4},{4,6},{7,5},{5,7},{10,8},{8,10},{11,... | collective-permute-start | bytes 1572872 | tf_op jit(solution)/shard_map/ppermute | solution.py:689
  82.6 22.2 %copy-start.33 = (bf16[1024,1024]{1,0:T(8,128)(2,1)}, bf16[1024,1024]{1,0:T(8,128)(2,1)S(1)}, u32[]{:S(2)}) copy-start(bf16[1024,1024]{1,0:T(8,128)(2,1)S(1)} %maximum_select_fusion.1.m_in) | copy-start | bytes 6291460
  83.3 28.5 %copy-start.4 = (bf16[1024,256]{1,0:T(8,128)(2,1)}, bf16[1024,256]{1,0:T(8,128)(2,1)S(1)}, u32[]{:S(2)}) copy-start(bf16[1024,256]{1,0:T(8,128)(2,1)S(1)} %convolution_convert_fusion.5.k_ref.k0) | copy-start | bytes 1572868
  84.0 27.8 %copy-start.5 = (bf16[1024,256]{1,0:T(8,128)(2,1)}, bf16[1024,256]{1,0:T(8,128)(2,1)S(1)}, u32[]{:S(2)}) copy-start(bf16[1024,256]{1,0:T(8,128)(2,1)S(1)} %fusion.6.v_ref.v0) | copy-start | bytes 1572868
  104.8 39.1 %copy-start.6 = (bf16[1024,256]{1,0:T(8,128)(2,1)}, bf16[1024,256]{1,0:T(8,128)(2,1)S(1)}, u32[]{:S(2)}) copy-start(bf16[1024,256]{1,0:T(8,128)(2,1)S(1)} %convolution_convert_fusion.4.k_ref.k1) | copy-start | bytes 1572868
  105.5 38.4 %copy-start.7 = (bf16[1024,256]{1,0:T(8,128)(2,1)}, bf16[1024,256]{1,0:T(8,128)(2,1)S(1)}, u32[]{:S(2)}) copy-start(bf16[1024,256]{1,0:T(8,128)(2,1)S(1)} %fusion.8.v_ref.v1) | copy-start | bytes 1572868
  155.7 4.2 collective-permute-start.10
  183.2 9.7 %collective-permute-start.11 = (bf16[1024,1024]{1,0:T(8,128)(2,1)S(1)}, bf16[1024,1024]{1,0:T(8,128)(2,1)}, u32[]{:S(2)}, u32[]{:S(2)}) collective-permute-start(bf16[1024,1024]{1,0:T(8,128)(2,1)S(1)} %get-tuple-element.78.part), channel_id=1, source_target_pairs={{0,1},{1,0},{2,3},{3,2},{4,5},{5,4},{6,7},{7,6},{8,9},{9,8},{10,11... | collective-permute-start | bytes 6291464 | tf_op jit(solution)/shard_map/ppermute | solution.py:663
  183.4 5.6 %collective-permute-start.12 = (bf16[512,1024]{1,0:T(8,128)(2,1)S(1)}, bf16[512,1024]{1,0:T(8,128)(2,1)}, u32[]{:S(2)}, u32[]{:S(2)}) collective-permute-start(bf16[512,1024]{1,0:T(8,128)(2,1)S(1)} %copy-done.42), channel_id=1, source_target_pairs={{0,1},{1,0},{2,3},{3,2},{4,5},{5,4},{6,7},{7,6},{8,9},{9,8},{10,11... | collective-permute-start | bytes 3145736 | tf_op jit(solution)/shard_map/ppermute | solution.py:663
  214.3 21.4 %collective-permute-start.13 = (bf16[1024,1024]{1,0:T(8,128)(2,1)}, bf16[1024,1024]{1,0:T(8,128)(2,1)}, u32[]{:S(2)}, u32[]{:S(2)}) collective-permute-start(bf16[1024,1024]{1,0:T(8,128)(2,1)} %get-tuple-element.84), channel_id=1, source_target_pairs={{0,1},{1,0},{2,3},{3,2},{4,5},{5,4},{6,7},{7,6},{8,9},{9,8},{10,11... | collective-permute-start | bytes 6291464 | tf_op jit(solution)/shard_map/ppermute | solution.py:663
  244.9 136.8 %copy-start.23 = (f32[1024,1024]{1,0:T(8,128)S(1)}, f32[1024,1024]{1,0:T(8,128)}, u32[]{:S(2)}) copy-start(f32[1024,1024]{1,0:T(8,128)} %copy-done.21) | copy-start | bytes 12582916
  (53 other events, 366.2 us)
Sparse Core Ops, SparseCore 0:
  63.6 73.6 all-gather.1

commit v9 on v8

--- a/solution.py
+++ b/solution.py
@@ -382,7 +382,7 @@
         out[pl.ds(first + i, bq), :] = tn(rows_in[:, i : i + bq], grads).astype(LOW)
 
 
-def share_rows(terms, core, part, got, sems, out, bq, pipe):
+def share_rows(terms, core, part, got, sems, out, bq, pipe, more):
     half = out.shape[0]
     copy = Pipeline.remote(part, got, sems[0], sems[1], {"c": 1 - core})
     for i in range(0, half, bq):
@@ -390,31 +390,64 @@
     copy.start()
     pipe.tick()
     mine = [back_rows(terms, core * half + i, bq) for i in range(0, half, bq)]
+    if more is not None:
+        mine = [rows + more(pl.ds(pl.multiple_of(core * half + at * bq, bq), bq)) for at, rows in enumerate(mine)]
     pipe.tick()
     copy.wait()
     for i in range(0, half, bq):
         out[pl.ds(i, bq), :] = (mine[i // bq] + got[pl.ds(i, bq), :].astype(F32)).astype(out.dtype)
 
 
-def self_back_kernel(carried, bq, len_ref, low, q0, k0, v0, o0, l0, q1, k1, v1, o1, l1, wo0, wo1, x_in, w0, w1, small0, small1, *rest):
+def norm_back(scale, grad_above, terms, unit_rows, inverse, gain, blocks, keep, low, sums, bq):
+    above, unit, sem = blocks
+    totals = None
+    for i in range(low.shape[0] // bq):
+        at = pl.ds(i * bq, bq)
+        loads = [pltpu.make_async_copy(grad_above.at[at, :], above, sem.at[0]), pltpu.make_async_copy(unit_rows.at[at, :], unit, sem.at[1])]
+        for load in loads:
+            load.start()
+        for load in loads:
+            load.wait()
+        incoming = scale * above[...] + terms(at)
+        grads = norm_backward(incoming, unit[...], inverse[at, :], gain[...])
+        low_rows = grads.astype(LOW)
+        low[at, :] = low_rows
+        keep(i, at, grads)
+        new = [jnp.sum(v, axis=0, keepdims=True) for v in (low_rows.astype(F32), incoming * unit[...], incoming)]
+        totals = new if totals is None else [x + y for x, y in zip(totals, new)]
+    for at, total in enumerate(totals):
+        sums[at : at + 1] = total
+
+
+def self_back_kernel(carried, bq, scale, len_ref, above_in, row_in, unit_in, inverse, gain, q0, k0, v0, o0, l0, q1, k1, v1, o1, l1, wo0, wo1, x_in, w0, w1, small0, small1, *rest):
     own, other, rest = rest[:carried], rest[carried : 2 * carried], rest[2 * carried :]
     token_out, rest = rest[0], rest[1:]
     outs, rest = rest[: carried + 3], rest[carried + 3 :]
-    gm, dq, dk, dv, dka, dva, go_own, go_other, gi_own, gi_other, sm_own, sm_other, part, got, part_send, part_recv = rest[:16]
+    gm, dq, dk, dv, dka, dva, go_own, go_other, gi_own, gi_other, sm_own, sm_other, part, got, part_send, part_recv, low, kept, sums, above, unit, loads = rest[:22]
     core = lax.axis_index("c")
     total = spot_count([ref.shape for ref in own] + [go_own.shape, sm_own.shape] + [(low.shape[1], gi_own.shape[1])] * 3, (carried + 4,))
-    pipe = Pipeline(total, rest[16:])
+    pipe = Pipeline(total, rest[22:])
     pipe.greet([{"c": 1 - core}])
     for a, b, out in zip(own, other, outs):
         pipe.add(a, b, out)
     shards = ((q0, k0, v0, o0, l0, wo0), (q1, k1, v1, o1, l1, wo1))
+
+    def keep(i, at, grads):
+        kept[at, :] = grads
+        pipe.tick()
+
+    norm_back(scale, above_in, lambda at: row_in[at, :].astype(F32), unit_in, inverse, gain, (above, unit, loads), keep, low, sums, bq)
     output_grads(shards, low, (go_own, go_other))
     pipe.add(go_own, go_other, outs[carried])
     attend_back(pipe, shards, len_ref[0], low, gm, dq, dk, dv, dka, dva, True, bq, 2)
     for s, (sm, small) in enumerate(((sm_own, small0), (sm_other, small1))):
         row = lax.broadcasted_iota(jnp.int32, sm.shape, 0)
-        sums = [jnp.sum(grads[s].astype(F32), axis=0, keepdims=True) for grads in (dq, dv)]
-        sm[...] = jnp.where(row == 9, sums[0], jnp.where(row == 10, sums[1], small[...])).astype(LOW)
+        shard = (pipe.seq + s) % 2 * 2 + core
+        mine = pl.ds(pl.multiple_of(shard * sm.shape[1], sm.shape[1]), sm.shape[1])
+        filled = small[...]
+        for at, value in ((0, sums[0:1, mine]), (3, sums[1:2, mine]), (6, sums[2:3, mine]), (9, jnp.sum(dq[s].astype(F32), axis=0, keepdims=True)), (10, jnp.sum(dv[s].astype(F32), axis=0, keepdims=True))):
+            filled = jnp.where(row == at, value, filled)
+        sm[...] = filled.astype(LOW)
     pipe.add(sm_own, sm_other, outs[carried + 2])
     model = x_in.shape[1]
     for m, grads in enumerate((dq, dk, dv)):
@@ -423,20 +456,32 @@
             pipe.tick()
         pipe.add(gi_own, gi_other, outs[carried + 1], m == 2, m * model, model)
     terms = [(grads, s, w[m]) for s, w in ((0, w0), (1, w1)) for m, grads in enumerate((dq, dk, dv))]
-    share_rows(terms, core, part, got, (part_send, part_recv), token_out, bq, pipe)
+    share_rows(terms, core, part, got, (part_send, part_recv), token_out, bq, pipe, lambda at: scale * kept[at, :])
     pipe.drain()
 
 
-def cross_back_kernel(carried, bq, len_ref, low, q0, k0, v0, o0, l0, q1, k1, v1, o1, l1, wo0, wo1, x_in, m_in, wq0, wq1, wm0, wm1, *rest):
+def cross_back_kernel(carried, bq, scale, len_ref, above_in, row_in, unit_in, inverse, gain, q0, k0, v0, o0, l0, q1, k1, v1, o1, l1, wo0, wo1, x_in, m_in, wq0, wq1, wm0, wm1, *rest):
     own, other, rest = rest[:carried], rest[carried : 2 * carried], rest[2 * carried :]
-    row_out, memory_out, sums_out, go_own, go_other, gq_own, gq_other, gm_own, gm_other = rest[:9]
-    outs, rest = rest[9 : 9 + carried], rest[9 + carried :]
-    gm, dq, dk, dv, dka, dva, part, got, part_send, part_recv, full_part, full_got, full_send, full_recv = rest[:14]
+    row_out, memory_out, sums_out, go_own, go_other, gq_own, gq_other, gm_own, gm_other, norm_sums, grad_out = rest[:11]
+    outs, rest = rest[11 : 11 + carried], rest[11 + carried :]
+    gm, dq, dk, dv, dka, dva, part, got, part_send, part_recv, full_part, full_got, full_send, full_recv, low, row_got, row_send, row_recv, above, unit, loads, stored = rest[:22]
     core = lax.axis_index("c")
-    pipe = Pipeline(spot_count([ref.shape for ref in own], (carried - 1,)), rest[14:])
+    pipe = Pipeline(spot_count([ref.shape for ref in own], (carried - 1,)), rest[22:])
     pipe.greet([{"c": 1 - core}])
+    rows_over = Pipeline.remote(row_in, row_got, row_send, row_recv, {"c": 1 - core})
+    rows_over.start()
     for at, (a, b, out) in enumerate(zip(own, other, outs)):
         pipe.add(a, b, out, at == carried - 1)
+    rows_over.wait()
+
+    def keep(i, at, grads):
+        above[...] = grads
+        copy = pltpu.make_async_copy(above, grad_out.at[at, :], stored)
+        copy.start()
+        pipe.tick()
+        copy.wait()
+
+    norm_back(scale, above_in, lambda at: row_in[at, :].astype(F32) + row_got[at, :].astype(F32), unit_in, inverse, gain, (above, unit, loads), keep, low, norm_sums, bq)
     shards = ((q0, k0, v0, o0, l0, wo0), (q1, k1, v1, o1, l1, wo1))
     attend_back(pipe, shards, len_ref[0], low, gm, dq, dk, dv, dka, dva, False, bq, 1)
     rows = low.shape[0]
@@ -449,7 +494,7 @@
     exchange.start()
     pipe.tick()
     terms = [(grads, s, w[m]) for s, w in ((0, wm0), (1, wm1)) for m, grads in enumerate((dk, dv))]
-    share_rows(terms, core, part, got, (part_send, part_recv), memory_out, bq, pipe)
+    share_rows(terms, core, part, got, (part_send, part_recv), memory_out, bq, pipe, None)
     output_grads(shards, low, (go_own, go_other))
     pipe.tick()
     for s, (gq, gkv) in enumerate(((gq_own, gm_own), (gq_other, gm_other))):
@@ -476,8 +521,8 @@
     return [low_ram(2, rows, width) for unused in range(4)] + [pltpu.VMEM((2, rows, 128), F32), pltpu.VMEM((2, rows, 128), F32)]
 
 
-def self_back(length, low, first, second, wo, x_in, w, smalls, pairs, bq=256):
-    rows, model = low.shape
+def self_back(length, above, row_part, unit, inverse, gain, first, second, wo, x_in, w, smalls, pairs, bq=256):
+    rows, model = above.shape
     width = wo[0].shape[0]
     carried = len(pairs)
     any_space = pl.BlockSpec(memory_space=pl.ANY)
@@ -486,22 +531,23 @@
     ends = [(width, model), (3 * rows, width), smalls[0].shape]
     total = spot_count([own.shape for own, unused in pairs] + [ends[0], ends[2]] + [(model, width)] * 3, (carried + 4,))
     return pl.pallas_call(
-        functools.partial(self_back_kernel, carried, bq),
-        out_shape=[jax.ShapeDtypeStruct((rows // 2, model), F32)] + [jax.ShapeDtypeStruct(own.shape, LOW) for own, unused in pairs] + [jax.ShapeDtypeStruct(shape, LOW) for shape in ends],
-        in_specs=[pl.BlockSpec(memory_space=pltpu.SMEM)] + [vmem] * 18 + [any_space] * (2 * carried),
+        functools.partial(self_back_kernel, carried, bq, residual_scale),
+        out_shape=[jax.ShapeDtypeStruct((rows // 2, model), LOW)] + [jax.ShapeDtypeStruct(own.shape, LOW) for own, unused in pairs] + [jax.ShapeDtypeStruct(shape, LOW) for shape in ends],
+        in_specs=[pl.BlockSpec(memory_space=pltpu.SMEM), any_space, vmem, any_space, vmem, vmem] + [vmem] * 17 + [any_space] * (2 * carried),
         out_specs=[vmem] + [any_space] * (carried + 3),
         scratch_shapes=back_scratch(rows, width)
         + [low_ram(width, model), low_ram(width, model), low_ram(3 * rows, width), low_ram(3 * rows, width), low_ram(*smalls[0].shape), low_ram(*smalls[0].shape)]
         + [low_ram(rows // 2, model), low_ram(rows // 2, model), dma, dma]
+        + [low_ram(rows, model), pltpu.VMEM((rows, model), F32), pltpu.VMEM((8, model), F32), pltpu.VMEM((bq, model), F32), pltpu.VMEM((bq, model), F32), dma((2,))]
         + Pipeline.scratch(total, CHUNK),
         compiler_params=pltpu.CompilerParams(collective_id=0, has_side_effects=True, vmem_limit_bytes=58 << 20),
         cost_estimate=pl.CostEstimate(flops=20 * rows * model * width, bytes_accessed=300 << 20, transcendentals=8 * rows * rows),
         name="self_backward",
-    )(length, low, *first, *second, *wo, x_in, *w, *smalls, *[p[0] for p in pairs], *[p[1] for p in pairs])
-
-
-def cross_back(length, low, first, second, wo, x_in, m_in, wq, wm, pairs, bq=256):
-    rows, model = low.shape
+    )(length, above, row_part, unit, inverse, gain, *first, *second, *wo, x_in, *w, *smalls, *[p[0] for p in pairs], *[p[1] for p in pairs])
+
+
+def cross_back(length, above, row_part, unit, inverse, gain, first, second, wo, x_in, m_in, wq, wm, pairs, bq=256):
+    rows, model = above.shape
     width = wo[0].shape[0]
     carried = len(pairs)
     any_space = pl.BlockSpec(memory_space=pl.ANY)
@@ -510,20 +556,21 @@
     total = spot_count([own.shape for own, unused in pairs], (carried - 1,))
     shape = jax.ShapeDtypeStruct
     return pl.pallas_call(
-        functools.partial(cross_back_kernel, carried, bq),
+        functools.partial(cross_back_kernel, carried, bq, residual_scale),
         out_shape=[shape((rows, model), LOW), shape((rows // 2, model), LOW), shape((2, 8, width), F32)]
-        + [shape((width, model), LOW)] * 2 + [shape((rows, width), LOW)] * 2 + [shape((2 * rows, width), LOW)] * 2
+        + [shape((width, model), LOW)] * 2 + [shape((rows, width), LOW)] * 2 + [shape((2 * rows, width), LOW)] * 2 + [shape((8, model), F32), shape((rows, model), F32)]
         + [shape(own.shape, LOW) for own, unused in pairs],
-        in_specs=[pl.BlockSpec(memory_space=pltpu.SMEM)] + [vmem] * 19 + [any_space] * (2 * carried),
-        out_specs=[vmem] * 9 + [any_space] * carried,
+        in_specs=[pl.BlockSpec(memory_space=pltpu.SMEM), any_space, vmem, any_space, vmem, vmem] + [vmem] * 18 + [any_space] * (2 * carried),
+        out_specs=[vmem] * 10 + [any_space] * (1 + carried),
         scratch_shapes=back_scratch(rows, width)
         + [low_ram(rows // 2, model), low_ram(rows // 2, model), dma, dma]
         + [low_ram(rows, model), low_ram(rows, model), dma, dma]
+        + [low_ram(rows, model), low_ram(rows, model), dma, dma, pltpu.VMEM((bq, model), F32), pltpu.VMEM((bq, model), F32), dma((2,)), dma]
         + Pipeline.scratch(total, CHUNK),
         compiler_params=pltpu.CompilerParams(collective_id=1, has_side_effects=True, vmem_limit_bytes=58 << 20),
         cost_estimate=pl.CostEstimate(flops=20 * rows * model * width, bytes_accessed=300 << 20, transcendentals=8 * rows * rows),
         name="cross_backward",
-    )(length, low, *first, *second, *wo, x_in, m_in, *wq, *wm, *[p[0] for p in pairs], *[p[1] for p in pairs])
+    )(length, above, row_part, unit, inverse, gain, *first, *second, *wo, x_in, m_in, *wq, *wm, *[p[0] for p in pairs], *[p[1] for p in pairs])
 
 
 def feed_kernel(count, rows_in, *refs):
@@ -746,8 +793,8 @@
     else:
         b_in = [part[4:].reshape(-1) for part in biases]
     b_proj = [part[:4] for part in biases]
-    w_self = spread(self_inputs, 2)
-    w_self_out = spread(after(self_output, token_all), 0)
+    slices = fetch_slices((feed_in, feed_out))
+    w_self = spread(after(self_inputs, token_all), 2)
     self_q, self_k, self_v, self_mixed, self_lse = [], [], [], [], []
     shards = range(len(w_self))
     for s in shards:
@@ -758,12 +805,12 @@
         self_mixed.append(mixed)
         self_lse.append(lse)
     first = self_mixed[0]
-    slices = fetch_slices([after(feed_in, first), after(feed_out, first)])
-    w_in, w_out = spread_wide((feed_in, feed_out), [[after(piece, self_mixed[-1]) for piece in got] for got in slices])
+    w_in, w_out = spread_wide((feed_in, feed_out), [[after(piece, first) for piece in got] for got in slices])
+    w_self_out = spread(after(self_output, self_q[0]), 0)
     memory_all = gather_rows(after(memory, first))
-    w_cross_mem = spread(after(cross_memory, self_q[-1]), 2)
-    w_cross_q = spread(after(cross_query, self_q[-1]), 1)
-    w_cross_out = spread(after(cross_output, self_q[-1]), 0)
+    w_cross_mem = spread(after(cross_memory, first), 2)
+    w_cross_q = spread(after(cross_query, first), 1)
+    w_cross_out = spread(after(cross_output, first), 0)
     cot_all = gather_rows(after(cotangent, self_mixed[-1]))
 
     cross_k = [_nn(memory_all, w_cross_mem[s][0]).astype(LOW) for s in shards]
@@ -799,10 +846,6 @@
         feed_sums = [jnp.sum(grad_pre[s].astype(F32), axis=0) for s in shards]
     feed_out_parts = parts_of([tn(hidden[s], low_three) for s in shards], 0)
     feed_in_parts = parts_of([tn(third, grad_pre[s]) for s in shards], 1)
-    grad_normed_two = residual_scale * grad_three + sum_all(row_part)
-    grad_two = norm_backward(grad_normed_two, unit_two, inverse_two, norm_gain[1])
-    low_two = grad_two.astype(LOW)
-
     def sums(rows):
         return jnp.sum(rows.astype(F32), axis=0)
 
@@ -810,13 +853,18 @@
         return [(part[0].astype(LOW), part[1].astype(LOW)) for part in parts]
 
     in_kernel = (zn, yn, gn, cn, width, joined) == (4, 2, 2, 2, SPAN, False)
+    if not in_kernel:
+        grad_normed_two = residual_scale * grad_three + sum_all(row_part)
+        grad_two = norm_backward(grad_normed_two, unit_two, inverse_two, norm_gain[1])
+        low_two = grad_two.astype(LOW)
+        sums_two = [sums(low_two), sums(grad_normed_two * unit_two), sums(grad_normed_two)]
     if in_kernel:
         per_shard = [(cross_q[s], cross_k[s], cross_v[s], cross_mixed[s], cross_lse[s]) for s in shards]
-        row_part, memory_part, cross_sums, go_own, go_other, gq_own, gq_other, gm_own, gm_other, feed_out_sum, feed_in_sum = cross_back(
-            memory_length, low_two, per_shard[0], per_shard[1], w_cross_out, second, memory_all, w_cross_q, w_cross_mem, low_pairs(feed_out_parts, feed_in_parts))
+        row_part, memory_part, cross_sums, go_own, go_other, gq_own, gq_other, gm_own, gm_other, sums_two, grad_two, feed_out_sum, feed_in_sum = cross_back(
+            memory_length, grad_three, row_part, unit_two, inverse_two, norm_gain[1:2], per_shard[0], per_shard[1], w_cross_out, second, memory_all, w_cross_q, w_cross_mem, low_pairs(feed_out_parts, feed_in_parts))
         cross_sums = [cross_sums[0, :2], cross_sums[1, :2]]
         grad_memory = memory_part
-        grad_normed_one = residual_scale * grad_two + row_part.astype(F32)
+        sums_one = [jnp.zeros_like(norm_gain[0])] * 3
     else:
         feed_out_sum, feed_in_sum = [sum_groups(send_home(part)) for part in (feed_out_parts, feed_in_parts)]
         grad_cross_mixed = [_nt(low_two, w_cross_out[s]).astype(LOW) for s in shards]
@@ -826,11 +874,12 @@
         cross_parts = [parts_of([tn(rows, grads[s]) for s in shards], 1) for rows, grads in ((second, cross_dq), (memory_all, cross_dk), (memory_all, cross_dv))]
         grad_memory = sum_own(sum(_nt(cross_dk[s], w_cross_mem[s][0]) + _nt(cross_dv[s], w_cross_mem[s][1]) for s in shards)).astype(LOW)
         cross_sums = parts_of([jnp.stack([sums(cross_dq[s]), sums(cross_dv[s])]) for s in shards], 1)
-    grad_one = norm_backward(grad_normed_one, unit_one, inverse_one, norm_gain[0])
-    low_one = grad_one.astype(LOW)
-
+    if not in_kernel:
+        grad_one = norm_backward(grad_normed_one, unit_one, inverse_one, norm_gain[0])
+        low_one = grad_one.astype(LOW)
+        sums_one = [sums(low_one), sums(grad_normed_one * unit_one), sums(grad_normed_one)]
     model = tokens.shape[1]
-    terms = jnp.stack([sums(low_one), sums(low_two), sums_three[0], sums(grad_normed_one * unit_one), sums(grad_normed_two * unit_two), sums_three[1], sums(grad_normed_one), sums(grad_normed_two), sums_three[2]])
+    terms = jnp.stack([norm_sums[at] for at in range(3) for norm_sums in (sums_one, sums_two, sums_three)])
     feed_sums = parts_of(feed_sums, 0)
     if not in_kernel:
         grad_self_mixed = [_nt(low_one, w_self_out[s]).astype(LOW) for s in shards]
@@ -848,13 +897,14 @@
     if in_kernel:
         per_shard = [(self_q[s], self_k[s], self_v[s], self_mixed[s], self_lse[s]) for s in shards]
         pairs = [(go_own, go_other), (gq_own, gq_other), (gm_own, gm_other)]
-        token_part, *sums_low = self_back(target_length, low_one, per_shard[0], per_shard[1], w_self_out, token_all, w_self, smalls, pairs)
+        grad_tokens, *sums_low = self_back(target_length, grad_two, row_part, unit_one, inverse_one, norm_gain[0:1], per_shard[0], per_shard[1], w_self_out, token_all, w_self, smalls, pairs)
     else:
         groups = [[cross_out_parts], cross_parts[:1], cross_parts[1:], [self_out_parts], [parts_of([tn(token_all, grads[s]) for s in shards], 1) for grads in (self_dq, self_dk, self_dv)], [smalls]]
         sums_low = [sum_groups(send_home([jnp.concatenate([part[k] for part in group]) for k in range(gn)])) for group in groups]
     cross_out_sum, cross_q_sum, cross_mem_sum, self_out_sum, self_in_sum, small = [rows.astype(F32) for rows in sums_low]
     feed_out_sum, feed_in_sum = feed_out_sum.astype(F32), feed_in_sum.astype(F32)
-    grad_tokens = (residual_scale * own_rows(grad_one) + token_part).astype(LOW)
+    if not in_kernel:
+        grad_tokens = (residual_scale * own_rows(grad_one) + token_part).astype(LOW)
     return (block_out, grad_tokens, grad_memory, self_in_sum.reshape(3, model, width), self_out_sum, cross_q_sum, cross_mem_sum.reshape(2, model, width), cross_out_sum, feed_in_sum, feed_out_sum, small[9:13], small[13:13 + feed_rows].reshape(-1), small[0:3], small[3:6], small[6:9])
 
 

time: 570 us -> 549 us (0.963)
  other arithmetic: 51.9 us -> 37.7 us
  Pallas kernels: 349 us -> 362 us
  waiting for transfers between devices: 69.8 us -> 57.7 us
    reduce_sum x4 -> x0, other arithmetic: 16.4 us -> none  [sums(): return jnp.sum(rows.astype(F32), axis=0)]
    pallas_call x2, Pallas kernels: 276 us -> 288 us  [the longest x1 144 us: cross_back(): pl.pallas_call(functools.partial(cross_back_kernel, carried, bq, residual...]
    all_gather x1, waiting for transfers between devices: 11 us -> 0.01 us  [spread_wide(): lax.all_gather(piece, ('z', 'y'), axis=1, tiled=True)]
  transfers between devices with their start and end apart: 15 -> 14, of which waited for: 6 -> 4; matrix products, arithmetic and copies ran while one was open for 11% -> 9% of each run, Pallas kernels for 6% -> 6%
where the time goes in v9:
time: 549 us; the launch traced here: 545 us
  Pallas kernels  362 us (66%)
  waiting for transfers between devices  57.7 us (11%)
  matrix products  38.2 us (7%)
  other arithmetic  37.7 us (7%)
  local copies, waits for them, and re-layouts  25.9 us (5%)
  between operations  15.4 us (3%)
  starting transfers between devices  8.37 us (2%)
    pallas_call x1, Pallas kernels, cross_back(): pl.pallas_call(functools.partial(cross_back_kernel, carried, bq, residual...  144 us
    pallas_call x1, Pallas kernels, self_back(): pl.pallas_call(functools.partial(self_back_kernel, carried, bq, residual_...  144 us
    ppermute x6, waiting for transfers between devices, spread(): lax.ppermute(shard, 'g', [((i + k) % gn, i) for i in range(gn)])  49.1 us
    pallas_call x4, Pallas kernels, attn_fwd(): pl.pallas_call(functools.partial(fwd_kernel, causal=causal, bq=bq), out_s...  35.2 us
    pallas_call x1, Pallas kernels, feed_backward(): pl.pallas_call(functools.partial(feed_back_kernel, count, residual_scale)...  21.6 us
    dot_general x16, matrix products, _nn(): lax.dot_general(a, b, (((1,), (0,)), ((), ())), preferred_element_type=jn...  21.5 us
    pallas_call x1, Pallas kernels, feed_forward(): pl.pallas_call(functools.partial(feed_kernel, count), grid=(rows // bq,),...  17 us
    dot_general x4, matrix products, tn(): lax.dot_general(rows, grads, (((0,), (0,)), ((), ())), preferred_element_...  16.8 us
  transfers between devices with their start and end apart: 14, of which 4 were waited for; matrix products, arithmetic and copies ran while one was open for 9% of the time, Pallas kernels for 6%

profile of v9, /device:TPU:0, one launch (start us, length us, event | category | flops | bytes accessed | tf_op | source)
XLA Modules:
  0.0 545.2 jit_solution(3947187802933696423)
XLA Ops:
  9.2 2.6 collective-permute-start.2
  14.3 2.6 maximum_select_fusion.x_in
  24.7 7.9 %attend_forward.4 = (bf16[1024,256]{1,0:T(8,128)(2,1)S(1)}, f32[1024,128]{1,0:T(8,128)S(1)}) custom-call(s32[1]{0:T(128)} %dynamic_slice.18.len_ref, bf16[1024,256]{1,0:T(8,128)(2,1)S(1)} %fusion.1.q_ref.q0, bf16[1024,256]{1,0:T(8,128)(2,1)S(1)} %convolution_convert_fusion.7.k_ref.k0, bf16[1024,256]{1,0:T(8,128)(2,1)S(1)} %fusion.2.v_ref.v0), custom_call_target="tpu_custom_call" | custom-call | flops 4294967296 | bytes 2097152 | tf_op jit(solution)/shard_map/attend_forward/pallas_call | solution.py:83
  34.7 27.7 %collective-permute-done.1.w1 = bf16[3,1024,256]{2,1,0:T(8,128)(2,1)} collective-permute-done((bf16[3,1024,256]{2,1,0:T(8,128)(2,1)}, bf16[3,1024,256]{2,1,0:T(8,128)(2,1)}, u32[]{:S(2)}, u32[]{:S(2)}) %collective-permute-start.1) | collective-permute-done | bytes 1572896 | tf_op jit(solution)/shard_map/ppermute | solution.py:736
  68.1 8.1 %attend_forward.5 = (bf16[1024,256]{1,0:T(8,128)(2,1)S(1)}, f32[1024,128]{1,0:T(8,128)S(1)}) custom-call(s32[1]{0:T(128)} %dynamic_slice.18.len_ref, bf16[1024,256]{1,0:T(8,128)(2,1)S(1)} %fusion.3.q_ref.q1, bf16[1024,256]{1,0:T(8,128)(2,1)S(1)} %convolution_convert_fusion.6.k_ref.k1, bf16[1024,256]{1,0:T(8,128)(2,1)S(1)} %fusion.4.v_ref.v1), custom_call_target="tpu_custom_call" | custom-call | flops 4294967296 | bytes 2097152 | tf_op jit(solution)/shard_map/attend_forward/pallas_call | solution.py:83
  82.8 21.4 %collective-permute-done.8.wm1 = bf16[2,1024,256]{2,1,0:T(8,128)(2,1)S(1)} collective-permute-done((bf16[2,1024,256]{2,1,0:T(8,128)(2,1)S(1)}, bf16[2,1024,256]{2,1,0:T(8,128)(2,1)S(1)}, u32[]{:S(2)}, u32[]{:S(2)}) %collective-permute-start.8) | collective-permute-done | bytes 1048608 | tf_op jit(solution)/shard_map/ppermute | solution.py:736
  110.2 3.2 fusion
  115.5 9.5 %attend_forward.6 = (bf16[1024,256]{1,0:T(8,128)(2,1)S(1)}, f32[1024,128]{1,0:T(8,128)S(1)}) custom-call(s32[1]{0:T(128)} %dynamic_slice.19.len_ref, bf16[1024,256]{1,0:T(8,128)(2,1)S(1)} %fusion.5.q_ref.q0, bf16[1024,256]{1,0:T(8,128)(2,1)S(1)} %convolution_convert_fusion.5.k_ref.k0, bf16[1024,256]{1,0:T(8,128)(2,1)S(1)} %fusion.6.v_ref.v0), custom_call_target="tpu_custom_call" | custom-call | flops 4294967296 | bytes 2097152 | tf_op jit(solution)/shard_map/attend_forward/pallas_call | solution.py:83
  125.8 2.7 fusion.29
  128.5 4.8 slice_bitcast_fusion
  135.1 9.7 %attend_forward.7 = (bf16[1024,256]{1,0:T(8,128)(2,1)S(1)}, f32[1024,128]{1,0:T(8,128)S(1)}) custom-call(s32[1]{0:T(128)} %dynamic_slice.19.len_ref, bf16[1024,256]{1,0:T(8,128)(2,1)S(1)} %fusion.7.q_ref.q1, bf16[1024,256]{1,0:T(8,128)(2,1)S(1)} %convolution_convert_fusion.4.k_ref.k1, bf16[1024,256]{1,0:T(8,128)(2,1)S(1)} %fusion.8.v_ref.v1), custom_call_target="tpu_custom_call" | custom-call | flops 4294967296 | bytes 2097152 | tf_op jit(solution)/shard_map/attend_forward/pallas_call | solution.py:83
  146.0 4.1 collective-permute-done.10
  152.1 4.8 fusion.20
  156.9 17.0 %feed_forward.1 = (bf16[1024,1024]{1,0:T(8,128)(2,1)S(1)}, bf16[1024,1024]{1,0:T(8,128)(2,1)}, bf16[1024,1024]{1,0:T(8,128)(2,1)}, bf16[1024,1024]{1,0:T(8,128)(2,1)}, bf16[1024,1024]{1,0:T(8,128)(2,1)}) custom-call(bf16[1024,1024]{1,0:T(8,128)(2,1)} %get-tuple-element.117.rows_in, bf16[1024,1024]{1,0:T(8,128)(2,1)} %refs_2_.1, ...), custom_call_target="tpu_custom_call" | custom-call | flops 8589934592 | bytes 16777216 | tf_op jit(solution)/shard_map/feed_forward/pallas_call | solution.py:596
  175.3 4.4 collective-permute-done.12
  179.7 3.9 maximum_select_fusion.2.cot_ref
  185.7 21.6 %feed_backward.1 = (bf16[512,1024]{1,0:T(8,128)(2,1)}, bf16[1024,1024]{1,0:T(8,128)(2,1)}, f32[1024,1024]{1,0:T(8,128)}, bf16[1024,1024]{1,0:T(8,128)(2,1)}, f32...) custom-call(s32[1]{0:T(128)} %bitcast.core_ref, ...), custom_call_target="tpu_custom_call" | custom-call | flops 8589934592 | bytes 31457280 | tf_op jit(solution)/shard_map/feed_backward/pallas_call | solution.py:659
  207.3 5.5 %convolution_convert_fusion.rest_3_ = bf16[1024,1024]{1,0:T(8,128)(2,1)} fusion(bf16[1024,1024]{1,0:T(8,128)(2,1)S(1)} %copy-done.34, bf16[1024,1024]{1,0:T(8,128)(2,1)} %get-tuple-element.91), kind=kOutput, calls=%fused_computation.16 | convolution fusion | flops 2148532224 | bytes 6291456 | tf_op jit(solution)/shard_map/dot_general | solution.py:683
  212.9 3.7 convolution_convert_fusion.2.rest_1_
  216.6 3.8 convolution_convert_fusion.1.rest_2_
  220.4 3.7 convolution_convert_fusion.3.rest_0_
  224.1 144.3 %cross_backward.1 = (bf16[1024,1024]{1,0:T(8,128)(2,1)}, bf16[512,1024]{1,0:T(8,128)(2,1)}, f32[2,8,256]{2,1,0:T(8,128)}, bf16[256,1024]{1,0:T(8,128)(2,1)}, bf1...) custom-call(s32[1]{0:T(128)} %dynamic_slice.19.len_ref, ...), custom_call_target="tpu_custom_call" | custom-call | flops 5368709120 | bytes 314572800 | tf_op jit(solution)/shard_map/cross_backward/pallas_call | solution.py:558
  374.3 143.8 %self_backward.1 = (bf16[512,1024]{1,0:T(8,128)(2,1)}, bf16[256,1024]{1,0:T(8,128)(2,1)}, bf16[1024,256]{1,0:T(8,128)(2,1)}, bf16[2048,256]{1,0:T(8,128)(2,1)}, ...) custom-call(s32[1]{0:T(128)} %dynamic_slice.18.len_ref, ...), custom_call_target="tpu_custom_call" | custom-call | flops 5368709120 | bytes 314572800 | tf_op jit(solution)/shard_map/self_backward/pallas_call | solution.py:533
  521.6 3.4 convert.10
  (217 shorter events, 65.5 us)
Async XLA Ops:
  7.2 121.3 %all-gather.2.cloned.1.call-start = ((), (), s32[]{:S(2)}) async-start(), calls=%async_computation | async-start | bytes 4718592 | tf_op jit(solution)/shard_map/all_gather | solution.py:773
  7.3 7.1 %collective-permute-start = (bf16[512,1024]{1,0:T(8,128)(2,1)}, bf16[512,1024]{1,0:T(8,128)(2,1)}, u32[]{:S(2)}, u32[]{:S(2)}) collective-permute-start(bf16[512,1024]{1,0:T(8,128)(2,1)} %param.17), channel_id=1, source_target_pairs={{0,1},{1,0},{2,3},{3,2},{4,5},{5,4},{6,7},{7,6},{8,9},{9,8},{10,11... | collective-permute-start | bytes 3145736 | tf_op jit(solution)/shard_map/ppermute | solution.py:710
  9.2 24.3 %collective-permute-start.2 = (bf16[8,256]{1,0:T(8,128)(2,1)S(1)}, bf16[8,256]{1,0:T(8,128)(2,1)S(1)}, u32[]{:S(2)}, u32[]{:S(2)}) collective-permute-start(bf16[8,256]{1,0:T(8,128)(2,1)S(1)} %pad_maximum_fusion.4), channel_id=1, source_target_pairs={{2,0},{0,2},{3,1},{1,3},{6,4},{4,6},{7,5},{5,7},{10,8},{8,10},{11,... | collective-permute-start | bytes 12296 | tf_op jit(solution)/shard_map/ppermute | solution.py:736
  13.6 19.8 %collective-permute-start.6 = (bf16[2,128,1024]{2,1,0:T(8,128)(2,1)}, bf16[2,128,1024]{2,1,0:T(8,128)(2,1)}, u32[]{:S(2)}, u32[]{:S(2)}) collective-permute-start(bf16[2,128,1024]{2,1,0:T(8,128)(2,1)} %pad_maximum_fusion), channel_id=1, source_target_pairs={{2,0},{0,2},{3,1},{1,3},{6,4},{4,6},{7,5},{5,7},{10,8},{8,10},{11,... | collective-permute-start | bytes 1572872 | tf_op jit(solution)/shard_map/ppermute | solution.py:768
  16.9 49.2 %copy-start.21 = (bf16[1024,1024]{1,0:T(8,128)(2,1)}, bf16[1024,1024]{1,0:T(8,128)(2,1)S(1)}, u32[]{:S(2)}) copy-start(bf16[1024,1024]{1,0:T(8,128)(2,1)S(1)} %maximum_select_fusion.x_in) | copy-start | bytes 6291460
  16.9 45.5 %collective-permute-start.1 = (bf16[3,1024,256]{2,1,0:T(8,128)(2,1)}, bf16[3,1024,256]{2,1,0:T(8,128)(2,1)}, u32[]{:S(2)}, u32[]{:S(2)}) collective-permute-start(bf16[3,1024,256]{2,1,0:T(8,128)(2,1)} %w0), channel_id=1, source_target_pairs={{2,0},{0,2},{3,1},{1,3},{6,4},{4,6},{7,5},{5,7},{10,8},{8,10},{11,... | collective-permute-start | bytes 4718600 | tf_op jit(solution)/shard_map/ppermute | solution.py:736
  33.5 42.8 %collective-permute-start.3 = (bf16[256,1024]{1,0:T(8,128)(2,1)S(1)}, bf16[256,1024]{1,0:T(8,128)(2,1)S(1)}, u32[]{:S(2)}, u32[]{:S(2)}) collective-permute-start(bf16[256,1024]{1,0:T(8,128)(2,1)S(1)} %copy-done.33), channel_id=1, source_target_pairs={{2,0},{0,2},{3,1},{1,3},{6,4},{4,6},{7,5},{5,7},{10,8},{8,10},{11,... | collective-permute-start | bytes 1572872 | tf_op jit(solution)/shard_map/ppermute | solution.py:736
  34.0 47.0 %collective-permute-start.5 = (bf16[512,1024]{1,0:T(8,128)(2,1)}, bf16[512,1024]{1,0:T(8,128)(2,1)S(1)}, u32[]{:S(2)}, u32[]{:S(2)}) collective-permute-start(bf16[512,1024]{1,0:T(8,128)(2,1)} %param.18), channel_id=1, source_target_pairs={{0,1},{1,0},{2,3},{3,2},{4,5},{5,4},{6,7},{7,6},{8,9},{9,8},{10,11... | collective-permute-start | bytes 3145736 | tf_op jit(solution)/shard_map/ppermute | solution.py:710
  77.4 28.9 %collective-permute-start.4 = (bf16[1024,1024]{1,0:T(8,128)(2,1)S(1)}, bf16[1024,1024]{1,0:T(8,128)(2,1)S(1)}, u32[]{:S(2)}, u32[]{:S(2)}) collective-permute-start(bf16[1024,1024]{1,0:T(8,128)(2,1)S(1)} %add_convert_fusion.1), channel_id=1, source_target_pairs={{0,1},{1,0},{2,3},{3,2},{4,5},{5,4},{6,7},{7,6},{8,9},{9,8},{10,11... | collective-permute-start | bytes 6291464 | tf_op jit(solution)/shard_map/ppermute | solution.py:710
  78.1 26.0 %collective-permute-start.8 = (bf16[2,1024,256]{2,1,0:T(8,128)(2,1)S(1)}, bf16[2,1024,256]{2,1,0:T(8,128)(2,1)S(1)}, u32[]{:S(2)}, u32[]{:S(2)}) collective-permute-start(bf16[2,1024,256]{2,1,0:T(8,128)(2,1)S(1)} %copy-done.38), channel_id=1, source_target_pairs={{2,0},{0,2},{3,1},{1,3},{6,4},{4,6},{7,5},{5,7},{10,8},{8,10},{11,... | collective-permute-start | bytes 3145736 | tf_op jit(solution)/shard_map/ppermute | solution.py:736
  78.8 71.4 %copy-start.47 = (f32[1,1024]{1,0:T(1,128)}, f32[1,1024]{1,0:T(1,128)S(1)}, u32[]{:S(2)}) copy-start(f32[1,1024]{1,0:T(1,128)S(1)} %get-tuple-element.143.gain) | copy-start | bytes 12292
  78.8 73.3 %copy-start.48 = (f32[1,1024]{1,0:T(1,128)}, f32[1,1024]{1,0:T(1,128)S(1)}, u32[]{:S(2)}) copy-start(f32[1,1024]{1,0:T(1,128)S(1)} %get-tuple-element.144.gain) | copy-start | bytes 12292
  78.8 54.5 %collective-permute-start.7 = (bf16[1024,256]{1,0:T(8,128)(2,1)S(1)}, bf16[1024,256]{1,0:T(8,128)(2,1)}, u32[]{:S(2)}, u32[]{:S(2)}) collective-permute-start(bf16[1024,256]{1,0:T(8,128)(2,1)S(1)} %copy-done.43), channel_id=1, source_target_pairs={{2,0},{0,2},{3,1},{1,3},{6,4},{4,6},{7,5},{5,7},{10,8},{8,10},{11,... | collective-permute-start | bytes 1572872 | tf_op jit(solution)/shard_map/ppermute | solution.py:736
  80.9 63.9 %collective-permute-start.9 = (bf16[256,1024]{1,0:T(8,128)(2,1)S(1)}, bf16[256,1024]{1,0:T(8,128)(2,1)S(1)}, u32[]{:S(2)}, u32[]{:S(2)}) collective-permute-start(bf16[256,1024]{1,0:T(8,128)(2,1)S(1)} %copy-done.29), channel_id=1, source_target_pairs={{2,0},{0,2},{3,1},{1,3},{6,4},{4,6},{7,5},{5,7},{10,8},{8,10},{11,... | collective-permute-start | bytes 1572872 | tf_op jit(solution)/shard_map/ppermute | solution.py:736
  82.0 23.6 %copy-start.25 = (bf16[1024,1024]{1,0:T(8,128)(2,1)}, bf16[1024,1024]{1,0:T(8,128)(2,1)S(1)}, u32[]{:S(2)}) copy-start(bf16[1024,1024]{1,0:T(8,128)(2,1)S(1)} %maximum_select_fusion.1.m_in) | copy-start | bytes 6291460
  82.7 32.7 %copy-start.4 = (bf16[1024,256]{1,0:T(8,128)(2,1)}, bf16[1024,256]{1,0:T(8,128)(2,1)S(1)}, u32[]{:S(2)}) copy-start(bf16[1024,256]{1,0:T(8,128)(2,1)S(1)} %convolution_convert_fusion.5.k_ref.k0) | copy-start | bytes 1572868
  104.8 30.2 %copy-start.5 = (bf16[1024,256]{1,0:T(8,128)(2,1)}, bf16[1024,256]{1,0:T(8,128)(2,1)S(1)}, u32[]{:S(2)}) copy-start(bf16[1024,256]{1,0:T(8,128)(2,1)S(1)} %convolution_convert_fusion.4.k_ref.k1) | copy-start | bytes 1572868
  106.3 28.8 %copy-start.7 = (bf16[1024,256]{1,0:T(8,128)(2,1)}, bf16[1024,256]{1,0:T(8,128)(2,1)S(1)}, u32[]{:S(2)}) copy-start(bf16[1024,256]{1,0:T(8,128)(2,1)S(1)} %fusion.8.v_ref.v1) | copy-start | bytes 1572868
  145.9 4.2 collective-permute-start.10
  173.9 11.8 %collective-permute-start.11 = (bf16[1024,1024]{1,0:T(8,128)(2,1)S(1)}, bf16[1024,1024]{1,0:T(8,128)(2,1)}, u32[]{:S(2)}, u32[]{:S(2)}) collective-permute-start(bf16[1024,1024]{1,0:T(8,128)(2,1)S(1)} %get-tuple-element.78.part), channel_id=1, source_target_pairs={{0,1},{1,0},{2,3},{3,2},{4,5},{5,4},{6,7},{7,6},{8,9},{9,8},{10,11... | collective-permute-start | bytes 6291464 | tf_op jit(solution)/shard_map/ppermute | solution.py:710
  174.1 5.7 %collective-permute-start.12 = (bf16[512,1024]{1,0:T(8,128)(2,1)S(1)}, bf16[512,1024]{1,0:T(8,128)(2,1)}, u32[]{:S(2)}, u32[]{:S(2)}) collective-permute-start(bf16[512,1024]{1,0:T(8,128)(2,1)S(1)} %copy-done.37), channel_id=1, source_target_pairs={{0,1},{1,0},{2,3},{3,2},{4,5},{5,4},{6,7},{7,6},{8,9},{9,8},{10,11... | collective-permute-start | bytes 3145736 | tf_op jit(solution)/shard_map/ppermute | solution.py:710
  185.7 21.6 %copy-start.34 = (bf16[1024,1024]{1,0:T(8,128)(2,1)S(1)}, bf16[1024,1024]{1,0:T(8,128)(2,1)}, u32[]{:S(2)}) copy-start(bf16[1024,1024]{1,0:T(8,128)(2,1)} %get-tuple-element.117.rows_in) | copy-start | bytes 6291460
  224.1 147.3 %copy-start.55 = (f32[1,1024]{1,0:T(1,128)S(1)}, f32[1,1024]{1,0:T(1,128)}, u32[]{:S(2)}) copy-start(f32[1,1024]{1,0:T(1,128)} %get-tuple-element.99) | copy-start | bytes 12292
  224.1 147.9 %copy-start.54 = (f32[1,1024]{1,0:T(1,128)S(1)}, f32[1,1024]{1,0:T(1,128)}, u32[]{:S(2)}) copy-start(f32[1,1024]{1,0:T(1,128)} %get-tuple-element.100) | copy-start | bytes 12292
  (52 other events, 209.6 us)
Sparse Core Ops, SparseCore 0:
  33.6 73.7 all-gather.1
